TPU v7x, 32 devices: a whole 2x2x4 slice. The times are simulated.
32 devices in a mesh: lev: 4 (over z), lat: 4 (over y, core), lon: 2 (over x).
Axes of the slice: x: 2, y: 2, z: 4, core: 2. Of those that a mesh axis runs over, the one named last changes fastest.
Arguments:
- latent: bfloat16 [256, 128, 256], P(None, 'lat', 'lon'), may hold values from -6 to 6
- conv_weight: bfloat16 [16, 128, 9, 256], P('lev'), may hold values from -0.125 to 0.125
- mid_weight: bfloat16 [16, 128, 128], P('lev'), may hold values from -0.5 to 0.5
- out_weight: bfloat16 [16, 48, 128], P('lev'), may hold values from -0.5 to 0.5
- vertical_inner_matrix: bfloat16 [1024, 768], replicated, may hold values from -0.21875 to 0.21875
- vertical_outer_matrix: bfloat16 [768, 1024], replicated, may hold values from -0.1875 to 0.1875
- obs_values: float32 [4, 2, 256, 768], P('lat', 'lon'), may hold values from -6 to 6
- obs_weight: float32 [768], replicated, may hold values from 0.25 to 4
- obs_index: int32 [4, 2, 256], P('lat', 'lon'), may hold values from 0 to 4095
- obs_count: int32 [4, 2], P('lat', 'lon'), may hold values from 64 to 256
Outputs:
- latent_grad: float32 [256, 128, 256], P('lev', 'lat', 'lon')
Inputs may be any that keep to these rules, and one draw needn't show every extreme that they name: `obs_index`: row-major index of a cell within its tile of 32 x 128 cells; indices may repeat. `obs_count`: slots from this number on hold no observation.
All inputs are finite; a program needn't handle non-finite values.
Results may differ from a plain program's by a relative error of at most 0.007.
Values may be sent and summed in bfloat16 or wider, within the bound.
No kernel may reach another device: no remote copies, remote signals or barrier semaphores. Data moves between devices by JAX's collectives and lax.ppermute only.
A program may use at most 192 MiB of HBM per device.

v0:
```python
import functools

import jax
import jax.numpy as jnp
from jax import lax
from jax.experimental import pallas as pl
from jax.experimental.pallas import tpu as pltpu
from jax.sharding import PartitionSpec as P

KAPPA = 0.7978845608028654
CUBIC = 0.044715
F32 = jnp.float32
BF16 = jnp.bfloat16


def gelu(pre):
    tanh_v = jnp.tanh(KAPPA * (pre + CUBIC * pre * pre * pre))
    return 0.5 * pre * (1.0 + tanh_v)


def gelu_slope(pre):
    square = pre * pre
    tanh_v = jnp.tanh(KAPPA * (pre + CUBIC * square * pre))
    value = 0.5 * pre * (1.0 + tanh_v)
    slope = 0.5 * (1.0 + tanh_v) + 0.5 * pre * (1.0 - tanh_v * tanh_v) * KAPPA * (
        1.0 + 3.0 * CUBIC * square
    )
    return value, slope


def nn(a, b):
    return lax.dot_general(a, b, (((1,), (0,)), ((), ())), preferred_element_type=F32)


def nt(a, b):
    return lax.dot_general(a, b, (((1,), (1,)), ((), ())), preferred_element_type=F32)


def tn(a, b):
    return lax.dot_general(a, b, (((0,), (0,)), ((), ())), preferred_element_type=F32)


def call(kernel, out_shape, in_specs, flops, **kwargs):
    bytes_out = sum(s.size * s.dtype.itemsize for s in jax.tree.leaves(out_shape))
    return pl.pallas_call(
        kernel,
        out_shape=out_shape,
        in_specs=in_specs,
        out_specs=jax.tree.map(lambda _: VM, out_shape),
        cost_estimate=pl.CostEstimate(
            flops=flops, bytes_accessed=4 * bytes_out, transcendentals=0
        ),
        **kwargs,
    )


VM = pl.BlockSpec(memory_space=pltpu.VMEM)
SM = pl.BlockSpec(memory_space=pltpu.SMEM)


def own_kernel(idx_ref, table_ref, valid_ref, w_ref, out_ref, x_ref):
    taps, slots = idx_ref.shape

    def body(i, carry):
        base = pl.multiple_of(i * 8, 8)
        for t in range(taps):
            for j in range(8):
                row = idx_ref[t, base + j]
                x_ref[t, pl.ds(base + j, 1), :] = table_ref[pl.ds(row, 1), :]
        return carry

    lax.fori_loop(0, slots // 8, body, 0)
    acc = None
    for t in range(taps):
        x = (x_ref[t] * valid_ref[:, t : t + 1]).astype(BF16)
        part = nt(w_ref[t], x)
        acc = part if acc is None else acc + part
    out_ref[...] = acc


def decode_kernel(
    idx_ref, pre_ref, halo_ref, w_ref, mid_ref, outw_ref, one_ref, two_ref, field_ref
):
    taps, slots = idx_ref.shape
    groups, hidden, _ = mid_ref.shape
    levels = outw_ref.shape[1]
    width = halo_ref.shape[1]
    acc = pre_ref[...]
    cells = lax.broadcasted_iota(jnp.int32, (width, slots), 0)
    for t in range(taps):
        hot = (cells == idx_ref[t : t + 1, :]).astype(F32).astype(BF16)
        x = nn(halo_ref[...], hot).astype(BF16)
        acc = acc + nn(w_ref[t], x)
    one_ref[...] = acc
    act = gelu(acc).astype(BF16)
    for g in range(groups):
        two = nn(mid_ref[g], act[g * hidden : (g + 1) * hidden])
        two_ref[g * hidden : (g + 1) * hidden, :] = two
        field_ref[g * levels : (g + 1) * levels, :] = nn(
            outw_ref[g], gelu(two).astype(BF16)
        ).astype(BF16)


def slope_kernel(one_ref, two_ref, s1_ref, s2_ref):
    s1_ref[...] = gelu_slope(one_ref[...])[1]
    s2_ref[...] = gelu_slope(two_ref[...])[1]


def column_kernel(
    lev_count,
    lev_ref,
    inner_ref,
    inner_own_ref,
    outer_ref,
    obs_ref,
    weight_ref,
    live_ref,
    s1_ref,
    s2_ref,
    w_ref,
    mid_ref,
    outw_ref,
    *rest,
):
    blocks = rest[:lev_count]
    outs = rest[lev_count : 2 * lev_count]
    f_ref, mis_ref, g_ref = rest[2 * lev_count :]
    lev = lev_ref[0]
    own = blocks[0].shape[0]
    for k in range(lev_count):
        at = pl.multiple_of(lax.rem(lev + k, lev_count) * own, 16)
        f_ref[pl.ds(at, own), :] = blocks[k][...]
    pre_col = nn(inner_ref[...], f_ref[...])
    act, slope = gelu_slope(pre_col)
    forecast = f_ref[...].astype(F32) + nn(outer_ref[...], act.astype(BF16))
    misfit = (forecast - obs_ref[...]) * live_ref[...] * weight_ref[...]
    mis_ref[...] = misfit
    grad_act = (tn(outer_ref[...], misfit.astype(BF16)) * slope).astype(BF16)
    mine = mis_ref[pl.ds(pl.multiple_of(lev * own, 16), own), :]
    grad_fields = (mine + nn(inner_own_ref[...], grad_act)).astype(BF16)
    groups, hidden, _ = mid_ref.shape
    levels = outw_ref.shape[1]
    ones = []
    for g in range(groups):
        span = slice(g * hidden, (g + 1) * hidden)
        two = (
            tn(outw_ref[g], grad_fields[g * levels : (g + 1) * levels]) * s2_ref[span, :]
        ).astype(BF16)
        ones.append((tn(mid_ref[g], two) * s1_ref[span, :]).astype(BF16))
    grad_one = jnp.concatenate(ones, 0)
    taps = w_ref.shape[0]
    portion = w_ref.shape[2] // lev_count
    for t in range(taps):
        patch = tn(w_ref[t], grad_one).astype(BF16)
        for d in range(lev_count):
            g_ref[d, t] = patch[d * portion : (d + 1) * portion]
    for k in range(lev_count):
        outs[k][...] = g_ref[lax.rem(lev + k, lev_count)]


def edge_kernel(rows, cols, row_ref, col_ref, rowc_ref, colc_ref, *rest):
    blocks, (sum_ref, rowout_ref, colout_ref) = rest[:-3], rest[-3:]
    total = blocks[0][...].astype(F32)
    for block in blocks[1:]:
        total = total + block[...].astype(F32)
    sum_ref[...] = total
    slots = row_ref.shape[1]
    wide = colout_ref.shape[2]
    row, col, rowc, colc = row_ref[...], col_ref[...], rowc_ref[...], colc_ref[...]
    cells = lax.broadcasted_iota(jnp.int32, (slots, cols), 1)
    lines = lax.broadcasted_iota(jnp.int32, (slots, wide), 1)
    for e, (edge, a) in enumerate(((0, 0), (rows - 1, 2))):
        acc = None
        for b in range(3):
            part = jnp.where(row == edge, total[3 * a + b], 0.0).astype(BF16)
            hot = (colc + (b - 1) == cells).astype(F32).astype(BF16)
            part = nn(part, hot)
            acc = part if acc is None else acc + part
        rowout_ref[e] = acc
    for e, (edge, b) in enumerate(((0, 0), (cols - 1, 2))):
        acc = None
        for a in range(3):
            part = jnp.where(col == edge, total[3 * a + b], 0.0).astype(BF16)
            hot = (rowc + a == lines).astype(F32).astype(BF16)
            part = nn(part, hot)
            acc = part if acc is None else acc + part
        colout_ref[e] = acc


def scatter_kernel(rows, cols, lev_ref, row_ref, colc_ref, sum_ref, own_ref, out_ref):
    slots = row_ref.shape[1]
    portion = out_ref.shape[0]
    cells = lax.broadcasted_iota(jnp.int32, (slots, cols), 1)
    hots = [(colc_ref[...] + (b - 1) == cells).astype(F32).astype(BF16) for b in range(3)]
    lines = lax.broadcasted_iota(jnp.int32, (rows, slots), 0)
    masks = [row_ref[...] + (a - 1) == lines for a in range(3)]
    step = 8
    for c0 in range(0, portion, step):
        acc = None
        for b in range(3):
            parts = []
            for c in range(c0, c0 + step):
                part = jnp.zeros((rows, slots), F32)
                for a in range(3):
                    line = jnp.broadcast_to(sum_ref[3 * a + b, c : c + 1, :], (rows, slots))
                    part = jnp.where(masks[a], line, part)
                parts.append(part.astype(BF16))
            part = nn(jnp.concatenate(parts, 0), hots[b])
            acc = part if acc is None else acc + part
        out_ref[c0 : c0 + step] = (
            acc.reshape(step, rows, cols) + own_ref[c0 : c0 + step].astype(F32)
        )


def shift(x, axis, by, wrap=True):
    size = lax.axis_size(axis)
    pairs = [(i, (i + by) % size) for i in range(size) if wrap or 0 <= i + by < size]
    return lax.ppermute(x, axis, pairs)


def swap_sides(first, last, axis):
    size = lax.axis_size(axis)
    if size == 2:
        both = shift(jnp.stack([first, last]), axis, 1)
        return both[0], both[1]
    return shift(first, axis, -1), shift(last, axis, 1)


def per_device(
    latent,
    conv_weight,
    mid_weight,
    out_weight,
    inner,
    outer,
    obs_values,
    obs_weight,
    obs_index,
    obs_count,
):
    chans, rows, cols = latent.shape
    groups, hidden, taps, _ = conv_weight.shape
    levels = out_weight.shape[1]
    slots = obs_index.shape[-1]
    own = groups * levels
    lev = lax.axis_index("lev")
    lev_count = lax.axis_size("lev")
    lev_arr = lev.reshape(1).astype(jnp.int32)
    portion = chans // lev_count

    above = shift(latent[:, rows - 1, :], "lat", 1, wrap=False)
    below = shift(latent[:, 0, :], "lat", -1, wrap=False)

    def column(at):
        return jnp.concatenate([above[:, at : at + 1], latent[:, :, at], below[:, at : at + 1]], 1)

    right, left = swap_sides(column(0), column(cols - 1), "lon")
    width = -(-(2 * cols + 2 * (rows + 2)) // 128) * 128
    halo = jnp.concatenate(
        [
            above,
            below,
            left,
            right,
            jnp.zeros((chans, width - 2 * cols - 2 * (rows + 2)), latent.dtype),
        ],
        1,
    )

    index = obs_index[0, 0]
    row, col = index // cols, index % cols
    at_row = row[None, :] + jnp.arange(3, dtype=jnp.int32).repeat(3)[:, None] - 1
    at_col = col[None, :] + jnp.tile(jnp.arange(3, dtype=jnp.int32), 3)[:, None] - 1
    in_row = (at_row >= 0) & (at_row < rows)
    in_col = (at_col >= 0) & (at_col < cols)
    inside = in_row & in_col
    cell = jnp.where(inside, at_row * cols + at_col, 0).astype(jnp.int32)
    rim = jnp.where(at_row < 0, at_col, cols + at_col)
    rim = jnp.where(at_col < 0, 2 * cols + at_row + 1, rim)
    rim = jnp.where(at_col >= cols, 2 * cols + rows + 2 + at_row + 1, rim)
    rim = jnp.where(inside, -1, rim).astype(jnp.int32)
    valid = inside.T.astype(F32)
    live = (jnp.arange(slots, dtype=jnp.int32) < obs_count[0, 0]).astype(F32)[None, :]

    table = jnp.transpose(latent, (1, 2, 0)).reshape(rows * cols, chans).astype(F32)
    w = jnp.transpose(conv_weight, (2, 0, 1, 3)).reshape(taps, groups * hidden, chans)
    wide = groups * hidden
    flops = 2 * taps * wide * chans * slots
    pre_own = call(
        own_kernel,
        jax.ShapeDtypeStruct((wide, slots), F32),
        [SM, VM, VM, VM],
        flops * 2,
        scratch_shapes=[pltpu.VMEM((taps, slots, chans), F32)],
    )(cell, table, valid, w)
    act_shape = jax.ShapeDtypeStruct((wide, slots), F32)
    one, two, fields = call(
        decode_kernel,
        (act_shape, act_shape, jax.ShapeDtypeStruct((own, slots), BF16)),
        [VM] * 6,
        flops * 2,
    )(rim, pre_own, halo, w, mid_weight, out_weight)

    blocks = [fields] + [shift(fields, "lev", -k) for k in range(1, lev_count)]
    slope_one, slope_two = call(slope_kernel, (act_shape, act_shape), [VM] * 2, flops)(one, two)

    inner_own = lax.dynamic_slice_in_dim(inner, lev * own, own, 1).T
    patch_shape = jax.ShapeDtypeStruct((taps, portion, slots), BF16)
    patches = call(
        functools.partial(column_kernel, lev_count),
        (patch_shape,) * lev_count,
        [SM] + [VM] * (11 + lev_count),
        flops * 4,
        scratch_shapes=[
            pltpu.VMEM((own * lev_count, slots), BF16),
            pltpu.VMEM((own * lev_count, slots), F32),
            pltpu.VMEM((lev_count, taps, portion, slots), BF16),
        ],
    )(
        lev_arr,
        inner,
        inner_own,
        outer,
        obs_values[0, 0].T,
        obs_weight[:, None],
        live,
        slope_one,
        slope_two,
        w,
        mid_weight,
        out_weight,
        *blocks,
    )
    parts = [patches[0]] + [shift(patches[k], "lev", k) for k in range(1, lev_count)]

    row_l, col_l = row[None, :], col[None, :]
    row_s, col_s = row[:, None], col[:, None]
    total, row_edge, col_edge = call(
        functools.partial(edge_kernel, rows, cols),
        (
            jax.ShapeDtypeStruct((taps, portion, slots), F32),
            jax.ShapeDtypeStruct((2, portion, cols), F32),
            jax.ShapeDtypeStruct((2, portion, 128), F32),
        ),
        [VM] * (4 + lev_count),
        flops // 8,
    )(row_l, col_l, row_s, col_s, *parts)
    mine = lax.dynamic_slice_in_dim(latent, lev * portion, portion, 0)
    result = call(
        functools.partial(scatter_kernel, rows, cols),
        jax.ShapeDtypeStruct((portion, rows, cols), F32),
        [SM] + [VM] * 4,
        flops // 4,
    )(lev_arr, row_l, col_s, total, mine)

    to_last, to_first = swap_sides(
        col_edge[0][:, : rows + 2], col_edge[1][:, : rows + 2], "lon"
    )

    def sides(at):
        return (
            jnp.pad(to_first[:, at : at + 1], ((0, 0), (0, cols - 1)))
            + jnp.pad(to_last[:, at : at + 1], ((0, 0), (cols - 1, 0)))
        )

    to_bottom = shift(row_edge[0] + sides(0), "lat", -1, wrap=False)
    to_top = shift(row_edge[1] + sides(rows + 1), "lat", 1, wrap=False)
    result = result.at[:, :, 0].add(to_first[:, 1 : rows + 1])
    result = result.at[:, :, cols - 1].add(to_last[:, 1 : rows + 1])
    result = result.at[:, 0, :].add(to_top)
    return result.at[:, rows - 1, :].add(to_bottom)


def solution(mesh):
    return jax.shard_map(
        per_device,
        mesh=mesh,
        in_specs=(
            P(None, "lat", "lon"),
            P("lev", None, None, None),
            P("lev", None, None),
            P("lev", None, None),
            P(),
            P(),
            P("lat", "lon", None, None),
            P(),
            P("lat", "lon", None),
            P("lat", "lon"),
        ),
        out_specs=P("lev", "lat", "lon"),
        check_vma=False,
    )
```

profile of v0, /device:TPU:9, one launch (start us, length us, event | category | flops | bytes accessed | tf_op | source)
XLA Modules:
  0.0 132.7 jit_solution(5609525332811741970)
XLA Ops:
  1.4 3.7 %collective-permute-start = (bf16[256,128]{1,0:T(8,128)(2,1)S(1)}, bf16[256,128]{1,0:T(8,128)(2,1)S(1)}, u32[]{:S(2)}, u32[]{:S(2)}) collective-permute-start(bf16[256,128]{1,0:T(8,128)(2,1)S(1)} %bitcast.84), channel_id=1, source_target_pairs={{0,2},{2,4},{4,6},{1,3},{3,5},{5,7},{8,10},{10,12},{12,14},{9,11},... | collective-permute-start | bytes 196616 | tf_op jit(solution)/shard_map/ppermute | solution.py:218
  5.2 1.9 %collective-permute-start.1 = (bf16[256,128]{1,0:T(8,128)(2,1)S(1)}, bf16[256,128]{1,0:T(8,128)(2,1)S(1)}, u32[]{:S(2)}, u32[]{:S(2)}) collective-permute-start(bf16[256,128]{1,0:T(8,128)(2,1)S(1)} %bitcast.85), channel_id=1, source_target_pairs={{2,0},{4,2},{6,4},{3,1},{5,3},{7,5},{10,8},{12,10},{14,12},{11,9},... | collective-permute-start | bytes 196616 | tf_op jit(solution)/shard_map/ppermute | solution.py:218
  7.1 4.3 %convert_bitcast_fusion = f32[32,128,256]{1,0,2:T(8,128)} fusion(bf16[256,32,128]{2,1,0:T(8,128)(2,1)} %param.18), kind=kLoop, calls=%fused_computation | loop fusion | flops 1048576 | bytes 6291456 | tf_op jit(solution)/shard_map/convert_element_type | solution.py:285
  13.7 3.0 %fusion.29 = (bf16[256,32,1]{2,1,0:T(8,128)(2,1)}, bf16[256,32,1]{2,1,0:T(8,128)(2,1)}) fusion(bf16[256,32,128]{2,1,0:T(8,128)(2,1)S(1)} %copy-done), kind=kLoop, calls=%fused_computation.79 | loop fusion | bytes 65536 | tf_op jit(solution)/shard_map/slice | solution.py:255
  16.7 5.4 %copy.120 = f32[32,128,256]{2,1,0:T(8,128)} copy(f32[32,128,256]{1,0,2:T(8,128)} %convert_bitcast_fusion) | data formatting | bytes 8388608 | tf_op jit(solution)/shard_map/convert_element_type | solution.py:285
  22.0 3.3 %copy.122 = bf16[9,4,128,256]{3,2,1,0:T(8,128)(2,1)} copy(bf16[9,4,128,256]{3,2,0,1:T(8,128)(2,1)} %bitcast.77) | data formatting | bytes 4718592 | tf_op jit(solution)/shard_map/transpose | solution.py:286
  25.4 2.9 %copy.137 = bf16[256,32,1]{1,0,2:T(8,128)(2,1)S(1)} copy(bf16[256,32,1]{2,1,0:T(8,128)(2,1)} %get-tuple-element.79) | data formatting | bytes 32768
  28.2 2.9 %copy.138 = bf16[256,32,1]{1,0,2:T(8,128)(2,1)S(1)} copy(bf16[256,32,1]{2,1,0:T(8,128)(2,1)} %get-tuple-element.80) | data formatting | bytes 32768
  34.2 11.9 %shard_map.100.pre_ref = f32[512,256]{1,0:T(8,128)} custom-call(s32[9,256]{1,0:T(8,128)} %get-tuple-element.101.idx_ref, f32[4096,256]{1,0:T(8,128)} %bitcast.72, f32[256,9]{1,0:T(8,128)} %fusion.6.valid_ref, bf16[9,512,256]{2,1,0:T(8,128)(2,1)} %bitcast.74), custom_call_target="tpu_custom_call" | custom-call | flops 1207959552 | bytes 2097152 | tf_op jit(solution)/shard_map/pallas_call | solution.py:289
  47.6 5.0 %shard_map.101 = (f32[512,256]{1,0:T(8,128)}, f32[512,256]{1,0:T(8,128)}, bf16[192,256]{1,0:T(8,128)(2,1)}) custom-call(s32[9,256]{1,0:T(8,128)} %get-tuple-element.102.idx_ref, f32[512,256]{1,0:T(8,128)} %shard_map.100.pre_ref, bf16[256,384]{1,0:T(8,128)(2,1)} %concatenate.19.halo_ref, bf16[9,512,256]{2,1,0:T(8,128)(2,1)} %bitcast.75, ...), custom_call_target="tpu_custom_call" | custom-call | flops 1207959552 | bytes 4587520 | tf_op jit(solution)/shard_map/pallas_call | solution.py:297
  52.8 2.3 %collective-permute-start.4 = (bf16[192,256]{1,0:T(8,128)(2,1)}, bf16[192,256]{1,0:T(8,128)(2,1)}, u32[]{:S(2)}, u32[]{:S(2)}) collective-permute-start(bf16[192,256]{1,0:T(8,128)(2,1)} %get-tuple-element.69.rest_0_), channel_id=1, source_target_pairs={{0,16},{8,24},{16,0},{24,8},{1,17},{9,25},{17,1},{25,9},{2,18},{10... | collective-permute-start | bytes 294920 | tf_op jit(solution)/shard_map/ppermute | solution.py:218
  55.1 2.1 %collective-permute-start.5 = (bf16[192,256]{1,0:T(8,128)(2,1)}, bf16[192,256]{1,0:T(8,128)(2,1)}, u32[]{:S(2)}, u32[]{:S(2)}) collective-permute-start(bf16[192,256]{1,0:T(8,128)(2,1)} %get-tuple-element.69.rest_0_), channel_id=1, source_target_pairs={{0,8},{8,16},{16,24},{24,0},{1,9},{9,17},{17,25},{25,1},{2,10},{10... | collective-permute-start | bytes 294920 | tf_op jit(solution)/shard_map/ppermute | solution.py:218
  60.8 2.6 %shard_map.102 = (f32[512,256]{1,0:T(8,128)}, f32[512,256]{1,0:T(8,128)}) custom-call(f32[512,256]{1,0:T(8,128)} %get-tuple-element.65.one_ref, f32[512,256]{1,0:T(8,128)} %get-tuple-element.66.two_ref), custom_call_target="tpu_custom_call" | custom-call | flops 603979776 | bytes 4194304 | tf_op jit(solution)/shard_map/pallas_call | solution.py:305
  64.0 9.1 %shard_map.103 = (bf16[9,64,256]{2,1,0:T(8,128)(2,1)}, bf16[9,64,256]{2,1,0:T(8,128)(2,1)}, bf16[9,64,256]{2,1,0:T(8,128)(2,1)}, bf16[9,64,256]{2,1,0:T(8,128)(2,1)}) custom-call(s32[1]{0:T(128)} %bitcast.lev_ref, bf16[1024,768]{1,0:T(8,128)(2,1)} %inner_ref.1, bf16[192,1024]{1,0:T(8,128)(2,1)} %bitcast.79, bf16[768,1024]{1,0:T(8,128)(2,1)} %outer_ref.1, ...), custom_call_target="tpu_custom_call" | custom-call | flops 2415919104 | bytes 4718592 | tf_op jit(solution)/shard_map/pallas_call | solution.py:309
  77.3 4.8 %collective-permute-done.6.rest_1_ = bf16[9,64,256]{2,1,0:T(8,128)(2,1)S(1)} collective-permute-done((bf16[9,64,256]{2,1,0:T(8,128)(2,1)}, bf16[9,64,256]{2,1,0:T(8,128)(2,1)S(1)}, u32[]{:S(2)}, u32[]{:S(2)}) %collective-permute-start.6) | collective-permute-done | bytes 294944 | tf_op jit(solution)/shard_map/ppermute | solution.py:218
  82.1 17.8 %collective-permute-done.7.rest_2_ = bf16[9,64,256]{2,1,0:T(8,128)(2,1)S(1)} collective-permute-done((bf16[9,64,256]{2,1,0:T(8,128)(2,1)}, bf16[9,64,256]{2,1,0:T(8,128)(2,1)S(1)}, u32[]{:S(2)}, u32[]{:S(2)}) %collective-permute-start.7) | collective-permute-done | bytes 294944 | tf_op jit(solution)/shard_map/ppermute | solution.py:218
  99.9 2.4 %collective-permute-done.8.rest_3_ = bf16[9,64,256]{2,1,0:T(8,128)(2,1)S(1)} collective-permute-done((bf16[9,64,256]{2,1,0:T(8,128)(2,1)}, bf16[9,64,256]{2,1,0:T(8,128)(2,1)S(1)}, u32[]{:S(2)}, u32[]{:S(2)}) %collective-permute-start.8) | collective-permute-done | bytes 294944 | tf_op jit(solution)/shard_map/ppermute | solution.py:218
  103.0 2.6 %shard_map.104 = (f32[9,64,256]{2,1,0:T(8,128)}, f32[2,64,128]{2,1,0:T(8,128)}, f32[2,64,128]{2,1,0:T(8,128)}) custom-call(s32[1,256]{1,0:T(1,128)} %and_select_fusion.1.row_ref, s32[1,256]{1,0:T(1,128)} %get-tuple-element.77.col_ref, s32[256,1]{1,0:T(8,128)} %get-tuple-element.85.rowc_ref, s32[256,1]{1,0:T(8,128)} %get-tuple-element.86.colc_ref, ...), custom_call_target="tpu_custom_call" | custom-call | flops 75497472 | bytes 2883584 | tf_op jit(solution)/shard_map/pallas_call | solution.py:338
  107.7 3.7 %shard_map.105 = f32[64,32,128]{2,1,0:T(8,128)} custom-call(s32[1]{0:T(128)} %bitcast.lev_ref, s32[1,256]{1,0:T(1,128)} %and_select_fusion.1.row_ref, s32[256,1]{1,0:T(8,128)} %get-tuple-element.86.colc_ref, f32[9,64,256]{2,1,0:T(8,128)} %get-tuple-element.74.sum_ref, bf16[64,32,128]{2,1,0:T(8,128)(2,1)} %constant_dynamic-slice_fusion.own_ref), custom_call_target="tpu_custom_call" | custom-call | flops 150994944 | bytes 4194304 | tf_op jit(solution)/shard_map/pallas_call | solution.py:349
  116.2 2.9 %collective-permute-start.10 = (f32[64,128]{1,0:T(8,128)S(1)}, f32[64,128]{1,0:T(8,128)S(1)}, u32[]{:S(2)}, u32[]{:S(2)}) collective-permute-start(f32[64,128]{1,0:T(8,128)S(1)} %get-tuple-element.88), channel_id=1, source_target_pairs={{0,2},{2,4},{4,6},{1,3},{3,5},{5,7},{8,10},{10,12},{12,14},{9,11},... | collective-permute-start | bytes 98312 | tf_op jit(solution)/shard_map/ppermute | solution.py:218
  119.6 6.0 %scatter-add.15 = f32[64,32,128]{2,1,0:T(8,128)S(1)} dynamic-update-slice(f32[64,32,128]{2,1,0:T(8,128)S(1)} %scatter-add.14, f32[64,32,1]{2,1,0:T(8,128)S(1)} %copy.131, s32[]{:T(128)} %constant.156.clone.1, s32[]{:T(128)} %constant.156.clone.1, s32[]{:T(128)} %constant.157.clone.1) | dynamic-update-slice | bytes 16388 | tf_op jit(solution)/shard_map/scatter-add | solution.py:369
  125.7 1.9 %collective-permute-start.11 = (f32[64,128]{1,0:T(8,128)S(1)}, f32[64,128]{1,0:T(8,128)S(1)}, u32[]{:S(2)}, u32[]{:S(2)}) collective-permute-start(f32[64,128]{1,0:T(8,128)S(1)} %get-tuple-element.87), channel_id=1, source_target_pairs={{2,0},{4,2},{6,4},{3,1},{5,3},{7,5},{10,8},{12,10},{14,12},{11,9},... | collective-permute-start | bytes 98312 | tf_op jit(solution)/shard_map/ppermute | solution.py:218
  127.8 3.1 %collective-permute-done.11 = f32[64,128]{1,0:T(8,128)S(1)} collective-permute-done((f32[64,128]{1,0:T(8,128)S(1)}, f32[64,128]{1,0:T(8,128)S(1)}, u32[]{:S(2)}, u32[]{:S(2)}) %collective-permute-start.11) | collective-permute-done | bytes 32800 | tf_op jit(solution)/shard_map/ppermute | solution.py:218
  131.0 1.7 %scatter-add.19 = f32[64,32,128]{2,1,0:T(8,128)} dynamic-update-slice(f32[64,32,128]{2,1,0:T(8,128)} %copy-done.2, f32[64,1,128]{2,1,0:T(1,128)S(1)} %slice_add_fusion, s32[]{:T(128)} %constant.156.clone.1, s32[]{:T(128)} %constant.169.clone.1, s32[]{:T(128)} %constant.156.clone.1) | dynamic-update-slice | bytes 65540 | tf_op jit(solution)/shard_map/scatter-add | solution.py:371
  (83 shorter events, 24.4 us)
Async XLA Ops:
  1.4 31.1 %collective-permute-start = (bf16[256,128]{1,0:T(8,128)(2,1)S(1)}, bf16[256,128]{1,0:T(8,128)(2,1)S(1)}, u32[]{:S(2)}, u32[]{:S(2)}) collective-permute-start(bf16[256,128]{1,0:T(8,128)(2,1)S(1)} %bitcast.84), channel_id=1, source_target_pairs={{0,2},{2,4},{4,6},{1,3},{3,5},{5,7},{8,10},{10,12},{12,14},{9,11},... | collective-permute-start | bytes 196616 | tf_op jit(solution)/shard_map/ppermute | solution.py:218
  5.2 27.3 %collective-permute-start.1 = (bf16[256,128]{1,0:T(8,128)(2,1)S(1)}, bf16[256,128]{1,0:T(8,128)(2,1)S(1)}, u32[]{:S(2)}, u32[]{:S(2)}) collective-permute-start(bf16[256,128]{1,0:T(8,128)(2,1)S(1)} %bitcast.85), channel_id=1, source_target_pairs={{2,0},{4,2},{6,4},{3,1},{5,3},{7,5},{10,8},{12,10},{14,12},{11,9},... | collective-permute-start | bytes 196616 | tf_op jit(solution)/shard_map/ppermute | solution.py:218
  7.1 4.3 %copy-start.8 = (s32[1,1,256]{2,1,0:T(1,128)S(1)}, s32[1,1,256]{2,1,0:T(1,128)}, u32[]{:S(2)}) copy-start(s32[1,1,256]{2,1,0:T(1,128)} %param.26) | copy-start | bytes 3076
  7.1 6.6 %copy-start = (bf16[256,32,128]{2,1,0:T(8,128)(2,1)S(1)}, bf16[256,32,128]{2,1,0:T(8,128)(2,1)}, u32[]{:S(2)}) copy-start(bf16[256,32,128]{2,1,0:T(8,128)(2,1)} %param.18) | copy-start | bytes 6291460
  32.9 13.8 %collective-permute-start.2 = (bf16[2,256,34]{2,1,0:T(8,128)(2,1)S(1)}, bf16[2,256,34]{2,1,0:T(8,128)(2,1)S(1)}, u32[]{:S(2)}, u32[]{:S(2)}) collective-permute-start(bf16[2,256,34]{2,1,0:T(8,128)(2,1)S(1)} %pad_maximum_fusion), channel_id=1, source_target_pairs={{0,1},{1,0},{2,3},{3,2},{4,5},{5,4},{6,7},{7,6},{8,9},{9,8},{10,11... | collective-permute-start | bytes 104456 | tf_op jit(solution)/shard_map/ppermute | solution.py:218
  47.6 11.2 %copy-start.3 = (f32[1,1,256,768]{3,2,1,0:T(8,128)S(1)}, f32[1,1,256,768]{3,2,1,0:T(8,128)}, u32[]{:S(2)}) copy-start(f32[1,1,256,768]{3,2,1,0:T(8,128)} %param.24) | copy-start | bytes 2359300
  52.6 7.3 %copy-start.9 = (f32[768]{0:T(1024)S(1)}, f32[768]{0:T(1024)}, u32[]{:S(2)}) copy-start(f32[768]{0:T(1024)} %param.25) | copy-start | bytes 9220
  52.6 10.8 %collective-permute-start.3 = (bf16[192,256]{1,0:T(8,128)(2,1)}, bf16[192,256]{1,0:T(8,128)(2,1)S(1)}, u32[]{:S(2)}, u32[]{:S(2)}) collective-permute-start(bf16[192,256]{1,0:T(8,128)(2,1)} %get-tuple-element.69.rest_0_), channel_id=1, source_target_pairs={{0,24},{8,0},{16,8},{24,16},{1,25},{9,1},{17,9},{25,17},{2,26},{10... | collective-permute-start | bytes 294920 | tf_op jit(solution)/shard_map/ppermute | solution.py:218
  52.8 10.6 %collective-permute-start.4 = (bf16[192,256]{1,0:T(8,128)(2,1)}, bf16[192,256]{1,0:T(8,128)(2,1)}, u32[]{:S(2)}, u32[]{:S(2)}) collective-permute-start(bf16[192,256]{1,0:T(8,128)(2,1)} %get-tuple-element.69.rest_0_), channel_id=1, source_target_pairs={{0,16},{8,24},{16,0},{24,8},{1,17},{9,25},{17,1},{25,9},{2,18},{10... | collective-permute-start | bytes 294920 | tf_op jit(solution)/shard_map/ppermute | solution.py:218
  55.1 8.3 %collective-permute-start.5 = (bf16[192,256]{1,0:T(8,128)(2,1)}, bf16[192,256]{1,0:T(8,128)(2,1)}, u32[]{:S(2)}, u32[]{:S(2)}) collective-permute-start(bf16[192,256]{1,0:T(8,128)(2,1)} %get-tuple-element.69.rest_0_), channel_id=1, source_target_pairs={{0,8},{8,16},{16,24},{24,0},{1,9},{9,17},{17,25},{25,1},{2,10},{10... | collective-permute-start | bytes 294920 | tf_op jit(solution)/shard_map/ppermute | solution.py:218
  63.4 0.6 copy-start.10
  73.2 8.9 %collective-permute-start.6 = (bf16[9,64,256]{2,1,0:T(8,128)(2,1)}, bf16[9,64,256]{2,1,0:T(8,128)(2,1)S(1)}, u32[]{:S(2)}, u32[]{:S(2)}) collective-permute-start(bf16[9,64,256]{2,1,0:T(8,128)(2,1)} %get-tuple-element.71), channel_id=1, source_target_pairs={{0,8},{8,16},{16,24},{24,0},{1,9},{9,17},{17,25},{25,1},{2,10},{10... | collective-permute-start | bytes 884744 | tf_op jit(solution)/shard_map/ppermute | solution.py:218
  74.5 25.4 %collective-permute-start.7 = (bf16[9,64,256]{2,1,0:T(8,128)(2,1)}, bf16[9,64,256]{2,1,0:T(8,128)(2,1)S(1)}, u32[]{:S(2)}, u32[]{:S(2)}) collective-permute-start(bf16[9,64,256]{2,1,0:T(8,128)(2,1)} %get-tuple-element.72), channel_id=1, source_target_pairs={{0,16},{8,24},{16,0},{24,8},{1,17},{9,25},{17,1},{25,9},{2,18},{10... | collective-permute-start | bytes 884744 | tf_op jit(solution)/shard_map/ppermute | solution.py:218
  75.5 26.8 %collective-permute-start.8 = (bf16[9,64,256]{2,1,0:T(8,128)(2,1)}, bf16[9,64,256]{2,1,0:T(8,128)(2,1)S(1)}, u32[]{:S(2)}, u32[]{:S(2)}) collective-permute-start(bf16[9,64,256]{2,1,0:T(8,128)(2,1)} %get-tuple-element.73), channel_id=1, source_target_pairs={{0,24},{8,0},{16,8},{24,16},{1,25},{9,1},{17,9},{25,17},{2,26},{10... | collective-permute-start | bytes 884744 | tf_op jit(solution)/shard_map/ppermute | solution.py:218
  82.1 20.2 %copy-start.4 = (bf16[9,64,256]{2,1,0:T(8,128)(2,1)}, bf16[9,64,256]{2,1,0:T(8,128)(2,1)S(1)}, u32[]{:S(2)}) copy-start(bf16[9,64,256]{2,1,0:T(8,128)(2,1)S(1)} %collective-permute-done.6.rest_1_) | copy-start | bytes 884740
  99.9 2.4 %copy-start.5 = (bf16[9,64,256]{2,1,0:T(8,128)(2,1)}, bf16[9,64,256]{2,1,0:T(8,128)(2,1)S(1)}, u32[]{:S(2)}) copy-start(bf16[9,64,256]{2,1,0:T(8,128)(2,1)S(1)} %collective-permute-done.7.rest_2_) | copy-start | bytes 884740
  102.3 0.7 copy-start.6
  106.5 6.6 %collective-permute-start.9 = (f32[2,64,34]{2,1,0:T(8,128)S(1)}, f32[2,64,34]{2,1,0:T(8,128)S(1)}, u32[]{:S(2)}, u32[]{:S(2)}) collective-permute-start(f32[2,64,34]{2,1,0:T(8,128)S(1)} %pad_maximum_fusion.1), channel_id=1, source_target_pairs={{0,1},{1,0},{2,3},{3,2},{4,5},{5,4},{6,7},{7,6},{8,9},{9,8},{10,11... | collective-permute-start | bytes 52232 | tf_op jit(solution)/shard_map/ppermute | solution.py:218
  111.3 2.4 %copy-start.1 = (f32[64,32,128]{2,1,0:T(8,128)S(1)}, f32[64,32,128]{2,1,0:T(8,128)}, u32[]{:S(2)}) copy-start(f32[64,32,128]{2,1,0:T(8,128)} %shard_map.105) | copy-start | bytes 3145732
  115.3 0.9 copy-start.7
  116.2 11.4 %collective-permute-start.10 = (f32[64,128]{1,0:T(8,128)S(1)}, f32[64,128]{1,0:T(8,128)S(1)}, u32[]{:S(2)}, u32[]{:S(2)}) collective-permute-start(f32[64,128]{1,0:T(8,128)S(1)} %get-tuple-element.88), channel_id=1, source_target_pairs={{0,2},{2,4},{4,6},{1,3},{3,5},{5,7},{8,10},{10,12},{12,14},{9,11},... | collective-permute-start | bytes 98312 | tf_op jit(solution)/shard_map/ppermute | solution.py:218
  125.7 5.2 %collective-permute-start.11 = (f32[64,128]{1,0:T(8,128)S(1)}, f32[64,128]{1,0:T(8,128)S(1)}, u32[]{:S(2)}, u32[]{:S(2)}) collective-permute-start(f32[64,128]{1,0:T(8,128)S(1)} %get-tuple-element.87), channel_id=1, source_target_pairs={{2,0},{4,2},{6,4},{3,1},{5,3},{7,5},{10,8},{12,10},{14,12},{11,9},... | collective-permute-start | bytes 98312 | tf_op jit(solution)/shard_map/ppermute | solution.py:218
  127.8 3.2 %copy-start.2 = (f32[64,32,128]{2,1,0:T(8,128)}, f32[64,32,128]{2,1,0:T(8,128)S(1)}, u32[]{:S(2)}) copy-start(f32[64,32,128]{2,1,0:T(8,128)S(1)} %scatter-add.16) | copy-start | bytes 3145732
where the time goes:
time: 133 us
  local copies, waits for them, and re-layouts  40.7 us (31%)
  Pallas kernels  34.9 us (26%)
  waiting for transfers between devices  28.1 us (21%)
  starting transfers between devices  19.2 us (14%)
  other arithmetic  8.88 us (7%)
    ppermute x12, waiting for transfers between devices, shift(): return lax.ppermute(x, axis, pairs)  28.1 us
    ppermute x12, starting transfers between devices, shift(): return lax.ppermute(x, axis, pairs)  19.2 us
    pallas_call x1, Pallas kernels, per_device(): call(own_kernel, jax.ShapeDtypeStruct((wide, slots), F32), [SM, VM, VM, V...  11.9 us
    unnamed x30, local copies, waits for them, and re-layouts  11.4 us
    pallas_call x1, Pallas kernels, per_device(): call(functools.partial(column_kernel, lev_count), (patch_shape,) * lev_co...  9.14 us
    scatter-add x1, local copies, waits for them, and re-layouts, per_device(): result = result.at[:, :, cols - 1].add(to_last[:, 1:rows + 1])  6.02 us
    convert_element_type x1, local copies, waits for them, and re-layouts, per_device(): jnp.transpose(latent, (1, 2, 0)).reshape(rows * cols, chans).astype(F32)  5.37 us
    pallas_call x1, Pallas kernels, per_device(): call(decode_kernel, (act_shape, act_shape, jax.ShapeDtypeStruct((own, slo...  5.01 us
  transfers between devices with their start and end apart: 12, of which 4 were waited for; matrix products, arithmetic and copies ran while one was open for 30% of the time, Pallas kernels for 14%

commit v1 on v0

v1 whole, which is shorter than its diff:
```python
import functools

import jax
import jax.numpy as jnp
from jax import lax
from jax.experimental import pallas as pl
from jax.experimental.pallas import tpu as pltpu
from jax.sharding import PartitionSpec as P

KAPPA = 0.7978845608028654
CUBIC = 0.044715
F32 = jnp.float32
BF16 = jnp.bfloat16


def gelu(pre):
    tanh_v = jnp.tanh(KAPPA * (pre + CUBIC * pre * pre * pre))
    return 0.5 * pre * (1.0 + tanh_v)


def gelu_slope(pre):
    square = pre * pre
    tanh_v = jnp.tanh(KAPPA * (pre + CUBIC * square * pre))
    value = 0.5 * pre * (1.0 + tanh_v)
    slope = 0.5 * (1.0 + tanh_v) + 0.5 * pre * (1.0 - tanh_v * tanh_v) * KAPPA * (
        1.0 + 3.0 * CUBIC * square
    )
    return value, slope


def nn(a, b):
    return lax.dot_general(a, b, (((1,), (0,)), ((), ())), preferred_element_type=F32)


def nt(a, b):
    return lax.dot_general(a, b, (((1,), (1,)), ((), ())), preferred_element_type=F32)


def tn(a, b):
    return lax.dot_general(a, b, (((0,), (0,)), ((), ())), preferred_element_type=F32)


def split(index, cols):
    if cols & (cols - 1):
        return index // cols, index % cols
    bits = cols.bit_length() - 1
    return index >> bits, index & (cols - 1)


def hot(mask):
    return mask.astype(F32).astype(BF16)


def upright(index_ref):
    slots = index_ref.shape[1]
    return jnp.broadcast_to(index_ref[...], (128, slots)).T


def call(kernel, out_shape, in_specs, flops, **kwargs):
    bytes_out = sum(s.size * s.dtype.itemsize for s in jax.tree.leaves(out_shape))
    return pl.pallas_call(
        kernel,
        out_shape=out_shape,
        in_specs=in_specs,
        out_specs=jax.tree.map(lambda _: VM, out_shape),
        cost_estimate=pl.CostEstimate(
            flops=flops, bytes_accessed=4 * bytes_out, transcendentals=0
        ),
        **kwargs,
    )


VM = pl.BlockSpec(memory_space=pltpu.VMEM)
SM = pl.BlockSpec(memory_space=pltpu.SMEM)


def strip_kernel(lat_ref, top_ref, bottom_ref, side_ref, wide_ref, keep_ref):
    chans, rows, cols = lat_ref.shape
    wide_ref[...] = lat_ref[...].reshape(chans * rows, cols).astype(F32)
    which = lax.broadcasted_iota(jnp.int32, (8, cols), 0)
    lane = lax.broadcasted_iota(jnp.int32, (8, cols), 1)
    pick = hot(((which == 0) & (lane == 0)) | ((which == 1) & (lane == cols - 1)))
    for r in range(rows):
        line = wide_ref[pl.ds(r, chans, stride=rows), :].astype(BF16)
        ends = nt(pick, line)
        keep_ref[0, r : r + 1, :] = ends[0:1]
        keep_ref[1, r : r + 1, :] = ends[1:2]
        if r == 0:
            top_ref[...] = line.T
        if r == rows - 1:
            bottom_ref[...] = line.T
    side_ref[...] = keep_ref[...].astype(BF16)


def gather_kernel(index_sm, index_ref, lat_ref, out_ref, wide_ref, table_ref, x_ref):
    chans, rows, cols = lat_ref.shape
    slots = index_ref.shape[1]
    halves = chans // 128
    lead = cols + 8
    wide_ref[...] = lat_ref[...].reshape(chans * rows, cols).astype(F32)
    for r in range(rows):
        line = wide_ref[pl.ds(r, chans, stride=rows), :].astype(BF16).T.astype(F32)
        for b in range(3):
            for h in range(halves):
                at = (lead + r * cols - b + 1) * 8 + halves * b + h
                table_ref[pl.ds(at, cols, stride=8), :] = line[:, h * 128 : (h + 1) * 128]

    def body(i, carry):
        for j in range(8):
            s = i * 8 + j
            base = (index_sm[0, s] + (lead - cols)) * 8
            for a in range(3):
                x_ref[a, pl.ds(pl.multiple_of(s * 8, 8), 8), :] = table_ref[
                    pl.ds(pl.multiple_of(base + a * cols * 8, 8), 8), :
                ]
        return carry

    lax.fori_loop(0, slots // 8, body, 0)
    row, col = split(upright(index_ref), cols)
    for a in range(3):
        for b in range(3):
            at_row, at_col = row + (a - 1), col + (b - 1)
            inside = (at_row >= 0) & (at_row < rows) & (at_col >= 0) & (at_col < cols)
            for h in range(halves):
                x = x_ref[a, pl.ds(halves * b + h, slots, stride=8), :]
                out_ref[3 * a + b, :, h * 128 : (h + 1) * 128] = jnp.where(inside, x, 0.0).astype(
                    BF16
                )


def decode_kernel(
    rows,
    cols,
    index_ref,
    x_ref,
    above_ref,
    below_ref,
    left_ref,
    right_ref,
    w_ref,
    mid_ref,
    outw_ref,
    one_ref,
    two_ref,
    field_ref,
    halo_ref,
):
    slots = index_ref.shape[1]
    groups, hidden, _ = mid_ref.shape
    levels = outw_ref.shape[1]
    width = halo_ref.shape[0]
    tall = (width - 2 * cols) // 2
    halo_ref[...] = jnp.zeros_like(halo_ref)
    halo_ref[0:cols, :] = above_ref[...]
    halo_ref[cols : 2 * cols, :] = below_ref[...]
    halo_ref[2 * cols : 2 * cols + rows + 2, :] = left_ref[...]
    halo_ref[2 * cols + tall : 2 * cols + tall + rows + 2, :] = right_ref[...]
    row, col = split(upright(index_ref), cols)
    cells = lax.broadcasted_iota(jnp.int32, (slots, width), 1)
    acc = None
    for a in range(3):
        for b in range(3):
            at_row, at_col = row + (a - 1), col + (b - 1)
            rim = jnp.where(at_row < 0, at_col, jnp.where(at_row >= rows, cols + at_col, -1))
            rim = jnp.where(at_col < 0, 2 * cols + at_row + 1, rim)
            rim = jnp.where(at_col >= cols, 2 * cols + tall + at_row + 1, rim)
            rim = jnp.concatenate([rim] * (width // 128), 1)
            x = x_ref[3 * a + b] + nn(hot(cells == rim), halo_ref[...]).astype(BF16)
            part = nt(w_ref[3 * a + b], x)
            acc = part if acc is None else acc + part
    one_ref[...] = acc
    act = gelu(acc).astype(BF16)
    for g in range(groups):
        two = nn(mid_ref[g], act[g * hidden : (g + 1) * hidden])
        two_ref[g * hidden : (g + 1) * hidden, :] = two
        field_ref[g * levels : (g + 1) * levels, :] = nn(
            outw_ref[g], gelu(two).astype(BF16)
        ).astype(BF16)


def prepare_kernel(
    lev_ref,
    count_ref,
    one_ref,
    two_ref,
    obs_ref,
    weight_ref,
    inner_ref,
    outer_ref,
    s1_ref,
    s2_ref,
    obst_ref,
    scale_ref,
    innert_ref,
    outert_ref,
    turn_ref,
):
    s1_ref[...] = gelu_slope(one_ref[...])[1]
    s2_ref[...] = gelu_slope(two_ref[...])[1]
    obst_ref[...] = obs_ref[...].T
    slots = obs_ref.shape[0]
    levels = weight_ref.shape[1]
    weight = jnp.broadcast_to(weight_ref[...], (128, levels)).T
    live = lax.broadcasted_iota(jnp.int32, (levels, 128), 1)
    for h in range(slots // 128):
        scale_ref[:, h * 128 : (h + 1) * 128] = jnp.where(
            live + h * 128 < count_ref[0, 0], weight, 0.0
        )
    turn_ref[...] = inner_ref[...].T
    own = innert_ref.shape[0]
    innert_ref[...] = turn_ref[pl.ds(pl.multiple_of(lev_ref[0] * own, 16), own), :]
    outert_ref[...] = outer_ref[...].T


def column_kernel(
    lev_count,
    lev_ref,
    inner_ref,
    innert_ref,
    outer_ref,
    outert_ref,
    obst_ref,
    scale_ref,
    s1_ref,
    s2_ref,
    w_ref,
    mid_ref,
    outw_ref,
    *rest,
):
    blocks = rest[:lev_count]
    outs = rest[lev_count : 2 * lev_count]
    f_ref, mis_ref, g_ref = rest[2 * lev_count :]
    lev = lev_ref[0]
    own = blocks[0].shape[0]
    for k in range(lev_count):
        at = pl.multiple_of(lax.rem(lev + k, lev_count) * own, 16)
        f_ref[pl.ds(at, own), :] = blocks[k][...]
    pre_col = nn(inner_ref[...], f_ref[...])
    act, slope = gelu_slope(pre_col)
    forecast = f_ref[...].astype(F32) + nn(outer_ref[...], act.astype(BF16))
    misfit = (forecast - obst_ref[...]) * scale_ref[...]
    mis_ref[...] = misfit
    grad_act = (nn(outert_ref[...], misfit.astype(BF16)) * slope).astype(BF16)
    mine = mis_ref[pl.ds(pl.multiple_of(lev * own, 16), own), :]
    grad_fields = (mine + nn(innert_ref[...], grad_act)).astype(BF16)
    groups, hidden, _ = mid_ref.shape
    levels = outw_ref.shape[1]
    ones = []
    for g in range(groups):
        span = slice(g * hidden, (g + 1) * hidden)
        two = (
            tn(outw_ref[g], grad_fields[g * levels : (g + 1) * levels]) * s2_ref[span, :]
        ).astype(BF16)
        ones.append((tn(mid_ref[g], two) * s1_ref[span, :]).astype(BF16))
    grad_one = jnp.concatenate(ones, 0)
    taps = w_ref.shape[0]
    portion = w_ref.shape[2] // lev_count
    for t in range(taps):
        patch = tn(w_ref[t], grad_one).astype(BF16)
        for d in range(lev_count):
            g_ref[d, t] = patch[d * portion : (d + 1) * portion]
    for k in range(lev_count):
        outs[k][...] = g_ref[lax.rem(lev + k, lev_count)]


def edge_kernel(rows, cols, index_ref, *rest):
    blocks, (rowout_ref, colout_ref) = rest[:-2], rest[-2:]
    row, col = split(index_ref[...], cols)
    rowc, colc = split(upright(index_ref), cols)
    slots = row.shape[1]
    cells = lax.broadcasted_iota(jnp.int32, (slots, cols), 1)
    lines = lax.broadcasted_iota(jnp.int32, (slots, 128), 1)
    for k, block in enumerate(blocks):
        for e, (edge, a) in enumerate(((0, 0), (rows - 1, 2))):
            acc = None
            for b in range(3):
                part = jnp.where(row == edge, block[3 * a + b].astype(F32), 0.0).astype(BF16)
                part = nn(part, hot(colc + (b - 1) == cells))
                acc = part if acc is None else acc + part
            rowout_ref[e, k] = acc.astype(BF16)
        acc = None
        for e, (edge, b) in enumerate(((0, 0), (cols - 1, 2))):
            for a in range(3):
                part = jnp.where(col == edge, block[3 * a + b].astype(F32), 0.0).astype(BF16)
                part = nn(part, hot(rowc + (a + 64 * e) == lines))
                acc = part if acc is None else acc + part
        colout_ref[k] = acc.astype(BF16)


def corner_kernel(rows, cols, rowin_ref, left_ref, right_ref, up_ref, down_ref, side_ref):
    from_left = left_ref[...].astype(F32)
    from_right = right_ref[...].astype(F32)
    lane = lax.broadcasted_iota(jnp.int32, up_ref.shape, 2)
    for e, (at, ref) in enumerate(((0, up_ref), (rows + 1, down_ref))):
        line = rowin_ref[e].astype(F32)
        line = line + jnp.where(lane == 0, from_left[:, :, 64 + at : 65 + at], 0.0)
        line = line + jnp.where(lane == cols - 1, from_right[:, :, at : at + 1], 0.0)
        ref[...] = line.astype(BF16)
    spot = lax.broadcasted_iota(jnp.int32, side_ref.shape, 2)
    side_ref[...] = jnp.where(spot < 64, right_ref[...].astype(F32), left_ref[...].astype(F32)).astype(BF16)


def final_kernel(rows, cols, count, index_ref, own_ref, *rest):
    blocks, edges, (out_ref, sum_ref, edge_ref) = rest[:count], rest[count:-3], rest[-3:]
    total = blocks[0][...].astype(F32)
    for block in blocks[1:]:
        total = total + block[...].astype(F32)
    sum_ref[...] = total
    total = edges[0][...].astype(F32)
    for edge in edges[1:]:
        total = total + edge[...].astype(F32)
    edge_ref[...] = total
    row, _ = split(index_ref[...], cols)
    _, colc = split(upright(index_ref), cols)
    slots = row.shape[1]
    portion = out_ref.shape[0]
    cells = lax.broadcasted_iota(jnp.int32, (slots, cols), 1)
    hots = [hot(colc + (b - 1) == cells) for b in range(3)]
    lines = lax.broadcasted_iota(jnp.int32, (rows, slots), 0)
    masks = [row + (a - 1) == lines for a in range(3)]
    spot = lax.broadcasted_iota(jnp.int32, (rows, 128), 1)
    line = lax.broadcasted_iota(jnp.int32, (rows, 128), 0)
    picks = [spot == line + 1, spot == line + 65]
    lane = lax.broadcasted_iota(jnp.int32, (rows, cols), 1)
    high = lax.broadcasted_iota(jnp.int32, (rows, cols), 0)
    step = 8
    for c0 in range(0, portion, step):
        acc = None
        for b in range(3):
            parts = []
            for c in range(c0, c0 + step):
                part = jnp.zeros((rows, slots), F32)
                for a in range(3):
                    values = jnp.broadcast_to(sum_ref[3 * a + b, c : c + 1, :], (rows, slots))
                    part = jnp.where(masks[a], values, part)
                parts.append(part.astype(BF16))
            part = nn(jnp.concatenate(parts, 0), hots[b])
            acc = part if acc is None else acc + part
        for c in range(c0, c0 + step):
            field = acc[(c - c0) * rows : (c - c0 + 1) * rows] + own_ref[c].astype(F32)
            above = jnp.broadcast_to(edge_ref[0, c : c + 1, :], (rows, cols))
            below = jnp.broadcast_to(edge_ref[1, c : c + 1, :], (rows, cols))
            side = jnp.broadcast_to(edge_ref[2, c : c + 1, :], (rows, 128))
            last = jnp.sum(jnp.where(picks[0], side, 0.0), 1, keepdims=True)
            first = jnp.sum(jnp.where(picks[1], side, 0.0), 1, keepdims=True)
            field = field + jnp.where(high == 0, above, 0.0)
            field = field + jnp.where(high == rows - 1, below, 0.0)
            field = field + jnp.where(lane == 0, first, 0.0)
            out_ref[c] = field + jnp.where(lane == cols - 1, last, 0.0)


def shift(x, axis, by, wrap=True):
    size = lax.axis_size(axis)
    pairs = [(i, (i + by) % size) for i in range(size) if wrap or 0 <= i + by < size]
    return lax.ppermute(x, axis, pairs)


def from_sides(x, axis):
    if lax.axis_size(axis) == 2:
        other = shift(x, axis, 1)
        return other, other
    return shift(x, axis, 1), shift(x, axis, -1)


def per_device(
    latent,
    conv_weight,
    mid_weight,
    out_weight,
    inner,
    outer,
    obs_values,
    obs_weight,
    obs_index,
    obs_count,
):
    chans, rows, cols = latent.shape
    groups, hidden, taps, _ = conv_weight.shape
    levels = out_weight.shape[1]
    slots = obs_index.shape[-1]
    own = groups * levels
    wide = groups * hidden
    lev = lax.axis_index("lev")
    lev_count = lax.axis_size("lev")
    lev_arr = lev.reshape(1).astype(jnp.int32)
    portion = chans // lev_count
    index = obs_index.reshape(1, slots)
    flops = 2 * taps * wide * chans * slots

    strip = jax.ShapeDtypeStruct((cols, chans), BF16)
    top, bottom, ends = call(
        strip_kernel,
        (strip, strip, jax.ShapeDtypeStruct((2, rows, chans), BF16)),
        [VM],
        flops // 4,
        scratch_shapes=[
            pltpu.VMEM((chans * rows, cols), F32),
            pltpu.VMEM((2, rows, chans), F32),
        ],
    )(latent)
    above = shift(bottom, "lat", 1, wrap=False)
    below = shift(top, "lat", -1, wrap=False)
    columns = jnp.stack(
        [
            jnp.concatenate([above[at : at + 1], ends[e], below[at : at + 1]], 0)
            for e, at in enumerate((0, cols - 1))
        ]
    )
    from_left, from_right = from_sides(columns, "lon")

    x = call(
        gather_kernel,
        jax.ShapeDtypeStruct((taps, slots, chans), BF16),
        [SM, VM, VM],
        flops,
        scratch_shapes=[
            pltpu.VMEM((chans * rows, cols), F32),
            pltpu.VMEM((((rows + 2) * cols + 16) * 8, 128), F32),
            pltpu.VMEM((3, slots * 8, 128), F32),
        ],
    )(index, index, latent)
    w = jnp.transpose(conv_weight, (2, 0, 1, 3)).reshape(taps, wide, chans)
    act_shape = jax.ShapeDtypeStruct((wide, slots), F32)
    one, two, fields = call(
        functools.partial(decode_kernel, rows, cols),
        (act_shape, act_shape, jax.ShapeDtypeStruct((own, slots), BF16)),
        [VM] * 9,
        flops * 2,
        scratch_shapes=[pltpu.VMEM((2 * cols + 128, chans), BF16)],
    )(index, x, above, below, from_left[1], from_right[0], w, mid_weight, out_weight)

    blocks = [fields] + [shift(fields, "lev", -k) for k in range(1, lev_count)]
    column_shape = jax.ShapeDtypeStruct((own * lev_count, slots), F32)
    turned = call(
        prepare_kernel,
        (
            act_shape,
            act_shape,
            column_shape,
            column_shape,
            jax.ShapeDtypeStruct((own, inner.shape[0]), BF16),
            jax.ShapeDtypeStruct((outer.shape[1], outer.shape[0]), BF16),
        ),
        [SM, SM] + [VM] * 6,
        flops,
        scratch_shapes=[pltpu.VMEM((inner.shape[1], inner.shape[0]), BF16)],
    )(lev_arr, obs_count, one, two, obs_values[0, 0], obs_weight[None, :], inner, outer)
    slope_one, slope_two, obs_turned, scale, inner_turned, outer_turned = turned

    patch_shape = jax.ShapeDtypeStruct((taps, portion, slots), BF16)
    patches = call(
        functools.partial(column_kernel, lev_count),
        (patch_shape,) * lev_count,
        [SM] + [VM] * (11 + lev_count),
        flops * 4,
        scratch_shapes=[
            pltpu.VMEM((own * lev_count, slots), BF16),
            pltpu.VMEM((own * lev_count, slots), F32),
            pltpu.VMEM((lev_count, taps, portion, slots), BF16),
        ],
    )(
        lev_arr,
        inner,
        inner_turned,
        outer,
        outer_turned,
        obs_turned,
        scale,
        slope_one,
        slope_two,
        w,
        mid_weight,
        out_weight,
        *blocks,
    )
    parts = [patches[0]] + [shift(patches[k], "lev", k) for k in range(1, lev_count)]

    line_shape = jax.ShapeDtypeStruct((lev_count, portion, cols), BF16)
    side_shape = jax.ShapeDtypeStruct((lev_count, portion, 128), BF16)
    row_edge, col_edge = call(
        functools.partial(edge_kernel, rows, cols),
        (jax.ShapeDtypeStruct((2, lev_count, portion, cols), BF16), side_shape),
        [VM] * (1 + lev_count),
        flops // 8,
    )(index, *patches)
    from_left, from_right = from_sides(col_edge, "lon")
    up, down, side = call(
        functools.partial(corner_kernel, rows, cols),
        (line_shape, line_shape, side_shape),
        [VM] * 3,
        flops // 64,
    )(row_edge, from_left, from_right)
    onto_first = shift(down, "lat", 1, wrap=False)
    onto_last = shift(up, "lat", -1, wrap=False)
    rims = [jnp.stack([onto_first[k], onto_last[k], side[k]]) for k in range(lev_count)]
    rims = [rims[0]] + [shift(rims[k], "lev", k) for k in range(1, lev_count)]

    mine = lax.dynamic_slice_in_dim(latent, lev * portion, portion, 0)
    return call(
        functools.partial(final_kernel, rows, cols, lev_count),
        jax.ShapeDtypeStruct((portion, rows, cols), F32),
        [VM] * (2 + 2 * lev_count),
        flops // 4,
        scratch_shapes=[
            pltpu.VMEM((taps, portion, slots), F32),
            pltpu.VMEM((3, portion, 128), F32),
        ],
    )(index, mine, *parts, *rims)


def solution(mesh):
    return jax.shard_map(
        per_device,
        mesh=mesh,
        in_specs=(
            P(None, "lat", "lon"),
            P("lev", None, None, None),
            P("lev", None, None),
            P("lev", None, None),
            P(),
            P(),
            P("lat", "lon", None, None),
            P(),
            P("lat", "lon", None),
            P("lat", "lon"),
        ),
        out_specs=P("lev", "lat", "lon"),
        check_vma=False,
    )
```

time: 133 us -> 101 us (0.76)
  the two profiles are of different devices: /device:TPU:9 before, /device:TPU:0 now
where the time goes in v1:
time: 101 us; the launch traced here: 100 us
  Pallas kernels  43.6 us (43%)
  starting transfers between devices  30.2 us (30%)
  waiting for transfers between devices  14.3 us (14%)
  local copies, waits for them, and re-layouts  10.8 us (11%)
    ppermute x15, starting transfers between devices, shift(): return lax.ppermute(x, axis, pairs)  30.2 us
    ppermute x15, waiting for transfers between devices, shift(): return lax.ppermute(x, axis, pairs)  14.3 us
    pallas_call x1, Pallas kernels, per_device(): call(functools.partial(column_kernel, lev_count), (patch_shape,) * lev_co...  9.7 us
    pallas_call x1, Pallas kernels, per_device(): call(gather_kernel, jax.ShapeDtypeStruct((taps, slots, chans), BF16), [SM...  8.76 us
    pallas_call x1, Pallas kernels, per_device(): call(functools.partial(decode_kernel, rows, cols), (act_shape, act_shape,...  5.76 us
    pallas_call x1, Pallas kernels, per_device(): call(prepare_kernel, (act_shape, act_shape, column_shape, column_shape, j...  5.62 us
    pallas_call x1, Pallas kernels, per_device(): call(strip_kernel, (strip, strip, jax.ShapeDtypeStruct((2, rows, chans),...  4.89 us
    pallas_call x1, Pallas kernels, per_device(): call(functools.partial(final_kernel, rows, cols, lev_count), jax.ShapeDty...  4.45 us
  transfers between devices with their start and end apart: 15, of which 5 were waited for; matrix products, arithmetic and copies ran while one was open for 8% of the time, Pallas kernels for 16%

profile of v1, /device:TPU:0, one launch (start us, length us, event | category | flops | bytes accessed | tf_op | source)
XLA Modules:
  0.0 100.4 jit_solution(5300761239169860298)
XLA Ops:
  0.0 4.9 %shard_map.101 = (bf16[128,256]{1,0:T(8,128)(2,1)}, bf16[128,256]{1,0:T(8,128)(2,1)}, bf16[2,32,256]{2,1,0:T(8,128)(2,1)}) custom-call(bf16[256,32,128]{2,1,0:T(8,128)(2,1)} %lat_ref.3), custom_call_target="tpu_custom_call" | custom-call | flops 150994944 | bytes 655360 | tf_op jit(solution)/shard_map/pallas_call | solution.py:392
  4.9 2.4 %collective-permute-start = (bf16[128,256]{1,0:T(8,128)(2,1)}, bf16[128,256]{1,0:T(8,128)(2,1)S(1)}, u32[]{:S(2)}, u32[]{:S(2)}) collective-permute-start(bf16[128,256]{1,0:T(8,128)(2,1)} %get-tuple-element.26), channel_id=1, source_target_pairs={{0,2},{2,4},{4,6},{1,3},{3,5},{5,7},{8,10},{10,12},{12,14},{9,11},... | collective-permute-start | bytes 196616 | tf_op jit(solution)/shard_map/ppermute | solution.py:356
  7.3 1.3 %collective-permute-start.1 = (bf16[128,256]{1,0:T(8,128)(2,1)}, bf16[128,256]{1,0:T(8,128)(2,1)S(1)}, u32[]{:S(2)}, u32[]{:S(2)}) collective-permute-start(bf16[128,256]{1,0:T(8,128)(2,1)} %get-tuple-element.27), channel_id=1, source_target_pairs={{2,0},{4,2},{6,4},{3,1},{5,3},{7,5},{10,8},{12,10},{14,12},{11,9},... | collective-permute-start | bytes 196616 | tf_op jit(solution)/shard_map/ppermute | solution.py:356
  9.3 3.3 %copy.11 = bf16[9,4,128,256]{3,2,1,0:T(8,128)(2,1)} copy(bf16[9,4,128,256]{3,2,0,1:T(8,128)(2,1)} %bitcast.19) | data formatting | bytes 4718592 | tf_op jit(solution)/shard_map/transpose | solution.py:423
  12.8 2.3 %collective-permute-start.2 = (bf16[2,34,256]{2,1,0:T(8,128)(2,1)S(1)}, bf16[2,34,256]{2,1,0:T(8,128)(2,1)S(1)}, u32[]{:S(2)}, u32[]{:S(2)}) collective-permute-start(bf16[2,34,256]{2,1,0:T(8,128)(2,1)S(1)} %pad_maximum_fusion.4), channel_id=1, source_target_pairs={{0,1},{1,0},{2,3},{3,2},{4,5},{5,4},{6,7},{7,6},{8,9},{9,8},{10,11... | collective-permute-start | bytes 104456 | tf_op jit(solution)/shard_map/ppermute | solution.py:356
  15.1 8.8 %shard_map.100.x_ref = bf16[9,256,256]{2,1,0:T(8,128)(2,1)} custom-call(s32[1,256]{1,0:T(1,128)} %bitcast.21, s32[1,256]{1,0:T(1,128)} %bitcast.22, bf16[256,32,128]{2,1,0:T(8,128)(2,1)} %lat_ref.3), custom_call_target="tpu_custom_call" | custom-call | flops 603979776 | bytes 4718592 | tf_op jit(solution)/shard_map/pallas_call | solution.py:412
  24.5 5.8 %shard_map.102 = (f32[512,256]{1,0:T(8,128)}, f32[512,256]{1,0:T(8,128)}, bf16[192,256]{1,0:T(8,128)(2,1)}) custom-call(s32[1,256]{1,0:T(1,128)} %bitcast.23, bf16[9,256,256]{2,1,0:T(8,128)(2,1)} %shard_map.100.x_ref, bf16[128,256]{1,0:T(8,128)(2,1)} %copy-done.14, bf16[128,256]{1,0:T(8,128)(2,1)} %copy-done.15, bf16[34,256]{1,0:T(8,128)(2,1)} %get-tuple-element.64.left_ref, ...), custom_call_target="tpu_custom_call" | custom-call | flops 1207959552 | bytes 4587520 | tf_op jit(solution)/shard_map/pallas_call | solution.py:425
  30.3 3.6 %collective-permute-start.3 = (bf16[192,256]{1,0:T(8,128)(2,1)}, bf16[192,256]{1,0:T(8,128)(2,1)S(1)}, u32[]{:S(2)}, u32[]{:S(2)}) collective-permute-start(bf16[192,256]{1,0:T(8,128)(2,1)} %get-tuple-element.37.rest_0_), channel_id=1, source_target_pairs={{0,24},{8,0},{16,8},{24,16},{1,25},{9,1},{17,9},{25,17},{2,26},{10... | collective-permute-start | bytes 294920 | tf_op jit(solution)/shard_map/ppermute | solution.py:356
  36.1 5.6 %shard_map.103 = (f32[512,256]{1,0:T(8,128)}, f32[512,256]{1,0:T(8,128)}, f32[768,256]{1,0:T(8,128)}, f32[768,256]{1,0:T(8,128)}, bf16[192,1024]{1,0:T(8,128)(2,1)}, /*index=5*/bf16[1024,768]{1,0:T(8,128)(2,1)}) custom-call(s32[1]{0:T(128)} %bitcast.1.lev_ref, s32[1,1]{1,0:T(1,128)S(6)} %copy.12.count_ref, f32[512,256]{1,0:T(8,128)} %get-tuple-element.29.one_ref, ...), custom_call_target="tpu_custom_call" | custom-call | flops 603979776 | bytes 18350080 | tf_op jit(solution)/shard_map/pallas_call | solution.py:435
  41.8 1.9 %collective-permute-done.4.rest_2_ = bf16[192,256]{1,0:T(8,128)(2,1)S(1)} collective-permute-done((bf16[192,256]{1,0:T(8,128)(2,1)}, bf16[192,256]{1,0:T(8,128)(2,1)S(1)}, u32[]{:S(2)}, u32[]{:S(2)}) %collective-permute-start.4) | collective-permute-done | bytes 98336 | tf_op jit(solution)/shard_map/ppermute | solution.py:356
  44.4 9.7 %shard_map.104 = (bf16[9,64,256]{2,1,0:T(8,128)(2,1)}, bf16[9,64,256]{2,1,0:T(8,128)(2,1)}, bf16[9,64,256]{2,1,0:T(8,128)(2,1)}, bf16[9,64,256]{2,1,0:T(8,128)(2,1)}) custom-call(s32[1]{0:T(128)} %bitcast.1.lev_ref, bf16[1024,768]{1,0:T(8,128)(2,1)} %inner_ref.3, bf16[192,1024]{1,0:T(8,128)(2,1)} %get-tuple-element.31.innert_ref, ...), custom_call_target="tpu_custom_call" | custom-call | flops 2415919104 | bytes 4718592 | tf_op jit(solution)/shard_map/pallas_call | solution.py:452
  54.1 2.6 %shard_map.105 = (bf16[2,4,64,128]{3,2,1,0:T(8,128)(2,1)}, bf16[4,64,128]{2,1,0:T(8,128)(2,1)}) custom-call(s32[1,256]{1,0:T(1,128)} %bitcast.24, bf16[9,64,256]{2,1,0:T(8,128)(2,1)} %get-tuple-element.38.rest_0_, bf16[9,64,256]{2,1,0:T(8,128)(2,1)} %get-tuple-element.39.rest_1_, bf16[9,64,256]{2,1,0:T(8,128)(2,1)} %get-tuple-element.40.rest_2_, ...), custom_call_target="tpu_custom_call" | custom-call | flops 75497472 | bytes 786432 | tf_op jit(solution)/shard_map/pallas_call | solution.py:481
  57.3 1.9 %constant_dynamic-slice_fusion.own_ref = bf16[64,32,128]{2,1,0:T(8,128)(2,1)} fusion(bf16[256,32,128]{2,1,0:T(8,128)(2,1)} %lat_ref.3, s32[]{:T(128)S(6)} %select_n.3), kind=kLoop, calls=%fused_computation.11 | loop fusion | bytes 1048580 | tf_op jit(solution)/shard_map/dynamic_slice | solution.py:499
  59.7 1.7 %collective-permute-start.7 = (bf16[9,64,256]{2,1,0:T(8,128)(2,1)S(1)}, bf16[9,64,256]{2,1,0:T(8,128)(2,1)S(1)}, u32[]{:S(2)}, u32[]{:S(2)}) collective-permute-start(bf16[9,64,256]{2,1,0:T(8,128)(2,1)S(1)} %copy-done.1), channel_id=1, source_target_pairs={{0,16},{8,24},{16,0},{24,8},{1,17},{9,25},{17,1},{25,9},{2,18},{10... | collective-permute-start | bytes 884744 | tf_op jit(solution)/shard_map/ppermute | solution.py:356
  61.5 2.9 %collective-permute-start.8 = (bf16[9,64,256]{2,1,0:T(8,128)(2,1)S(1)}, bf16[9,64,256]{2,1,0:T(8,128)(2,1)S(1)}, u32[]{:S(2)}, u32[]{:S(2)}) collective-permute-start(bf16[9,64,256]{2,1,0:T(8,128)(2,1)S(1)} %copy-done), channel_id=1, source_target_pairs={{0,24},{8,0},{16,8},{24,16},{1,25},{9,1},{17,9},{25,17},{2,26},{10... | collective-permute-start | bytes 884744 | tf_op jit(solution)/shard_map/ppermute | solution.py:356
  64.9 1.8 %shard_map.106 = (bf16[4,64,128]{2,1,0:T(8,128)(2,1)}, bf16[4,64,128]{2,1,0:T(8,128)(2,1)}, bf16[4,64,128]{2,1,0:T(8,128)(2,1)}) custom-call(bf16[2,4,64,128]{3,2,1,0:T(8,128)(2,1)} %get-tuple-element.42.rowin_ref, bf16[4,64,128]{2,1,0:T(8,128)(2,1)} %copy-done.6, bf16[4,64,128]{2,1,0:T(8,128)(2,1)} %copy-done.6), custom_call_target="tpu_custom_call" | custom-call | flops 9437184 | bytes 786432 | tf_op jit(solution)/shard_map/pallas_call | solution.py:488
  66.7 1.3 %collective-permute-start.10 = (bf16[4,64,128]{2,1,0:T(8,128)(2,1)}, bf16[4,64,128]{2,1,0:T(8,128)(2,1)S(1)}, u32[]{:S(2)}, u32[]{:S(2)}) collective-permute-start(bf16[4,64,128]{2,1,0:T(8,128)(2,1)} %get-tuple-element.44), channel_id=1, source_target_pairs={{0,2},{2,4},{4,6},{1,3},{3,5},{5,7},{8,10},{10,12},{12,14},{9,11},... | collective-permute-start | bytes 196616 | tf_op jit(solution)/shard_map/ppermute | solution.py:356
  68.0 1.3 %collective-permute-start.11 = (bf16[4,64,128]{2,1,0:T(8,128)(2,1)}, bf16[4,64,128]{2,1,0:T(8,128)(2,1)S(1)}, u32[]{:S(2)}, u32[]{:S(2)}) collective-permute-start(bf16[4,64,128]{2,1,0:T(8,128)(2,1)} %get-tuple-element.45), channel_id=1, source_target_pairs={{2,0},{4,2},{6,4},{3,1},{5,3},{7,5},{10,8},{12,10},{14,12},{11,9},... | collective-permute-start | bytes 196616 | tf_op jit(solution)/shard_map/ppermute | solution.py:356
  70.1 3.4 %collective-permute-done.11 = bf16[4,64,128]{2,1,0:T(8,128)(2,1)S(1)} collective-permute-done((bf16[4,64,128]{2,1,0:T(8,128)(2,1)}, bf16[4,64,128]{2,1,0:T(8,128)(2,1)S(1)}, u32[]{:S(2)}, u32[]{:S(2)}) %collective-permute-start.11) | collective-permute-done | bytes 65568 | tf_op jit(solution)/shard_map/ppermute | solution.py:356
  73.5 2.0 %collective-permute-start.14 = (bf16[3,64,128]{2,1,0:T(8,128)(2,1)S(1)}, bf16[3,64,128]{2,1,0:T(8,128)(2,1)S(1)}, u32[]{:S(2)}, u32[]{:S(2)}) collective-permute-start(bf16[3,64,128]{2,1,0:T(8,128)(2,1)S(1)} %pad_maximum_fusion.3), channel_id=1, source_target_pairs={{0,24},{8,0},{16,8},{24,16},{1,25},{9,1},{17,9},{25,17},{2,26},{10... | collective-permute-start | bytes 147464 | tf_op jit(solution)/shard_map/ppermute | solution.py:356
  75.6 7.8 %collective-permute-done.14.rest_7_ = bf16[3,64,128]{2,1,0:T(8,128)(2,1)S(1)} collective-permute-done((bf16[3,64,128]{2,1,0:T(8,128)(2,1)S(1)}, bf16[3,64,128]{2,1,0:T(8,128)(2,1)S(1)}, u32[]{:S(2)}, u32[]{:S(2)}) %collective-permute-start.14) | collective-permute-done | bytes 49184 | tf_op jit(solution)/shard_map/ppermute | solution.py:356
  83.4 9.2 %collective-permute-start.12 = (bf16[3,64,128]{2,1,0:T(8,128)(2,1)S(1)}, bf16[3,64,128]{2,1,0:T(8,128)(2,1)S(1)}, u32[]{:S(2)}, u32[]{:S(2)}) collective-permute-start(bf16[3,64,128]{2,1,0:T(8,128)(2,1)S(1)} %pad_maximum_fusion.1), channel_id=1, source_target_pairs={{0,8},{8,16},{16,24},{24,0},{1,9},{9,17},{17,25},{25,1},{2,10},{10... | collective-permute-start | bytes 147464 | tf_op jit(solution)/shard_map/ppermute | solution.py:356
  93.2 1.1 %collective-permute-done.12.rest_5_ = bf16[3,64,128]{2,1,0:T(8,128)(2,1)S(1)} collective-permute-done((bf16[3,64,128]{2,1,0:T(8,128)(2,1)S(1)}, bf16[3,64,128]{2,1,0:T(8,128)(2,1)S(1)}, u32[]{:S(2)}, u32[]{:S(2)}) %collective-permute-start.12) | collective-permute-done | bytes 49184 | tf_op jit(solution)/shard_map/ppermute | solution.py:356
  95.9 4.5 %shard_map.107 = f32[64,32,128]{2,1,0:T(8,128)} custom-call(s32[1,256]{1,0:T(1,128)} %bitcast.25, bf16[64,32,128]{2,1,0:T(8,128)(2,1)} %constant_dynamic-slice_fusion.own_ref, bf16[9,64,256]{2,1,0:T(8,128)(2,1)} %get-tuple-element.38.rest_0_, bf16[9,64,256]{2,1,0:T(8,128)(2,1)} %copy-done.3, bf16[9,64,256]{2,1,0:T(8,128)(2,1)} %copy-done.4, ...), custom_call_target="tpu_custom_call" | custom-call | flops 150994944 | bytes 4194304 | tf_op jit(solution)/shard_map/pallas_call | solution.py:500
  (62 shorter events, 8.6 us)
Async XLA Ops:
  4.9 7.8 %collective-permute-start = (bf16[128,256]{1,0:T(8,128)(2,1)}, bf16[128,256]{1,0:T(8,128)(2,1)S(1)}, u32[]{:S(2)}, u32[]{:S(2)}) collective-permute-start(bf16[128,256]{1,0:T(8,128)(2,1)} %get-tuple-element.26), channel_id=1, source_target_pairs={{0,2},{2,4},{4,6},{1,3},{3,5},{5,7},{8,10},{10,12},{12,14},{9,11},... | collective-permute-start | bytes 196616 | tf_op jit(solution)/shard_map/ppermute | solution.py:356
  7.3 5.5 %collective-permute-start.1 = (bf16[128,256]{1,0:T(8,128)(2,1)}, bf16[128,256]{1,0:T(8,128)(2,1)S(1)}, u32[]{:S(2)}, u32[]{:S(2)}) collective-permute-start(bf16[128,256]{1,0:T(8,128)(2,1)} %get-tuple-element.27), channel_id=1, source_target_pairs={{2,0},{4,2},{6,4},{3,1},{5,3},{7,5},{10,8},{12,10},{14,12},{11,9},... | collective-permute-start | bytes 196616 | tf_op jit(solution)/shard_map/ppermute | solution.py:356
  12.7 11.8 %copy-start.14 = (bf16[128,256]{1,0:T(8,128)(2,1)}, bf16[128,256]{1,0:T(8,128)(2,1)S(1)}, u32[]{:S(2)}) copy-start(bf16[128,256]{1,0:T(8,128)(2,1)S(1)} %collective-permute-done.above_ref) | copy-start | bytes 196612
  12.8 11.7 %copy-start.15 = (bf16[128,256]{1,0:T(8,128)(2,1)}, bf16[128,256]{1,0:T(8,128)(2,1)S(1)}, u32[]{:S(2)}) copy-start(bf16[128,256]{1,0:T(8,128)(2,1)S(1)} %collective-permute-done.1.below_ref) | copy-start | bytes 196612
  12.8 11.1 %collective-permute-start.2 = (bf16[2,34,256]{2,1,0:T(8,128)(2,1)S(1)}, bf16[2,34,256]{2,1,0:T(8,128)(2,1)S(1)}, u32[]{:S(2)}, u32[]{:S(2)}) collective-permute-start(bf16[2,34,256]{2,1,0:T(8,128)(2,1)S(1)} %pad_maximum_fusion.4), channel_id=1, source_target_pairs={{0,1},{1,0},{2,3},{3,2},{4,5},{5,4},{6,7},{7,6},{8,9},{9,8},{10,11... | collective-permute-start | bytes 104456 | tf_op jit(solution)/shard_map/ppermute | solution.py:356
  24.5 10.4 %copy-start.13 = (f32[768]{0:T(1024)S(1)}, f32[768]{0:T(1024)}, u32[]{:S(2)}) copy-start(f32[768]{0:T(1024)} %param.17) | copy-start | bytes 9220
  30.3 11.5 %collective-permute-start.3 = (bf16[192,256]{1,0:T(8,128)(2,1)}, bf16[192,256]{1,0:T(8,128)(2,1)S(1)}, u32[]{:S(2)}, u32[]{:S(2)}) collective-permute-start(bf16[192,256]{1,0:T(8,128)(2,1)} %get-tuple-element.37.rest_0_), channel_id=1, source_target_pairs={{0,24},{8,0},{16,8},{24,16},{1,25},{9,1},{17,9},{25,17},{2,26},{10... | collective-permute-start | bytes 294920 | tf_op jit(solution)/shard_map/ppermute | solution.py:356
  33.9 9.8 %collective-permute-start.4 = (bf16[192,256]{1,0:T(8,128)(2,1)}, bf16[192,256]{1,0:T(8,128)(2,1)S(1)}, u32[]{:S(2)}, u32[]{:S(2)}) collective-permute-start(bf16[192,256]{1,0:T(8,128)(2,1)} %get-tuple-element.37.rest_0_), channel_id=1, source_target_pairs={{0,16},{8,24},{16,0},{24,8},{1,17},{9,25},{17,1},{25,9},{2,18},{10... | collective-permute-start | bytes 294920 | tf_op jit(solution)/shard_map/ppermute | solution.py:356
  33.9 9.8 %collective-permute-start.5 = (bf16[192,256]{1,0:T(8,128)(2,1)}, bf16[192,256]{1,0:T(8,128)(2,1)S(1)}, u32[]{:S(2)}, u32[]{:S(2)}) collective-permute-start(bf16[192,256]{1,0:T(8,128)(2,1)} %get-tuple-element.37.rest_0_), channel_id=1, source_target_pairs={{0,8},{8,16},{16,24},{24,0},{1,9},{9,17},{17,25},{25,1},{2,10},{10... | collective-permute-start | bytes 294920 | tf_op jit(solution)/shard_map/ppermute | solution.py:356
  41.7 1.9 %copy-start.7 = (bf16[192,256]{1,0:T(8,128)(2,1)}, bf16[192,256]{1,0:T(8,128)(2,1)S(1)}, u32[]{:S(2)}) copy-start(bf16[192,256]{1,0:T(8,128)(2,1)S(1)} %collective-permute-done.3.rest_1_) | copy-start | bytes 294916
  54.1 5.1 %copy-start.2 = (bf16[9,64,256]{2,1,0:T(8,128)(2,1)S(1)}, bf16[9,64,256]{2,1,0:T(8,128)(2,1)}, u32[]{:S(2)}) copy-start(bf16[9,64,256]{2,1,0:T(8,128)(2,1)} %get-tuple-element.39.rest_1_) | copy-start | bytes 884740
  54.1 5.6 %copy-start.1 = (bf16[9,64,256]{2,1,0:T(8,128)(2,1)S(1)}, bf16[9,64,256]{2,1,0:T(8,128)(2,1)}, u32[]{:S(2)}) copy-start(bf16[9,64,256]{2,1,0:T(8,128)(2,1)} %get-tuple-element.40.rest_2_) | copy-start | bytes 884740
  54.1 7.3 %copy-start = (bf16[9,64,256]{2,1,0:T(8,128)(2,1)S(1)}, bf16[9,64,256]{2,1,0:T(8,128)(2,1)}, u32[]{:S(2)}) copy-start(bf16[9,64,256]{2,1,0:T(8,128)(2,1)} %get-tuple-element.41.rest_3_) | copy-start | bytes 884740
  56.7 7.6 %collective-permute-start.9 = (bf16[4,64,128]{2,1,0:T(8,128)(2,1)}, bf16[4,64,128]{2,1,0:T(8,128)(2,1)S(1)}, u32[]{:S(2)}, u32[]{:S(2)}) collective-permute-start(bf16[4,64,128]{2,1,0:T(8,128)(2,1)} %get-tuple-element.43), channel_id=1, source_target_pairs={{0,1},{1,0},{2,3},{3,2},{4,5},{5,4},{6,7},{7,6},{8,9},{9,8},{10,11... | collective-permute-start | bytes 196616 | tf_op jit(solution)/shard_map/ppermute | solution.py:356
  59.2 35.2 %collective-permute-start.6 = (bf16[9,64,256]{2,1,0:T(8,128)(2,1)S(1)}, bf16[9,64,256]{2,1,0:T(8,128)(2,1)S(1)}, u32[]{:S(2)}, u32[]{:S(2)}) collective-permute-start(bf16[9,64,256]{2,1,0:T(8,128)(2,1)S(1)} %copy-done.2), channel_id=1, source_target_pairs={{0,8},{8,16},{16,24},{24,0},{1,9},{9,17},{17,25},{25,1},{2,10},{10... | collective-permute-start | bytes 884744 | tf_op jit(solution)/shard_map/ppermute | solution.py:356
  59.7 34.6 %collective-permute-start.7 = (bf16[9,64,256]{2,1,0:T(8,128)(2,1)S(1)}, bf16[9,64,256]{2,1,0:T(8,128)(2,1)S(1)}, u32[]{:S(2)}, u32[]{:S(2)}) collective-permute-start(bf16[9,64,256]{2,1,0:T(8,128)(2,1)S(1)} %copy-done.1), channel_id=1, source_target_pairs={{0,16},{8,24},{16,0},{24,8},{1,17},{9,25},{17,1},{25,9},{2,18},{10... | collective-permute-start | bytes 884744 | tf_op jit(solution)/shard_map/ppermute | solution.py:356
  61.5 32.9 %collective-permute-start.8 = (bf16[9,64,256]{2,1,0:T(8,128)(2,1)S(1)}, bf16[9,64,256]{2,1,0:T(8,128)(2,1)S(1)}, u32[]{:S(2)}, u32[]{:S(2)}) collective-permute-start(bf16[9,64,256]{2,1,0:T(8,128)(2,1)S(1)} %copy-done), channel_id=1, source_target_pairs={{0,24},{8,0},{16,8},{24,16},{1,25},{9,1},{17,9},{25,17},{2,26},{10... | collective-permute-start | bytes 884744 | tf_op jit(solution)/shard_map/ppermute | solution.py:356
  66.7 3.4 %collective-permute-start.10 = (bf16[4,64,128]{2,1,0:T(8,128)(2,1)}, bf16[4,64,128]{2,1,0:T(8,128)(2,1)S(1)}, u32[]{:S(2)}, u32[]{:S(2)}) collective-permute-start(bf16[4,64,128]{2,1,0:T(8,128)(2,1)} %get-tuple-element.44), channel_id=1, source_target_pairs={{0,2},{2,4},{4,6},{1,3},{3,5},{5,7},{8,10},{10,12},{12,14},{9,11},... | collective-permute-start | bytes 196616 | tf_op jit(solution)/shard_map/ppermute | solution.py:356
  68.0 5.5 %collective-permute-start.11 = (bf16[4,64,128]{2,1,0:T(8,128)(2,1)}, bf16[4,64,128]{2,1,0:T(8,128)(2,1)S(1)}, u32[]{:S(2)}, u32[]{:S(2)}) collective-permute-start(bf16[4,64,128]{2,1,0:T(8,128)(2,1)} %get-tuple-element.45), channel_id=1, source_target_pairs={{2,0},{4,2},{6,4},{3,1},{5,3},{7,5},{10,8},{12,10},{14,12},{11,9},... | collective-permute-start | bytes 196616 | tf_op jit(solution)/shard_map/ppermute | solution.py:356
  73.5 9.9 %collective-permute-start.14 = (bf16[3,64,128]{2,1,0:T(8,128)(2,1)S(1)}, bf16[3,64,128]{2,1,0:T(8,128)(2,1)S(1)}, u32[]{:S(2)}, u32[]{:S(2)}) collective-permute-start(bf16[3,64,128]{2,1,0:T(8,128)(2,1)S(1)} %pad_maximum_fusion.3), channel_id=1, source_target_pairs={{0,24},{8,0},{16,8},{24,16},{1,25},{9,1},{17,9},{25,17},{2,26},{10... | collective-permute-start | bytes 147464 | tf_op jit(solution)/shard_map/ppermute | solution.py:356
  75.5 17.7 %collective-permute-start.13 = (bf16[3,64,128]{2,1,0:T(8,128)(2,1)S(1)}, bf16[3,64,128]{2,1,0:T(8,128)(2,1)S(1)}, u32[]{:S(2)}, u32[]{:S(2)}) collective-permute-start(bf16[3,64,128]{2,1,0:T(8,128)(2,1)S(1)} %pad_maximum_fusion.2), channel_id=1, source_target_pairs={{0,16},{8,24},{16,0},{24,8},{1,17},{9,25},{17,1},{25,9},{2,18},{10... | collective-permute-start | bytes 147464 | tf_op jit(solution)/shard_map/ppermute | solution.py:356
  83.4 11.0 %copy-start.10 = (bf16[3,64,128]{2,1,0:T(8,128)(2,1)}, bf16[3,64,128]{2,1,0:T(8,128)(2,1)S(1)}, u32[]{:S(2)}) copy-start(bf16[3,64,128]{2,1,0:T(8,128)(2,1)S(1)} %collective-permute-done.14.rest_7_) | copy-start | bytes 147460
  83.4 11.0 %collective-permute-start.12 = (bf16[3,64,128]{2,1,0:T(8,128)(2,1)S(1)}, bf16[3,64,128]{2,1,0:T(8,128)(2,1)S(1)}, u32[]{:S(2)}, u32[]{:S(2)}) collective-permute-start(bf16[3,64,128]{2,1,0:T(8,128)(2,1)S(1)} %pad_maximum_fusion.1), channel_id=1, source_target_pairs={{0,8},{8,16},{16,24},{24,0},{1,9},{9,17},{17,25},{25,1},{2,10},{10... | collective-permute-start | bytes 147464 | tf_op jit(solution)/shard_map/ppermute | solution.py:356
  93.2 1.2 %copy-start.11 = (bf16[3,64,128]{2,1,0:T(8,128)(2,1)}, bf16[3,64,128]{2,1,0:T(8,128)(2,1)S(1)}, u32[]{:S(2)}) copy-start(bf16[3,64,128]{2,1,0:T(8,128)(2,1)S(1)} %collective-permute-done.13.rest_6_) | copy-start | bytes 147460
  (7 other events, 4.9 us)

commit v2 on v1

--- a/solution.py
+++ b/solution.py
@@ -56,7 +56,7 @@
     return jnp.broadcast_to(index_ref[...], (128, slots)).T
 
 
-def call(kernel, out_shape, in_specs, flops, **kwargs):
+def call(kernel, out_shape, in_specs, flops, mib, **kwargs):
     bytes_out = sum(s.size * s.dtype.itemsize for s in jax.tree.leaves(out_shape))
     return pl.pallas_call(
         kernel,
@@ -66,40 +66,40 @@
         cost_estimate=pl.CostEstimate(
             flops=flops, bytes_accessed=4 * bytes_out, transcendentals=0
         ),
+        compiler_params=pltpu.CompilerParams(vmem_limit_bytes=mib << 20),
         **kwargs,
     )
 
 
+EARLY = 5
+
 VM = pl.BlockSpec(memory_space=pltpu.VMEM)
 SM = pl.BlockSpec(memory_space=pltpu.SMEM)
-
-
-def strip_kernel(lat_ref, top_ref, bottom_ref, side_ref, wide_ref, keep_ref):
+ANY = pl.BlockSpec(memory_space=pl.ANY)
+
+
+def turn_kernel(lat_ref, tile_ref, top_ref, bottom_ref, side_ref, wide_ref, keep_ref):
     chans, rows, cols = lat_ref.shape
     wide_ref[...] = lat_ref[...].reshape(chans * rows, cols).astype(F32)
-    which = lax.broadcasted_iota(jnp.int32, (8, cols), 0)
-    lane = lax.broadcasted_iota(jnp.int32, (8, cols), 1)
-    pick = hot(((which == 0) & (lane == 0)) | ((which == 1) & (lane == cols - 1)))
     for r in range(rows):
-        line = wide_ref[pl.ds(r, chans, stride=rows), :].astype(BF16)
-        ends = nt(pick, line)
-        keep_ref[0, r : r + 1, :] = ends[0:1]
-        keep_ref[1, r : r + 1, :] = ends[1:2]
+        line = wide_ref[pl.ds(r, chans, stride=rows), :].astype(BF16).T
+        tile_ref[r * cols : (r + 1) * cols, :] = line
+        keep_ref[0, r : r + 1, :] = line[0:1].astype(F32)
+        keep_ref[1, r : r + 1, :] = line[cols - 1 : cols].astype(F32)
         if r == 0:
-            top_ref[...] = line.T
+            top_ref[...] = line
         if r == rows - 1:
-            bottom_ref[...] = line.T
+            bottom_ref[...] = line
     side_ref[...] = keep_ref[...].astype(BF16)
 
 
-def gather_kernel(index_sm, index_ref, lat_ref, out_ref, wide_ref, table_ref, x_ref):
-    chans, rows, cols = lat_ref.shape
+def gather_kernel(rows, cols, index_sm, index_ref, tile_ref, out_ref, table_ref, x_ref):
+    chans = tile_ref.shape[1]
     slots = index_ref.shape[1]
     halves = chans // 128
     lead = cols + 8
-    wide_ref[...] = lat_ref[...].reshape(chans * rows, cols).astype(F32)
     for r in range(rows):
-        line = wide_ref[pl.ds(r, chans, stride=rows), :].astype(BF16).T.astype(F32)
+        line = tile_ref[r * cols : (r + 1) * cols, :].astype(F32)
         for b in range(3):
             for h in range(halves):
                 at = (lead + r * cols - b + 1) * 8 + halves * b + h
@@ -153,8 +153,8 @@
     halo_ref[...] = jnp.zeros_like(halo_ref)
     halo_ref[0:cols, :] = above_ref[...]
     halo_ref[cols : 2 * cols, :] = below_ref[...]
-    halo_ref[2 * cols : 2 * cols + rows + 2, :] = left_ref[...]
-    halo_ref[2 * cols + tall : 2 * cols + tall + rows + 2, :] = right_ref[...]
+    halo_ref[2 * cols : 2 * cols + rows + 2, :] = left_ref[1]
+    halo_ref[2 * cols + tall : 2 * cols + tall + rows + 2, :] = right_ref[0]
     row, col = split(upright(index_ref), cols)
     cells = lax.broadcasted_iota(jnp.int32, (slots, width), 1)
     acc = None
@@ -229,8 +229,9 @@
     *rest,
 ):
     blocks = rest[:lev_count]
-    outs = rest[lev_count : 2 * lev_count]
-    f_ref, mis_ref, g_ref = rest[2 * lev_count :]
+    early = rest[lev_count : 2 * lev_count]
+    late = rest[2 * lev_count : 3 * lev_count]
+    f_ref, mis_ref, g_ref = rest[3 * lev_count :]
     lev = lev_ref[0]
     own = blocks[0].shape[0]
     for k in range(lev_count):
@@ -261,60 +262,86 @@
         for d in range(lev_count):
             g_ref[d, t] = patch[d * portion : (d + 1) * portion]
     for k in range(lev_count):
-        outs[k][...] = g_ref[lax.rem(lev + k, lev_count)]
+        to = lax.rem(lev + k, lev_count)
+        early[k][...] = g_ref[to, 0:EARLY]
+        late[k][...] = g_ref[to, EARLY:taps]
 
 
 def edge_kernel(rows, cols, index_ref, *rest):
     blocks, (rowout_ref, colout_ref) = rest[:-2], rest[-2:]
+    half = len(blocks) // 2
     row, col = split(index_ref[...], cols)
     rowc, colc = split(upright(index_ref), cols)
     slots = row.shape[1]
     cells = lax.broadcasted_iota(jnp.int32, (slots, cols), 1)
     lines = lax.broadcasted_iota(jnp.int32, (slots, 128), 1)
-    for k, block in enumerate(blocks):
+    for k in range(half):
+        block = [blocks[k].at[t] for t in range(EARLY)]
+        block += [blocks[half + k].at[t] for t in range(9 - EARLY)]
         for e, (edge, a) in enumerate(((0, 0), (rows - 1, 2))):
             acc = None
             for b in range(3):
-                part = jnp.where(row == edge, block[3 * a + b].astype(F32), 0.0).astype(BF16)
+                part = jnp.where(row == edge, block[3 * a + b][...].astype(F32), 0.0).astype(BF16)
                 part = nn(part, hot(colc + (b - 1) == cells))
                 acc = part if acc is None else acc + part
             rowout_ref[e, k] = acc.astype(BF16)
         acc = None
         for e, (edge, b) in enumerate(((0, 0), (cols - 1, 2))):
             for a in range(3):
-                part = jnp.where(col == edge, block[3 * a + b].astype(F32), 0.0).astype(BF16)
+                part = jnp.where(col == edge, block[3 * a + b][...].astype(F32), 0.0).astype(BF16)
                 part = nn(part, hot(rowc + (a + 64 * e) == lines))
                 acc = part if acc is None else acc + part
         colout_ref[k] = acc.astype(BF16)
 
 
-def corner_kernel(rows, cols, rowin_ref, left_ref, right_ref, up_ref, down_ref, side_ref):
-    from_left = left_ref[...].astype(F32)
-    from_right = right_ref[...].astype(F32)
+def corner_kernel(rows, cols, rowin_ref, left_ref, right_ref, up_ref, down_ref):
     lane = lax.broadcasted_iota(jnp.int32, up_ref.shape, 2)
     for e, (at, ref) in enumerate(((0, up_ref), (rows + 1, down_ref))):
         line = rowin_ref[e].astype(F32)
-        line = line + jnp.where(lane == 0, from_left[:, :, 64 + at : 65 + at], 0.0)
-        line = line + jnp.where(lane == cols - 1, from_right[:, :, at : at + 1], 0.0)
+        line = line + jnp.where(lane == 0, left_ref[:, :, 64 + at : 65 + at].astype(F32), 0.0)
+        line = line + jnp.where(
+            lane == cols - 1, right_ref[:, :, at : at + 1].astype(F32), 0.0
+        )
         ref[...] = line.astype(BF16)
-    spot = lax.broadcasted_iota(jnp.int32, side_ref.shape, 2)
-    side_ref[...] = jnp.where(spot < 64, right_ref[...].astype(F32), left_ref[...].astype(F32)).astype(BF16)
-
-
-def final_kernel(rows, cols, count, index_ref, own_ref, *rest):
-    blocks, edges, (out_ref, sum_ref, edge_ref) = rest[:count], rest[count:-3], rest[-3:]
-    total = blocks[0][...].astype(F32)
-    for block in blocks[1:]:
+
+
+def join_kernel(count, *refs):
+    late, (top_ref, bottom_ref, left_ref, right_ref) = refs[:count], refs[count : count + 4]
+    outs = refs[count + 4 :]
+    taps, portion, _ = late[0].shape
+    spot = lax.broadcasted_iota(jnp.int32, (portion, 128), 1)
+    for k in range(count):
+        outs[k][0:taps] = late[k][...]
+        outs[k][taps, :, 0:128] = top_ref[k]
+        outs[k][taps, :, 128:256] = bottom_ref[k]
+        side = jnp.where(spot < 64, right_ref[k].astype(F32), left_ref[k].astype(F32))
+        outs[k][taps + 1, :, 0:128] = side.astype(BF16)
+        outs[k][taps + 1, :, 128:256] = jnp.zeros_like(top_ref[k])
+
+
+def final_kernel(rows, cols, count, lev_ref, index_ref, latent_ref, *rest):
+    early, late = rest[:count], rest[count : 2 * count]
+    out_ref, own_ref, sum_ref, edge_ref, sem = rest[2 * count :]
+    portion = out_ref.shape[0]
+    fetch = pltpu.make_async_copy(
+        latent_ref.at[pl.ds(pl.multiple_of(lev_ref[0] * portion, 8), portion)], own_ref, sem
+    )
+    fetch.start()
+    total = early[0][...].astype(F32)
+    for block in early[1:]:
         total = total + block[...].astype(F32)
-    sum_ref[...] = total
-    total = edges[0][...].astype(F32)
-    for edge in edges[1:]:
-        total = total + edge[...].astype(F32)
-    edge_ref[...] = total
+    sum_ref[0:EARLY] = total
+    total = late[0][...].astype(F32)
+    for block in late[1:]:
+        total = total + block[...].astype(F32)
+    sum_ref[EARLY:] = total[: 9 - EARLY]
+    edge_ref[0] = total[9 - EARLY, :, 0:128]
+    edge_ref[1] = total[9 - EARLY, :, 128:256]
+    edge_ref[2] = total[10 - EARLY, :, 0:128]
+    fetch.wait()
     row, _ = split(index_ref[...], cols)
     _, colc = split(upright(index_ref), cols)
     slots = row.shape[1]
-    portion = out_ref.shape[0]
     cells = lax.broadcasted_iota(jnp.int32, (slots, cols), 1)
     hots = [hot(colc + (b - 1) == cells) for b in range(3)]
     lines = lax.broadcasted_iota(jnp.int32, (rows, slots), 0)
@@ -363,7 +390,7 @@
     return shift(x, axis, 1), shift(x, axis, -1)
 
 
-def per_device(
+def steps(
     latent,
     conv_weight,
     mid_weight,
@@ -389,11 +416,17 @@
     flops = 2 * taps * wide * chans * slots
 
     strip = jax.ShapeDtypeStruct((cols, chans), BF16)
-    top, bottom, ends = call(
-        strip_kernel,
-        (strip, strip, jax.ShapeDtypeStruct((2, rows, chans), BF16)),
+    tile, top, bottom, ends = call(
+        turn_kernel,
+        (
+            jax.ShapeDtypeStruct((rows * cols, chans), BF16),
+            strip,
+            strip,
+            jax.ShapeDtypeStruct((2, rows, chans), BF16),
+        ),
         [VM],
         flops // 4,
+        16,
         scratch_shapes=[
             pltpu.VMEM((chans * rows, cols), F32),
             pltpu.VMEM((2, rows, chans), F32),
@@ -410,16 +443,16 @@
     from_left, from_right = from_sides(columns, "lon")
 
     x = call(
-        gather_kernel,
+        functools.partial(gather_kernel, rows, cols),
         jax.ShapeDtypeStruct((taps, slots, chans), BF16),
         [SM, VM, VM],
         flops,
+        40,
         scratch_shapes=[
-            pltpu.VMEM((chans * rows, cols), F32),
             pltpu.VMEM((((rows + 2) * cols + 16) * 8, 128), F32),
             pltpu.VMEM((3, slots * 8, 128), F32),
         ],
-    )(index, index, latent)
+    )(index, index, tile)
     w = jnp.transpose(conv_weight, (2, 0, 1, 3)).reshape(taps, wide, chans)
     act_shape = jax.ShapeDtypeStruct((wide, slots), F32)
     one, two, fields = call(
@@ -427,8 +460,9 @@
         (act_shape, act_shape, jax.ShapeDtypeStruct((own, slots), BF16)),
         [VM] * 9,
         flops * 2,
+        20,
         scratch_shapes=[pltpu.VMEM((2 * cols + 128, chans), BF16)],
-    )(index, x, above, below, from_left[1], from_right[0], w, mid_weight, out_weight)
+    )(index, x, above, below, from_left, from_right, w, mid_weight, out_weight)
 
     blocks = [fields] + [shift(fields, "lev", -k) for k in range(1, lev_count)]
     column_shape = jax.ShapeDtypeStruct((own * lev_count, slots), F32)
@@ -444,16 +478,19 @@
         ),
         [SM, SM] + [VM] * 6,
         flops,
+        24,
         scratch_shapes=[pltpu.VMEM((inner.shape[1], inner.shape[0]), BF16)],
     )(lev_arr, obs_count, one, two, obs_values[0, 0], obs_weight[None, :], inner, outer)
     slope_one, slope_two, obs_turned, scale, inner_turned, outer_turned = turned
 
-    patch_shape = jax.ShapeDtypeStruct((taps, portion, slots), BF16)
+    early_shape = jax.ShapeDtypeStruct((EARLY, portion, slots), BF16)
+    late_shape = jax.ShapeDtypeStruct((taps - EARLY, portion, slots), BF16)
     patches = call(
         functools.partial(column_kernel, lev_count),
-        (patch_shape,) * lev_count,
+        (early_shape,) * lev_count + (late_shape,) * lev_count,
         [SM] + [VM] * (11 + lev_count),
         flops * 4,
+        32,
         scratch_shapes=[
             pltpu.VMEM((own * lev_count, slots), BF16),
             pltpu.VMEM((own * lev_count, slots), F32),
@@ -474,44 +511,56 @@
         out_weight,
         *blocks,
     )
-    parts = [patches[0]] + [shift(patches[k], "lev", k) for k in range(1, lev_count)]
+    early = [patches[0]]
+    for k in range(1, lev_count):
+        early.append(shift(patches[k], "lev", k))
 
     line_shape = jax.ShapeDtypeStruct((lev_count, portion, cols), BF16)
     side_shape = jax.ShapeDtypeStruct((lev_count, portion, 128), BF16)
     row_edge, col_edge = call(
         functools.partial(edge_kernel, rows, cols),
         (jax.ShapeDtypeStruct((2, lev_count, portion, cols), BF16), side_shape),
-        [VM] * (1 + lev_count),
+        [VM] * (1 + 2 * lev_count),
         flops // 8,
+        12,
     )(index, *patches)
     from_left, from_right = from_sides(col_edge, "lon")
-    up, down, side = call(
+    up, down = call(
         functools.partial(corner_kernel, rows, cols),
-        (line_shape, line_shape, side_shape),
+        (line_shape, line_shape),
         [VM] * 3,
         flops // 64,
+        8,
     )(row_edge, from_left, from_right)
     onto_first = shift(down, "lat", 1, wrap=False)
     onto_last = shift(up, "lat", -1, wrap=False)
-    rims = [jnp.stack([onto_first[k], onto_last[k], side[k]]) for k in range(lev_count)]
-    rims = [rims[0]] + [shift(rims[k], "lev", k) for k in range(1, lev_count)]
-
-    mine = lax.dynamic_slice_in_dim(latent, lev * portion, portion, 0)
+    joined = call(
+        functools.partial(join_kernel, lev_count),
+        (jax.ShapeDtypeStruct((taps - EARLY + 2, portion, slots), BF16),) * lev_count,
+        [VM] * (4 + lev_count),
+        flops // 64,
+        12,
+    )(*patches[lev_count:], onto_first, onto_last, from_left, from_right)
+    late = [joined[0]] + [shift(joined[k], "lev", k) for k in range(1, lev_count)]
+
     return call(
         functools.partial(final_kernel, rows, cols, lev_count),
         jax.ShapeDtypeStruct((portion, rows, cols), F32),
-        [VM] * (2 + 2 * lev_count),
+        [SM, VM, ANY] + [VM] * (2 * lev_count),
         flops // 4,
+        16,
         scratch_shapes=[
+            pltpu.VMEM((portion, rows, cols), BF16),
             pltpu.VMEM((taps, portion, slots), F32),
             pltpu.VMEM((3, portion, 128), F32),
+            pltpu.SemaphoreType.DMA,
         ],
-    )(index, mine, *parts, *rims)
+    )(lev_arr, index, latent, *early, *late)
 
 
 def solution(mesh):
     return jax.shard_map(
-        per_device,
+        steps,
         mesh=mesh,
         in_specs=(
             P(None, "lat", "lon"),

time: 101 us -> 88.9 us (0.88)
  the two profiles are of different devices: /device:TPU:0 before, /device:TPU:9 now
where the time goes in v2:
time: 88.9 us; the launch traced here: 88.5 us
  waiting for transfers between devices  32.1 us (36%)
  Pallas kernels  22.6 us (25%)
  starting transfers between devices  22.6 us (25%)
  local copies, waits for them, and re-layouts  9.97 us (11%)
  between operations  1.12 us (1%)
    ppermute x15, waiting for transfers between devices, shift(): return lax.ppermute(x, axis, pairs)  32.1 us
    ppermute x15, starting transfers between devices, shift(): return lax.ppermute(x, axis, pairs)  22.6 us
    unnamed x30, local copies, waits for them, and re-layouts  8.12 us
    pallas_call x1, Pallas kernels, steps(): call(functools.partial(column_kernel, lev_count), (early_shape,) * lev_co...  5.64 us
    pallas_call x1, Pallas kernels, steps(): call(turn_kernel, (jax.ShapeDtypeStruct((rows * cols, chans), BF16), stri...  4.1 us
    pallas_call x1, Pallas kernels, steps(): call(functools.partial(gather_kernel, rows, cols), jax.ShapeDtypeStruct((...  3.76 us
    pallas_call x1, Pallas kernels, steps(): call(functools.partial(final_kernel, rows, cols, lev_count), jax.ShapeDty...  3.06 us
    pallas_call x1, Pallas kernels, steps(): call(functools.partial(decode_kernel, rows, cols), (act_shape, act_shape,...  2.87 us
  transfers between devices with their start and end apart: 15, of which 5 were waited for; matrix products, arithmetic and copies ran while one was open for 2% of the time, Pallas kernels for 7%

profile of v2, /device:TPU:9, one launch (start us, length us, event | category | flops | bytes accessed | tf_op | source)
XLA Modules:
  0.0 88.5 jit_solution(2971295083943820006)
XLA Ops:
  0.0 1.6 %copy-done = bf16[256,32,128]{2,1,0:T(8,128)(2,1)S(1)} copy-done((bf16[256,32,128]{2,1,0:T(8,128)(2,1)S(1)}, bf16[256,32,128]{2,1,0:T(8,128)(2,1)}, u32[]{:S(2)}) %copy-start) | copy-done | bytes 2097176
  1.6 4.1 %shard_map.100 = (bf16[4096,256]{1,0:T(8,128)(2,1)S(1)}, bf16[128,256]{1,0:T(8,128)(2,1)S(1)}, bf16[128,256]{1,0:T(8,128)(2,1)S(1)}, bf16[2,32,256]{2,1,0:T(8,128)(2,1)S(1)}) custom-call(bf16[256,32,128]{2,1,0:T(8,128)(2,1)S(1)} %copy-done), custom_call_target="tpu_custom_call" | custom-call | flops 150994944 | bytes 9043968 | tf_op jit(solution)/shard_map/pallas_call | solution.py:419
  5.7 3.7 %collective-permute-start = (bf16[128,256]{1,0:T(8,128)(2,1)S(1)}, bf16[128,256]{1,0:T(8,128)(2,1)S(1)}, u32[]{:S(2)}, u32[]{:S(2)}) collective-permute-start(bf16[128,256]{1,0:T(8,128)(2,1)S(1)} %get-tuple-element.35), channel_id=1, source_target_pairs={{0,2},{2,4},{4,6},{1,3},{3,5},{5,7},{8,10},{10,12},{12,14},{9,11},... | collective-permute-start | bytes 196616 | tf_op jit(solution)/shard_map/ppermute | solution.py:383
  9.4 1.9 %collective-permute-start.1 = (bf16[128,256]{1,0:T(8,128)(2,1)S(1)}, bf16[128,256]{1,0:T(8,128)(2,1)S(1)}, u32[]{:S(2)}, u32[]{:S(2)}) collective-permute-start(bf16[128,256]{1,0:T(8,128)(2,1)S(1)} %get-tuple-element.36), channel_id=1, source_target_pairs={{2,0},{4,2},{6,4},{3,1},{5,3},{7,5},{10,8},{12,10},{14,12},{11,9},... | collective-permute-start | bytes 196616 | tf_op jit(solution)/shard_map/ppermute | solution.py:383
  11.4 1.8 %copy.11 = bf16[9,4,128,256]{3,2,1,0:T(8,128)(2,1)S(1)} copy(bf16[9,4,128,256]{3,2,0,1:T(8,128)(2,1)} %bitcast.21) | data formatting | bytes 4718592 | tf_op jit(solution)/shard_map/transpose | solution.py:456
  13.2 1.8 %collective-permute-done.1.below_ref = bf16[128,256]{1,0:T(8,128)(2,1)S(1)} collective-permute-done((bf16[128,256]{1,0:T(8,128)(2,1)S(1)}, bf16[128,256]{1,0:T(8,128)(2,1)S(1)}, u32[]{:S(2)}, u32[]{:S(2)}) %collective-permute-start.1) | collective-permute-done | bytes 65568 | tf_op jit(solution)/shard_map/ppermute | solution.py:383
  15.0 1.3 %collective-permute-start.2 = (bf16[2,34,256]{2,1,0:T(8,128)(2,1)S(1)}, bf16[2,34,256]{2,1,0:T(8,128)(2,1)S(1)}, u32[]{:S(2)}, u32[]{:S(2)}) collective-permute-start(bf16[2,34,256]{2,1,0:T(8,128)(2,1)S(1)} %pad_maximum_fusion), channel_id=1, source_target_pairs={{0,1},{1,0},{2,3},{3,2},{4,5},{5,4},{6,7},{7,6},{8,9},{9,8},{10,11... | collective-permute-start | bytes 104456 | tf_op jit(solution)/shard_map/ppermute | solution.py:383
  16.3 3.8 %shard_map.101.x_ref = bf16[9,256,256]{2,1,0:T(8,128)(2,1)S(1)} custom-call(s32[1,256]{1,0:T(1,128)S(1)} %bitcast.16, s32[1,256]{1,0:T(1,128)S(1)} %bitcast.17, bf16[4096,256]{1,0:T(8,128)(2,1)S(1)} %get-tuple-element.34.tile_ref), custom_call_target="tpu_custom_call" | custom-call | flops 603979776 | bytes 4718592 | tf_op jit(solution)/shard_map/pallas_call | solution.py:445
  20.1 2.9 %shard_map.102 = (f32[512,256]{1,0:T(8,128)S(1)}, f32[512,256]{1,0:T(8,128)S(1)}, bf16[192,256]{1,0:T(8,128)(2,1)S(1)}) custom-call(s32[1,256]{1,0:T(1,128)S(1)} %bitcast.18, bf16[9,256,256]{2,1,0:T(8,128)(2,1)S(1)} %shard_map.101.x_ref, bf16[128,256]{1,0:T(8,128)(2,1)S(1)} %collective-permute-done.above_ref, ...), custom_call_target="tpu_custom_call" | custom-call | flops 1207959552 | bytes 4587520 | tf_op jit(solution)/shard_map/pallas_call | solution.py:458
  24.6 1.3 %collective-permute-start.5 = (bf16[192,256]{1,0:T(8,128)(2,1)S(1)}, bf16[192,256]{1,0:T(8,128)(2,1)S(1)}, u32[]{:S(2)}, u32[]{:S(2)}) collective-permute-start(bf16[192,256]{1,0:T(8,128)(2,1)S(1)} %get-tuple-element.46.rest_0_), channel_id=1, source_target_pairs={{0,8},{8,16},{16,24},{24,0},{1,9},{9,17},{17,25},{25,1},{2,10},{10... | collective-permute-start | bytes 294920 | tf_op jit(solution)/shard_map/ppermute | solution.py:383
  26.9 1.5 %collective-permute-start.3 = (bf16[192,256]{1,0:T(8,128)(2,1)S(1)}, bf16[192,256]{1,0:T(8,128)(2,1)}, u32[]{:S(2)}, u32[]{:S(2)}) collective-permute-start(bf16[192,256]{1,0:T(8,128)(2,1)S(1)} %get-tuple-element.46.rest_0_), channel_id=1, source_target_pairs={{0,24},{8,0},{16,8},{24,16},{1,25},{9,1},{17,9},{25,17},{2,26},{10... | collective-permute-start | bytes 294920 | tf_op jit(solution)/shard_map/ppermute | solution.py:383
  29.1 1.4 %copy-done.2 = bf16[1024,768]{1,0:T(8,128)(2,1)S(1)} copy-done((bf16[1024,768]{1,0:T(8,128)(2,1)S(1)}, bf16[1024,768]{1,0:T(8,128)(2,1)}, u32[]{:S(2)}) %copy-start.2) | copy-done | bytes 1572888
  30.5 1.4 %copy-done.4 = bf16[768,1024]{1,0:T(8,128)(2,1)S(1)} copy-done((bf16[768,1024]{1,0:T(8,128)(2,1)S(1)}, bf16[768,1024]{1,0:T(8,128)(2,1)}, u32[]{:S(2)}) %copy-start.4) | copy-done | bytes 1572888
  34.0 2.3 %shard_map.103 = (f32[512,256]{1,0:T(8,128)S(1)}, f32[512,256]{1,0:T(8,128)S(1)}, f32[768,256]{1,0:T(8,128)S(1)}, f32[768,256]{1,0:T(8,128)S(1)}, bf16[192,1024]...) custom-call(s32[1]{0:T(128)} %bitcast.lev_ref, s32[1,1]{1,0:T(1,128)S(6)} %copy.12.count_ref, f32[512,256]{1,0:T(8,128)S(1)} %copy-done.8, ...), custom_call_target="tpu_custom_call" | custom-call | flops 603979776 | bytes 18350080 | tf_op jit(solution)/shard_map/pallas_call | solution.py:469
  36.3 5.6 %shard_map.104 = (bf16[5,64,256]{2,1,0:T(8,128)(2,1)S(1)}, bf16[5,64,256]{2,1,0:T(8,128)(2,1)S(1)}, bf16[5,64,256]{2,1,0:T(8,128)(2,1)S(1)}, bf16[5,64,256]{2,1,...) custom-call(s32[1]{0:T(128)} %bitcast.lev_ref, ...), custom_call_target="tpu_custom_call" | custom-call | flops 2415919104 | bytes 4718592 | tf_op jit(solution)/shard_map/pallas_call | solution.py:488
  43.0 3.2 %collective-permute-done.9.left_ref.right_ref.refs_6_.refs_7_ = bf16[4,64,128]{2,1,0:T(8,128)(2,1)S(1)} collective-permute-done((bf16[4,64,128]{2,1,0:T(8,128)(2,1)S(1)}, bf16[4,64,128]{2,1,0:T(8,128)(2,1)S(1)}, u32[]{:S(2)}, u32[]{:S(2)}) %collective-permute-start.9) | collective-permute-done | bytes 65568 | tf_op jit(solution)/shard_map/ppermute | solution.py:383
  46.3 3.9 %collective-permute-start.10 = (bf16[4,64,128]{2,1,0:T(8,128)(2,1)S(1)}, bf16[4,64,128]{2,1,0:T(8,128)(2,1)S(1)}, u32[]{:S(2)}, u32[]{:S(2)}) collective-permute-start(bf16[4,64,128]{2,1,0:T(8,128)(2,1)S(1)} %get-tuple-element.57), channel_id=1, source_target_pairs={{0,2},{2,4},{4,6},{1,3},{3,5},{5,7},{8,10},{10,12},{12,14},{9,11},... | collective-permute-start | bytes 196616 | tf_op jit(solution)/shard_map/ppermute | solution.py:383
  50.2 1.9 %collective-permute-start.11 = (bf16[4,64,128]{2,1,0:T(8,128)(2,1)S(1)}, bf16[4,64,128]{2,1,0:T(8,128)(2,1)S(1)}, u32[]{:S(2)}, u32[]{:S(2)}) collective-permute-start(bf16[4,64,128]{2,1,0:T(8,128)(2,1)S(1)} %get-tuple-element.58), channel_id=1, source_target_pairs={{2,0},{4,2},{6,4},{3,1},{5,3},{7,5},{10,8},{12,10},{14,12},{11,9},... | collective-permute-start | bytes 196616 | tf_op jit(solution)/shard_map/ppermute | solution.py:383
  52.1 3.6 %collective-permute-done.11.refs_5_ = bf16[4,64,128]{2,1,0:T(8,128)(2,1)S(1)} collective-permute-done((bf16[4,64,128]{2,1,0:T(8,128)(2,1)S(1)}, bf16[4,64,128]{2,1,0:T(8,128)(2,1)S(1)}, u32[]{:S(2)}, u32[]{:S(2)}) %collective-permute-start.11) | collective-permute-done | bytes 65568 | tf_op jit(solution)/shard_map/ppermute | solution.py:383
  55.9 3.1 %collective-permute-start.13 = (bf16[6,64,256]{2,1,0:T(8,128)(2,1)S(1)}, bf16[6,64,256]{2,1,0:T(8,128)(2,1)S(1)}, u32[]{:S(2)}, u32[]{:S(2)}) collective-permute-start(bf16[6,64,256]{2,1,0:T(8,128)(2,1)S(1)} %get-tuple-element.61), channel_id=1, source_target_pairs={{0,16},{8,24},{16,0},{24,8},{1,17},{9,25},{17,1},{25,9},{2,18},{10... | collective-permute-start | bytes 589832 | tf_op jit(solution)/shard_map/ppermute | solution.py:383
  59.7 2.0 %collective-permute-start.8 = (bf16[5,64,256]{2,1,0:T(8,128)(2,1)S(1)}, bf16[5,64,256]{2,1,0:T(8,128)(2,1)S(1)}, u32[]{:S(2)}, u32[]{:S(2)}) collective-permute-start(bf16[5,64,256]{2,1,0:T(8,128)(2,1)S(1)} %get-tuple-element.50.rest_3_), channel_id=1, source_target_pairs={{0,24},{8,0},{16,8},{24,16},{1,25},{9,1},{17,9},{25,17},{2,26},{10... | collective-permute-start | bytes 491528 | tf_op jit(solution)/shard_map/ppermute | solution.py:383
  61.7 20.1 %collective-permute-done.7.rest_2_ = bf16[5,64,256]{2,1,0:T(8,128)(2,1)S(1)} collective-permute-done((bf16[5,64,256]{2,1,0:T(8,128)(2,1)S(1)}, bf16[5,64,256]{2,1,0:T(8,128)(2,1)S(1)}, u32[]{:S(2)}, u32[]{:S(2)}) %collective-permute-start.7) | collective-permute-done | bytes 163872 | tf_op jit(solution)/shard_map/ppermute | solution.py:383
  81.7 3.5 %collective-permute-done.8.rest_3_ = bf16[5,64,256]{2,1,0:T(8,128)(2,1)S(1)} collective-permute-done((bf16[5,64,256]{2,1,0:T(8,128)(2,1)S(1)}, bf16[5,64,256]{2,1,0:T(8,128)(2,1)S(1)}, u32[]{:S(2)}, u32[]{:S(2)}) %collective-permute-start.8) | collective-permute-done | bytes 163872 | tf_op jit(solution)/shard_map/ppermute | solution.py:383
  85.2 3.1 %shard_map.108 = f32[64,32,128]{2,1,0:T(8,128)} custom-call(s32[1]{0:T(128)} %bitcast.lev_ref, s32[1,256]{1,0:T(1,128)S(1)} %bitcast.20, bf16[256,32,128]{2,1,0:T(8,128)(2,1)S(1)} %copy-done.1, bf16[5,64,256]{2,1,0:T(8,128)(2,1)S(1)} %get-tuple-element.47.rest_0_, bf16[5,64,256]{2,1,0:T(8,128)(2,1)S(1)} %collective-permute-done.6.rest_1_, ...), custom_call_target="tpu_custom_call" | custom-call | flops 150994944 | bytes 4194304 | tf_op jit(solution)/shard_map/pallas_call | solution.py:546
  (52 shorter events, 6.8 us)
Async XLA Ops:
  0.0 1.6 %copy-start = (bf16[256,32,128]{2,1,0:T(8,128)(2,1)S(1)}, bf16[256,32,128]{2,1,0:T(8,128)(2,1)}, u32[]{:S(2)}) copy-start(bf16[256,32,128]{2,1,0:T(8,128)(2,1)} %latent_ref.1) | copy-start | bytes 6291460
  5.7 7.5 %collective-permute-start = (bf16[128,256]{1,0:T(8,128)(2,1)S(1)}, bf16[128,256]{1,0:T(8,128)(2,1)S(1)}, u32[]{:S(2)}, u32[]{:S(2)}) collective-permute-start(bf16[128,256]{1,0:T(8,128)(2,1)S(1)} %get-tuple-element.35), channel_id=1, source_target_pairs={{0,2},{2,4},{4,6},{1,3},{3,5},{5,7},{8,10},{10,12},{12,14},{9,11},... | collective-permute-start | bytes 196616 | tf_op jit(solution)/shard_map/ppermute | solution.py:383
  9.4 5.6 %collective-permute-start.1 = (bf16[128,256]{1,0:T(8,128)(2,1)S(1)}, bf16[128,256]{1,0:T(8,128)(2,1)S(1)}, u32[]{:S(2)}, u32[]{:S(2)}) collective-permute-start(bf16[128,256]{1,0:T(8,128)(2,1)S(1)} %get-tuple-element.36), channel_id=1, source_target_pairs={{2,0},{4,2},{6,4},{3,1},{5,3},{7,5},{10,8},{12,10},{14,12},{11,9},... | collective-permute-start | bytes 196616 | tf_op jit(solution)/shard_map/ppermute | solution.py:383
  11.3 5.0 %copy-start.13 = (s32[1,1,256]{2,1,0:T(1,128)S(1)}, s32[1,1,256]{2,1,0:T(1,128)}, u32[]{:S(2)}) copy-start(s32[1,1,256]{2,1,0:T(1,128)} %param.18) | copy-start | bytes 3076
  13.2 6.9 %copy-start.11 = (bf16[4,128,128]{2,1,0:T(8,128)(2,1)S(1)}, bf16[4,128,128]{2,1,0:T(8,128)(2,1)}, u32[]{:S(2)}) copy-start(bf16[4,128,128]{2,1,0:T(8,128)(2,1)} %mid_ref.3) | copy-start | bytes 393220
  13.2 6.9 %copy-start.12 = (bf16[4,48,128]{2,1,0:T(8,128)(2,1)S(1)}, bf16[4,48,128]{2,1,0:T(8,128)(2,1)}, u32[]{:S(2)}) copy-start(bf16[4,48,128]{2,1,0:T(8,128)(2,1)} %outw_ref.3) | copy-start | bytes 147460
  15.0 5.0 %collective-permute-start.2 = (bf16[2,34,256]{2,1,0:T(8,128)(2,1)S(1)}, bf16[2,34,256]{2,1,0:T(8,128)(2,1)S(1)}, u32[]{:S(2)}, u32[]{:S(2)}) collective-permute-start(bf16[2,34,256]{2,1,0:T(8,128)(2,1)S(1)} %pad_maximum_fusion), channel_id=1, source_target_pairs={{0,1},{1,0},{2,3},{3,2},{4,5},{5,4},{6,7},{7,6},{8,9},{9,8},{10,11... | collective-permute-start | bytes 104456 | tf_op jit(solution)/shard_map/ppermute | solution.py:383
  20.1 8.9 %copy-start.14 = (f32[768]{0:T(1024)S(1)}, f32[768]{0:T(1024)}, u32[]{:S(2)}) copy-start(f32[768]{0:T(1024)} %param.17) | copy-start | bytes 9220
  20.1 8.9 %copy-start.6 = (f32[1,1,256,768]{3,2,1,0:T(8,128)S(1)}, f32[1,1,256,768]{3,2,1,0:T(8,128)}, u32[]{:S(2)}) copy-start(f32[1,1,256,768]{3,2,1,0:T(8,128)} %param.16) | copy-start | bytes 2359300
  24.6 11.6 %collective-permute-start.5 = (bf16[192,256]{1,0:T(8,128)(2,1)S(1)}, bf16[192,256]{1,0:T(8,128)(2,1)S(1)}, u32[]{:S(2)}, u32[]{:S(2)}) collective-permute-start(bf16[192,256]{1,0:T(8,128)(2,1)S(1)} %get-tuple-element.46.rest_0_), channel_id=1, source_target_pairs={{0,8},{8,16},{16,24},{24,0},{1,9},{9,17},{17,25},{25,1},{2,10},{10... | collective-permute-start | bytes 294920 | tf_op jit(solution)/shard_map/ppermute | solution.py:383
  25.9 10.4 %collective-permute-start.4 = (bf16[192,256]{1,0:T(8,128)(2,1)S(1)}, bf16[192,256]{1,0:T(8,128)(2,1)}, u32[]{:S(2)}, u32[]{:S(2)}) collective-permute-start(bf16[192,256]{1,0:T(8,128)(2,1)S(1)} %get-tuple-element.46.rest_0_), channel_id=1, source_target_pairs={{0,16},{8,24},{16,0},{24,8},{1,17},{9,25},{17,1},{25,9},{2,18},{10... | collective-permute-start | bytes 294920 | tf_op jit(solution)/shard_map/ppermute | solution.py:383
  26.9 9.3 %collective-permute-start.3 = (bf16[192,256]{1,0:T(8,128)(2,1)S(1)}, bf16[192,256]{1,0:T(8,128)(2,1)}, u32[]{:S(2)}, u32[]{:S(2)}) collective-permute-start(bf16[192,256]{1,0:T(8,128)(2,1)S(1)} %get-tuple-element.46.rest_0_), channel_id=1, source_target_pairs={{0,24},{8,0},{16,8},{24,16},{1,25},{9,1},{17,9},{25,17},{2,26},{10... | collective-permute-start | bytes 294920 | tf_op jit(solution)/shard_map/ppermute | solution.py:383
  34.0 2.3 %copy-start.3 = (bf16[1024,768]{1,0:T(8,128)(2,1)S(1)}, bf16[1024,768]{1,0:T(8,128)(2,1)}, u32[]{:S(2)}) copy-start(bf16[1024,768]{1,0:T(8,128)(2,1)} %inner_ref.3) | copy-start | bytes 4718596
  34.0 2.3 %copy-start.5 = (bf16[768,1024]{1,0:T(8,128)(2,1)S(1)}, bf16[768,1024]{1,0:T(8,128)(2,1)}, u32[]{:S(2)}) copy-start(bf16[768,1024]{1,0:T(8,128)(2,1)} %outer_ref.3) | copy-start | bytes 4718596
  41.9 43.3 %copy-start.1 = (bf16[256,32,128]{2,1,0:T(8,128)(2,1)S(1)}, bf16[256,32,128]{2,1,0:T(8,128)(2,1)}, u32[]{:S(2)}) copy-start(bf16[256,32,128]{2,1,0:T(8,128)(2,1)} %latent_ref.1) | copy-start | bytes 6291460
  42.7 3.5 %collective-permute-start.9 = (bf16[4,64,128]{2,1,0:T(8,128)(2,1)S(1)}, bf16[4,64,128]{2,1,0:T(8,128)(2,1)S(1)}, u32[]{:S(2)}, u32[]{:S(2)}) collective-permute-start(bf16[4,64,128]{2,1,0:T(8,128)(2,1)S(1)} %get-tuple-element.56), channel_id=1, source_target_pairs={{0,1},{1,0},{2,3},{3,2},{4,5},{5,4},{6,7},{7,6},{8,9},{9,8},{10,11... | collective-permute-start | bytes 196616 | tf_op jit(solution)/shard_map/ppermute | solution.py:383
  43.0 16.7 %collective-permute-start.6 = (bf16[5,64,256]{2,1,0:T(8,128)(2,1)S(1)}, bf16[5,64,256]{2,1,0:T(8,128)(2,1)S(1)}, u32[]{:S(2)}, u32[]{:S(2)}) collective-permute-start(bf16[5,64,256]{2,1,0:T(8,128)(2,1)S(1)} %get-tuple-element.48.rest_1_), channel_id=1, source_target_pairs={{0,8},{8,16},{16,24},{24,0},{1,9},{9,17},{17,25},{25,1},{2,10},{10... | collective-permute-start | bytes 491528 | tf_op jit(solution)/shard_map/ppermute | solution.py:383
  46.3 5.8 %collective-permute-start.10 = (bf16[4,64,128]{2,1,0:T(8,128)(2,1)S(1)}, bf16[4,64,128]{2,1,0:T(8,128)(2,1)S(1)}, u32[]{:S(2)}, u32[]{:S(2)}) collective-permute-start(bf16[4,64,128]{2,1,0:T(8,128)(2,1)S(1)} %get-tuple-element.57), channel_id=1, source_target_pairs={{0,2},{2,4},{4,6},{1,3},{3,5},{5,7},{8,10},{10,12},{12,14},{9,11},... | collective-permute-start | bytes 196616 | tf_op jit(solution)/shard_map/ppermute | solution.py:383
  50.2 5.6 %collective-permute-start.11 = (bf16[4,64,128]{2,1,0:T(8,128)(2,1)S(1)}, bf16[4,64,128]{2,1,0:T(8,128)(2,1)S(1)}, u32[]{:S(2)}, u32[]{:S(2)}) collective-permute-start(bf16[4,64,128]{2,1,0:T(8,128)(2,1)S(1)} %get-tuple-element.58), channel_id=1, source_target_pairs={{2,0},{4,2},{6,4},{3,1},{5,3},{7,5},{10,8},{12,10},{14,12},{11,9},... | collective-permute-start | bytes 196616 | tf_op jit(solution)/shard_map/ppermute | solution.py:383
  55.8 29.4 %collective-permute-start.12 = (bf16[6,64,256]{2,1,0:T(8,128)(2,1)S(1)}, bf16[6,64,256]{2,1,0:T(8,128)(2,1)S(1)}, u32[]{:S(2)}, u32[]{:S(2)}) collective-permute-start(bf16[6,64,256]{2,1,0:T(8,128)(2,1)S(1)} %get-tuple-element.60), channel_id=1, source_target_pairs={{0,8},{8,16},{16,24},{24,0},{1,9},{9,17},{17,25},{25,1},{2,10},{10... | collective-permute-start | bytes 589832 | tf_op jit(solution)/shard_map/ppermute | solution.py:383
  55.9 29.3 %collective-permute-start.13 = (bf16[6,64,256]{2,1,0:T(8,128)(2,1)S(1)}, bf16[6,64,256]{2,1,0:T(8,128)(2,1)S(1)}, u32[]{:S(2)}, u32[]{:S(2)}) collective-permute-start(bf16[6,64,256]{2,1,0:T(8,128)(2,1)S(1)} %get-tuple-element.61), channel_id=1, source_target_pairs={{0,16},{8,24},{16,0},{24,8},{1,17},{9,25},{17,1},{25,9},{2,18},{10... | collective-permute-start | bytes 589832 | tf_op jit(solution)/shard_map/ppermute | solution.py:383
  59.0 26.2 %collective-permute-start.14 = (bf16[6,64,256]{2,1,0:T(8,128)(2,1)S(1)}, bf16[6,64,256]{2,1,0:T(8,128)(2,1)S(1)}, u32[]{:S(2)}, u32[]{:S(2)}) collective-permute-start(bf16[6,64,256]{2,1,0:T(8,128)(2,1)S(1)} %get-tuple-element.62), channel_id=1, source_target_pairs={{0,24},{8,0},{16,8},{24,16},{1,25},{9,1},{17,9},{25,17},{2,26},{10... | collective-permute-start | bytes 589832 | tf_op jit(solution)/shard_map/ppermute | solution.py:383
  59.0 22.7 %collective-permute-start.7 = (bf16[5,64,256]{2,1,0:T(8,128)(2,1)S(1)}, bf16[5,64,256]{2,1,0:T(8,128)(2,1)S(1)}, u32[]{:S(2)}, u32[]{:S(2)}) collective-permute-start(bf16[5,64,256]{2,1,0:T(8,128)(2,1)S(1)} %get-tuple-element.49.rest_2_), channel_id=1, source_target_pairs={{0,16},{8,24},{16,0},{24,8},{1,17},{9,25},{17,1},{25,9},{2,18},{10... | collective-permute-start | bytes 491528 | tf_op jit(solution)/shard_map/ppermute | solution.py:383
  59.7 25.5 %collective-permute-start.8 = (bf16[5,64,256]{2,1,0:T(8,128)(2,1)S(1)}, bf16[5,64,256]{2,1,0:T(8,128)(2,1)S(1)}, u32[]{:S(2)}, u32[]{:S(2)}) collective-permute-start(bf16[5,64,256]{2,1,0:T(8,128)(2,1)S(1)} %get-tuple-element.50.rest_3_), channel_id=1, source_target_pairs={{0,24},{8,0},{16,8},{24,16},{1,25},{9,1},{17,9},{25,17},{2,26},{10... | collective-permute-start | bytes 491528 | tf_op jit(solution)/shard_map/ppermute | solution.py:383
  (6 other events, 6.5 us)

commit v3 on v2

--- a/solution.py
+++ b/solution.py
@@ -11,11 +11,6 @@
 CUBIC = 0.044715
 F32 = jnp.float32
 BF16 = jnp.bfloat16
-
-
-def gelu(pre):
-    tanh_v = jnp.tanh(KAPPA * (pre + CUBIC * pre * pre * pre))
-    return 0.5 * pre * (1.0 + tanh_v)
 
 
 def gelu_slope(pre):
@@ -71,25 +66,36 @@
     )
 
 
-EARLY = 5
+LEV, INNER, TO = 0, 1, 2
 
 VM = pl.BlockSpec(memory_space=pltpu.VMEM)
 SM = pl.BlockSpec(memory_space=pltpu.SMEM)
-ANY = pl.BlockSpec(memory_space=pl.ANY)
-
-
-def turn_kernel(lat_ref, tile_ref, top_ref, bottom_ref, side_ref, wide_ref, keep_ref):
+HBM = pl.BlockSpec(memory_space=pltpu.MemorySpace.HBM)
+
+
+def turn_kernel(
+    _, lat_ref, tile_ref, top_ref, bottom_ref, side_ref, near_ref, wide_ref, keep_ref, sems
+):
     chans, rows, cols = lat_ref.shape
-    wide_ref[...] = lat_ref[...].reshape(chans * rows, cols).astype(F32)
-    for r in range(rows):
-        line = wide_ref[pl.ds(r, chans, stride=rows), :].astype(BF16).T
-        tile_ref[r * cols : (r + 1) * cols, :] = line
-        keep_ref[0, r : r + 1, :] = line[0:1].astype(F32)
-        keep_ref[1, r : r + 1, :] = line[cols - 1 : cols].astype(F32)
-        if r == 0:
-            top_ref[...] = line
-        if r == rows - 1:
-            bottom_ref[...] = line
+    count = rows // 8
+    copies = [
+        pltpu.make_async_copy(lat_ref.at[:, pl.ds(8 * i, 8)], near_ref.at[i], sems.at[i])
+        for i in range(count)
+    ]
+    for copy in copies:
+        copy.start()
+    for i, copy in enumerate(copies):
+        copy.wait()
+        wide_ref[i] = near_ref[i].reshape(chans * 8, cols).astype(F32)
+        for r in range(8 * i, 8 * i + 8):
+            line = wide_ref[i, pl.ds(r - 8 * i, chans, stride=8), :].astype(BF16).T
+            tile_ref[r * cols : (r + 1) * cols, :] = line
+            keep_ref[0, r : r + 1, :] = line[0:1].astype(F32)
+            keep_ref[1, r : r + 1, :] = line[cols - 1 : cols].astype(F32)
+            if r == 0:
+                top_ref[...] = line
+            if r == rows - 1:
+                bottom_ref[...] = line
     side_ref[...] = keep_ref[...].astype(BF16)
 
 
@@ -140,8 +146,8 @@
     w_ref,
     mid_ref,
     outw_ref,
-    one_ref,
-    two_ref,
+    s1_ref,
+    s2_ref,
     field_ref,
     halo_ref,
 ):
@@ -168,35 +174,33 @@
             x = x_ref[3 * a + b] + nn(hot(cells == rim), halo_ref[...]).astype(BF16)
             part = nt(w_ref[3 * a + b], x)
             acc = part if acc is None else acc + part
-    one_ref[...] = acc
-    act = gelu(acc).astype(BF16)
+    act, slope = gelu_slope(acc)
+    s1_ref[...] = slope.astype(BF16)
+    act = act.astype(BF16)
     for g in range(groups):
         two = nn(mid_ref[g], act[g * hidden : (g + 1) * hidden])
-        two_ref[g * hidden : (g + 1) * hidden, :] = two
+        value, slope = gelu_slope(two)
+        s2_ref[g * hidden : (g + 1) * hidden, :] = slope.astype(BF16)
         field_ref[g * levels : (g + 1) * levels, :] = nn(
-            outw_ref[g], gelu(two).astype(BF16)
+            outw_ref[g], value.astype(BF16)
         ).astype(BF16)
 
 
 def prepare_kernel(
-    lev_ref,
+    scal_ref,
     count_ref,
-    one_ref,
-    two_ref,
     obs_ref,
     weight_ref,
     inner_ref,
     outer_ref,
-    s1_ref,
-    s2_ref,
+    w_ref,
     obst_ref,
     scale_ref,
     innert_ref,
     outert_ref,
+    wt_ref,
     turn_ref,
 ):
-    s1_ref[...] = gelu_slope(one_ref[...])[1]
-    s2_ref[...] = gelu_slope(two_ref[...])[1]
     obst_ref[...] = obs_ref[...].T
     slots = obs_ref.shape[0]
     levels = weight_ref.shape[1]
@@ -208,13 +212,15 @@
         )
     turn_ref[...] = inner_ref[...].T
     own = innert_ref.shape[0]
-    innert_ref[...] = turn_ref[pl.ds(pl.multiple_of(lev_ref[0] * own, 16), own), :]
+    innert_ref[...] = turn_ref[pl.ds(pl.multiple_of(scal_ref[LEV] * own, 16), own), :]
     outert_ref[...] = outer_ref[...].T
+    for t in range(w_ref.shape[0]):
+        wt_ref[t] = w_ref[t].T
 
 
 def column_kernel(
     lev_count,
-    lev_ref,
+    scal_ref,
     inner_ref,
     innert_ref,
     outer_ref,
@@ -223,16 +229,15 @@
     scale_ref,
     s1_ref,
     s2_ref,
-    w_ref,
+    wt_ref,
     mid_ref,
     outw_ref,
     *rest,
 ):
     blocks = rest[:lev_count]
-    early = rest[lev_count : 2 * lev_count]
-    late = rest[2 * lev_count : 3 * lev_count]
-    f_ref, mis_ref, g_ref = rest[3 * lev_count :]
-    lev = lev_ref[0]
+    outs = rest[lev_count : 2 * lev_count]
+    f_ref, mis_ref, g_ref = rest[2 * lev_count :]
+    lev = scal_ref[LEV]
     own = blocks[0].shape[0]
     for k in range(lev_count):
         at = pl.multiple_of(lax.rem(lev + k, lev_count) * own, 16)
@@ -251,44 +256,39 @@
     for g in range(groups):
         span = slice(g * hidden, (g + 1) * hidden)
         two = (
-            tn(outw_ref[g], grad_fields[g * levels : (g + 1) * levels]) * s2_ref[span, :]
+            tn(outw_ref[g], grad_fields[g * levels : (g + 1) * levels]) * s2_ref[span, :].astype(F32)
         ).astype(BF16)
-        ones.append((tn(mid_ref[g], two) * s1_ref[span, :]).astype(BF16))
+        ones.append((tn(mid_ref[g], two) * s1_ref[span, :].astype(F32)).astype(BF16))
     grad_one = jnp.concatenate(ones, 0)
-    taps = w_ref.shape[0]
-    portion = w_ref.shape[2] // lev_count
+    taps = wt_ref.shape[0]
+    portion = wt_ref.shape[1] // lev_count
     for t in range(taps):
-        patch = tn(w_ref[t], grad_one).astype(BF16)
+        patch = nn(wt_ref[t], grad_one).astype(BF16)
         for d in range(lev_count):
             g_ref[d, t] = patch[d * portion : (d + 1) * portion]
     for k in range(lev_count):
-        to = lax.rem(lev + k, lev_count)
-        early[k][...] = g_ref[to, 0:EARLY]
-        late[k][...] = g_ref[to, EARLY:taps]
+        outs[k][...] = g_ref[scal_ref[TO + k]]
 
 
 def edge_kernel(rows, cols, index_ref, *rest):
     blocks, (rowout_ref, colout_ref) = rest[:-2], rest[-2:]
-    half = len(blocks) // 2
     row, col = split(index_ref[...], cols)
     rowc, colc = split(upright(index_ref), cols)
     slots = row.shape[1]
     cells = lax.broadcasted_iota(jnp.int32, (slots, cols), 1)
     lines = lax.broadcasted_iota(jnp.int32, (slots, 128), 1)
-    for k in range(half):
-        block = [blocks[k].at[t] for t in range(EARLY)]
-        block += [blocks[half + k].at[t] for t in range(9 - EARLY)]
+    for k, block in enumerate(blocks):
         for e, (edge, a) in enumerate(((0, 0), (rows - 1, 2))):
             acc = None
             for b in range(3):
-                part = jnp.where(row == edge, block[3 * a + b][...].astype(F32), 0.0).astype(BF16)
+                part = jnp.where(row == edge, block[3 * a + b].astype(F32), 0.0).astype(BF16)
                 part = nn(part, hot(colc + (b - 1) == cells))
                 acc = part if acc is None else acc + part
             rowout_ref[e, k] = acc.astype(BF16)
         acc = None
         for e, (edge, b) in enumerate(((0, 0), (cols - 1, 2))):
             for a in range(3):
-                part = jnp.where(col == edge, block[3 * a + b][...].astype(F32), 0.0).astype(BF16)
+                part = jnp.where(col == edge, block[3 * a + b].astype(F32), 0.0).astype(BF16)
                 part = nn(part, hot(rowc + (a + 64 * e) == lines))
                 acc = part if acc is None else acc + part
         colout_ref[k] = acc.astype(BF16)
@@ -305,39 +305,39 @@
         ref[...] = line.astype(BF16)
 
 
-def join_kernel(count, *refs):
-    late, (top_ref, bottom_ref, left_ref, right_ref) = refs[:count], refs[count : count + 4]
-    outs = refs[count + 4 :]
-    taps, portion, _ = late[0].shape
+def join_kernel(count, scal_ref, top_ref, bottom_ref, left_ref, right_ref, *outs):
+    portion = top_ref.shape[1]
     spot = lax.broadcasted_iota(jnp.int32, (portion, 128), 1)
     for k in range(count):
-        outs[k][0:taps] = late[k][...]
-        outs[k][taps, :, 0:128] = top_ref[k]
-        outs[k][taps, :, 128:256] = bottom_ref[k]
-        side = jnp.where(spot < 64, right_ref[k].astype(F32), left_ref[k].astype(F32))
-        outs[k][taps + 1, :, 0:128] = side.astype(BF16)
-        outs[k][taps + 1, :, 128:256] = jnp.zeros_like(top_ref[k])
-
-
-def final_kernel(rows, cols, count, lev_ref, index_ref, latent_ref, *rest):
-    early, late = rest[:count], rest[count : 2 * count]
-    out_ref, own_ref, sum_ref, edge_ref, sem = rest[2 * count :]
+        at = scal_ref[TO + count + k]
+        outs[k][0] = top_ref[at]
+        outs[k][1] = bottom_ref[at]
+        side = jnp.where(spot < 64, right_ref[at].astype(F32), left_ref[at].astype(F32))
+        outs[k][2] = side.astype(BF16)
+
+
+def relay_kernel(scal_ref, block_ref, got_ref, out_ref):
+    keep = jnp.where(scal_ref[INNER] == 1, 1.0, 0.0)
+    out_ref[...] = (block_ref[...].astype(F32) + got_ref[...].astype(F32) * keep).astype(BF16)
+
+
+def final_kernel(rows, cols, count, scal_ref, index_ref, latent_ref, *rest):
+    own, relayed, parts = rest[0], rest[1], rest[2:count]
+    rims, (out_ref, own_ref, sum_ref, edge_ref, sem) = rest[count:-5], rest[-5:]
     portion = out_ref.shape[0]
     fetch = pltpu.make_async_copy(
-        latent_ref.at[pl.ds(pl.multiple_of(lev_ref[0] * portion, 8), portion)], own_ref, sem
+        latent_ref.at[pl.ds(pl.multiple_of(scal_ref[LEV] * portion, 8), portion)], own_ref, sem
     )
     fetch.start()
-    total = early[0][...].astype(F32)
-    for block in early[1:]:
+    keep = jnp.where(scal_ref[INNER] == 1, 0.0, 1.0)
+    total = own[...].astype(F32) + relayed[...].astype(F32) * keep
+    for block in parts:
         total = total + block[...].astype(F32)
-    sum_ref[0:EARLY] = total
-    total = late[0][...].astype(F32)
-    for block in late[1:]:
+    sum_ref[...] = total
+    total = rims[0][...].astype(F32)
+    for block in rims[1:]:
         total = total + block[...].astype(F32)
-    sum_ref[EARLY:] = total[: 9 - EARLY]
-    edge_ref[0] = total[9 - EARLY, :, 0:128]
-    edge_ref[1] = total[9 - EARLY, :, 128:256]
-    edge_ref[2] = total[10 - EARLY, :, 0:128]
+    edge_ref[...] = total
     fetch.wait()
     row, _ = split(index_ref[...], cols)
     _, colc = split(upright(index_ref), cols)
@@ -377,6 +377,20 @@
             out_ref[c] = field + jnp.where(lane == cols - 1, last, 0.0)
 
 
+ROUTES = ((3, 2, 1), (0, 2, 3), (3, 1, 0), (0, 1, 2))
+
+
+def route_table(count):
+    rows = []
+    for i in range(count):
+        if count == 4:
+            to = [i, *ROUTES[i]]
+            rows.append([i, int(i in (1, 2)), *to, *(to.index(i ^ k) for k in range(4))])
+        else:
+            rows.append([i, 0, *((i + k) % count for k in range(count)), *range(count)])
+    return rows
+
+
 def shift(x, axis, by, wrap=True):
     size = lax.axis_size(axis)
     pairs = [(i, (i + by) % size) for i in range(size) if wrap or 0 <= i + by < size]
@@ -408,9 +422,8 @@
     slots = obs_index.shape[-1]
     own = groups * levels
     wide = groups * hidden
-    lev = lax.axis_index("lev")
     lev_count = lax.axis_size("lev")
-    lev_arr = lev.reshape(1).astype(jnp.int32)
+    scal = jnp.array(route_table(lev_count), jnp.int32)[lax.axis_index("lev")]
     portion = chans // lev_count
     index = obs_index.reshape(1, slots)
     flops = 2 * taps * wide * chans * slots
@@ -424,14 +437,16 @@
             strip,
             jax.ShapeDtypeStruct((2, rows, chans), BF16),
         ),
-        [VM],
+        [SM, HBM],
         flops // 4,
         16,
         scratch_shapes=[
-            pltpu.VMEM((chans * rows, cols), F32),
+            pltpu.VMEM((rows // 8, chans, 8, cols), BF16),
+            pltpu.VMEM((rows // 8, chans * 8, cols), F32),
             pltpu.VMEM((2, rows, chans), F32),
+            pltpu.SemaphoreType.DMA((rows // 8,)),
         ],
-    )(latent)
+    )(scal, latent)
     above = shift(bottom, "lat", 1, wrap=False)
     below = shift(top, "lat", -1, wrap=False)
     columns = jnp.stack(
@@ -447,15 +462,15 @@
         jax.ShapeDtypeStruct((taps, slots, chans), BF16),
         [SM, VM, VM],
         flops,
-        40,
+        26,
         scratch_shapes=[
             pltpu.VMEM((((rows + 2) * cols + 16) * 8, 128), F32),
             pltpu.VMEM((3, slots * 8, 128), F32),
         ],
     )(index, index, tile)
     w = jnp.transpose(conv_weight, (2, 0, 1, 3)).reshape(taps, wide, chans)
-    act_shape = jax.ShapeDtypeStruct((wide, slots), F32)
-    one, two, fields = call(
+    act_shape = jax.ShapeDtypeStruct((wide, slots), BF16)
+    slope_one, slope_two, fields = call(
         functools.partial(decode_kernel, rows, cols),
         (act_shape, act_shape, jax.ShapeDtypeStruct((own, slots), BF16)),
         [VM] * 9,
@@ -464,30 +479,30 @@
         scratch_shapes=[pltpu.VMEM((2 * cols + 128, chans), BF16)],
     )(index, x, above, below, from_left, from_right, w, mid_weight, out_weight)
 
-    blocks = [fields] + [shift(fields, "lev", -k) for k in range(1, lev_count)]
+    blocks = [fields]
+    for k in range(1, lev_count):
+        blocks.append(shift(fields, "lev", -k))
     column_shape = jax.ShapeDtypeStruct((own * lev_count, slots), F32)
     turned = call(
         prepare_kernel,
         (
-            act_shape,
-            act_shape,
             column_shape,
             column_shape,
             jax.ShapeDtypeStruct((own, inner.shape[0]), BF16),
             jax.ShapeDtypeStruct((outer.shape[1], outer.shape[0]), BF16),
+            jax.ShapeDtypeStruct((taps, chans, wide), BF16),
         ),
-        [SM, SM] + [VM] * 6,
+        [SM, SM] + [VM] * 5,
         flops,
         24,
         scratch_shapes=[pltpu.VMEM((inner.shape[1], inner.shape[0]), BF16)],
-    )(lev_arr, obs_count, one, two, obs_values[0, 0], obs_weight[None, :], inner, outer)
-    slope_one, slope_two, obs_turned, scale, inner_turned, outer_turned = turned
-
-    early_shape = jax.ShapeDtypeStruct((EARLY, portion, slots), BF16)
-    late_shape = jax.ShapeDtypeStruct((taps - EARLY, portion, slots), BF16)
+    )(scal, obs_count, obs_values[0, 0], obs_weight[None, :], inner, outer, w)
+    obs_turned, scale, inner_turned, outer_turned, w_turned = turned
+
+    patch_shape = jax.ShapeDtypeStruct((taps, portion, slots), BF16)
     patches = call(
         functools.partial(column_kernel, lev_count),
-        (early_shape,) * lev_count + (late_shape,) * lev_count,
+        (patch_shape,) * lev_count,
         [SM] + [VM] * (11 + lev_count),
         flops * 4,
         32,
@@ -497,7 +512,7 @@
             pltpu.VMEM((lev_count, taps, portion, slots), BF16),
         ],
     )(
-        lev_arr,
+        scal,
         inner,
         inner_turned,
         outer,
@@ -506,21 +521,31 @@
         scale,
         slope_one,
         slope_two,
-        w,
+        w_turned,
         mid_weight,
         out_weight,
         *blocks,
     )
-    early = [patches[0]]
-    for k in range(1, lev_count):
-        early.append(shift(patches[k], "lev", k))
+    if lev_count == 4:
+        relayed = lax.ppermute(patches[1], "lev", [(0, 1), (1, 0), (2, 3), (3, 2)])
+        parts = [lax.ppermute(patches[2], "lev", [(1, 2), (2, 1)])]
+        parts.append(lax.ppermute(patches[2], "lev", [(0, 2), (3, 1)]))
+        passed = call(
+            relay_kernel, patch_shape, [SM, VM, VM], flops // 64, 8
+        )(scal, patches[3], relayed)
+        parts.append(lax.ppermute(passed, "lev", [(0, 1), (1, 3), (3, 2), (2, 0)]))
+    else:
+        parts = []
+        for k in range(1, lev_count):
+            parts.append(shift(patches[k], "lev", k))
+        relayed = parts.pop(0)
 
     line_shape = jax.ShapeDtypeStruct((lev_count, portion, cols), BF16)
     side_shape = jax.ShapeDtypeStruct((lev_count, portion, 128), BF16)
     row_edge, col_edge = call(
         functools.partial(edge_kernel, rows, cols),
         (jax.ShapeDtypeStruct((2, lev_count, portion, cols), BF16), side_shape),
-        [VM] * (1 + 2 * lev_count),
+        [VM] * (1 + lev_count),
         flops // 8,
         12,
     )(index, *patches)
@@ -536,17 +561,22 @@
     onto_last = shift(up, "lat", -1, wrap=False)
     joined = call(
         functools.partial(join_kernel, lev_count),
-        (jax.ShapeDtypeStruct((taps - EARLY + 2, portion, slots), BF16),) * lev_count,
-        [VM] * (4 + lev_count),
+        (jax.ShapeDtypeStruct((3, portion, 128), BF16),) * lev_count,
+        [SM] + [VM] * 4,
         flops // 64,
         12,
-    )(*patches[lev_count:], onto_first, onto_last, from_left, from_right)
-    late = [joined[0]] + [shift(joined[k], "lev", k) for k in range(1, lev_count)]
+    )(scal, onto_first, onto_last, from_left, from_right)
+    rims = [joined[0]]
+    for k in range(1, lev_count):
+        if lev_count == 4:
+            rims.append(lax.ppermute(joined[k], "lev", [(i, i ^ k) for i in range(4)]))
+        else:
+            rims.append(shift(joined[k], "lev", k))
 
     return call(
-        functools.partial(final_kernel, rows, cols, lev_count),
+        functools.partial(final_kernel, rows, cols, 2 + len(parts)),
         jax.ShapeDtypeStruct((portion, rows, cols), F32),
-        [SM, VM, ANY] + [VM] * (2 * lev_count),
+        [SM, VM, HBM] + [VM] * (2 + len(parts) + lev_count),
         flops // 4,
         16,
         scratch_shapes=[
@@ -555,7 +585,7 @@
             pltpu.VMEM((3, portion, 128), F32),
             pltpu.SemaphoreType.DMA,
         ],
-    )(lev_arr, index, latent, *early, *late)
+    )(scal, index, latent, patches[0], relayed, *parts, *rims)
 
 
 def solution(mesh):

time: 88.9 us -> 76.6 us (0.86)
  the two profiles are of different devices: /device:TPU:9 before, /device:TPU:1 now
where the time goes in v3:
time: 76.6 us; the launch traced here: 76.2 us
  starting transfers between devices  29.3 us (38%)
  Pallas kernels  22.3 us (29%)
  waiting for transfers between devices  19.3 us (25%)
  local copies, waits for them, and re-layouts  4.17 us (5%)
  between operations  1.14 us (1%)
    ppermute x9, starting transfers between devices, shift(): return lax.ppermute(x, axis, pairs)  20.1 us
    ppermute x9, waiting for transfers between devices, shift(): return lax.ppermute(x, axis, pairs)  10.4 us
    ppermute x3, waiting for transfers between devices, steps(): rims.append(lax.ppermute(joined[k], 'lev', [(i, i ^ k) for i in range(4)]))  5.63 us
    pallas_call x1, Pallas kernels, steps(): call(functools.partial(column_kernel, lev_count), (patch_shape,) * lev_co...  5.18 us
    pallas_call x1, Pallas kernels, steps(): call(functools.partial(gather_kernel, rows, cols), jax.ShapeDtypeStruct((...  3.76 us
    pallas_call x1, Pallas kernels, steps(): call(functools.partial(final_kernel, rows, cols, 2 + len(parts)), jax.Sha...  3.65 us
    ppermute x1, starting transfers between devices, steps(): parts.append(lax.ppermute(patches[2], 'lev', [(0, 2), (3, 1)]))  3.5 us
    ppermute x1, waiting for transfers between devices, steps(): relayed = lax.ppermute(patches[1], 'lev', [(0, 1), (1, 0), (2, 3), (3, 2)])  3.23 us
  transfers between devices with their start and end apart: 16, of which 8 were waited for; matrix products, arithmetic and copies ran while one was open for 2% of the time, Pallas kernels for 11%

profile of v3, /device:TPU:1, one launch (start us, length us, event | category | flops | bytes accessed | tf_op | source)
XLA Modules:
  0.0 76.2 jit_solution(18209241382558486085)
XLA Ops:
  0.7 1.6 %copy-done = bf16[256,32,128]{2,1,0:T(8,128)(2,1)S(1)} copy-done((bf16[256,32,128]{2,1,0:T(8,128)(2,1)S(1)}, bf16[256,32,128]{2,1,0:T(8,128)(2,1)}, u32[]{:S(2)}) %copy-start) | copy-done | bytes 2097176
  2.3 2.2 %shard_map.110 = (bf16[4096,256]{1,0:T(8,128)(2,1)S(1)}, bf16[128,256]{1,0:T(8,128)(2,1)S(1)}, bf16[128,256]{1,0:T(8,128)(2,1)S(1)}, bf16[2,32,256]{2,1,0:T(8,128)(2,1)S(1)}) custom-call(s32[10]{0:T(128)S(1)} %dynamic-slice_bitcast_fusion.scal_ref._, bf16[256,32,128]{2,1,0:T(8,128)(2,1)S(1)} %copy-done), custom_call_target="tpu_custom_call" | custom-call | flops 150994944 | bytes 9043968 | tf_op jit(solution)/shard_map/pallas_call | solution.py:432
  4.5 4.5 %collective-permute-start = (bf16[128,256]{1,0:T(8,128)(2,1)S(1)}, bf16[128,256]{1,0:T(8,128)(2,1)S(1)}, u32[]{:S(2)}, u32[]{:S(2)}) collective-permute-start(bf16[128,256]{1,0:T(8,128)(2,1)S(1)} %get-tuple-element.34), channel_id=1, source_target_pairs={{0,2},{2,4},{4,6},{1,3},{3,5},{5,7},{8,10},{10,12},{12,14},{9,11},... | collective-permute-start | bytes 196616 | tf_op jit(solution)/shard_map/ppermute | solution.py:397
  9.0 1.9 %collective-permute-start.1 = (bf16[128,256]{1,0:T(8,128)(2,1)S(1)}, bf16[128,256]{1,0:T(8,128)(2,1)S(1)}, u32[]{:S(2)}, u32[]{:S(2)}) collective-permute-start(bf16[128,256]{1,0:T(8,128)(2,1)S(1)} %get-tuple-element.35), channel_id=1, source_target_pairs={{2,0},{4,2},{6,4},{3,1},{5,3},{7,5},{10,8},{12,10},{14,12},{11,9},... | collective-permute-start | bytes 196616 | tf_op jit(solution)/shard_map/ppermute | solution.py:397
  11.0 1.8 %copy.12 = bf16[9,4,128,256]{3,2,1,0:T(8,128)(2,1)S(1)} copy(bf16[9,4,128,256]{3,2,0,1:T(8,128)(2,1)} %bitcast.22) | data formatting | bytes 4718592 | tf_op jit(solution)/shard_map/transpose | solution.py:471
  12.8 1.8 %collective-permute-done.1.below_ref = bf16[128,256]{1,0:T(8,128)(2,1)S(1)} collective-permute-done((bf16[128,256]{1,0:T(8,128)(2,1)S(1)}, bf16[128,256]{1,0:T(8,128)(2,1)S(1)}, u32[]{:S(2)}, u32[]{:S(2)}) %collective-permute-start.1) | collective-permute-done | bytes 65568 | tf_op jit(solution)/shard_map/ppermute | solution.py:397
  14.6 1.3 %collective-permute-start.2 = (bf16[2,34,256]{2,1,0:T(8,128)(2,1)S(1)}, bf16[2,34,256]{2,1,0:T(8,128)(2,1)S(1)}, u32[]{:S(2)}, u32[]{:S(2)}) collective-permute-start(bf16[2,34,256]{2,1,0:T(8,128)(2,1)S(1)} %pad_maximum_fusion), channel_id=1, source_target_pairs={{0,1},{1,0},{2,3},{3,2},{4,5},{5,4},{6,7},{7,6},{8,9},{9,8},{10,11... | collective-permute-start | bytes 104456 | tf_op jit(solution)/shard_map/ppermute | solution.py:397
  15.9 3.8 %shard_map.111.x_ref = bf16[9,256,256]{2,1,0:T(8,128)(2,1)S(1)} custom-call(s32[1,256]{1,0:T(1,128)S(1)} %bitcast.17, s32[1,256]{1,0:T(1,128)S(1)} %bitcast.18, bf16[4096,256]{1,0:T(8,128)(2,1)S(1)} %get-tuple-element.33.tile_ref), custom_call_target="tpu_custom_call" | custom-call | flops 603979776 | bytes 4718592 | tf_op jit(solution)/shard_map/pallas_call | solution.py:460
  19.8 3.2 %shard_map.112 = (bf16[512,256]{1,0:T(8,128)(2,1)S(1)}, bf16[512,256]{1,0:T(8,128)(2,1)S(1)}, bf16[192,256]{1,0:T(8,128)(2,1)S(1)}) custom-call(s32[1,256]{1,0:T(1,128)S(1)} %bitcast.19, bf16[9,256,256]{2,1,0:T(8,128)(2,1)S(1)} %shard_map.111.x_ref, bf16[128,256]{1,0:T(8,128)(2,1)S(1)} %collective-permute-done.above_ref, ...), custom_call_target="tpu_custom_call" | custom-call | flops 1207959552 | bytes 2490368 | tf_op jit(solution)/shard_map/pallas_call | solution.py:473
  22.9 1.3 %collective-permute-start.5 = (bf16[192,256]{1,0:T(8,128)(2,1)S(1)}, bf16[192,256]{1,0:T(8,128)(2,1)S(1)}, u32[]{:S(2)}, u32[]{:S(2)}) collective-permute-start(bf16[192,256]{1,0:T(8,128)(2,1)S(1)} %get-tuple-element.40.rest_0_), channel_id=1, source_target_pairs={{0,8},{8,16},{16,24},{24,0},{1,9},{9,17},{17,25},{25,1},{2,10},{10... | collective-permute-start | bytes 294920 | tf_op jit(solution)/shard_map/ppermute | solution.py:397
  24.3 2.3 %collective-permute-start.4 = (bf16[192,256]{1,0:T(8,128)(2,1)S(1)}, bf16[192,256]{1,0:T(8,128)(2,1)S(1)}, u32[]{:S(2)}, u32[]{:S(2)}) collective-permute-start(bf16[192,256]{1,0:T(8,128)(2,1)S(1)} %get-tuple-element.40.rest_0_), channel_id=1, source_target_pairs={{0,16},{8,24},{16,0},{24,8},{1,17},{9,25},{17,1},{25,9},{2,18},{10... | collective-permute-start | bytes 294920 | tf_op jit(solution)/shard_map/ppermute | solution.py:397
  28.4 2.3 %shard_map.109 = (f32[768,256]{1,0:T(8,128)S(1)}, f32[768,256]{1,0:T(8,128)S(1)}, bf16[192,1024]{1,0:T(8,128)(2,1)S(1)}, bf16[1024,768]{1,0:T(8,128)(2,1)S(1)}, bf16[9,256,512]{2,1,0:T(8,128)(2,1)S(1)}) custom-call(s32[10]{0:T(128)S(1)} %dynamic-slice_bitcast_fusion.scal_ref._, s32[1,1]{1,0:T(1,128)S(6)} %copy.13.count_ref, f32[256,768]{1,0:T(8,128)S(1)} %bitcast.16, ...), custom_call_target="tpu_custom_call" | custom-call | flops 603979776 | bytes 23592960 | tf_op jit(solution)/shard_map/pallas_call | solution.py:486
  30.7 1.8 %collective-permute-done.4.rest_2_ = bf16[192,256]{1,0:T(8,128)(2,1)S(1)} collective-permute-done((bf16[192,256]{1,0:T(8,128)(2,1)S(1)}, bf16[192,256]{1,0:T(8,128)(2,1)S(1)}, u32[]{:S(2)}, u32[]{:S(2)}) %collective-permute-start.4) | collective-permute-done | bytes 98336 | tf_op jit(solution)/shard_map/ppermute | solution.py:397
  32.6 5.2 %shard_map.113 = (bf16[9,64,256]{2,1,0:T(8,128)(2,1)S(1)}, bf16[9,64,256]{2,1,0:T(8,128)(2,1)S(1)}, bf16[9,64,256]{2,1,0:T(8,128)(2,1)S(1)}, bf16[9,64,256]{2,1,0:T(8,128)(2,1)S(1)}) custom-call(s32[10]{0:T(128)S(1)} %dynamic-slice_bitcast_fusion.scal_ref._, bf16[1024,768]{1,0:T(8,128)(2,1)S(1)} %copy-done.2, ...), custom_call_target="tpu_custom_call" | custom-call | flops 2415919104 | bytes 4718592 | tf_op jit(solution)/shard_map/pallas_call | solution.py:503
  37.8 1.7 %collective-permute-start.6 = (bf16[9,64,256]{2,1,0:T(8,128)(2,1)S(1)}, bf16[9,64,256]{2,1,0:T(8,128)(2,1)S(1)}, u32[]{:S(2)}, u32[]{:S(2)}) collective-permute-start(bf16[9,64,256]{2,1,0:T(8,128)(2,1)S(1)} %get-tuple-element.42.rest_1_), channel_id=1, source_target_pairs={{0,8},{8,0},{16,24},{24,16},{1,9},{9,1},{17,25},{25,17},{2,10},{10... | collective-permute-start | bytes 884744 | tf_op jit(solution)/shard_map/ppermute | solution.py:530
  39.5 3.5 %collective-permute-start.8 = (bf16[9,64,256]{2,1,0:T(8,128)(2,1)S(1)}, bf16[9,64,256]{2,1,0:T(8,128)(2,1)S(1)}, u32[]{:S(2)}, u32[]{:S(2)}) collective-permute-start(bf16[9,64,256]{2,1,0:T(8,128)(2,1)S(1)} %get-tuple-element.43.rest_2_), channel_id=1, source_target_pairs={{0,16},{24,8},{1,17},{25,9},{2,18},{26,10},{3,19},{27,11},{4,20},{... | collective-permute-start | bytes 884744 | tf_op jit(solution)/shard_map/ppermute | solution.py:532
  43.7 3.2 %collective-permute-done.6.got_ref.rest_1_ = bf16[9,64,256]{2,1,0:T(8,128)(2,1)S(1)} collective-permute-done((bf16[9,64,256]{2,1,0:T(8,128)(2,1)S(1)}, bf16[9,64,256]{2,1,0:T(8,128)(2,1)S(1)}, u32[]{:S(2)}, u32[]{:S(2)}) %collective-permute-start.6) | collective-permute-done | bytes 294944 | tf_op jit(solution)/shard_map/ppermute | solution.py:530
  49.8 2.9 %collective-permute-done.10.left_ref.right_ref = bf16[4,64,128]{2,1,0:T(8,128)(2,1)S(1)} collective-permute-done((bf16[4,64,128]{2,1,0:T(8,128)(2,1)S(1)}, bf16[4,64,128]{2,1,0:T(8,128)(2,1)S(1)}, u32[]{:S(2)}, u32[]{:S(2)}) %collective-permute-start.10) | collective-permute-done | bytes 65568 | tf_op jit(solution)/shard_map/ppermute | solution.py:397
  52.8 5.4 %collective-permute-start.11 = (bf16[4,64,128]{2,1,0:T(8,128)(2,1)S(1)}, bf16[4,64,128]{2,1,0:T(8,128)(2,1)S(1)}, u32[]{:S(2)}, u32[]{:S(2)}) collective-permute-start(bf16[4,64,128]{2,1,0:T(8,128)(2,1)S(1)} %get-tuple-element.47), channel_id=1, source_target_pairs={{0,2},{2,4},{4,6},{1,3},{3,5},{5,7},{8,10},{10,12},{12,14},{9,11},... | collective-permute-start | bytes 196616 | tf_op jit(solution)/shard_map/ppermute | solution.py:397
  58.2 1.9 %collective-permute-start.12 = (bf16[4,64,128]{2,1,0:T(8,128)(2,1)S(1)}, bf16[4,64,128]{2,1,0:T(8,128)(2,1)S(1)}, u32[]{:S(2)}, u32[]{:S(2)}) collective-permute-start(bf16[4,64,128]{2,1,0:T(8,128)(2,1)S(1)} %get-tuple-element.48), channel_id=1, source_target_pairs={{2,0},{4,2},{6,4},{3,1},{5,3},{7,5},{10,8},{12,10},{14,12},{11,9},... | collective-permute-start | bytes 196616 | tf_op jit(solution)/shard_map/ppermute | solution.py:397
  60.1 3.9 %collective-permute-done.12.bottom_ref = bf16[4,64,128]{2,1,0:T(8,128)(2,1)S(1)} collective-permute-done((bf16[4,64,128]{2,1,0:T(8,128)(2,1)S(1)}, bf16[4,64,128]{2,1,0:T(8,128)(2,1)S(1)}, u32[]{:S(2)}, u32[]{:S(2)}) %collective-permute-start.12) | collective-permute-done | bytes 65568 | tf_op jit(solution)/shard_map/ppermute | solution.py:397
  65.9 1.8 %collective-permute-done.13.rest_6_ = bf16[3,64,128]{2,1,0:T(8,128)(2,1)S(1)} collective-permute-done((bf16[3,64,128]{2,1,0:T(8,128)(2,1)S(1)}, bf16[3,64,128]{2,1,0:T(8,128)(2,1)S(1)}, u32[]{:S(2)}, u32[]{:S(2)}) %collective-permute-start.13) | collective-permute-done | bytes 49184 | tf_op jit(solution)/shard_map/ppermute | solution.py:572
  68.8 3.5 %collective-permute-done.15.rest_8_ = bf16[3,64,128]{2,1,0:T(8,128)(2,1)S(1)} collective-permute-done((bf16[3,64,128]{2,1,0:T(8,128)(2,1)S(1)}, bf16[3,64,128]{2,1,0:T(8,128)(2,1)S(1)}, u32[]{:S(2)}, u32[]{:S(2)}) %collective-permute-start.15) | collective-permute-done | bytes 49184 | tf_op jit(solution)/shard_map/ppermute | solution.py:572
  72.4 3.7 %shard_map.118 = f32[64,32,128]{2,1,0:T(8,128)} custom-call(s32[10]{0:T(128)S(1)} %dynamic-slice_bitcast_fusion.scal_ref._, s32[1,256]{1,0:T(1,128)S(1)} %bitcast.21, bf16[256,32,128]{2,1,0:T(8,128)(2,1)S(1)} %copy-done.1, bf16[9,64,256]{2,1,0:T(8,128)(2,1)S(1)} %get-tuple-element.41.rest_0_, bf16[9,64,256]{2,1,0:T(8,128)(2,1)S(1)} %collective-permute-done.6.got_ref.rest_1_, ...), custom_call_target="tpu_custom_call" | custom-call | flops 150994944 | bytes 4194304 | tf_op jit(solution)/shard_map/pallas_call | solution.py:576
  (44 shorter events, 8.6 us)
Async XLA Ops:
  4.5 8.3 %collective-permute-start = (bf16[128,256]{1,0:T(8,128)(2,1)S(1)}, bf16[128,256]{1,0:T(8,128)(2,1)S(1)}, u32[]{:S(2)}, u32[]{:S(2)}) collective-permute-start(bf16[128,256]{1,0:T(8,128)(2,1)S(1)} %get-tuple-element.34), channel_id=1, source_target_pairs={{0,2},{2,4},{4,6},{1,3},{3,5},{5,7},{8,10},{10,12},{12,14},{9,11},... | collective-permute-start | bytes 196616 | tf_op jit(solution)/shard_map/ppermute | solution.py:397
  9.0 5.6 %collective-permute-start.1 = (bf16[128,256]{1,0:T(8,128)(2,1)S(1)}, bf16[128,256]{1,0:T(8,128)(2,1)S(1)}, u32[]{:S(2)}, u32[]{:S(2)}) collective-permute-start(bf16[128,256]{1,0:T(8,128)(2,1)S(1)} %get-tuple-element.35), channel_id=1, source_target_pairs={{2,0},{4,2},{6,4},{3,1},{5,3},{7,5},{10,8},{12,10},{14,12},{11,9},... | collective-permute-start | bytes 196616 | tf_op jit(solution)/shard_map/ppermute | solution.py:397
  11.0 5.0 %copy-start.7 = (s32[1,1,256]{2,1,0:T(1,128)S(1)}, s32[1,1,256]{2,1,0:T(1,128)}, u32[]{:S(2)}) copy-start(s32[1,1,256]{2,1,0:T(1,128)} %param.19) | copy-start | bytes 3076
  12.8 6.9 %copy-start.5 = (bf16[4,128,128]{2,1,0:T(8,128)(2,1)S(1)}, bf16[4,128,128]{2,1,0:T(8,128)(2,1)}, u32[]{:S(2)}) copy-start(bf16[4,128,128]{2,1,0:T(8,128)(2,1)} %mid_ref.3) | copy-start | bytes 393220
  12.8 6.9 %copy-start.6 = (bf16[4,48,128]{2,1,0:T(8,128)(2,1)S(1)}, bf16[4,48,128]{2,1,0:T(8,128)(2,1)}, u32[]{:S(2)}) copy-start(bf16[4,48,128]{2,1,0:T(8,128)(2,1)} %outw_ref.3) | copy-start | bytes 147460
  14.6 5.0 %collective-permute-start.2 = (bf16[2,34,256]{2,1,0:T(8,128)(2,1)S(1)}, bf16[2,34,256]{2,1,0:T(8,128)(2,1)S(1)}, u32[]{:S(2)}, u32[]{:S(2)}) collective-permute-start(bf16[2,34,256]{2,1,0:T(8,128)(2,1)S(1)} %pad_maximum_fusion), channel_id=1, source_target_pairs={{0,1},{1,0},{2,3},{3,2},{4,5},{5,4},{6,7},{7,6},{8,9},{9,8},{10,11... | collective-permute-start | bytes 104456 | tf_op jit(solution)/shard_map/ppermute | solution.py:397
  19.7 8.6 %copy-start.8 = (f32[768]{0:T(1024)S(1)}, f32[768]{0:T(1024)}, u32[]{:S(2)}) copy-start(f32[768]{0:T(1024)} %param.18) | copy-start | bytes 9220
  19.7 8.6 %copy-start.2 = (bf16[1024,768]{1,0:T(8,128)(2,1)S(1)}, bf16[1024,768]{1,0:T(8,128)(2,1)}, u32[]{:S(2)}) copy-start(bf16[1024,768]{1,0:T(8,128)(2,1)} %inner_ref.3) | copy-start | bytes 4718596
  19.7 8.6 %copy-start.3 = (bf16[768,1024]{1,0:T(8,128)(2,1)S(1)}, bf16[768,1024]{1,0:T(8,128)(2,1)}, u32[]{:S(2)}) copy-start(bf16[768,1024]{1,0:T(8,128)(2,1)} %outer_ref.3) | copy-start | bytes 4718596
  19.8 8.6 %copy-start.4 = (f32[1,1,256,768]{3,2,1,0:T(8,128)S(1)}, f32[1,1,256,768]{3,2,1,0:T(8,128)}, u32[]{:S(2)}) copy-start(f32[1,1,256,768]{3,2,1,0:T(8,128)} %param.17) | copy-start | bytes 2359300
  22.9 7.8 %collective-permute-start.5 = (bf16[192,256]{1,0:T(8,128)(2,1)S(1)}, bf16[192,256]{1,0:T(8,128)(2,1)S(1)}, u32[]{:S(2)}, u32[]{:S(2)}) collective-permute-start(bf16[192,256]{1,0:T(8,128)(2,1)S(1)} %get-tuple-element.40.rest_0_), channel_id=1, source_target_pairs={{0,8},{8,16},{16,24},{24,0},{1,9},{9,17},{17,25},{25,1},{2,10},{10... | collective-permute-start | bytes 294920 | tf_op jit(solution)/shard_map/ppermute | solution.py:397
  24.3 8.3 %collective-permute-start.4 = (bf16[192,256]{1,0:T(8,128)(2,1)S(1)}, bf16[192,256]{1,0:T(8,128)(2,1)S(1)}, u32[]{:S(2)}, u32[]{:S(2)}) collective-permute-start(bf16[192,256]{1,0:T(8,128)(2,1)S(1)} %get-tuple-element.40.rest_0_), channel_id=1, source_target_pairs={{0,16},{8,24},{16,0},{24,8},{1,17},{9,25},{17,1},{25,9},{2,18},{10... | collective-permute-start | bytes 294920 | tf_op jit(solution)/shard_map/ppermute | solution.py:397
  26.6 6.0 %collective-permute-start.3 = (bf16[192,256]{1,0:T(8,128)(2,1)S(1)}, bf16[192,256]{1,0:T(8,128)(2,1)S(1)}, u32[]{:S(2)}, u32[]{:S(2)}) collective-permute-start(bf16[192,256]{1,0:T(8,128)(2,1)S(1)} %get-tuple-element.40.rest_0_), channel_id=1, source_target_pairs={{0,24},{8,0},{16,8},{24,16},{1,25},{9,1},{17,9},{25,17},{2,26},{10... | collective-permute-start | bytes 294920 | tf_op jit(solution)/shard_map/ppermute | solution.py:397
  37.8 34.6 %copy-start.1 = (bf16[256,32,128]{2,1,0:T(8,128)(2,1)S(1)}, bf16[256,32,128]{2,1,0:T(8,128)(2,1)}, u32[]{:S(2)}) copy-start(bf16[256,32,128]{2,1,0:T(8,128)(2,1)} %latent_ref.1) | copy-start | bytes 6291460
  37.8 9.2 %collective-permute-start.6 = (bf16[9,64,256]{2,1,0:T(8,128)(2,1)S(1)}, bf16[9,64,256]{2,1,0:T(8,128)(2,1)S(1)}, u32[]{:S(2)}, u32[]{:S(2)}) collective-permute-start(bf16[9,64,256]{2,1,0:T(8,128)(2,1)S(1)} %get-tuple-element.42.rest_1_), channel_id=1, source_target_pairs={{0,8},{8,0},{16,24},{24,16},{1,9},{9,1},{17,25},{25,17},{2,10},{10... | collective-permute-start | bytes 884744 | tf_op jit(solution)/shard_map/ppermute | solution.py:530
  39.5 32.9 %collective-permute-start.8 = (bf16[9,64,256]{2,1,0:T(8,128)(2,1)S(1)}, bf16[9,64,256]{2,1,0:T(8,128)(2,1)S(1)}, u32[]{:S(2)}, u32[]{:S(2)}) collective-permute-start(bf16[9,64,256]{2,1,0:T(8,128)(2,1)S(1)} %get-tuple-element.43.rest_2_), channel_id=1, source_target_pairs={{0,16},{24,8},{1,17},{25,9},{2,18},{26,10},{3,19},{27,11},{4,20},{... | collective-permute-start | bytes 884744 | tf_op jit(solution)/shard_map/ppermute | solution.py:532
  43.0 29.4 %collective-permute-start.7 = (bf16[9,64,256]{2,1,0:T(8,128)(2,1)S(1)}, bf16[9,64,256]{2,1,0:T(8,128)(2,1)S(1)}, u32[]{:S(2)}, u32[]{:S(2)}) collective-permute-start(bf16[9,64,256]{2,1,0:T(8,128)(2,1)S(1)} %get-tuple-element.43.rest_2_), channel_id=1, source_target_pairs={{8,16},{16,8},{9,17},{17,9},{10,18},{18,10},{11,19},{19,11},{12,20... | collective-permute-start | bytes 884744 | tf_op jit(solution)/shard_map/ppermute | solution.py:531
  47.6 24.8 %collective-permute-start.9 = (bf16[9,64,256]{2,1,0:T(8,128)(2,1)S(1)}, bf16[9,64,256]{2,1,0:T(8,128)(2,1)S(1)}, u32[]{:S(2)}, u32[]{:S(2)}) collective-permute-start(bf16[9,64,256]{2,1,0:T(8,128)(2,1)S(1)} %shard_map.114), channel_id=1, source_target_pairs={{0,8},{8,24},{24,16},{16,0},{1,9},{9,25},{25,17},{17,1},{2,10},{10... | collective-permute-start | bytes 884744 | tf_op jit(solution)/shard_map/ppermute | solution.py:536
  49.5 3.2 %collective-permute-start.10 = (bf16[4,64,128]{2,1,0:T(8,128)(2,1)S(1)}, bf16[4,64,128]{2,1,0:T(8,128)(2,1)S(1)}, u32[]{:S(2)}, u32[]{:S(2)}) collective-permute-start(bf16[4,64,128]{2,1,0:T(8,128)(2,1)S(1)} %get-tuple-element.46), channel_id=1, source_target_pairs={{0,1},{1,0},{2,3},{3,2},{4,5},{5,4},{6,7},{7,6},{8,9},{9,8},{10,11... | collective-permute-start | bytes 196616 | tf_op jit(solution)/shard_map/ppermute | solution.py:397
  52.8 7.3 %collective-permute-start.11 = (bf16[4,64,128]{2,1,0:T(8,128)(2,1)S(1)}, bf16[4,64,128]{2,1,0:T(8,128)(2,1)S(1)}, u32[]{:S(2)}, u32[]{:S(2)}) collective-permute-start(bf16[4,64,128]{2,1,0:T(8,128)(2,1)S(1)} %get-tuple-element.47), channel_id=1, source_target_pairs={{0,2},{2,4},{4,6},{1,3},{3,5},{5,7},{8,10},{10,12},{12,14},{9,11},... | collective-permute-start | bytes 196616 | tf_op jit(solution)/shard_map/ppermute | solution.py:397
  58.2 5.9 %collective-permute-start.12 = (bf16[4,64,128]{2,1,0:T(8,128)(2,1)S(1)}, bf16[4,64,128]{2,1,0:T(8,128)(2,1)S(1)}, u32[]{:S(2)}, u32[]{:S(2)}) collective-permute-start(bf16[4,64,128]{2,1,0:T(8,128)(2,1)S(1)} %get-tuple-element.48), channel_id=1, source_target_pairs={{2,0},{4,2},{6,4},{3,1},{5,3},{7,5},{10,8},{12,10},{14,12},{11,9},... | collective-permute-start | bytes 196616 | tf_op jit(solution)/shard_map/ppermute | solution.py:397
  64.6 3.0 %collective-permute-start.13 = (bf16[3,64,128]{2,1,0:T(8,128)(2,1)S(1)}, bf16[3,64,128]{2,1,0:T(8,128)(2,1)S(1)}, u32[]{:S(2)}, u32[]{:S(2)}) collective-permute-start(bf16[3,64,128]{2,1,0:T(8,128)(2,1)S(1)} %get-tuple-element.50), channel_id=1, source_target_pairs={{0,8},{8,0},{16,24},{24,16},{1,9},{9,1},{17,25},{25,17},{2,10},{10... | collective-permute-start | bytes 147464 | tf_op jit(solution)/shard_map/ppermute | solution.py:572
  64.7 4.1 %collective-permute-start.14 = (bf16[3,64,128]{2,1,0:T(8,128)(2,1)S(1)}, bf16[3,64,128]{2,1,0:T(8,128)(2,1)S(1)}, u32[]{:S(2)}, u32[]{:S(2)}) collective-permute-start(bf16[3,64,128]{2,1,0:T(8,128)(2,1)S(1)} %get-tuple-element.51), channel_id=1, source_target_pairs={{0,16},{8,24},{16,0},{24,8},{1,17},{9,25},{17,1},{25,9},{2,18},{10... | collective-permute-start | bytes 147464 | tf_op jit(solution)/shard_map/ppermute | solution.py:572
  67.7 4.7 %collective-permute-start.15 = (bf16[3,64,128]{2,1,0:T(8,128)(2,1)S(1)}, bf16[3,64,128]{2,1,0:T(8,128)(2,1)S(1)}, u32[]{:S(2)}, u32[]{:S(2)}) collective-permute-start(bf16[3,64,128]{2,1,0:T(8,128)(2,1)S(1)} %get-tuple-element.52), channel_id=1, source_target_pairs={{0,24},{8,16},{16,8},{24,0},{1,25},{9,17},{17,9},{25,1},{2,26},{10... | collective-permute-start | bytes 147464 | tf_op jit(solution)/shard_map/ppermute | solution.py:572
  (1 other events, 1.6 us)

commit v4 on v3

--- a/solution.py
+++ b/solution.py
@@ -33,6 +33,32 @@
 
 def tn(a, b):
     return lax.dot_general(a, b, (((0,), (0,)), ((), ())), preferred_element_type=F32)
+
+
+ROUTES = ((0, 3, 2, 1), (1, 0, 2, 3), (2, 3, 1, 0), (3, 0, 1, 2))
+
+
+def lookup(lev, values):
+    found = jnp.int32(values[0])
+    for i, value in enumerate(values[1:], 1):
+        found = jnp.where(lev == i, value, found)
+    return found
+
+
+def relays(lev, count):
+    return (lev == 1) | (lev == 2) if count == 4 else lev < 0
+
+
+def target(lev, count, k):
+    if count == 4:
+        return lookup(lev, [ROUTES[i][k] for i in range(4)])
+    return lax.rem(lev + k, count)
+
+
+def place(lev, count, k):
+    if count == 4:
+        return lookup(lev, [ROUTES[i].index(i ^ k) for i in range(4)])
+    return k
 
 
 def split(index, cols):
@@ -65,8 +91,6 @@
         **kwargs,
     )
 
-
-LEV, INNER, TO = 0, 1, 2
 
 VM = pl.BlockSpec(memory_space=pltpu.VMEM)
 SM = pl.BlockSpec(memory_space=pltpu.SMEM)
@@ -187,7 +211,7 @@
 
 
 def prepare_kernel(
-    scal_ref,
+    lev_ref,
     count_ref,
     obs_ref,
     weight_ref,
@@ -212,7 +236,7 @@
         )
     turn_ref[...] = inner_ref[...].T
     own = innert_ref.shape[0]
-    innert_ref[...] = turn_ref[pl.ds(pl.multiple_of(scal_ref[LEV] * own, 16), own), :]
+    innert_ref[...] = turn_ref[pl.ds(pl.multiple_of(lev_ref[0] * own, 16), own), :]
     outert_ref[...] = outer_ref[...].T
     for t in range(w_ref.shape[0]):
         wt_ref[t] = w_ref[t].T
@@ -220,7 +244,7 @@
 
 def column_kernel(
     lev_count,
-    scal_ref,
+    lev_ref,
     inner_ref,
     innert_ref,
     outer_ref,
@@ -237,7 +261,7 @@
     blocks = rest[:lev_count]
     outs = rest[lev_count : 2 * lev_count]
     f_ref, mis_ref, g_ref = rest[2 * lev_count :]
-    lev = scal_ref[LEV]
+    lev = lev_ref[0]
     own = blocks[0].shape[0]
     for k in range(lev_count):
         at = pl.multiple_of(lax.rem(lev + k, lev_count) * own, 16)
@@ -267,7 +291,7 @@
         for d in range(lev_count):
             g_ref[d, t] = patch[d * portion : (d + 1) * portion]
     for k in range(lev_count):
-        outs[k][...] = g_ref[scal_ref[TO + k]]
+        outs[k][...] = g_ref[target(lev, lev_count, k)]
 
 
 def edge_kernel(rows, cols, index_ref, *rest):
@@ -305,31 +329,31 @@
         ref[...] = line.astype(BF16)
 
 
-def join_kernel(count, scal_ref, top_ref, bottom_ref, left_ref, right_ref, *outs):
+def join_kernel(count, lev_ref, top_ref, bottom_ref, left_ref, right_ref, *outs):
     portion = top_ref.shape[1]
     spot = lax.broadcasted_iota(jnp.int32, (portion, 128), 1)
     for k in range(count):
-        at = scal_ref[TO + count + k]
+        at = place(lev_ref[0], count, k)
         outs[k][0] = top_ref[at]
         outs[k][1] = bottom_ref[at]
         side = jnp.where(spot < 64, right_ref[at].astype(F32), left_ref[at].astype(F32))
         outs[k][2] = side.astype(BF16)
 
 
-def relay_kernel(scal_ref, block_ref, got_ref, out_ref):
-    keep = jnp.where(scal_ref[INNER] == 1, 1.0, 0.0)
+def relay_kernel(count, lev_ref, block_ref, got_ref, out_ref):
+    keep = jnp.where(relays(lev_ref[0], count), 1.0, 0.0)
     out_ref[...] = (block_ref[...].astype(F32) + got_ref[...].astype(F32) * keep).astype(BF16)
 
 
-def final_kernel(rows, cols, count, scal_ref, index_ref, latent_ref, *rest):
-    own, relayed, parts = rest[0], rest[1], rest[2:count]
-    rims, (out_ref, own_ref, sum_ref, edge_ref, sem) = rest[count:-5], rest[-5:]
+def final_kernel(rows, cols, count, lev_ref, index_ref, latent_ref, *rest):
+    rims, own, relayed = rest[:count], rest[count], rest[count + 1]
+    parts, (out_ref, own_ref, sum_ref, edge_ref, sem) = rest[count + 2 : -5], rest[-5:]
     portion = out_ref.shape[0]
     fetch = pltpu.make_async_copy(
-        latent_ref.at[pl.ds(pl.multiple_of(scal_ref[LEV] * portion, 8), portion)], own_ref, sem
+        latent_ref.at[pl.ds(pl.multiple_of(lev_ref[0] * portion, 8), portion)], own_ref, sem
     )
     fetch.start()
-    keep = jnp.where(scal_ref[INNER] == 1, 0.0, 1.0)
+    keep = jnp.where(relays(lev_ref[0], count), 0.0, 1.0)
     total = own[...].astype(F32) + relayed[...].astype(F32) * keep
     for block in parts:
         total = total + block[...].astype(F32)
@@ -377,20 +401,6 @@
             out_ref[c] = field + jnp.where(lane == cols - 1, last, 0.0)
 
 
-ROUTES = ((3, 2, 1), (0, 2, 3), (3, 1, 0), (0, 1, 2))
-
-
-def route_table(count):
-    rows = []
-    for i in range(count):
-        if count == 4:
-            to = [i, *ROUTES[i]]
-            rows.append([i, int(i in (1, 2)), *to, *(to.index(i ^ k) for k in range(4))])
-        else:
-            rows.append([i, 0, *((i + k) % count for k in range(count)), *range(count)])
-    return rows
-
-
 def shift(x, axis, by, wrap=True):
     size = lax.axis_size(axis)
     pairs = [(i, (i + by) % size) for i in range(size) if wrap or 0 <= i + by < size]
@@ -423,9 +433,10 @@
     own = groups * levels
     wide = groups * hidden
     lev_count = lax.axis_size("lev")
-    scal = jnp.array(route_table(lev_count), jnp.int32)[lax.axis_index("lev")]
+    lev = lax.axis_index("lev").astype(jnp.int32).reshape(1)
     portion = chans // lev_count
     index = obs_index.reshape(1, slots)
+    far = pltpu.with_memory_space_constraint(latent, pltpu.MemorySpace.HBM)
     flops = 2 * taps * wide * chans * slots
 
     strip = jax.ShapeDtypeStruct((cols, chans), BF16)
@@ -446,7 +457,7 @@
             pltpu.VMEM((2, rows, chans), F32),
             pltpu.SemaphoreType.DMA((rows // 8,)),
         ],
-    )(scal, latent)
+    )(lev, far)
     above = shift(bottom, "lat", 1, wrap=False)
     below = shift(top, "lat", -1, wrap=False)
     columns = jnp.stack(
@@ -496,7 +507,7 @@
         flops,
         24,
         scratch_shapes=[pltpu.VMEM((inner.shape[1], inner.shape[0]), BF16)],
-    )(scal, obs_count, obs_values[0, 0], obs_weight[None, :], inner, outer, w)
+    )(lev, obs_count, obs_values[0, 0], obs_weight[None, :], inner, outer, w)
     obs_turned, scale, inner_turned, outer_turned, w_turned = turned
 
     patch_shape = jax.ShapeDtypeStruct((taps, portion, slots), BF16)
@@ -512,7 +523,7 @@
             pltpu.VMEM((lev_count, taps, portion, slots), BF16),
         ],
     )(
-        scal,
+        lev,
         inner,
         inner_turned,
         outer,
@@ -531,8 +542,8 @@
         parts = [lax.ppermute(patches[2], "lev", [(1, 2), (2, 1)])]
         parts.append(lax.ppermute(patches[2], "lev", [(0, 2), (3, 1)]))
         passed = call(
-            relay_kernel, patch_shape, [SM, VM, VM], flops // 64, 8
-        )(scal, patches[3], relayed)
+            functools.partial(relay_kernel, lev_count), patch_shape, [SM, VM, VM], flops // 64, 8
+        )(lev, patches[3], relayed)
         parts.append(lax.ppermute(passed, "lev", [(0, 1), (1, 3), (3, 2), (2, 0)]))
     else:
         parts = []
@@ -565,7 +576,7 @@
         [SM] + [VM] * 4,
         flops // 64,
         12,
-    )(scal, onto_first, onto_last, from_left, from_right)
+    )(lev, onto_first, onto_last, from_left, from_right)
     rims = [joined[0]]
     for k in range(1, lev_count):
         if lev_count == 4:
@@ -574,7 +585,7 @@
             rims.append(shift(joined[k], "lev", k))
 
     return call(
-        functools.partial(final_kernel, rows, cols, 2 + len(parts)),
+        functools.partial(final_kernel, rows, cols, lev_count),
         jax.ShapeDtypeStruct((portion, rows, cols), F32),
         [SM, VM, HBM] + [VM] * (2 + len(parts) + lev_count),
         flops // 4,
@@ -585,7 +596,7 @@
             pltpu.VMEM((3, portion, 128), F32),
             pltpu.SemaphoreType.DMA,
         ],
-    )(scal, index, latent, patches[0], relayed, *parts, *rims)
+    )(lev, index, far, *rims, patches[0], relayed, *parts)
 
 
 def solution(mesh):

time: 76.6 us -> 74.2 us (0.969)
  the two profiles are of different devices: /device:TPU:1 before, /device:TPU:0 now
where the time goes in v4:
time: 74.2 us; the launch traced here: 73.9 us
  starting transfers between devices  28.3 us (38%)
  waiting for transfers between devices  22 us (30%)
  Pallas kernels  20.6 us (28%)
  local copies, waits for them, and re-layouts  1.89 us (3%)
  between operations  1.1 us (1%)
    ppermute x9, starting transfers between devices, shift(): return lax.ppermute(x, axis, pairs)  14 us
    ppermute x9, waiting for transfers between devices, shift(): return lax.ppermute(x, axis, pairs)  11.8 us
    ppermute x3, waiting for transfers between devices, steps(): rims.append(lax.ppermute(joined[k], 'lev', [(i, i ^ k) for i in range(4)]))  6.35 us
    ppermute x3, starting transfers between devices, steps(): rims.append(lax.ppermute(joined[k], 'lev', [(i, i ^ k) for i in range(4)]))  5.33 us
    pallas_call x1, Pallas kernels, steps(): call(functools.partial(column_kernel, lev_count), (patch_shape,) * lev_co...  4.69 us
    pallas_call x1, Pallas kernels, steps(): call(functools.partial(final_kernel, rows, cols, lev_count), jax.ShapeDty...  3.9 us
    ppermute x1, waiting for transfers between devices, steps(): relayed = lax.ppermute(patches[1], 'lev', [(0, 1), (1, 0), (2, 3), (3, 2)])  3.83 us
    pallas_call x1, Pallas kernels, steps(): call(functools.partial(gather_kernel, rows, cols), jax.ShapeDtypeStruct((...  3.76 us
  transfers between devices with their start and end apart: 16, of which 8 were waited for; matrix products, arithmetic and copies ran while one was open for 2% of the time, Pallas kernels for 9%

profile of v4, /device:TPU:0, one launch (start us, length us, event | category | flops | bytes accessed | tf_op | source)
XLA Modules:
  0.0 73.9 jit_solution(18443781369704864804)
XLA Ops:
  0.0 2.3 %shard_map.101 = (bf16[4096,256]{1,0:T(8,128)(2,1)S(1)}, bf16[128,256]{1,0:T(8,128)(2,1)S(1)}, bf16[128,256]{1,0:T(8,128)(2,1)S(1)}, bf16[2,32,256]{2,1,0:T(8,128)(2,1)S(1)}) custom-call(s32[1]{0:T(128)} %bitcast.lev_ref._, bf16[256,32,128]{2,1,0:T(8,128)(2,1)} %latent_ref.1), custom_call_target="tpu_custom_call" | custom-call | flops 150994944 | bytes 9043968 | tf_op jit(solution)/shard_map/pallas_call | solution.py:443
  2.3 2.4 %collective-permute-start = (bf16[128,256]{1,0:T(8,128)(2,1)S(1)}, bf16[128,256]{1,0:T(8,128)(2,1)S(1)}, u32[]{:S(2)}, u32[]{:S(2)}) collective-permute-start(bf16[128,256]{1,0:T(8,128)(2,1)S(1)} %get-tuple-element.34), channel_id=1, source_target_pairs={{0,2},{2,4},{4,6},{1,3},{3,5},{5,7},{8,10},{10,12},{12,14},{9,11},... | collective-permute-start | bytes 196616 | tf_op jit(solution)/shard_map/ppermute | solution.py:407
  6.1 1.8 %copy.11 = bf16[9,4,128,256]{3,2,1,0:T(8,128)(2,1)S(1)} copy(bf16[9,4,128,256]{3,2,0,1:T(8,128)(2,1)} %bitcast.21) | data formatting | bytes 4718592 | tf_op jit(solution)/shard_map/transpose | solution.py:482
  7.9 2.1 %collective-permute-done.1.below_ref = bf16[128,256]{1,0:T(8,128)(2,1)S(1)} collective-permute-done((bf16[128,256]{1,0:T(8,128)(2,1)S(1)}, bf16[128,256]{1,0:T(8,128)(2,1)S(1)}, u32[]{:S(2)}, u32[]{:S(2)}) %collective-permute-start.1) | collective-permute-done | bytes 65568 | tf_op jit(solution)/shard_map/ppermute | solution.py:407
  10.1 1.6 %collective-permute-start.2 = (bf16[2,34,256]{2,1,0:T(8,128)(2,1)S(1)}, bf16[2,34,256]{2,1,0:T(8,128)(2,1)S(1)}, u32[]{:S(2)}, u32[]{:S(2)}) collective-permute-start(bf16[2,34,256]{2,1,0:T(8,128)(2,1)S(1)} %pad_maximum_fusion), channel_id=1, source_target_pairs={{0,1},{1,0},{2,3},{3,2},{4,5},{5,4},{6,7},{7,6},{8,9},{9,8},{10,11... | collective-permute-start | bytes 104456 | tf_op jit(solution)/shard_map/ppermute | solution.py:407
  11.6 3.8 %shard_map.102.x_ref = bf16[9,256,256]{2,1,0:T(8,128)(2,1)S(1)} custom-call(s32[1,256]{1,0:T(1,128)S(1)} %bitcast.16, s32[1,256]{1,0:T(1,128)S(1)} %bitcast.17, bf16[4096,256]{1,0:T(8,128)(2,1)S(1)} %get-tuple-element.33.tile_ref), custom_call_target="tpu_custom_call" | custom-call | flops 603979776 | bytes 4718592 | tf_op jit(solution)/shard_map/pallas_call | solution.py:471
  15.5 3.2 %shard_map.103 = (bf16[512,256]{1,0:T(8,128)(2,1)S(1)}, bf16[512,256]{1,0:T(8,128)(2,1)S(1)}, bf16[192,256]{1,0:T(8,128)(2,1)S(1)}) custom-call(s32[1,256]{1,0:T(1,128)S(1)} %bitcast.18, bf16[9,256,256]{2,1,0:T(8,128)(2,1)S(1)} %shard_map.102.x_ref, bf16[128,256]{1,0:T(8,128)(2,1)S(1)} %collective-permute-done.above_ref, ...), custom_call_target="tpu_custom_call" | custom-call | flops 1207959552 | bytes 2490368 | tf_op jit(solution)/shard_map/pallas_call | solution.py:484
  18.6 1.6 %collective-permute-start.5 = (bf16[192,256]{1,0:T(8,128)(2,1)S(1)}, bf16[192,256]{1,0:T(8,128)(2,1)S(1)}, u32[]{:S(2)}, u32[]{:S(2)}) collective-permute-start(bf16[192,256]{1,0:T(8,128)(2,1)S(1)} %get-tuple-element.40.rest_0_), channel_id=1, source_target_pairs={{0,8},{8,16},{16,24},{24,0},{1,9},{9,17},{17,25},{25,1},{2,10},{10... | collective-permute-start | bytes 294920 | tf_op jit(solution)/shard_map/ppermute | solution.py:407
  20.3 2.6 %collective-permute-start.4 = (bf16[192,256]{1,0:T(8,128)(2,1)S(1)}, bf16[192,256]{1,0:T(8,128)(2,1)S(1)}, u32[]{:S(2)}, u32[]{:S(2)}) collective-permute-start(bf16[192,256]{1,0:T(8,128)(2,1)S(1)} %get-tuple-element.40.rest_0_), channel_id=1, source_target_pairs={{0,16},{8,24},{16,0},{24,8},{1,17},{9,25},{17,1},{25,9},{2,18},{10... | collective-permute-start | bytes 294920 | tf_op jit(solution)/shard_map/ppermute | solution.py:407
  22.9 1.3 %collective-permute-start.3 = (bf16[192,256]{1,0:T(8,128)(2,1)S(1)}, bf16[192,256]{1,0:T(8,128)(2,1)S(1)}, u32[]{:S(2)}, u32[]{:S(2)}) collective-permute-start(bf16[192,256]{1,0:T(8,128)(2,1)S(1)} %get-tuple-element.40.rest_0_), channel_id=1, source_target_pairs={{0,24},{8,0},{16,8},{24,16},{1,25},{9,1},{17,9},{25,17},{2,26},{10... | collective-permute-start | bytes 294920 | tf_op jit(solution)/shard_map/ppermute | solution.py:407
  24.9 1.8 %shard_map.100 = (f32[768,256]{1,0:T(8,128)S(1)}, f32[768,256]{1,0:T(8,128)S(1)}, bf16[192,1024]{1,0:T(8,128)(2,1)S(1)}, bf16[1024,768]{1,0:T(8,128)(2,1)S(1)}, bf16[9,256,512]{2,1,0:T(8,128)(2,1)S(1)}) custom-call(s32[1]{0:T(128)} %bitcast.lev_ref._, s32[1,1]{1,0:T(1,128)S(6)} %copy.12.count_ref, f32[256,768]{1,0:T(8,128)S(1)} %bitcast.15, ...), custom_call_target="tpu_custom_call" | custom-call | flops 603979776 | bytes 23592960 | tf_op jit(solution)/shard_map/pallas_call | solution.py:497
  26.7 2.5 %collective-permute-done.4.rest_2_ = bf16[192,256]{1,0:T(8,128)(2,1)S(1)} collective-permute-done((bf16[192,256]{1,0:T(8,128)(2,1)S(1)}, bf16[192,256]{1,0:T(8,128)(2,1)S(1)}, u32[]{:S(2)}, u32[]{:S(2)}) %collective-permute-start.4) | collective-permute-done | bytes 98336 | tf_op jit(solution)/shard_map/ppermute | solution.py:407
  29.4 4.7 %shard_map.104 = (bf16[9,64,256]{2,1,0:T(8,128)(2,1)S(1)}, bf16[9,64,256]{2,1,0:T(8,128)(2,1)S(1)}, bf16[9,64,256]{2,1,0:T(8,128)(2,1)S(1)}, bf16[9,64,256]{2,1,0:T(8,128)(2,1)S(1)}) custom-call(s32[1]{0:T(128)} %bitcast.lev_ref._, bf16[1024,768]{1,0:T(8,128)(2,1)S(1)} %copy-done, bf16[192,1024]{1,0:T(8,128)(2,1)S(1)} %get-tuple-element.29.innert_ref, ...), custom_call_target="tpu_custom_call" | custom-call | flops 2415919104 | bytes 4718592 | tf_op jit(solution)/shard_map/pallas_call | solution.py:514
  34.1 2.9 %collective-permute-start.12 = (bf16[9,64,256]{2,1,0:T(8,128)(2,1)S(1)}, bf16[9,64,256]{2,1,0:T(8,128)(2,1)S(1)}, u32[]{:S(2)}, u32[]{:S(2)}) collective-permute-start(bf16[9,64,256]{2,1,0:T(8,128)(2,1)S(1)} %get-tuple-element.42.rest_1_), channel_id=1, source_target_pairs={{0,8},{8,0},{16,24},{24,16},{1,9},{9,1},{17,25},{25,17},{2,10},{10... | collective-permute-start | bytes 884744 | tf_op jit(solution)/shard_map/ppermute | solution.py:541
  37.1 3.2 %collective-permute-start.14 = (bf16[9,64,256]{2,1,0:T(8,128)(2,1)S(1)}, bf16[9,64,256]{2,1,0:T(8,128)(2,1)S(1)}, u32[]{:S(2)}, u32[]{:S(2)}) collective-permute-start(bf16[9,64,256]{2,1,0:T(8,128)(2,1)S(1)} %get-tuple-element.43.rest_2_), channel_id=1, source_target_pairs={{0,16},{24,8},{1,17},{25,9},{2,18},{26,10},{3,19},{27,11},{4,20},{... | collective-permute-start | bytes 884744 | tf_op jit(solution)/shard_map/ppermute | solution.py:543
  41.0 3.8 %collective-permute-done.12.got_ref.rest_5_ = bf16[9,64,256]{2,1,0:T(8,128)(2,1)S(1)} collective-permute-done((bf16[9,64,256]{2,1,0:T(8,128)(2,1)S(1)}, bf16[9,64,256]{2,1,0:T(8,128)(2,1)S(1)}, u32[]{:S(2)}, u32[]{:S(2)}) %collective-permute-start.12) | collective-permute-done | bytes 294944 | tf_op jit(solution)/shard_map/ppermute | solution.py:541
  44.9 2.2 %collective-permute-start.15 = (bf16[9,64,256]{2,1,0:T(8,128)(2,1)S(1)}, bf16[9,64,256]{2,1,0:T(8,128)(2,1)S(1)}, u32[]{:S(2)}, u32[]{:S(2)}) collective-permute-start(bf16[9,64,256]{2,1,0:T(8,128)(2,1)S(1)} %shard_map.108), channel_id=1, source_target_pairs={{0,8},{8,24},{24,16},{16,0},{1,9},{9,25},{25,17},{17,1},{2,10},{10... | collective-permute-start | bytes 884744 | tf_op jit(solution)/shard_map/ppermute | solution.py:547
  48.4 3.7 %collective-permute-done.6.left_ref.right_ref = bf16[4,64,128]{2,1,0:T(8,128)(2,1)S(1)} collective-permute-done((bf16[4,64,128]{2,1,0:T(8,128)(2,1)S(1)}, bf16[4,64,128]{2,1,0:T(8,128)(2,1)S(1)}, u32[]{:S(2)}, u32[]{:S(2)}) %collective-permute-start.6) | collective-permute-done | bytes 65568 | tf_op jit(solution)/shard_map/ppermute | solution.py:407
  54.9 3.3 %collective-permute-done.8.bottom_ref = bf16[4,64,128]{2,1,0:T(8,128)(2,1)S(1)} collective-permute-done((bf16[4,64,128]{2,1,0:T(8,128)(2,1)S(1)}, bf16[4,64,128]{2,1,0:T(8,128)(2,1)S(1)}, u32[]{:S(2)}, u32[]{:S(2)}) %collective-permute-start.8) | collective-permute-done | bytes 65568 | tf_op jit(solution)/shard_map/ppermute | solution.py:407
  58.2 1.7 %collective-permute-start.10 = (bf16[3,64,128]{2,1,0:T(8,128)(2,1)S(1)}, bf16[3,64,128]{2,1,0:T(8,128)(2,1)S(1)}, u32[]{:S(2)}, u32[]{:S(2)}) collective-permute-start(bf16[3,64,128]{2,1,0:T(8,128)(2,1)S(1)} %get-tuple-element.51), channel_id=1, source_target_pairs={{0,16},{8,24},{16,0},{24,8},{1,17},{9,25},{17,1},{25,9},{2,18},{10... | collective-permute-start | bytes 147464 | tf_op jit(solution)/shard_map/ppermute | solution.py:583
  60.0 3.5 %collective-permute-done.9.rest_1_ = bf16[3,64,128]{2,1,0:T(8,128)(2,1)S(1)} collective-permute-done((bf16[3,64,128]{2,1,0:T(8,128)(2,1)S(1)}, bf16[3,64,128]{2,1,0:T(8,128)(2,1)S(1)}, u32[]{:S(2)}, u32[]{:S(2)}) %collective-permute-start.9) | collective-permute-done | bytes 49184 | tf_op jit(solution)/shard_map/ppermute | solution.py:583
  63.5 3.5 %collective-permute-start.11 = (bf16[3,64,128]{2,1,0:T(8,128)(2,1)S(1)}, bf16[3,64,128]{2,1,0:T(8,128)(2,1)S(1)}, u32[]{:S(2)}, u32[]{:S(2)}) collective-permute-start(bf16[3,64,128]{2,1,0:T(8,128)(2,1)S(1)} %get-tuple-element.52), channel_id=1, source_target_pairs={{0,24},{8,16},{16,8},{24,0},{1,25},{9,17},{17,9},{25,1},{2,26},{10... | collective-permute-start | bytes 147464 | tf_op jit(solution)/shard_map/ppermute | solution.py:583
  67.0 2.9 %collective-permute-done.11.rest_3_ = bf16[3,64,128]{2,1,0:T(8,128)(2,1)S(1)} collective-permute-done((bf16[3,64,128]{2,1,0:T(8,128)(2,1)S(1)}, bf16[3,64,128]{2,1,0:T(8,128)(2,1)S(1)}, u32[]{:S(2)}, u32[]{:S(2)}) %collective-permute-start.11) | collective-permute-done | bytes 49184 | tf_op jit(solution)/shard_map/ppermute | solution.py:583
  69.9 3.9 %shard_map.109 = f32[64,32,128]{2,1,0:T(8,128)} custom-call(s32[1]{0:T(128)} %bitcast.lev_ref._, s32[1,256]{1,0:T(1,128)S(1)} %bitcast.20, bf16[256,32,128]{2,1,0:T(8,128)(2,1)} %latent_ref.1, bf16[3,64,128]{2,1,0:T(8,128)(2,1)S(1)} %get-tuple-element.49.rest_0_, bf16[3,64,128]{2,1,0:T(8,128)(2,1)S(1)} %collective-permute-done.9.rest_1_, ...), custom_call_target="tpu_custom_call" | custom-call | flops 150994944 | bytes 4194304 | tf_op jit(solution)/shard_map/pallas_call | solution.py:587
  (39 shorter events, 6.5 us)
Async XLA Ops:
  2.3 5.6 %collective-permute-start = (bf16[128,256]{1,0:T(8,128)(2,1)S(1)}, bf16[128,256]{1,0:T(8,128)(2,1)S(1)}, u32[]{:S(2)}, u32[]{:S(2)}) collective-permute-start(bf16[128,256]{1,0:T(8,128)(2,1)S(1)} %get-tuple-element.34), channel_id=1, source_target_pairs={{0,2},{2,4},{4,6},{1,3},{3,5},{5,7},{8,10},{10,12},{12,14},{9,11},... | collective-permute-start | bytes 196616 | tf_op jit(solution)/shard_map/ppermute | solution.py:407
  4.7 5.3 %collective-permute-start.1 = (bf16[128,256]{1,0:T(8,128)(2,1)S(1)}, bf16[128,256]{1,0:T(8,128)(2,1)S(1)}, u32[]{:S(2)}, u32[]{:S(2)}) collective-permute-start(bf16[128,256]{1,0:T(8,128)(2,1)S(1)} %get-tuple-element.35), channel_id=1, source_target_pairs={{2,0},{4,2},{6,4},{3,1},{5,3},{7,5},{10,8},{12,10},{14,12},{11,9},... | collective-permute-start | bytes 196616 | tf_op jit(solution)/shard_map/ppermute | solution.py:407
  6.1 5.6 %copy-start.5 = (s32[1,1,256]{2,1,0:T(1,128)S(1)}, s32[1,1,256]{2,1,0:T(1,128)}, u32[]{:S(2)}) copy-start(s32[1,1,256]{2,1,0:T(1,128)} %param.18) | copy-start | bytes 3076
  7.9 7.5 %copy-start.3 = (bf16[4,128,128]{2,1,0:T(8,128)(2,1)S(1)}, bf16[4,128,128]{2,1,0:T(8,128)(2,1)}, u32[]{:S(2)}) copy-start(bf16[4,128,128]{2,1,0:T(8,128)(2,1)} %mid_ref.3) | copy-start | bytes 393220
  7.9 7.5 %copy-start.4 = (bf16[4,48,128]{2,1,0:T(8,128)(2,1)S(1)}, bf16[4,48,128]{2,1,0:T(8,128)(2,1)}, u32[]{:S(2)}) copy-start(bf16[4,48,128]{2,1,0:T(8,128)(2,1)} %outw_ref.3) | copy-start | bytes 147460
  10.1 5.3 %collective-permute-start.2 = (bf16[2,34,256]{2,1,0:T(8,128)(2,1)S(1)}, bf16[2,34,256]{2,1,0:T(8,128)(2,1)S(1)}, u32[]{:S(2)}, u32[]{:S(2)}) collective-permute-start(bf16[2,34,256]{2,1,0:T(8,128)(2,1)S(1)} %pad_maximum_fusion), channel_id=1, source_target_pairs={{0,1},{1,0},{2,3},{3,2},{4,5},{5,4},{6,7},{7,6},{8,9},{9,8},{10,11... | collective-permute-start | bytes 104456 | tf_op jit(solution)/shard_map/ppermute | solution.py:407
  15.4 9.5 %copy-start.6 = (f32[768]{0:T(1024)S(1)}, f32[768]{0:T(1024)}, u32[]{:S(2)}) copy-start(f32[768]{0:T(1024)} %param.17) | copy-start | bytes 9220
  15.4 9.5 %copy-start = (bf16[1024,768]{1,0:T(8,128)(2,1)S(1)}, bf16[1024,768]{1,0:T(8,128)(2,1)}, u32[]{:S(2)}) copy-start(bf16[1024,768]{1,0:T(8,128)(2,1)} %inner_ref.3) | copy-start | bytes 4718596
  15.4 9.5 %copy-start.1 = (bf16[768,1024]{1,0:T(8,128)(2,1)S(1)}, bf16[768,1024]{1,0:T(8,128)(2,1)}, u32[]{:S(2)}) copy-start(bf16[768,1024]{1,0:T(8,128)(2,1)} %outer_ref.3) | copy-start | bytes 4718596
  15.4 9.5 %copy-start.2 = (f32[1,1,256,768]{3,2,1,0:T(8,128)S(1)}, f32[1,1,256,768]{3,2,1,0:T(8,128)}, u32[]{:S(2)}) copy-start(f32[1,1,256,768]{3,2,1,0:T(8,128)} %param.16) | copy-start | bytes 2359300
  18.6 8.1 %collective-permute-start.5 = (bf16[192,256]{1,0:T(8,128)(2,1)S(1)}, bf16[192,256]{1,0:T(8,128)(2,1)S(1)}, u32[]{:S(2)}, u32[]{:S(2)}) collective-permute-start(bf16[192,256]{1,0:T(8,128)(2,1)S(1)} %get-tuple-element.40.rest_0_), channel_id=1, source_target_pairs={{0,8},{8,16},{16,24},{24,0},{1,9},{9,17},{17,25},{25,1},{2,10},{10... | collective-permute-start | bytes 294920 | tf_op jit(solution)/shard_map/ppermute | solution.py:407
  20.3 8.9 %collective-permute-start.4 = (bf16[192,256]{1,0:T(8,128)(2,1)S(1)}, bf16[192,256]{1,0:T(8,128)(2,1)S(1)}, u32[]{:S(2)}, u32[]{:S(2)}) collective-permute-start(bf16[192,256]{1,0:T(8,128)(2,1)S(1)} %get-tuple-element.40.rest_0_), channel_id=1, source_target_pairs={{0,16},{8,24},{16,0},{24,8},{1,17},{9,25},{17,1},{25,9},{2,18},{10... | collective-permute-start | bytes 294920 | tf_op jit(solution)/shard_map/ppermute | solution.py:407
  22.9 6.6 %collective-permute-start.3 = (bf16[192,256]{1,0:T(8,128)(2,1)S(1)}, bf16[192,256]{1,0:T(8,128)(2,1)S(1)}, u32[]{:S(2)}, u32[]{:S(2)}) collective-permute-start(bf16[192,256]{1,0:T(8,128)(2,1)S(1)} %get-tuple-element.40.rest_0_), channel_id=1, source_target_pairs={{0,24},{8,0},{16,8},{24,16},{1,25},{9,1},{17,9},{25,17},{2,26},{10... | collective-permute-start | bytes 294920 | tf_op jit(solution)/shard_map/ppermute | solution.py:407
  34.1 10.7 %collective-permute-start.12 = (bf16[9,64,256]{2,1,0:T(8,128)(2,1)S(1)}, bf16[9,64,256]{2,1,0:T(8,128)(2,1)S(1)}, u32[]{:S(2)}, u32[]{:S(2)}) collective-permute-start(bf16[9,64,256]{2,1,0:T(8,128)(2,1)S(1)} %get-tuple-element.42.rest_1_), channel_id=1, source_target_pairs={{0,8},{8,0},{16,24},{24,16},{1,9},{9,1},{17,25},{25,17},{2,10},{10... | collective-permute-start | bytes 884744 | tf_op jit(solution)/shard_map/ppermute | solution.py:541
  37.1 32.8 %collective-permute-start.14 = (bf16[9,64,256]{2,1,0:T(8,128)(2,1)S(1)}, bf16[9,64,256]{2,1,0:T(8,128)(2,1)S(1)}, u32[]{:S(2)}, u32[]{:S(2)}) collective-permute-start(bf16[9,64,256]{2,1,0:T(8,128)(2,1)S(1)} %get-tuple-element.43.rest_2_), channel_id=1, source_target_pairs={{0,16},{24,8},{1,17},{25,9},{2,18},{26,10},{3,19},{27,11},{4,20},{... | collective-permute-start | bytes 884744 | tf_op jit(solution)/shard_map/ppermute | solution.py:543
  40.3 29.6 %collective-permute-start.13 = (bf16[9,64,256]{2,1,0:T(8,128)(2,1)S(1)}, bf16[9,64,256]{2,1,0:T(8,128)(2,1)S(1)}, u32[]{:S(2)}, u32[]{:S(2)}) collective-permute-start(bf16[9,64,256]{2,1,0:T(8,128)(2,1)S(1)} %get-tuple-element.43.rest_2_), channel_id=1, source_target_pairs={{8,16},{16,8},{9,17},{17,9},{10,18},{18,10},{11,19},{19,11},{12,20... | collective-permute-start | bytes 884744 | tf_op jit(solution)/shard_map/ppermute | solution.py:542
  44.9 25.0 %collective-permute-start.15 = (bf16[9,64,256]{2,1,0:T(8,128)(2,1)S(1)}, bf16[9,64,256]{2,1,0:T(8,128)(2,1)S(1)}, u32[]{:S(2)}, u32[]{:S(2)}) collective-permute-start(bf16[9,64,256]{2,1,0:T(8,128)(2,1)S(1)} %shard_map.108), channel_id=1, source_target_pairs={{0,8},{8,24},{24,16},{16,0},{1,9},{9,25},{25,17},{17,1},{2,10},{10... | collective-permute-start | bytes 884744 | tf_op jit(solution)/shard_map/ppermute | solution.py:547
  47.8 4.3 %collective-permute-start.6 = (bf16[4,64,128]{2,1,0:T(8,128)(2,1)S(1)}, bf16[4,64,128]{2,1,0:T(8,128)(2,1)S(1)}, u32[]{:S(2)}, u32[]{:S(2)}) collective-permute-start(bf16[4,64,128]{2,1,0:T(8,128)(2,1)S(1)} %get-tuple-element.46), channel_id=1, source_target_pairs={{0,1},{1,0},{2,3},{3,2},{4,5},{5,4},{6,7},{7,6},{8,9},{9,8},{10,11... | collective-permute-start | bytes 196616 | tf_op jit(solution)/shard_map/ppermute | solution.py:407
  52.3 2.6 %collective-permute-start.7 = (bf16[4,64,128]{2,1,0:T(8,128)(2,1)S(1)}, bf16[4,64,128]{2,1,0:T(8,128)(2,1)S(1)}, u32[]{:S(2)}, u32[]{:S(2)}) collective-permute-start(bf16[4,64,128]{2,1,0:T(8,128)(2,1)S(1)} %get-tuple-element.47), channel_id=1, source_target_pairs={{0,2},{2,4},{4,6},{1,3},{3,5},{5,7},{8,10},{10,12},{12,14},{9,11},... | collective-permute-start | bytes 196616 | tf_op jit(solution)/shard_map/ppermute | solution.py:407
  53.6 4.6 %collective-permute-start.8 = (bf16[4,64,128]{2,1,0:T(8,128)(2,1)S(1)}, bf16[4,64,128]{2,1,0:T(8,128)(2,1)S(1)}, u32[]{:S(2)}, u32[]{:S(2)}) collective-permute-start(bf16[4,64,128]{2,1,0:T(8,128)(2,1)S(1)} %get-tuple-element.48), channel_id=1, source_target_pairs={{2,0},{4,2},{6,4},{3,1},{5,3},{7,5},{10,8},{12,10},{14,12},{11,9},... | collective-permute-start | bytes 196616 | tf_op jit(solution)/shard_map/ppermute | solution.py:407
  58.2 5.3 %collective-permute-start.9 = (bf16[3,64,128]{2,1,0:T(8,128)(2,1)S(1)}, bf16[3,64,128]{2,1,0:T(8,128)(2,1)S(1)}, u32[]{:S(2)}, u32[]{:S(2)}) collective-permute-start(bf16[3,64,128]{2,1,0:T(8,128)(2,1)S(1)} %get-tuple-element.50), channel_id=1, source_target_pairs={{0,8},{8,0},{16,24},{24,16},{1,9},{9,1},{17,25},{25,17},{2,10},{10... | collective-permute-start | bytes 147464 | tf_op jit(solution)/shard_map/ppermute | solution.py:583
  58.2 8.7 %collective-permute-start.10 = (bf16[3,64,128]{2,1,0:T(8,128)(2,1)S(1)}, bf16[3,64,128]{2,1,0:T(8,128)(2,1)S(1)}, u32[]{:S(2)}, u32[]{:S(2)}) collective-permute-start(bf16[3,64,128]{2,1,0:T(8,128)(2,1)S(1)} %get-tuple-element.51), channel_id=1, source_target_pairs={{0,16},{8,24},{16,0},{24,8},{1,17},{9,25},{17,1},{25,9},{2,18},{10... | collective-permute-start | bytes 147464 | tf_op jit(solution)/shard_map/ppermute | solution.py:583
  63.5 6.4 %collective-permute-start.11 = (bf16[3,64,128]{2,1,0:T(8,128)(2,1)S(1)}, bf16[3,64,128]{2,1,0:T(8,128)(2,1)S(1)}, u32[]{:S(2)}, u32[]{:S(2)}) collective-permute-start(bf16[3,64,128]{2,1,0:T(8,128)(2,1)S(1)} %get-tuple-element.52), channel_id=1, source_target_pairs={{0,24},{8,16},{16,8},{24,0},{1,25},{9,17},{17,9},{25,1},{2,26},{10... | collective-permute-start | bytes 147464 | tf_op jit(solution)/shard_map/ppermute | solution.py:583

commit v5 on v4

--- a/solution.py
+++ b/solution.py
@@ -49,6 +49,10 @@
     return (lev == 1) | (lev == 2) if count == 4 else lev < 0
 
 
+def source(lev, count, k):
+    return lax.bitwise_xor(lev, k) if count == 4 else lax.rem(lev + k, count)
+
+
 def target(lev, count, k):
     if count == 4:
         return lookup(lev, [ROUTES[i][k] for i in range(4)])
@@ -57,7 +61,7 @@
 
 def place(lev, count, k):
     if count == 4:
-        return lookup(lev, [ROUTES[i].index(i ^ k) for i in range(4)])
+        return lookup(lev, [ROUTES[i].index(i ^ (0, 2, 1, 3)[k]) for i in range(4)])
     return k
 
 
@@ -77,13 +81,13 @@
     return jnp.broadcast_to(index_ref[...], (128, slots)).T
 
 
-def call(kernel, out_shape, in_specs, flops, mib, **kwargs):
+def call(kernel, out_shape, in_specs, flops, mib, out_specs=None, **kwargs):
     bytes_out = sum(s.size * s.dtype.itemsize for s in jax.tree.leaves(out_shape))
     return pl.pallas_call(
         kernel,
         out_shape=out_shape,
         in_specs=in_specs,
-        out_specs=jax.tree.map(lambda _: VM, out_shape),
+        out_specs=out_specs or jax.tree.map(lambda _: VM, out_shape),
         cost_estimate=pl.CostEstimate(
             flops=flops, bytes_accessed=4 * bytes_out, transcendentals=0
         ),
@@ -91,6 +95,8 @@
         **kwargs,
     )
 
+
+STEP = 8
 
 VM = pl.BlockSpec(memory_space=pltpu.VMEM)
 SM = pl.BlockSpec(memory_space=pltpu.SMEM)
@@ -128,6 +134,10 @@
     slots = index_ref.shape[1]
     halves = chans // 128
     lead = cols + 8
+    size = table_ref.shape[0]
+    margin = (lead + 1) * 8
+    table_ref[0:margin, :] = jnp.zeros((margin, 128), F32)
+    table_ref[size - margin : size, :] = jnp.zeros((margin, 128), F32)
     for r in range(rows):
         line = tile_ref[r * cols : (r + 1) * cols, :].astype(F32)
         for b in range(3):
@@ -146,16 +156,14 @@
         return carry
 
     lax.fori_loop(0, slots // 8, body, 0)
-    row, col = split(upright(index_ref), cols)
+    _, col = split(upright(index_ref), cols)
     for a in range(3):
         for b in range(3):
-            at_row, at_col = row + (a - 1), col + (b - 1)
-            inside = (at_row >= 0) & (at_row < rows) & (at_col >= 0) & (at_col < cols)
             for h in range(halves):
                 x = x_ref[a, pl.ds(halves * b + h, slots, stride=8), :]
-                out_ref[3 * a + b, :, h * 128 : (h + 1) * 128] = jnp.where(inside, x, 0.0).astype(
-                    BF16
-                )
+                if b != 1:
+                    x = jnp.where(col == (0 if b == 0 else cols - 1), 0.0, x)
+                out_ref[3 * a + b, :, h * 128 : (h + 1) * 128] = x.astype(BF16)
 
 
 def decode_kernel(
@@ -187,7 +195,7 @@
     halo_ref[2 * cols + tall : 2 * cols + tall + rows + 2, :] = right_ref[0]
     row, col = split(upright(index_ref), cols)
     cells = lax.broadcasted_iota(jnp.int32, (slots, width), 1)
-    acc = None
+    lefts, rights = [], []
     for a in range(3):
         for b in range(3):
             at_row, at_col = row + (a - 1), col + (b - 1)
@@ -196,8 +204,9 @@
             rim = jnp.where(at_col >= cols, 2 * cols + tall + at_row + 1, rim)
             rim = jnp.concatenate([rim] * (width // 128), 1)
             x = x_ref[3 * a + b] + nn(hot(cells == rim), halo_ref[...]).astype(BF16)
-            part = nt(w_ref[3 * a + b], x)
-            acc = part if acc is None else acc + part
+            lefts.append(w_ref[3 * a + b])
+            rights.append(x)
+    acc = nt(jnp.concatenate(lefts, 1), jnp.concatenate(rights, 1))
     act, slope = gelu_slope(acc)
     s1_ref[...] = slope.astype(BF16)
     act = act.astype(BF16)
@@ -260,18 +269,34 @@
 ):
     blocks = rest[:lev_count]
     outs = rest[lev_count : 2 * lev_count]
-    f_ref, mis_ref, g_ref = rest[2 * lev_count :]
+    f_ref, mis_ref = rest[2 * lev_count :]
     lev = lev_ref[0]
     own = blocks[0].shape[0]
     for k in range(lev_count):
-        at = pl.multiple_of(lax.rem(lev + k, lev_count) * own, 16)
+        at = pl.multiple_of(source(lev, lev_count, k) * own, 16)
         f_ref[pl.ds(at, own), :] = blocks[k][...]
-    pre_col = nn(inner_ref[...], f_ref[...])
-    act, slope = gelu_slope(pre_col)
-    forecast = f_ref[...].astype(F32) + nn(outer_ref[...], act.astype(BF16))
-    misfit = (forecast - obst_ref[...]) * scale_ref[...]
-    mis_ref[...] = misfit
-    grad_act = (nn(outert_ref[...], misfit.astype(BF16)) * slope).astype(BF16)
+    wide = inner_ref.shape[0]
+    fields = f_ref[...]
+    acts, slopes = [], []
+    for j in range(0, wide, 256):
+        act, slope = gelu_slope(nn(inner_ref[j : j + 256, :], fields))
+        acts.append(act.astype(BF16))
+        slopes.append(slope)
+    act = jnp.concatenate(acts, 0)
+    misfits = []
+    for j in range(0, own * lev_count, 256):
+        forecast = f_ref[j : j + 256, :].astype(F32) + nn(outer_ref[j : j + 256, :], act)
+        misfit = (forecast - obst_ref[j : j + 256, :]) * scale_ref[j : j + 256, :]
+        mis_ref[j : j + 256, :] = misfit
+        misfits.append(misfit.astype(BF16))
+    misfit = jnp.concatenate(misfits, 0)
+    grad_act = jnp.concatenate(
+        [
+            (nn(outert_ref[j : j + 256, :], misfit) * slopes[j // 256]).astype(BF16)
+            for j in range(0, wide, 256)
+        ],
+        0,
+    )
     mine = mis_ref[pl.ds(pl.multiple_of(lev * own, 16), own), :]
     grad_fields = (mine + nn(innert_ref[...], grad_act)).astype(BF16)
     groups, hidden, _ = mid_ref.shape
@@ -286,12 +311,10 @@
     grad_one = jnp.concatenate(ones, 0)
     taps = wt_ref.shape[0]
     portion = wt_ref.shape[1] // lev_count
-    for t in range(taps):
-        patch = nn(wt_ref[t], grad_one).astype(BF16)
-        for d in range(lev_count):
-            g_ref[d, t] = patch[d * portion : (d + 1) * portion]
     for k in range(lev_count):
-        outs[k][...] = g_ref[target(lev, lev_count, k)]
+        at = pl.multiple_of(target(lev, lev_count, k) * portion, 16)
+        left = jnp.concatenate([wt_ref[t, pl.ds(at, portion), :] for t in range(taps)], 0)
+        outs[k][...] = nn(left, grad_one).astype(BF16).reshape(taps, portion, -1)
 
 
 def edge_kernel(rows, cols, index_ref, *rest):
@@ -332,12 +355,19 @@
 def join_kernel(count, lev_ref, top_ref, bottom_ref, left_ref, right_ref, *outs):
     portion = top_ref.shape[1]
     spot = lax.broadcasted_iota(jnp.int32, (portion, 128), 1)
+    each = count // len(outs)
     for k in range(count):
+        out = outs[k // each].at[k % each]
         at = place(lev_ref[0], count, k)
-        outs[k][0] = top_ref[at]
-        outs[k][1] = bottom_ref[at]
+        out[0] = top_ref[at]
+        out[1] = bottom_ref[at]
         side = jnp.where(spot < 64, right_ref[at].astype(F32), left_ref[at].astype(F32))
-        outs[k][2] = side.astype(BF16)
+        out[2] = side.astype(BF16)
+
+
+def fold_kernel(kept_ref, got_ref, mine_ref, pass_ref):
+    mine_ref[...] = (kept_ref[0].astype(F32) + got_ref[0].astype(F32)).astype(BF16)
+    pass_ref[...] = (kept_ref[1].astype(F32) + got_ref[1].astype(F32)).astype(BF16)
 
 
 def relay_kernel(count, lev_ref, block_ref, got_ref, out_ref):
@@ -345,66 +375,77 @@
     out_ref[...] = (block_ref[...].astype(F32) + got_ref[...].astype(F32) * keep).astype(BF16)
 
 
-def final_kernel(rows, cols, count, lev_ref, index_ref, latent_ref, *rest):
-    rims, own, relayed = rest[:count], rest[count], rest[count + 1]
-    parts, (out_ref, own_ref, sum_ref, edge_ref, sem) = rest[count + 2 : -5], rest[-5:]
+def final_kernel(rows, cols, count, edges, lev_ref, index_ref, latent_ref, *rest):
+    rims, own, relayed = rest[:edges], rest[edges], rest[edges + 1]
+    parts = rest[edges + 2 : -7]
+    out_ref, own_ref, sum_ref, edge_ref, wait_ref, sem, sems = rest[-7:]
     portion = out_ref.shape[0]
     fetch = pltpu.make_async_copy(
         latent_ref.at[pl.ds(pl.multiple_of(lev_ref[0] * portion, 8), portion)], own_ref, sem
     )
     fetch.start()
-    keep = jnp.where(relays(lev_ref[0], count), 0.0, 1.0)
-    total = own[...].astype(F32) + relayed[...].astype(F32) * keep
-    for block in parts:
-        total = total + block[...].astype(F32)
-    sum_ref[...] = total
+    row, _ = split(index_ref[...], cols)
+    _, colc = split(upright(index_ref), cols)
+    slots = row.shape[1]
     total = rims[0][...].astype(F32)
     for block in rims[1:]:
         total = total + block[...].astype(F32)
     edge_ref[...] = total
-    fetch.wait()
-    row, _ = split(index_ref[...], cols)
-    _, colc = split(upright(index_ref), cols)
-    slots = row.shape[1]
     cells = lax.broadcasted_iota(jnp.int32, (slots, cols), 1)
-    hots = [hot(colc + (b - 1) == cells) for b in range(3)]
+    lane = lax.broadcasted_iota(jnp.int32, (128, cols), 0)
+    spot = lax.broadcasted_iota(jnp.int32, (128, cols), 1)
+    ends = hot(((lane < 64) & (spot == cols - 1)) | ((lane >= 64) & (spot == 0)))
+    hots = jnp.concatenate([hot(colc + (b - 1) == cells) for b in range(3)] + [ends], 0)
     lines = lax.broadcasted_iota(jnp.int32, (rows, slots), 0)
     masks = [row + (a - 1) == lines for a in range(3)]
-    spot = lax.broadcasted_iota(jnp.int32, (rows, 128), 1)
-    line = lax.broadcasted_iota(jnp.int32, (rows, 128), 0)
-    picks = [spot == line + 1, spot == line + 65]
-    lane = lax.broadcasted_iota(jnp.int32, (rows, cols), 1)
+    place_of = lax.broadcasted_iota(jnp.int32, (rows, 128), 1)
+    line_of = lax.broadcasted_iota(jnp.int32, (rows, 128), 0)
+    picks = (place_of == line_of + 1) | (place_of == line_of + 65)
     high = lax.broadcasted_iota(jnp.int32, (rows, cols), 0)
-    step = 8
-    for c0 in range(0, portion, step):
-        acc = None
-        for b in range(3):
-            parts = []
-            for c in range(c0, c0 + step):
+    keep = jnp.where(relays(lev_ref[0], count), 0.0, 1.0)
+    step = sum_ref.shape[2]
+    outs = []
+    fetch.wait()
+    for i, c0 in enumerate(range(0, portion, step)):
+        span = slice(c0, c0 + step)
+        total = own[:, span, :].astype(F32) + relayed[:, span, :].astype(F32) * keep
+        for block in parts:
+            total = total + block[:, span, :].astype(F32)
+        sum_ref[i] = total
+        lefts = []
+        for c in range(step):
+            pieces = []
+            for b in range(3):
                 part = jnp.zeros((rows, slots), F32)
                 for a in range(3):
-                    values = jnp.broadcast_to(sum_ref[3 * a + b, c : c + 1, :], (rows, slots))
+                    values = jnp.broadcast_to(sum_ref[i, 3 * a + b, c : c + 1, :], (rows, slots))
                     part = jnp.where(masks[a], values, part)
-                parts.append(part.astype(BF16))
-            part = nn(jnp.concatenate(parts, 0), hots[b])
-            acc = part if acc is None else acc + part
-        for c in range(c0, c0 + step):
-            field = acc[(c - c0) * rows : (c - c0 + 1) * rows] + own_ref[c].astype(F32)
-            above = jnp.broadcast_to(edge_ref[0, c : c + 1, :], (rows, cols))
-            below = jnp.broadcast_to(edge_ref[1, c : c + 1, :], (rows, cols))
-            side = jnp.broadcast_to(edge_ref[2, c : c + 1, :], (rows, 128))
-            last = jnp.sum(jnp.where(picks[0], side, 0.0), 1, keepdims=True)
-            first = jnp.sum(jnp.where(picks[1], side, 0.0), 1, keepdims=True)
-            field = field + jnp.where(high == 0, above, 0.0)
-            field = field + jnp.where(high == rows - 1, below, 0.0)
-            field = field + jnp.where(lane == 0, first, 0.0)
-            out_ref[c] = field + jnp.where(lane == cols - 1, last, 0.0)
+                pieces.append(part.astype(BF16))
+            side = jnp.broadcast_to(edge_ref[2, c0 + c : c0 + c + 1, :], (rows, 128))
+            pieces.append(jnp.where(picks, side, 0.0).astype(BF16))
+            lefts.append(jnp.concatenate(pieces, 1))
+        acc = nn(jnp.concatenate(lefts, 0), hots)
+        for c in range(step):
+            field = acc[c * rows : (c + 1) * rows] + own_ref[c0 + c].astype(F32)
+            above = jnp.broadcast_to(edge_ref[0, c0 + c : c0 + c + 1, :], (rows, cols))
+            below = jnp.broadcast_to(edge_ref[1, c0 + c : c0 + c + 1, :], (rows, cols))
+            edge = jnp.where(high == 0, above, jnp.where(high == rows - 1, below, 0.0))
+            wait_ref[c0 + c] = field + edge
+        out = pltpu.make_async_copy(wait_ref.at[span], out_ref.at[span], sems.at[i])
+        out.start()
+        outs.append(out)
+    for out in outs:
+        out.wait()
 
 
 def shift(x, axis, by, wrap=True):
     size = lax.axis_size(axis)
     pairs = [(i, (i + by) % size) for i in range(size) if wrap or 0 <= i + by < size]
     return lax.ppermute(x, axis, pairs)
+
+
+def paired(x, k):
+    return lax.ppermute(x, "lev", [(i, i ^ k) for i in range(4)])
 
 
 def from_sides(x, axis):
@@ -492,7 +533,7 @@
 
     blocks = [fields]
     for k in range(1, lev_count):
-        blocks.append(shift(fields, "lev", -k))
+        blocks.append(paired(fields, k) if lev_count == 4 else shift(fields, "lev", -k))
     column_shape = jax.ShapeDtypeStruct((own * lev_count, slots), F32)
     turned = call(
         prepare_kernel,
@@ -520,7 +561,6 @@
         scratch_shapes=[
             pltpu.VMEM((own * lev_count, slots), BF16),
             pltpu.VMEM((own * lev_count, slots), F32),
-            pltpu.VMEM((lev_count, taps, portion, slots), BF16),
         ],
     )(
         lev,
@@ -570,32 +610,40 @@
     )(row_edge, from_left, from_right)
     onto_first = shift(down, "lat", 1, wrap=False)
     onto_last = shift(up, "lat", -1, wrap=False)
+    each = 2 if lev_count == 4 else 1
     joined = call(
         functools.partial(join_kernel, lev_count),
-        (jax.ShapeDtypeStruct((3, portion, 128), BF16),) * lev_count,
+        (jax.ShapeDtypeStruct((each, 3, portion, 128), BF16),) * (lev_count // each),
         [SM] + [VM] * 4,
         flops // 64,
         12,
     )(lev, onto_first, onto_last, from_left, from_right)
-    rims = [joined[0]]
-    for k in range(1, lev_count):
-        if lev_count == 4:
-            rims.append(lax.ppermute(joined[k], "lev", [(i, i ^ k) for i in range(4)]))
-        else:
-            rims.append(shift(joined[k], "lev", k))
+    if lev_count == 4:
+        got = paired(joined[1], 1)
+        rim_shape = jax.ShapeDtypeStruct((3, portion, 128), BF16)
+        kept, passing = call(fold_kernel, (rim_shape,) * 2, [VM] * 2, flops // 64, 8)(
+            joined[0], got
+        )
+        rims = [kept, paired(passing, 2)]
+    else:
+        rims = [joined[0][0]]
+        rims += [shift(joined[k], "lev", k)[0] for k in range(1, lev_count)]
 
     return call(
-        functools.partial(final_kernel, rows, cols, lev_count),
+        functools.partial(final_kernel, rows, cols, lev_count, len(rims)),
         jax.ShapeDtypeStruct((portion, rows, cols), F32),
-        [SM, VM, HBM] + [VM] * (2 + len(parts) + lev_count),
+        [SM, VM, HBM] + [VM] * (2 + len(parts) + len(rims)),
         flops // 4,
         16,
         scratch_shapes=[
             pltpu.VMEM((portion, rows, cols), BF16),
-            pltpu.VMEM((taps, portion, slots), F32),
+            pltpu.VMEM((portion // STEP, taps, STEP, slots), F32),
             pltpu.VMEM((3, portion, 128), F32),
+            pltpu.VMEM((portion, rows, cols), F32),
             pltpu.SemaphoreType.DMA,
+            pltpu.SemaphoreType.DMA((portion // STEP,)),
         ],
+        out_specs=HBM,
     )(lev, index, far, *rims, patches[0], relayed, *parts)
 
 

time: 74.2 us -> 71.6 us (0.965)
  starting transfers between devices: 28.3 us -> 19 us
  waiting for transfers between devices: 22 us -> 31 us
  Pallas kernels: 20.6 us -> 18.2 us
    ppermute x3 -> x5, waiting for transfers between devices: 6.35 us -> 16.6 us  [paired(): return lax.ppermute(x, 'lev', [(i, i ^ k) for i in range(4)])]
    ppermute x9 -> x6, starting transfers between devices: 14 us -> 8.49 us  [shift(): return lax.ppermute(x, axis, pairs)]
    ppermute x1, starting transfers between devices: 2.92 us -> 0.07 us  [steps(): relayed = lax.ppermute(patches[1], 'lev', [(0, 1), (1, 0), (2, 3), (3, 2)])]
    ppermute x9 -> x6, waiting for transfers between devices: 11.8 us -> 9.27 us  [shift(): return lax.ppermute(x, axis, pairs)]
    pallas_call x1, Pallas kernels: 4.69 us -> 3.24 us  [steps(): call(functools.partial(column_kernel, lev_count), (patch_shape,) * lev_co...]
    ppermute x1, starting transfers between devices: 2.2 us -> 0.8 us  [steps(): parts.append(lax.ppermute(passed, 'lev', [(0, 1), (1, 3), (3, 2), (2, 0)]))]
    ppermute x1, waiting for transfers between devices: 3.83 us -> 5.11 us  [steps(): relayed = lax.ppermute(patches[1], 'lev', [(0, 1), (1, 0), (2, 3), (3, 2)])]
    pallas_call x2 -> x3, Pallas kernels: 3.92 us -> 3.6 us  [the longest x1 3.55 us: steps(): call(functools.partial(final_kernel, rows, cols, lev_count, len(rims)), j...]
  transfers between devices with their start and end apart: 16 -> 15, of which waited for: 8 -> 7; matrix products, arithmetic and copies ran while one was open for 2% -> 3% of each run, Pallas kernels for 9% -> 9%
where the time goes in v5:
time: 71.6 us; the launch traced here: 71.3 us
  waiting for transfers between devices  31 us (43%)
  starting transfers between devices  19 us (27%)
  Pallas kernels  18.2 us (25%)
  local copies, waits for them, and re-layouts  1.89 us (3%)
  between operations  1.11 us (2%)
    ppermute x5, waiting for transfers between devices, paired(): return lax.ppermute(x, 'lev', [(i, i ^ k) for i in range(4)])  16.6 us
    ppermute x6, waiting for transfers between devices, shift(): return lax.ppermute(x, axis, pairs)  9.27 us
    ppermute x6, starting transfers between devices, shift(): return lax.ppermute(x, axis, pairs)  8.49 us
    ppermute x5, starting transfers between devices, paired(): return lax.ppermute(x, 'lev', [(i, i ^ k) for i in range(4)])  5.49 us
    ppermute x1, waiting for transfers between devices, steps(): relayed = lax.ppermute(patches[1], 'lev', [(0, 1), (1, 0), (2, 3), (3, 2)])  5.11 us
    pallas_call x1, Pallas kernels, steps(): call(functools.partial(final_kernel, rows, cols, lev_count, len(rims)), j...  3.55 us
    ppermute x1, starting transfers between devices, steps(): parts.append(lax.ppermute(patches[2], 'lev', [(0, 2), (3, 1)]))  3.5 us
    pallas_call x1, Pallas kernels, steps(): call(functools.partial(gather_kernel, rows, cols), jax.ShapeDtypeStruct((...  3.36 us
  transfers between devices with their start and end apart: 15, of which 7 were waited for; matrix products, arithmetic and copies ran while one was open for 3% of the time, Pallas kernels for 9%

profile of v5, /device:TPU:0, one launch (start us, length us, event | category | flops | bytes accessed | tf_op | source)
XLA Modules:
  0.0 71.3 jit_solution(14518886309373230702)
XLA Ops:
  0.0 2.3 %shard_map.101 = (bf16[4096,256]{1,0:T(8,128)(2,1)S(1)}, bf16[128,256]{1,0:T(8,128)(2,1)S(1)}, bf16[128,256]{1,0:T(8,128)(2,1)S(1)}, bf16[2,32,256]{2,1,0:T(8,128)(2,1)S(1)}) custom-call(s32[1]{0:T(128)} %bitcast.lev_ref._, bf16[256,32,128]{2,1,0:T(8,128)(2,1)} %latent_ref.1), custom_call_target="tpu_custom_call" | custom-call | flops 150994944 | bytes 9043968 | tf_op jit(solution)/shard_map/pallas_call | solution.py:484
  2.3 2.4 %collective-permute-start = (bf16[128,256]{1,0:T(8,128)(2,1)S(1)}, bf16[128,256]{1,0:T(8,128)(2,1)S(1)}, u32[]{:S(2)}, u32[]{:S(2)}) collective-permute-start(bf16[128,256]{1,0:T(8,128)(2,1)S(1)} %get-tuple-element.34), channel_id=1, source_target_pairs={{0,2},{2,4},{4,6},{1,3},{3,5},{5,7},{8,10},{10,12},{12,14},{9,11},... | collective-permute-start | bytes 196616 | tf_op jit(solution)/shard_map/ppermute | solution.py:444
  4.7 1.3 %collective-permute-start.1 = (bf16[128,256]{1,0:T(8,128)(2,1)S(1)}, bf16[128,256]{1,0:T(8,128)(2,1)S(1)}, u32[]{:S(2)}, u32[]{:S(2)}) collective-permute-start(bf16[128,256]{1,0:T(8,128)(2,1)S(1)} %get-tuple-element.35), channel_id=1, source_target_pairs={{2,0},{4,2},{6,4},{3,1},{5,3},{7,5},{10,8},{12,10},{14,12},{11,9},... | collective-permute-start | bytes 196616 | tf_op jit(solution)/shard_map/ppermute | solution.py:444
  6.1 1.8 %copy.11 = bf16[9,4,128,256]{3,2,1,0:T(8,128)(2,1)S(1)} copy(bf16[9,4,128,256]{3,2,0,1:T(8,128)(2,1)} %bitcast.21) | data formatting | bytes 4718592 | tf_op jit(solution)/shard_map/transpose | solution.py:523
  7.9 2.1 %collective-permute-done.1.below_ref = bf16[128,256]{1,0:T(8,128)(2,1)S(1)} collective-permute-done((bf16[128,256]{1,0:T(8,128)(2,1)S(1)}, bf16[128,256]{1,0:T(8,128)(2,1)S(1)}, u32[]{:S(2)}, u32[]{:S(2)}) %collective-permute-start.1) | collective-permute-done | bytes 65568 | tf_op jit(solution)/shard_map/ppermute | solution.py:444
  10.1 1.6 %collective-permute-start.2 = (bf16[2,34,256]{2,1,0:T(8,128)(2,1)S(1)}, bf16[2,34,256]{2,1,0:T(8,128)(2,1)S(1)}, u32[]{:S(2)}, u32[]{:S(2)}) collective-permute-start(bf16[2,34,256]{2,1,0:T(8,128)(2,1)S(1)} %pad_maximum_fusion), channel_id=1, source_target_pairs={{0,1},{1,0},{2,3},{3,2},{4,5},{5,4},{6,7},{7,6},{8,9},{9,8},{10,11... | collective-permute-start | bytes 104456 | tf_op jit(solution)/shard_map/ppermute | solution.py:444
  11.6 3.4 %shard_map.102.x_ref = bf16[9,256,256]{2,1,0:T(8,128)(2,1)S(1)} custom-call(s32[1,256]{1,0:T(1,128)S(1)} %bitcast.16, s32[1,256]{1,0:T(1,128)S(1)} %bitcast.17, bf16[4096,256]{1,0:T(8,128)(2,1)S(1)} %get-tuple-element.33.tile_ref), custom_call_target="tpu_custom_call" | custom-call | flops 603979776 | bytes 4718592 | tf_op jit(solution)/shard_map/pallas_call | solution.py:512
  15.1 3.0 %shard_map.103 = (bf16[512,256]{1,0:T(8,128)(2,1)S(1)}, bf16[512,256]{1,0:T(8,128)(2,1)S(1)}, bf16[192,256]{1,0:T(8,128)(2,1)S(1)}) custom-call(s32[1,256]{1,0:T(1,128)S(1)} %bitcast.18, bf16[9,256,256]{2,1,0:T(8,128)(2,1)S(1)} %shard_map.102.x_ref, bf16[128,256]{1,0:T(8,128)(2,1)S(1)} %collective-permute-done.above_ref, ...), custom_call_target="tpu_custom_call" | custom-call | flops 1207959552 | bytes 2490368 | tf_op jit(solution)/shard_map/pallas_call | solution.py:525
  18.0 3.7 %collective-permute-start.5 = (bf16[192,256]{1,0:T(8,128)(2,1)S(1)}, bf16[192,256]{1,0:T(8,128)(2,1)S(1)}, u32[]{:S(2)}, u32[]{:S(2)}) collective-permute-start(bf16[192,256]{1,0:T(8,128)(2,1)S(1)} %get-tuple-element.40.rest_0_), channel_id=1, source_target_pairs={{0,24},{8,16},{16,8},{24,0},{1,25},{9,17},{17,9},{25,1},{2,26},{10... | collective-permute-start | bytes 294920 | tf_op jit(solution)/shard_map/ppermute | solution.py:448
  21.7 0.8 %collective-permute-start.3 = (bf16[192,256]{1,0:T(8,128)(2,1)S(1)}, bf16[192,256]{1,0:T(8,128)(2,1)S(1)}, u32[]{:S(2)}, u32[]{:S(2)}) collective-permute-start(bf16[192,256]{1,0:T(8,128)(2,1)S(1)} %get-tuple-element.40.rest_0_), channel_id=1, source_target_pairs={{0,8},{8,0},{16,24},{24,16},{1,9},{9,1},{17,25},{25,17},{2,10},{10... | collective-permute-start | bytes 294920 | tf_op jit(solution)/shard_map/ppermute | solution.py:448
  23.2 1.8 %shard_map.100 = (f32[768,256]{1,0:T(8,128)S(1)}, f32[768,256]{1,0:T(8,128)S(1)}, bf16[192,1024]{1,0:T(8,128)(2,1)S(1)}, bf16[1024,768]{1,0:T(8,128)(2,1)S(1)}, bf16[9,256,512]{2,1,0:T(8,128)(2,1)S(1)}) custom-call(s32[1]{0:T(128)} %bitcast.lev_ref._, s32[1,1]{1,0:T(1,128)S(6)} %copy.12.count_ref, f32[256,768]{1,0:T(8,128)S(1)} %bitcast.15, ...), custom_call_target="tpu_custom_call" | custom-call | flops 603979776 | bytes 23592960 | tf_op jit(solution)/shard_map/pallas_call | solution.py:538
  25.0 5.5 %collective-permute-done.4.rest_2_ = bf16[192,256]{1,0:T(8,128)(2,1)S(1)} collective-permute-done((bf16[192,256]{1,0:T(8,128)(2,1)S(1)}, bf16[192,256]{1,0:T(8,128)(2,1)S(1)}, u32[]{:S(2)}, u32[]{:S(2)}) %collective-permute-start.4) | collective-permute-done | bytes 98336 | tf_op jit(solution)/shard_map/ppermute | solution.py:448
  30.5 3.2 %shard_map.104 = (bf16[9,64,256]{2,1,0:T(8,128)(2,1)S(1)}, bf16[9,64,256]{2,1,0:T(8,128)(2,1)S(1)}, bf16[9,64,256]{2,1,0:T(8,128)(2,1)S(1)}, bf16[9,64,256]{2,1,0:T(8,128)(2,1)S(1)}) custom-call(s32[1]{0:T(128)} %bitcast.lev_ref._, bf16[1024,768]{1,0:T(8,128)(2,1)S(1)} %copy-done, bf16[192,1024]{1,0:T(8,128)(2,1)S(1)} %get-tuple-element.29.innert_ref, ...), custom_call_target="tpu_custom_call" | custom-call | flops 2415919104 | bytes 4718592 | tf_op jit(solution)/shard_map/pallas_call | solution.py:555
  33.9 3.5 %collective-permute-start.13 = (bf16[9,64,256]{2,1,0:T(8,128)(2,1)S(1)}, bf16[9,64,256]{2,1,0:T(8,128)(2,1)S(1)}, u32[]{:S(2)}, u32[]{:S(2)}) collective-permute-start(bf16[9,64,256]{2,1,0:T(8,128)(2,1)S(1)} %get-tuple-element.43.rest_2_), channel_id=1, source_target_pairs={{0,16},{24,8},{1,17},{25,9},{2,18},{26,10},{3,19},{27,11},{4,20},{... | collective-permute-start | bytes 884744 | tf_op jit(solution)/shard_map/ppermute | solution.py:583
  38.1 5.1 %collective-permute-done.11.got_ref.rest_3_ = bf16[9,64,256]{2,1,0:T(8,128)(2,1)S(1)} collective-permute-done((bf16[9,64,256]{2,1,0:T(8,128)(2,1)S(1)}, bf16[9,64,256]{2,1,0:T(8,128)(2,1)S(1)}, u32[]{:S(2)}, u32[]{:S(2)}) %collective-permute-start.11) | collective-permute-done | bytes 294944 | tf_op jit(solution)/shard_map/ppermute | solution.py:581
  43.3 0.8 %collective-permute-start.14 = (bf16[9,64,256]{2,1,0:T(8,128)(2,1)S(1)}, bf16[9,64,256]{2,1,0:T(8,128)(2,1)S(1)}, u32[]{:S(2)}, u32[]{:S(2)}) collective-permute-start(bf16[9,64,256]{2,1,0:T(8,128)(2,1)S(1)} %shard_map.109), channel_id=1, source_target_pairs={{0,8},{8,24},{24,16},{16,0},{1,9},{9,25},{25,17},{17,1},{2,10},{10... | collective-permute-start | bytes 884744 | tf_op jit(solution)/shard_map/ppermute | solution.py:587
  45.4 3.7 %collective-permute-done.6.left_ref.right_ref = bf16[4,64,128]{2,1,0:T(8,128)(2,1)S(1)} collective-permute-done((bf16[4,64,128]{2,1,0:T(8,128)(2,1)S(1)}, bf16[4,64,128]{2,1,0:T(8,128)(2,1)S(1)}, u32[]{:S(2)}, u32[]{:S(2)}) %collective-permute-start.6) | collective-permute-done | bytes 65568 | tf_op jit(solution)/shard_map/ppermute | solution.py:444
  49.2 1.3 %collective-permute-start.7 = (bf16[4,64,128]{2,1,0:T(8,128)(2,1)S(1)}, bf16[4,64,128]{2,1,0:T(8,128)(2,1)S(1)}, u32[]{:S(2)}, u32[]{:S(2)}) collective-permute-start(bf16[4,64,128]{2,1,0:T(8,128)(2,1)S(1)} %get-tuple-element.47), channel_id=1, source_target_pairs={{0,2},{2,4},{4,6},{1,3},{3,5},{5,7},{8,10},{10,12},{12,14},{9,11},... | collective-permute-start | bytes 196616 | tf_op jit(solution)/shard_map/ppermute | solution.py:444
  50.5 1.3 %collective-permute-start.8 = (bf16[4,64,128]{2,1,0:T(8,128)(2,1)S(1)}, bf16[4,64,128]{2,1,0:T(8,128)(2,1)S(1)}, u32[]{:S(2)}, u32[]{:S(2)}) collective-permute-start(bf16[4,64,128]{2,1,0:T(8,128)(2,1)S(1)} %get-tuple-element.48), channel_id=1, source_target_pairs={{2,0},{4,2},{6,4},{3,1},{5,3},{7,5},{10,8},{12,10},{14,12},{11,9},... | collective-permute-start | bytes 196616 | tf_op jit(solution)/shard_map/ppermute | solution.py:444
  51.8 3.5 %collective-permute-done.8.bottom_ref = bf16[4,64,128]{2,1,0:T(8,128)(2,1)S(1)} collective-permute-done((bf16[4,64,128]{2,1,0:T(8,128)(2,1)S(1)}, bf16[4,64,128]{2,1,0:T(8,128)(2,1)S(1)}, u32[]{:S(2)}, u32[]{:S(2)}) %collective-permute-start.8) | collective-permute-done | bytes 65568 | tf_op jit(solution)/shard_map/ppermute | solution.py:444
  55.5 5.8 %collective-permute-done.9.got_ref = bf16[2,3,64,128]{3,2,1,0:T(8,128)(2,1)S(1)} collective-permute-done((bf16[2,3,64,128]{3,2,1,0:T(8,128)(2,1)S(1)}, bf16[2,3,64,128]{3,2,1,0:T(8,128)(2,1)S(1)}, u32[]{:S(2)}, u32[]{:S(2)}) %collective-permute-start.9) | collective-permute-done | bytes 98336 | tf_op jit(solution)/shard_map/ppermute | solution.py:448
  61.3 1.0 %collective-permute-start.10 = (bf16[3,64,128]{2,1,0:T(8,128)(2,1)S(1)}, bf16[3,64,128]{2,1,0:T(8,128)(2,1)S(1)}, u32[]{:S(2)}, u32[]{:S(2)}) collective-permute-start(bf16[3,64,128]{2,1,0:T(8,128)(2,1)S(1)} %get-tuple-element.52), channel_id=1, source_target_pairs={{0,16},{8,24},{16,0},{24,8},{1,17},{9,25},{17,1},{25,9},{2,18},{10... | collective-permute-start | bytes 147464 | tf_op jit(solution)/shard_map/ppermute | solution.py:448
  62.2 5.3 %collective-permute-done.10.rest_1_ = bf16[3,64,128]{2,1,0:T(8,128)(2,1)S(1)} collective-permute-done((bf16[3,64,128]{2,1,0:T(8,128)(2,1)S(1)}, bf16[3,64,128]{2,1,0:T(8,128)(2,1)S(1)}, u32[]{:S(2)}, u32[]{:S(2)}) %collective-permute-start.10) | collective-permute-done | bytes 49184 | tf_op jit(solution)/shard_map/ppermute | solution.py:448
  67.6 3.6 %shard_map.110 = f32[64,32,128]{2,1,0:T(8,128)} custom-call(s32[1]{0:T(128)} %bitcast.lev_ref._, s32[1,256]{1,0:T(1,128)S(1)} %bitcast.20, bf16[256,32,128]{2,1,0:T(8,128)(2,1)} %latent_ref.1, bf16[3,64,128]{2,1,0:T(8,128)(2,1)S(1)} %get-tuple-element.51.rest_0_, bf16[3,64,128]{2,1,0:T(8,128)(2,1)S(1)} %collective-permute-done.10.rest_1_, ...), custom_call_target="tpu_custom_call" | custom-call | flops 150994944 | bytes 4194304 | tf_op jit(solution)/shard_map/pallas_call | solution.py:632
  (38 shorter events, 2.6 us)
Async XLA Ops:
  2.3 5.6 %collective-permute-start = (bf16[128,256]{1,0:T(8,128)(2,1)S(1)}, bf16[128,256]{1,0:T(8,128)(2,1)S(1)}, u32[]{:S(2)}, u32[]{:S(2)}) collective-permute-start(bf16[128,256]{1,0:T(8,128)(2,1)S(1)} %get-tuple-element.34), channel_id=1, source_target_pairs={{0,2},{2,4},{4,6},{1,3},{3,5},{5,7},{8,10},{10,12},{12,14},{9,11},... | collective-permute-start | bytes 196616 | tf_op jit(solution)/shard_map/ppermute | solution.py:444
  4.7 5.3 %collective-permute-start.1 = (bf16[128,256]{1,0:T(8,128)(2,1)S(1)}, bf16[128,256]{1,0:T(8,128)(2,1)S(1)}, u32[]{:S(2)}, u32[]{:S(2)}) collective-permute-start(bf16[128,256]{1,0:T(8,128)(2,1)S(1)} %get-tuple-element.35), channel_id=1, source_target_pairs={{2,0},{4,2},{6,4},{3,1},{5,3},{7,5},{10,8},{12,10},{14,12},{11,9},... | collective-permute-start | bytes 196616 | tf_op jit(solution)/shard_map/ppermute | solution.py:444
  6.1 5.6 %copy-start.5 = (s32[1,1,256]{2,1,0:T(1,128)S(1)}, s32[1,1,256]{2,1,0:T(1,128)}, u32[]{:S(2)}) copy-start(s32[1,1,256]{2,1,0:T(1,128)} %param.18) | copy-start | bytes 3076
  7.9 7.1 %copy-start.3 = (bf16[4,128,128]{2,1,0:T(8,128)(2,1)S(1)}, bf16[4,128,128]{2,1,0:T(8,128)(2,1)}, u32[]{:S(2)}) copy-start(bf16[4,128,128]{2,1,0:T(8,128)(2,1)} %mid_ref.3) | copy-start | bytes 393220
  7.9 7.1 %copy-start.4 = (bf16[4,48,128]{2,1,0:T(8,128)(2,1)S(1)}, bf16[4,48,128]{2,1,0:T(8,128)(2,1)}, u32[]{:S(2)}) copy-start(bf16[4,48,128]{2,1,0:T(8,128)(2,1)} %outw_ref.3) | copy-start | bytes 147460
  10.1 4.9 %collective-permute-start.2 = (bf16[2,34,256]{2,1,0:T(8,128)(2,1)S(1)}, bf16[2,34,256]{2,1,0:T(8,128)(2,1)S(1)}, u32[]{:S(2)}, u32[]{:S(2)}) collective-permute-start(bf16[2,34,256]{2,1,0:T(8,128)(2,1)S(1)} %pad_maximum_fusion), channel_id=1, source_target_pairs={{0,1},{1,0},{2,3},{3,2},{4,5},{5,4},{6,7},{7,6},{8,9},{9,8},{10,11... | collective-permute-start | bytes 104456 | tf_op jit(solution)/shard_map/ppermute | solution.py:444
  15.0 8.1 %copy-start.6 = (f32[768]{0:T(1024)S(1)}, f32[768]{0:T(1024)}, u32[]{:S(2)}) copy-start(f32[768]{0:T(1024)} %param.17) | copy-start | bytes 9220
  15.0 8.1 %copy-start = (bf16[1024,768]{1,0:T(8,128)(2,1)S(1)}, bf16[1024,768]{1,0:T(8,128)(2,1)}, u32[]{:S(2)}) copy-start(bf16[1024,768]{1,0:T(8,128)(2,1)} %inner_ref.3) | copy-start | bytes 4718596
  15.0 8.1 %copy-start.1 = (bf16[768,1024]{1,0:T(8,128)(2,1)S(1)}, bf16[768,1024]{1,0:T(8,128)(2,1)}, u32[]{:S(2)}) copy-start(bf16[768,1024]{1,0:T(8,128)(2,1)} %outer_ref.3) | copy-start | bytes 4718596
  15.1 8.1 %copy-start.2 = (f32[1,1,256,768]{3,2,1,0:T(8,128)S(1)}, f32[1,1,256,768]{3,2,1,0:T(8,128)}, u32[]{:S(2)}) copy-start(f32[1,1,256,768]{3,2,1,0:T(8,128)} %param.16) | copy-start | bytes 2359300
  18.0 7.0 %collective-permute-start.5 = (bf16[192,256]{1,0:T(8,128)(2,1)S(1)}, bf16[192,256]{1,0:T(8,128)(2,1)S(1)}, u32[]{:S(2)}, u32[]{:S(2)}) collective-permute-start(bf16[192,256]{1,0:T(8,128)(2,1)S(1)} %get-tuple-element.40.rest_0_), channel_id=1, source_target_pairs={{0,24},{8,16},{16,8},{24,0},{1,25},{9,17},{17,9},{25,1},{2,26},{10... | collective-permute-start | bytes 294920 | tf_op jit(solution)/shard_map/ppermute | solution.py:448
  21.7 8.8 %collective-permute-start.4 = (bf16[192,256]{1,0:T(8,128)(2,1)S(1)}, bf16[192,256]{1,0:T(8,128)(2,1)S(1)}, u32[]{:S(2)}, u32[]{:S(2)}) collective-permute-start(bf16[192,256]{1,0:T(8,128)(2,1)S(1)} %get-tuple-element.40.rest_0_), channel_id=1, source_target_pairs={{0,16},{8,24},{16,0},{24,8},{1,17},{9,25},{17,1},{25,9},{2,18},{10... | collective-permute-start | bytes 294920 | tf_op jit(solution)/shard_map/ppermute | solution.py:448
  21.7 8.8 %collective-permute-start.3 = (bf16[192,256]{1,0:T(8,128)(2,1)S(1)}, bf16[192,256]{1,0:T(8,128)(2,1)S(1)}, u32[]{:S(2)}, u32[]{:S(2)}) collective-permute-start(bf16[192,256]{1,0:T(8,128)(2,1)S(1)} %get-tuple-element.40.rest_0_), channel_id=1, source_target_pairs={{0,8},{8,0},{16,24},{24,16},{1,9},{9,1},{17,25},{25,17},{2,10},{10... | collective-permute-start | bytes 294920 | tf_op jit(solution)/shard_map/ppermute | solution.py:448
  33.8 9.4 %collective-permute-start.11 = (bf16[9,64,256]{2,1,0:T(8,128)(2,1)S(1)}, bf16[9,64,256]{2,1,0:T(8,128)(2,1)S(1)}, u32[]{:S(2)}, u32[]{:S(2)}) collective-permute-start(bf16[9,64,256]{2,1,0:T(8,128)(2,1)S(1)} %get-tuple-element.42.rest_1_), channel_id=1, source_target_pairs={{0,8},{8,0},{16,24},{24,16},{1,9},{9,1},{17,25},{25,17},{2,10},{10... | collective-permute-start | bytes 884744 | tf_op jit(solution)/shard_map/ppermute | solution.py:581
  33.9 33.7 %collective-permute-start.13 = (bf16[9,64,256]{2,1,0:T(8,128)(2,1)S(1)}, bf16[9,64,256]{2,1,0:T(8,128)(2,1)S(1)}, u32[]{:S(2)}, u32[]{:S(2)}) collective-permute-start(bf16[9,64,256]{2,1,0:T(8,128)(2,1)S(1)} %get-tuple-element.43.rest_2_), channel_id=1, source_target_pairs={{0,16},{24,8},{1,17},{25,9},{2,18},{26,10},{3,19},{27,11},{4,20},{... | collective-permute-start | bytes 884744 | tf_op jit(solution)/shard_map/ppermute | solution.py:583
  37.4 30.2 %collective-permute-start.12 = (bf16[9,64,256]{2,1,0:T(8,128)(2,1)S(1)}, bf16[9,64,256]{2,1,0:T(8,128)(2,1)S(1)}, u32[]{:S(2)}, u32[]{:S(2)}) collective-permute-start(bf16[9,64,256]{2,1,0:T(8,128)(2,1)S(1)} %get-tuple-element.43.rest_2_), channel_id=1, source_target_pairs={{8,16},{16,8},{9,17},{17,9},{10,18},{18,10},{11,19},{19,11},{12,20... | collective-permute-start | bytes 884744 | tf_op jit(solution)/shard_map/ppermute | solution.py:582
  43.3 24.3 %collective-permute-start.14 = (bf16[9,64,256]{2,1,0:T(8,128)(2,1)S(1)}, bf16[9,64,256]{2,1,0:T(8,128)(2,1)S(1)}, u32[]{:S(2)}, u32[]{:S(2)}) collective-permute-start(bf16[9,64,256]{2,1,0:T(8,128)(2,1)S(1)} %shard_map.109), channel_id=1, source_target_pairs={{0,8},{8,24},{24,16},{16,0},{1,9},{9,25},{25,17},{17,1},{2,10},{10... | collective-permute-start | bytes 884744 | tf_op jit(solution)/shard_map/ppermute | solution.py:587
  44.7 4.3 %collective-permute-start.6 = (bf16[4,64,128]{2,1,0:T(8,128)(2,1)S(1)}, bf16[4,64,128]{2,1,0:T(8,128)(2,1)S(1)}, u32[]{:S(2)}, u32[]{:S(2)}) collective-permute-start(bf16[4,64,128]{2,1,0:T(8,128)(2,1)S(1)} %get-tuple-element.46), channel_id=1, source_target_pairs={{0,1},{1,0},{2,3},{3,2},{4,5},{5,4},{6,7},{7,6},{8,9},{9,8},{10,11... | collective-permute-start | bytes 196616 | tf_op jit(solution)/shard_map/ppermute | solution.py:444
  49.2 2.6 %collective-permute-start.7 = (bf16[4,64,128]{2,1,0:T(8,128)(2,1)S(1)}, bf16[4,64,128]{2,1,0:T(8,128)(2,1)S(1)}, u32[]{:S(2)}, u32[]{:S(2)}) collective-permute-start(bf16[4,64,128]{2,1,0:T(8,128)(2,1)S(1)} %get-tuple-element.47), channel_id=1, source_target_pairs={{0,2},{2,4},{4,6},{1,3},{3,5},{5,7},{8,10},{10,12},{12,14},{9,11},... | collective-permute-start | bytes 196616 | tf_op jit(solution)/shard_map/ppermute | solution.py:444
  50.5 4.8 %collective-permute-start.8 = (bf16[4,64,128]{2,1,0:T(8,128)(2,1)S(1)}, bf16[4,64,128]{2,1,0:T(8,128)(2,1)S(1)}, u32[]{:S(2)}, u32[]{:S(2)}) collective-permute-start(bf16[4,64,128]{2,1,0:T(8,128)(2,1)S(1)} %get-tuple-element.48), channel_id=1, source_target_pairs={{2,0},{4,2},{6,4},{3,1},{5,3},{7,5},{10,8},{12,10},{14,12},{11,9},... | collective-permute-start | bytes 196616 | tf_op jit(solution)/shard_map/ppermute | solution.py:444
  55.4 5.9 %collective-permute-start.9 = (bf16[2,3,64,128]{3,2,1,0:T(8,128)(2,1)S(1)}, bf16[2,3,64,128]{3,2,1,0:T(8,128)(2,1)S(1)}, u32[]{:S(2)}, u32[]{:S(2)}) collective-permute-start(bf16[2,3,64,128]{3,2,1,0:T(8,128)(2,1)S(1)} %get-tuple-element.50), channel_id=1, source_target_pairs={{0,8},{8,0},{16,24},{24,16},{1,9},{9,1},{17,25},{25,17},{2,10},{10... | collective-permute-start | bytes 294920 | tf_op jit(solution)/shard_map/ppermute | solution.py:448
  61.3 6.3 %collective-permute-start.10 = (bf16[3,64,128]{2,1,0:T(8,128)(2,1)S(1)}, bf16[3,64,128]{2,1,0:T(8,128)(2,1)S(1)}, u32[]{:S(2)}, u32[]{:S(2)}) collective-permute-start(bf16[3,64,128]{2,1,0:T(8,128)(2,1)S(1)} %get-tuple-element.52), channel_id=1, source_target_pairs={{0,16},{8,24},{16,0},{24,8},{1,17},{9,25},{17,1},{25,9},{2,18},{10... | collective-permute-start | bytes 147464 | tf_op jit(solution)/shard_map/ppermute | solution.py:448

commit v6 on v5

--- a/solution.py
+++ b/solution.py
@@ -222,6 +222,7 @@
 def prepare_kernel(
     lev_ref,
     count_ref,
+    latent_ref,
     obs_ref,
     weight_ref,
     inner_ref,
@@ -232,8 +233,15 @@
     innert_ref,
     outert_ref,
     wt_ref,
+    own_ref,
     turn_ref,
+    sem,
 ):
+    portion = own_ref.shape[0]
+    fetch = pltpu.make_async_copy(
+        latent_ref.at[pl.ds(pl.multiple_of(lev_ref[0] * portion, 8), portion)], own_ref, sem
+    )
+    fetch.start()
     obst_ref[...] = obs_ref[...].T
     slots = obs_ref.shape[0]
     levels = weight_ref.shape[1]
@@ -249,6 +257,7 @@
     outert_ref[...] = outer_ref[...].T
     for t in range(w_ref.shape[0]):
         wt_ref[t] = w_ref[t].T
+    fetch.wait()
 
 
 def column_kernel(
@@ -375,15 +384,11 @@
     out_ref[...] = (block_ref[...].astype(F32) + got_ref[...].astype(F32) * keep).astype(BF16)
 
 
-def final_kernel(rows, cols, count, edges, lev_ref, index_ref, latent_ref, *rest):
+def final_kernel(rows, cols, count, edges, lev_ref, index_ref, own_ref, *rest):
     rims, own, relayed = rest[:edges], rest[edges], rest[edges + 1]
-    parts = rest[edges + 2 : -7]
-    out_ref, own_ref, sum_ref, edge_ref, wait_ref, sem, sems = rest[-7:]
+    parts = rest[edges + 2 : -5]
+    out_ref, sum_ref, edge_ref, wait_ref, sems = rest[-5:]
     portion = out_ref.shape[0]
-    fetch = pltpu.make_async_copy(
-        latent_ref.at[pl.ds(pl.multiple_of(lev_ref[0] * portion, 8), portion)], own_ref, sem
-    )
-    fetch.start()
     row, _ = split(index_ref[...], cols)
     _, colc = split(upright(index_ref), cols)
     slots = row.shape[1]
@@ -405,7 +410,6 @@
     keep = jnp.where(relays(lev_ref[0], count), 0.0, 1.0)
     step = sum_ref.shape[2]
     outs = []
-    fetch.wait()
     for i, c0 in enumerate(range(0, portion, step)):
         span = slice(c0, c0 + step)
         total = own[:, span, :].astype(F32) + relayed[:, span, :].astype(F32) * keep
@@ -543,13 +547,17 @@
             jax.ShapeDtypeStruct((own, inner.shape[0]), BF16),
             jax.ShapeDtypeStruct((outer.shape[1], outer.shape[0]), BF16),
             jax.ShapeDtypeStruct((taps, chans, wide), BF16),
+            jax.ShapeDtypeStruct((portion, rows, cols), BF16),
         ),
-        [SM, SM] + [VM] * 5,
+        [SM, SM, HBM] + [VM] * 5,
         flops,
         24,
-        scratch_shapes=[pltpu.VMEM((inner.shape[1], inner.shape[0]), BF16)],
-    )(lev, obs_count, obs_values[0, 0], obs_weight[None, :], inner, outer, w)
-    obs_turned, scale, inner_turned, outer_turned, w_turned = turned
+        scratch_shapes=[
+            pltpu.VMEM((inner.shape[1], inner.shape[0]), BF16),
+            pltpu.SemaphoreType.DMA,
+        ],
+    )(lev, obs_count, far, obs_values[0, 0], obs_weight[None, :], inner, outer, w)
+    obs_turned, scale, inner_turned, outer_turned, w_turned, mine = turned
 
     patch_shape = jax.ShapeDtypeStruct((taps, portion, slots), BF16)
     patches = call(
@@ -632,19 +640,17 @@
     return call(
         functools.partial(final_kernel, rows, cols, lev_count, len(rims)),
         jax.ShapeDtypeStruct((portion, rows, cols), F32),
-        [SM, VM, HBM] + [VM] * (2 + len(parts) + len(rims)),
+        [SM, VM, VM] + [VM] * (2 + len(parts) + len(rims)),
         flops // 4,
         16,
         scratch_shapes=[
-            pltpu.VMEM((portion, rows, cols), BF16),
             pltpu.VMEM((portion // STEP, taps, STEP, slots), F32),
             pltpu.VMEM((3, portion, 128), F32),
             pltpu.VMEM((portion, rows, cols), F32),
-            pltpu.SemaphoreType.DMA,
             pltpu.SemaphoreType.DMA((portion // STEP,)),
         ],
         out_specs=HBM,
-    )(lev, index, far, *rims, patches[0], relayed, *parts)
+    )(lev, index, mine, *rims, patches[0], relayed, *parts)
 
 
 def solution(mesh):

time: 71.6 us -> 70.7 us (0.987)
  Pallas kernels: 18.2 us -> 17.4 us
    pallas_call x1, Pallas kernels: 3.55 us -> 2.62 us  [steps(): call(functools.partial(final_kernel, rows, cols, lev_count, len(rims)), j...]
where the time goes in v6:
time: 70.7 us; the launch traced here: 70.4 us
  waiting for transfers between devices  31 us (44%)
  starting transfers between devices  19 us (27%)
  Pallas kernels  17.4 us (25%)
  local copies, waits for them, and re-layouts  1.89 us (3%)
  between operations  1.11 us (2%)
    ppermute x5, waiting for transfers between devices, paired(): return lax.ppermute(x, 'lev', [(i, i ^ k) for i in range(4)])  16.6 us
    ppermute x6, waiting for transfers between devices, shift(): return lax.ppermute(x, axis, pairs)  9.27 us
    ppermute x6, starting transfers between devices, shift(): return lax.ppermute(x, axis, pairs)  8.49 us
    ppermute x5, starting transfers between devices, paired(): return lax.ppermute(x, 'lev', [(i, i ^ k) for i in range(4)])  5.49 us
    ppermute x1, waiting for transfers between devices, steps(): relayed = lax.ppermute(patches[1], 'lev', [(0, 1), (1, 0), (2, 3), (3, 2)])  5.11 us
    ppermute x1, starting transfers between devices, steps(): parts.append(lax.ppermute(patches[2], 'lev', [(0, 2), (3, 1)]))  3.5 us
    pallas_call x1, Pallas kernels, steps(): call(functools.partial(gather_kernel, rows, cols), jax.ShapeDtypeStruct((...  3.36 us
    pallas_call x1, Pallas kernels, steps(): call(functools.partial(column_kernel, lev_count), (patch_shape,) * lev_co...  3.28 us
  transfers between devices with their start and end apart: 15, of which 7 were waited for; matrix products, arithmetic and copies ran while one was open for 3% of the time, Pallas kernels for 9%

profile of v6, /device:TPU:0, one launch (start us, length us, event | category | flops | bytes accessed | tf_op | source)
XLA Modules:
  0.0 70.4 jit_solution(18315567792011345678)
XLA Ops:
  0.0 2.3 %shard_map.101 = (bf16[4096,256]{1,0:T(8,128)(2,1)S(1)}, bf16[128,256]{1,0:T(8,128)(2,1)S(1)}, bf16[128,256]{1,0:T(8,128)(2,1)S(1)}, bf16[2,32,256]{2,1,0:T(8,128)(2,1)S(1)}) custom-call(s32[1]{0:T(128)} %bitcast.lev_ref._, bf16[256,32,128]{2,1,0:T(8,128)(2,1)} %lat_ref.1), custom_call_target="tpu_custom_call" | custom-call | flops 150994944 | bytes 9043968 | tf_op jit(solution)/shard_map/pallas_call | solution.py:488
  2.3 2.4 %collective-permute-start = (bf16[128,256]{1,0:T(8,128)(2,1)S(1)}, bf16[128,256]{1,0:T(8,128)(2,1)S(1)}, u32[]{:S(2)}, u32[]{:S(2)}) collective-permute-start(bf16[128,256]{1,0:T(8,128)(2,1)S(1)} %get-tuple-element.36), channel_id=1, source_target_pairs={{0,2},{2,4},{4,6},{1,3},{3,5},{5,7},{8,10},{10,12},{12,14},{9,11},... | collective-permute-start | bytes 196616 | tf_op jit(solution)/shard_map/ppermute | solution.py:448
  4.7 1.3 %collective-permute-start.1 = (bf16[128,256]{1,0:T(8,128)(2,1)S(1)}, bf16[128,256]{1,0:T(8,128)(2,1)S(1)}, u32[]{:S(2)}, u32[]{:S(2)}) collective-permute-start(bf16[128,256]{1,0:T(8,128)(2,1)S(1)} %get-tuple-element.37), channel_id=1, source_target_pairs={{2,0},{4,2},{6,4},{3,1},{5,3},{7,5},{10,8},{12,10},{14,12},{11,9},... | collective-permute-start | bytes 196616 | tf_op jit(solution)/shard_map/ppermute | solution.py:448
  6.1 1.8 %copy.11 = bf16[9,4,128,256]{3,2,1,0:T(8,128)(2,1)S(1)} copy(bf16[9,4,128,256]{3,2,0,1:T(8,128)(2,1)} %bitcast.21) | data formatting | bytes 4718592 | tf_op jit(solution)/shard_map/transpose | solution.py:527
  7.9 2.1 %collective-permute-done.1.below_ref = bf16[128,256]{1,0:T(8,128)(2,1)S(1)} collective-permute-done((bf16[128,256]{1,0:T(8,128)(2,1)S(1)}, bf16[128,256]{1,0:T(8,128)(2,1)S(1)}, u32[]{:S(2)}, u32[]{:S(2)}) %collective-permute-start.1) | collective-permute-done | bytes 65568 | tf_op jit(solution)/shard_map/ppermute | solution.py:448
  10.1 1.6 %collective-permute-start.2 = (bf16[2,34,256]{2,1,0:T(8,128)(2,1)S(1)}, bf16[2,34,256]{2,1,0:T(8,128)(2,1)S(1)}, u32[]{:S(2)}, u32[]{:S(2)}) collective-permute-start(bf16[2,34,256]{2,1,0:T(8,128)(2,1)S(1)} %pad_maximum_fusion), channel_id=1, source_target_pairs={{0,1},{1,0},{2,3},{3,2},{4,5},{5,4},{6,7},{7,6},{8,9},{9,8},{10,11... | collective-permute-start | bytes 104456 | tf_op jit(solution)/shard_map/ppermute | solution.py:448
  11.6 3.4 %shard_map.102.x_ref = bf16[9,256,256]{2,1,0:T(8,128)(2,1)S(1)} custom-call(s32[1,256]{1,0:T(1,128)S(1)} %bitcast.16, s32[1,256]{1,0:T(1,128)S(1)} %bitcast.17, bf16[4096,256]{1,0:T(8,128)(2,1)S(1)} %get-tuple-element.35.tile_ref), custom_call_target="tpu_custom_call" | custom-call | flops 603979776 | bytes 4718592 | tf_op jit(solution)/shard_map/pallas_call | solution.py:516
  15.1 3.0 %shard_map.103 = (bf16[512,256]{1,0:T(8,128)(2,1)S(1)}, bf16[512,256]{1,0:T(8,128)(2,1)S(1)}, bf16[192,256]{1,0:T(8,128)(2,1)S(1)}) custom-call(s32[1,256]{1,0:T(1,128)S(1)} %bitcast.18, bf16[9,256,256]{2,1,0:T(8,128)(2,1)S(1)} %shard_map.102.x_ref, bf16[128,256]{1,0:T(8,128)(2,1)S(1)} %collective-permute-done.above_ref, ...), custom_call_target="tpu_custom_call" | custom-call | flops 1207959552 | bytes 2490368 | tf_op jit(solution)/shard_map/pallas_call | solution.py:529
  18.0 3.7 %collective-permute-start.5 = (bf16[192,256]{1,0:T(8,128)(2,1)S(1)}, bf16[192,256]{1,0:T(8,128)(2,1)S(1)}, u32[]{:S(2)}, u32[]{:S(2)}) collective-permute-start(bf16[192,256]{1,0:T(8,128)(2,1)S(1)} %get-tuple-element.42.rest_0_), channel_id=1, source_target_pairs={{0,24},{8,16},{16,8},{24,0},{1,25},{9,17},{17,9},{25,1},{2,26},{10... | collective-permute-start | bytes 294920 | tf_op jit(solution)/shard_map/ppermute | solution.py:452
  21.7 0.8 %collective-permute-start.3 = (bf16[192,256]{1,0:T(8,128)(2,1)S(1)}, bf16[192,256]{1,0:T(8,128)(2,1)S(1)}, u32[]{:S(2)}, u32[]{:S(2)}) collective-permute-start(bf16[192,256]{1,0:T(8,128)(2,1)S(1)} %get-tuple-element.42.rest_0_), channel_id=1, source_target_pairs={{0,8},{8,0},{16,24},{24,16},{1,9},{9,1},{17,25},{25,17},{2,10},{10... | collective-permute-start | bytes 294920 | tf_op jit(solution)/shard_map/ppermute | solution.py:452
  23.2 1.8 %shard_map.100 = (f32[768,256]{1,0:T(8,128)S(1)}, f32[768,256]{1,0:T(8,128)S(1)}, bf16[192,1024]{1,0:T(8,128)(2,1)S(1)}, bf16[1024,768]{1,0:T(8,128)(2,1)S(1)}, ...) custom-call(s32[1]{0:T(128)} %bitcast.lev_ref._, s32[1,1]{1,0:T(1,128)S(6)} %copy.12.count_ref, ...), custom_call_target="tpu_custom_call" | custom-call | flops 603979776 | bytes 25690112 | tf_op jit(solution)/shard_map/pallas_call | solution.py:542
  25.0 5.5 %collective-permute-done.4.rest_2_ = bf16[192,256]{1,0:T(8,128)(2,1)S(1)} collective-permute-done((bf16[192,256]{1,0:T(8,128)(2,1)S(1)}, bf16[192,256]{1,0:T(8,128)(2,1)S(1)}, u32[]{:S(2)}, u32[]{:S(2)}) %collective-permute-start.4) | collective-permute-done | bytes 98336 | tf_op jit(solution)/shard_map/ppermute | solution.py:452
  30.5 3.3 %shard_map.104 = (bf16[9,64,256]{2,1,0:T(8,128)(2,1)S(1)}, bf16[9,64,256]{2,1,0:T(8,128)(2,1)S(1)}, bf16[9,64,256]{2,1,0:T(8,128)(2,1)S(1)}, bf16[9,64,256]{2,1,0:T(8,128)(2,1)S(1)}) custom-call(s32[1]{0:T(128)} %bitcast.lev_ref._, bf16[1024,768]{1,0:T(8,128)(2,1)S(1)} %copy-done, bf16[192,1024]{1,0:T(8,128)(2,1)S(1)} %get-tuple-element.31.innert_ref, ...), custom_call_target="tpu_custom_call" | custom-call | flops 2415919104 | bytes 4718592 | tf_op jit(solution)/shard_map/pallas_call | solution.py:563
  33.9 3.5 %collective-permute-start.13 = (bf16[9,64,256]{2,1,0:T(8,128)(2,1)S(1)}, bf16[9,64,256]{2,1,0:T(8,128)(2,1)S(1)}, u32[]{:S(2)}, u32[]{:S(2)}) collective-permute-start(bf16[9,64,256]{2,1,0:T(8,128)(2,1)S(1)} %get-tuple-element.45.rest_2_), channel_id=1, source_target_pairs={{0,16},{24,8},{1,17},{25,9},{2,18},{26,10},{3,19},{27,11},{4,20},{... | collective-permute-start | bytes 884744 | tf_op jit(solution)/shard_map/ppermute | solution.py:591
  38.1 5.1 %collective-permute-done.11.got_ref.rest_3_ = bf16[9,64,256]{2,1,0:T(8,128)(2,1)S(1)} collective-permute-done((bf16[9,64,256]{2,1,0:T(8,128)(2,1)S(1)}, bf16[9,64,256]{2,1,0:T(8,128)(2,1)S(1)}, u32[]{:S(2)}, u32[]{:S(2)}) %collective-permute-start.11) | collective-permute-done | bytes 294944 | tf_op jit(solution)/shard_map/ppermute | solution.py:589
  43.3 0.8 %collective-permute-start.14 = (bf16[9,64,256]{2,1,0:T(8,128)(2,1)S(1)}, bf16[9,64,256]{2,1,0:T(8,128)(2,1)S(1)}, u32[]{:S(2)}, u32[]{:S(2)}) collective-permute-start(bf16[9,64,256]{2,1,0:T(8,128)(2,1)S(1)} %shard_map.109), channel_id=1, source_target_pairs={{0,8},{8,24},{24,16},{16,0},{1,9},{9,25},{25,17},{17,1},{2,10},{10... | collective-permute-start | bytes 884744 | tf_op jit(solution)/shard_map/ppermute | solution.py:595
  45.4 3.7 %collective-permute-done.6.left_ref.right_ref = bf16[4,64,128]{2,1,0:T(8,128)(2,1)S(1)} collective-permute-done((bf16[4,64,128]{2,1,0:T(8,128)(2,1)S(1)}, bf16[4,64,128]{2,1,0:T(8,128)(2,1)S(1)}, u32[]{:S(2)}, u32[]{:S(2)}) %collective-permute-start.6) | collective-permute-done | bytes 65568 | tf_op jit(solution)/shard_map/ppermute | solution.py:448
  49.3 1.3 %collective-permute-start.7 = (bf16[4,64,128]{2,1,0:T(8,128)(2,1)S(1)}, bf16[4,64,128]{2,1,0:T(8,128)(2,1)S(1)}, u32[]{:S(2)}, u32[]{:S(2)}) collective-permute-start(bf16[4,64,128]{2,1,0:T(8,128)(2,1)S(1)} %get-tuple-element.49), channel_id=1, source_target_pairs={{0,2},{2,4},{4,6},{1,3},{3,5},{5,7},{8,10},{10,12},{12,14},{9,11},... | collective-permute-start | bytes 196616 | tf_op jit(solution)/shard_map/ppermute | solution.py:448
  50.6 1.3 %collective-permute-start.8 = (bf16[4,64,128]{2,1,0:T(8,128)(2,1)S(1)}, bf16[4,64,128]{2,1,0:T(8,128)(2,1)S(1)}, u32[]{:S(2)}, u32[]{:S(2)}) collective-permute-start(bf16[4,64,128]{2,1,0:T(8,128)(2,1)S(1)} %get-tuple-element.50), channel_id=1, source_target_pairs={{2,0},{4,2},{6,4},{3,1},{5,3},{7,5},{10,8},{12,10},{14,12},{11,9},... | collective-permute-start | bytes 196616 | tf_op jit(solution)/shard_map/ppermute | solution.py:448
  51.9 3.5 %collective-permute-done.8.bottom_ref = bf16[4,64,128]{2,1,0:T(8,128)(2,1)S(1)} collective-permute-done((bf16[4,64,128]{2,1,0:T(8,128)(2,1)S(1)}, bf16[4,64,128]{2,1,0:T(8,128)(2,1)S(1)}, u32[]{:S(2)}, u32[]{:S(2)}) %collective-permute-start.8) | collective-permute-done | bytes 65568 | tf_op jit(solution)/shard_map/ppermute | solution.py:448
  55.5 5.8 %collective-permute-done.9.got_ref = bf16[2,3,64,128]{3,2,1,0:T(8,128)(2,1)S(1)} collective-permute-done((bf16[2,3,64,128]{3,2,1,0:T(8,128)(2,1)S(1)}, bf16[2,3,64,128]{3,2,1,0:T(8,128)(2,1)S(1)}, u32[]{:S(2)}, u32[]{:S(2)}) %collective-permute-start.9) | collective-permute-done | bytes 98336 | tf_op jit(solution)/shard_map/ppermute | solution.py:452
  61.3 1.0 %collective-permute-start.10 = (bf16[3,64,128]{2,1,0:T(8,128)(2,1)S(1)}, bf16[3,64,128]{2,1,0:T(8,128)(2,1)S(1)}, u32[]{:S(2)}, u32[]{:S(2)}) collective-permute-start(bf16[3,64,128]{2,1,0:T(8,128)(2,1)S(1)} %get-tuple-element.54), channel_id=1, source_target_pairs={{0,16},{8,24},{16,0},{24,8},{1,17},{9,25},{17,1},{25,9},{2,18},{10... | collective-permute-start | bytes 147464 | tf_op jit(solution)/shard_map/ppermute | solution.py:452
  62.3 5.3 %collective-permute-done.10.rest_1_ = bf16[3,64,128]{2,1,0:T(8,128)(2,1)S(1)} collective-permute-done((bf16[3,64,128]{2,1,0:T(8,128)(2,1)S(1)}, bf16[3,64,128]{2,1,0:T(8,128)(2,1)S(1)}, u32[]{:S(2)}, u32[]{:S(2)}) %collective-permute-start.10) | collective-permute-done | bytes 49184 | tf_op jit(solution)/shard_map/ppermute | solution.py:452
  67.6 2.6 %shard_map.110 = f32[64,32,128]{2,1,0:T(8,128)} custom-call(s32[1]{0:T(128)} %bitcast.lev_ref._, s32[1,256]{1,0:T(1,128)S(1)} %bitcast.20, bf16[64,32,128]{2,1,0:T(8,128)(2,1)S(1)} %get-tuple-element.30.own_ref, bf16[3,64,128]{2,1,0:T(8,128)(2,1)S(1)} %get-tuple-element.53.rest_0_, bf16[3,64,128]{2,1,0:T(8,128)(2,1)S(1)} %collective-permute-done.10.rest_1_, ...), custom_call_target="tpu_custom_call" | custom-call | flops 150994944 | bytes 4194304 | tf_op jit(solution)/shard_map/pallas_call | solution.py:640
  (38 shorter events, 2.6 us)
Async XLA Ops:
  2.3 5.6 %collective-permute-start = (bf16[128,256]{1,0:T(8,128)(2,1)S(1)}, bf16[128,256]{1,0:T(8,128)(2,1)S(1)}, u32[]{:S(2)}, u32[]{:S(2)}) collective-permute-start(bf16[128,256]{1,0:T(8,128)(2,1)S(1)} %get-tuple-element.36), channel_id=1, source_target_pairs={{0,2},{2,4},{4,6},{1,3},{3,5},{5,7},{8,10},{10,12},{12,14},{9,11},... | collective-permute-start | bytes 196616 | tf_op jit(solution)/shard_map/ppermute | solution.py:448
  4.7 5.3 %collective-permute-start.1 = (bf16[128,256]{1,0:T(8,128)(2,1)S(1)}, bf16[128,256]{1,0:T(8,128)(2,1)S(1)}, u32[]{:S(2)}, u32[]{:S(2)}) collective-permute-start(bf16[128,256]{1,0:T(8,128)(2,1)S(1)} %get-tuple-element.37), channel_id=1, source_target_pairs={{2,0},{4,2},{6,4},{3,1},{5,3},{7,5},{10,8},{12,10},{14,12},{11,9},... | collective-permute-start | bytes 196616 | tf_op jit(solution)/shard_map/ppermute | solution.py:448
  6.1 5.6 %copy-start.5 = (s32[1,1,256]{2,1,0:T(1,128)S(1)}, s32[1,1,256]{2,1,0:T(1,128)}, u32[]{:S(2)}) copy-start(s32[1,1,256]{2,1,0:T(1,128)} %param.18) | copy-start | bytes 3076
  7.9 7.1 %copy-start.3 = (bf16[4,128,128]{2,1,0:T(8,128)(2,1)S(1)}, bf16[4,128,128]{2,1,0:T(8,128)(2,1)}, u32[]{:S(2)}) copy-start(bf16[4,128,128]{2,1,0:T(8,128)(2,1)} %mid_ref.3) | copy-start | bytes 393220
  7.9 7.1 %copy-start.4 = (bf16[4,48,128]{2,1,0:T(8,128)(2,1)S(1)}, bf16[4,48,128]{2,1,0:T(8,128)(2,1)}, u32[]{:S(2)}) copy-start(bf16[4,48,128]{2,1,0:T(8,128)(2,1)} %outw_ref.3) | copy-start | bytes 147460
  10.1 4.9 %collective-permute-start.2 = (bf16[2,34,256]{2,1,0:T(8,128)(2,1)S(1)}, bf16[2,34,256]{2,1,0:T(8,128)(2,1)S(1)}, u32[]{:S(2)}, u32[]{:S(2)}) collective-permute-start(bf16[2,34,256]{2,1,0:T(8,128)(2,1)S(1)} %pad_maximum_fusion), channel_id=1, source_target_pairs={{0,1},{1,0},{2,3},{3,2},{4,5},{5,4},{6,7},{7,6},{8,9},{9,8},{10,11... | collective-permute-start | bytes 104456 | tf_op jit(solution)/shard_map/ppermute | solution.py:448
  15.0 8.1 %copy-start.6 = (f32[768]{0:T(1024)S(1)}, f32[768]{0:T(1024)}, u32[]{:S(2)}) copy-start(f32[768]{0:T(1024)} %param.17) | copy-start | bytes 9220
  15.0 8.1 %copy-start = (bf16[1024,768]{1,0:T(8,128)(2,1)S(1)}, bf16[1024,768]{1,0:T(8,128)(2,1)}, u32[]{:S(2)}) copy-start(bf16[1024,768]{1,0:T(8,128)(2,1)} %inner_ref.3) | copy-start | bytes 4718596
  15.0 8.1 %copy-start.1 = (bf16[768,1024]{1,0:T(8,128)(2,1)S(1)}, bf16[768,1024]{1,0:T(8,128)(2,1)}, u32[]{:S(2)}) copy-start(bf16[768,1024]{1,0:T(8,128)(2,1)} %outer_ref.3) | copy-start | bytes 4718596
  15.1 8.1 %copy-start.2 = (f32[1,1,256,768]{3,2,1,0:T(8,128)S(1)}, f32[1,1,256,768]{3,2,1,0:T(8,128)}, u32[]{:S(2)}) copy-start(f32[1,1,256,768]{3,2,1,0:T(8,128)} %param.16) | copy-start | bytes 2359300
  18.0 7.0 %collective-permute-start.5 = (bf16[192,256]{1,0:T(8,128)(2,1)S(1)}, bf16[192,256]{1,0:T(8,128)(2,1)S(1)}, u32[]{:S(2)}, u32[]{:S(2)}) collective-permute-start(bf16[192,256]{1,0:T(8,128)(2,1)S(1)} %get-tuple-element.42.rest_0_), channel_id=1, source_target_pairs={{0,24},{8,16},{16,8},{24,0},{1,25},{9,17},{17,9},{25,1},{2,26},{10... | collective-permute-start | bytes 294920 | tf_op jit(solution)/shard_map/ppermute | solution.py:452
  21.7 8.8 %collective-permute-start.4 = (bf16[192,256]{1,0:T(8,128)(2,1)S(1)}, bf16[192,256]{1,0:T(8,128)(2,1)S(1)}, u32[]{:S(2)}, u32[]{:S(2)}) collective-permute-start(bf16[192,256]{1,0:T(8,128)(2,1)S(1)} %get-tuple-element.42.rest_0_), channel_id=1, source_target_pairs={{0,16},{8,24},{16,0},{24,8},{1,17},{9,25},{17,1},{25,9},{2,18},{10... | collective-permute-start | bytes 294920 | tf_op jit(solution)/shard_map/ppermute | solution.py:452
  21.7 8.8 %collective-permute-start.3 = (bf16[192,256]{1,0:T(8,128)(2,1)S(1)}, bf16[192,256]{1,0:T(8,128)(2,1)S(1)}, u32[]{:S(2)}, u32[]{:S(2)}) collective-permute-start(bf16[192,256]{1,0:T(8,128)(2,1)S(1)} %get-tuple-element.42.rest_0_), channel_id=1, source_target_pairs={{0,8},{8,0},{16,24},{24,16},{1,9},{9,1},{17,25},{25,17},{2,10},{10... | collective-permute-start | bytes 294920 | tf_op jit(solution)/shard_map/ppermute | solution.py:452
  33.8 9.4 %collective-permute-start.11 = (bf16[9,64,256]{2,1,0:T(8,128)(2,1)S(1)}, bf16[9,64,256]{2,1,0:T(8,128)(2,1)S(1)}, u32[]{:S(2)}, u32[]{:S(2)}) collective-permute-start(bf16[9,64,256]{2,1,0:T(8,128)(2,1)S(1)} %get-tuple-element.44.rest_1_), channel_id=1, source_target_pairs={{0,8},{8,0},{16,24},{24,16},{1,9},{9,1},{17,25},{25,17},{2,10},{10... | collective-permute-start | bytes 884744 | tf_op jit(solution)/shard_map/ppermute | solution.py:589
  33.9 33.7 %collective-permute-start.13 = (bf16[9,64,256]{2,1,0:T(8,128)(2,1)S(1)}, bf16[9,64,256]{2,1,0:T(8,128)(2,1)S(1)}, u32[]{:S(2)}, u32[]{:S(2)}) collective-permute-start(bf16[9,64,256]{2,1,0:T(8,128)(2,1)S(1)} %get-tuple-element.45.rest_2_), channel_id=1, source_target_pairs={{0,16},{24,8},{1,17},{25,9},{2,18},{26,10},{3,19},{27,11},{4,20},{... | collective-permute-start | bytes 884744 | tf_op jit(solution)/shard_map/ppermute | solution.py:591
  37.4 30.2 %collective-permute-start.12 = (bf16[9,64,256]{2,1,0:T(8,128)(2,1)S(1)}, bf16[9,64,256]{2,1,0:T(8,128)(2,1)S(1)}, u32[]{:S(2)}, u32[]{:S(2)}) collective-permute-start(bf16[9,64,256]{2,1,0:T(8,128)(2,1)S(1)} %get-tuple-element.45.rest_2_), channel_id=1, source_target_pairs={{8,16},{16,8},{9,17},{17,9},{10,18},{18,10},{11,19},{19,11},{12,20... | collective-permute-start | bytes 884744 | tf_op jit(solution)/shard_map/ppermute | solution.py:590
  43.3 24.3 %collective-permute-start.14 = (bf16[9,64,256]{2,1,0:T(8,128)(2,1)S(1)}, bf16[9,64,256]{2,1,0:T(8,128)(2,1)S(1)}, u32[]{:S(2)}, u32[]{:S(2)}) collective-permute-start(bf16[9,64,256]{2,1,0:T(8,128)(2,1)S(1)} %shard_map.109), channel_id=1, source_target_pairs={{0,8},{8,24},{24,16},{16,0},{1,9},{9,25},{25,17},{17,1},{2,10},{10... | collective-permute-start | bytes 884744 | tf_op jit(solution)/shard_map/ppermute | solution.py:595
  44.8 4.3 %collective-permute-start.6 = (bf16[4,64,128]{2,1,0:T(8,128)(2,1)S(1)}, bf16[4,64,128]{2,1,0:T(8,128)(2,1)S(1)}, u32[]{:S(2)}, u32[]{:S(2)}) collective-permute-start(bf16[4,64,128]{2,1,0:T(8,128)(2,1)S(1)} %get-tuple-element.48), channel_id=1, source_target_pairs={{0,1},{1,0},{2,3},{3,2},{4,5},{5,4},{6,7},{7,6},{8,9},{9,8},{10,11... | collective-permute-start | bytes 196616 | tf_op jit(solution)/shard_map/ppermute | solution.py:448
  49.3 2.6 %collective-permute-start.7 = (bf16[4,64,128]{2,1,0:T(8,128)(2,1)S(1)}, bf16[4,64,128]{2,1,0:T(8,128)(2,1)S(1)}, u32[]{:S(2)}, u32[]{:S(2)}) collective-permute-start(bf16[4,64,128]{2,1,0:T(8,128)(2,1)S(1)} %get-tuple-element.49), channel_id=1, source_target_pairs={{0,2},{2,4},{4,6},{1,3},{3,5},{5,7},{8,10},{10,12},{12,14},{9,11},... | collective-permute-start | bytes 196616 | tf_op jit(solution)/shard_map/ppermute | solution.py:448
  50.6 4.8 %collective-permute-start.8 = (bf16[4,64,128]{2,1,0:T(8,128)(2,1)S(1)}, bf16[4,64,128]{2,1,0:T(8,128)(2,1)S(1)}, u32[]{:S(2)}, u32[]{:S(2)}) collective-permute-start(bf16[4,64,128]{2,1,0:T(8,128)(2,1)S(1)} %get-tuple-element.50), channel_id=1, source_target_pairs={{2,0},{4,2},{6,4},{3,1},{5,3},{7,5},{10,8},{12,10},{14,12},{11,9},... | collective-permute-start | bytes 196616 | tf_op jit(solution)/shard_map/ppermute | solution.py:448
  55.4 5.9 %collective-permute-start.9 = (bf16[2,3,64,128]{3,2,1,0:T(8,128)(2,1)S(1)}, bf16[2,3,64,128]{3,2,1,0:T(8,128)(2,1)S(1)}, u32[]{:S(2)}, u32[]{:S(2)}) collective-permute-start(bf16[2,3,64,128]{3,2,1,0:T(8,128)(2,1)S(1)} %get-tuple-element.52), channel_id=1, source_target_pairs={{0,8},{8,0},{16,24},{24,16},{1,9},{9,1},{17,25},{25,17},{2,10},{10... | collective-permute-start | bytes 294920 | tf_op jit(solution)/shard_map/ppermute | solution.py:452
  61.3 6.3 %collective-permute-start.10 = (bf16[3,64,128]{2,1,0:T(8,128)(2,1)S(1)}, bf16[3,64,128]{2,1,0:T(8,128)(2,1)S(1)}, u32[]{:S(2)}, u32[]{:S(2)}) collective-permute-start(bf16[3,64,128]{2,1,0:T(8,128)(2,1)S(1)} %get-tuple-element.54), channel_id=1, source_target_pairs={{0,16},{8,24},{16,0},{24,8},{1,17},{9,25},{17,1},{25,9},{2,18},{10... | collective-permute-start | bytes 147464 | tf_op jit(solution)/shard_map/ppermute | solution.py:452

commit v7 on v6

--- a/solution.py
+++ b/solution.py
@@ -194,7 +194,11 @@
     halo_ref[2 * cols : 2 * cols + rows + 2, :] = left_ref[1]
     halo_ref[2 * cols + tall : 2 * cols + tall + rows + 2, :] = right_ref[0]
     row, col = split(upright(index_ref), cols)
-    cells = lax.broadcasted_iota(jnp.int32, (slots, width), 1)
+    starts = (0, cols, 2 * cols, width)
+    cells = [
+        lax.broadcasted_iota(jnp.int32, (slots, starts[i + 1] - starts[i]), 1) + starts[i]
+        for i in range(3)
+    ]
     lefts, rights = [], []
     for a in range(3):
         for b in range(3):
@@ -202,8 +206,16 @@
             rim = jnp.where(at_row < 0, at_col, jnp.where(at_row >= rows, cols + at_col, -1))
             rim = jnp.where(at_col < 0, 2 * cols + at_row + 1, rim)
             rim = jnp.where(at_col >= cols, 2 * cols + tall + at_row + 1, rim)
-            rim = jnp.concatenate([rim] * (width // 128), 1)
-            x = x_ref[3 * a + b] + nn(hot(cells == rim), halo_ref[...]).astype(BF16)
+            x = x_ref[3 * a + b]
+            reach = [i for i, near in enumerate((a == 0, a == 2, b != 1)) if near]
+            if reach:
+                picks, found = [], []
+                for i in reach:
+                    wide = jnp.concatenate([rim] * (cells[i].shape[1] // 128), 1)
+                    picks.append(hot(cells[i] == wide))
+                    found.append(halo_ref[starts[i] : starts[i + 1], :])
+                picks, found = jnp.concatenate(picks, 1), jnp.concatenate(found, 0)
+                x = x + nn(picks, found).astype(BF16)
             lefts.append(w_ref[3 * a + b])
             rights.append(x)
     acc = nt(jnp.concatenate(lefts, 1), jnp.concatenate(rights, 1))
@@ -333,21 +345,28 @@
     slots = row.shape[1]
     cells = lax.broadcasted_iota(jnp.int32, (slots, cols), 1)
     lines = lax.broadcasted_iota(jnp.int32, (slots, 128), 1)
-    for k, block in enumerate(blocks):
-        for e, (edge, a) in enumerate(((0, 0), (rows - 1, 2))):
-            acc = None
-            for b in range(3):
-                part = jnp.where(row == edge, block[3 * a + b].astype(F32), 0.0).astype(BF16)
-                part = nn(part, hot(colc + (b - 1) == cells))
-                acc = part if acc is None else acc + part
-            rowout_ref[e, k] = acc.astype(BF16)
-        acc = None
-        for e, (edge, b) in enumerate(((0, 0), (cols - 1, 2))):
-            for a in range(3):
-                part = jnp.where(col == edge, block[3 * a + b].astype(F32), 0.0).astype(BF16)
-                part = nn(part, hot(rowc + (a + 64 * e) == lines))
-                acc = part if acc is None else acc + part
-        colout_ref[k] = acc.astype(BF16)
+    portion = rowout_ref.shape[2]
+    across = jnp.concatenate([hot(colc + (b - 1) == cells) for b in range(3)], 0)
+    down = jnp.concatenate([hot(rowc + (a + 64 * e) == lines) for e in (0, 1) for a in range(3)], 0)
+
+    def take(taps, where):
+        return jnp.concatenate(
+            [
+                jnp.concatenate(
+                    [jnp.where(where[i], block[t].astype(F32), 0.0).astype(BF16) for i, t in enumerate(taps)],
+                    1,
+                )
+                for block in blocks
+            ],
+            0,
+        )
+
+    for e, (edge, a) in enumerate(((0, 0), (rows - 1, 2))):
+        out = nn(take([3 * a + b for b in range(3)], [row == edge] * 3), across)
+        rowout_ref[e] = out.astype(BF16).reshape(len(blocks), portion, cols)
+    taps = [3 * a + b for b in (0, 2) for a in range(3)]
+    out = nn(take(taps, [col == 0] * 3 + [col == cols - 1] * 3), down)
+    colout_ref[...] = out.astype(BF16).reshape(len(blocks), portion, 128)
 
 
 def corner_kernel(rows, cols, rowin_ref, left_ref, right_ref, up_ref, down_ref):

time: 70.7 us -> 69.9 us (0.989)
  no operation moved by 1% of the time
where the time goes in v7:
time: 69.9 us; the launch traced here: 69.6 us
  waiting for transfers between devices  31.2 us (45%)
  starting transfers between devices  18.7 us (27%)
  Pallas kernels  16.9 us (24%)
  local copies, waits for them, and re-layouts  1.89 us (3%)
  between operations  0.95 us (1%)
    ppermute x5, waiting for transfers between devices, paired(): return lax.ppermute(x, 'lev', [(i, i ^ k) for i in range(4)])  16.8 us
    ppermute x6, waiting for transfers between devices, shift(): return lax.ppermute(x, axis, pairs)  9.28 us
    ppermute x6, starting transfers between devices, shift(): return lax.ppermute(x, axis, pairs)  8.49 us
    ppermute x5, starting transfers between devices, paired(): return lax.ppermute(x, 'lev', [(i, i ^ k) for i in range(4)])  5.31 us
    ppermute x1, waiting for transfers between devices, steps(): relayed = lax.ppermute(patches[1], 'lev', [(0, 1), (1, 0), (2, 3), (3, 2)])  5.12 us
    ppermute x1, starting transfers between devices, steps(): parts.append(lax.ppermute(patches[2], 'lev', [(0, 2), (3, 1)]))  3.49 us
    pallas_call x1, Pallas kernels, steps(): call(functools.partial(gather_kernel, rows, cols), jax.ShapeDtypeStruct((...  3.36 us
    pallas_call x1, Pallas kernels, steps(): call(functools.partial(column_kernel, lev_count), (patch_shape,) * lev_co...  3.27 us
  transfers between devices with their start and end apart: 15, of which 7 were waited for; matrix products, arithmetic and copies ran while one was open for 3% of the time, Pallas kernels for 9%

profile of v7, /device:TPU:0, one launch (start us, length us, event | category | flops | bytes accessed | tf_op | source)
XLA Modules:
  0.0 69.6 jit_solution(13365976585758499944)
XLA Ops:
  0.0 2.3 %shard_map.101 = (bf16[4096,256]{1,0:T(8,128)(2,1)S(1)}, bf16[128,256]{1,0:T(8,128)(2,1)S(1)}, bf16[128,256]{1,0:T(8,128)(2,1)S(1)}, bf16[2,32,256]{2,1,0:T(8,128)(2,1)S(1)}) custom-call(s32[1]{0:T(128)} %bitcast.lev_ref._, bf16[256,32,128]{2,1,0:T(8,128)(2,1)} %lat_ref.1), custom_call_target="tpu_custom_call" | custom-call | flops 150994944 | bytes 9043968 | tf_op jit(solution)/shard_map/pallas_call | solution.py:507
  2.3 2.4 %collective-permute-start = (bf16[128,256]{1,0:T(8,128)(2,1)S(1)}, bf16[128,256]{1,0:T(8,128)(2,1)S(1)}, u32[]{:S(2)}, u32[]{:S(2)}) collective-permute-start(bf16[128,256]{1,0:T(8,128)(2,1)S(1)} %get-tuple-element.36), channel_id=1, source_target_pairs={{0,2},{2,4},{4,6},{1,3},{3,5},{5,7},{8,10},{10,12},{12,14},{9,11},... | collective-permute-start | bytes 196616 | tf_op jit(solution)/shard_map/ppermute | solution.py:467
  4.7 1.3 %collective-permute-start.1 = (bf16[128,256]{1,0:T(8,128)(2,1)S(1)}, bf16[128,256]{1,0:T(8,128)(2,1)S(1)}, u32[]{:S(2)}, u32[]{:S(2)}) collective-permute-start(bf16[128,256]{1,0:T(8,128)(2,1)S(1)} %get-tuple-element.37), channel_id=1, source_target_pairs={{2,0},{4,2},{6,4},{3,1},{5,3},{7,5},{10,8},{12,10},{14,12},{11,9},... | collective-permute-start | bytes 196616 | tf_op jit(solution)/shard_map/ppermute | solution.py:467
  6.1 1.8 %copy.11 = bf16[9,4,128,256]{3,2,1,0:T(8,128)(2,1)S(1)} copy(bf16[9,4,128,256]{3,2,0,1:T(8,128)(2,1)} %bitcast.21) | data formatting | bytes 4718592 | tf_op jit(solution)/shard_map/transpose | solution.py:546
  7.9 2.1 %collective-permute-done.1.below_ref = bf16[128,256]{1,0:T(8,128)(2,1)S(1)} collective-permute-done((bf16[128,256]{1,0:T(8,128)(2,1)S(1)}, bf16[128,256]{1,0:T(8,128)(2,1)S(1)}, u32[]{:S(2)}, u32[]{:S(2)}) %collective-permute-start.1) | collective-permute-done | bytes 65568 | tf_op jit(solution)/shard_map/ppermute | solution.py:467
  10.1 1.6 %collective-permute-start.2 = (bf16[2,34,256]{2,1,0:T(8,128)(2,1)S(1)}, bf16[2,34,256]{2,1,0:T(8,128)(2,1)S(1)}, u32[]{:S(2)}, u32[]{:S(2)}) collective-permute-start(bf16[2,34,256]{2,1,0:T(8,128)(2,1)S(1)} %pad_maximum_fusion), channel_id=1, source_target_pairs={{0,1},{1,0},{2,3},{3,2},{4,5},{5,4},{6,7},{7,6},{8,9},{9,8},{10,11... | collective-permute-start | bytes 104456 | tf_op jit(solution)/shard_map/ppermute | solution.py:467
  11.6 3.4 %shard_map.102.x_ref = bf16[9,256,256]{2,1,0:T(8,128)(2,1)S(1)} custom-call(s32[1,256]{1,0:T(1,128)S(1)} %bitcast.16, s32[1,256]{1,0:T(1,128)S(1)} %bitcast.17, bf16[4096,256]{1,0:T(8,128)(2,1)S(1)} %get-tuple-element.35.tile_ref), custom_call_target="tpu_custom_call" | custom-call | flops 603979776 | bytes 4718592 | tf_op jit(solution)/shard_map/pallas_call | solution.py:535
  15.1 2.5 %shard_map.103 = (bf16[512,256]{1,0:T(8,128)(2,1)S(1)}, bf16[512,256]{1,0:T(8,128)(2,1)S(1)}, bf16[192,256]{1,0:T(8,128)(2,1)S(1)}) custom-call(s32[1,256]{1,0:T(1,128)S(1)} %bitcast.18, bf16[9,256,256]{2,1,0:T(8,128)(2,1)S(1)} %shard_map.102.x_ref, bf16[128,256]{1,0:T(8,128)(2,1)S(1)} %collective-permute-done.above_ref, ...), custom_call_target="tpu_custom_call" | custom-call | flops 1207959552 | bytes 2490368 | tf_op jit(solution)/shard_map/pallas_call | solution.py:548
  17.6 3.7 %collective-permute-start.5 = (bf16[192,256]{1,0:T(8,128)(2,1)S(1)}, bf16[192,256]{1,0:T(8,128)(2,1)S(1)}, u32[]{:S(2)}, u32[]{:S(2)}) collective-permute-start(bf16[192,256]{1,0:T(8,128)(2,1)S(1)} %get-tuple-element.42.rest_0_), channel_id=1, source_target_pairs={{0,24},{8,16},{16,8},{24,0},{1,25},{9,17},{17,9},{25,1},{2,26},{10... | collective-permute-start | bytes 294920 | tf_op jit(solution)/shard_map/ppermute | solution.py:471
  21.3 0.8 %collective-permute-start.3 = (bf16[192,256]{1,0:T(8,128)(2,1)S(1)}, bf16[192,256]{1,0:T(8,128)(2,1)S(1)}, u32[]{:S(2)}, u32[]{:S(2)}) collective-permute-start(bf16[192,256]{1,0:T(8,128)(2,1)S(1)} %get-tuple-element.42.rest_0_), channel_id=1, source_target_pairs={{0,8},{8,0},{16,24},{24,16},{1,9},{9,1},{17,25},{25,17},{2,10},{10... | collective-permute-start | bytes 294920 | tf_op jit(solution)/shard_map/ppermute | solution.py:471
  22.8 1.8 %shard_map.100 = (f32[768,256]{1,0:T(8,128)S(1)}, f32[768,256]{1,0:T(8,128)S(1)}, bf16[192,1024]{1,0:T(8,128)(2,1)S(1)}, bf16[1024,768]{1,0:T(8,128)(2,1)S(1)}, ...) custom-call(s32[1]{0:T(128)} %bitcast.lev_ref._, s32[1,1]{1,0:T(1,128)S(6)} %copy.12.count_ref, ...), custom_call_target="tpu_custom_call" | custom-call | flops 603979776 | bytes 25690112 | tf_op jit(solution)/shard_map/pallas_call | solution.py:561
  24.6 5.5 %collective-permute-done.4.rest_2_ = bf16[192,256]{1,0:T(8,128)(2,1)S(1)} collective-permute-done((bf16[192,256]{1,0:T(8,128)(2,1)S(1)}, bf16[192,256]{1,0:T(8,128)(2,1)S(1)}, u32[]{:S(2)}, u32[]{:S(2)}) %collective-permute-start.4) | collective-permute-done | bytes 98336 | tf_op jit(solution)/shard_map/ppermute | solution.py:471
  30.1 3.3 %shard_map.104 = (bf16[9,64,256]{2,1,0:T(8,128)(2,1)S(1)}, bf16[9,64,256]{2,1,0:T(8,128)(2,1)S(1)}, bf16[9,64,256]{2,1,0:T(8,128)(2,1)S(1)}, bf16[9,64,256]{2,1,0:T(8,128)(2,1)S(1)}) custom-call(s32[1]{0:T(128)} %bitcast.lev_ref._, bf16[1024,768]{1,0:T(8,128)(2,1)S(1)} %copy-done, bf16[192,1024]{1,0:T(8,128)(2,1)S(1)} %get-tuple-element.31.innert_ref, ...), custom_call_target="tpu_custom_call" | custom-call | flops 2415919104 | bytes 4718592 | tf_op jit(solution)/shard_map/pallas_call | solution.py:582
  33.4 3.5 %collective-permute-start.13 = (bf16[9,64,256]{2,1,0:T(8,128)(2,1)S(1)}, bf16[9,64,256]{2,1,0:T(8,128)(2,1)S(1)}, u32[]{:S(2)}, u32[]{:S(2)}) collective-permute-start(bf16[9,64,256]{2,1,0:T(8,128)(2,1)S(1)} %get-tuple-element.45.rest_2_), channel_id=1, source_target_pairs={{0,16},{24,8},{1,17},{25,9},{2,18},{26,10},{3,19},{27,11},{4,20},{... | collective-permute-start | bytes 884744 | tf_op jit(solution)/shard_map/ppermute | solution.py:610
  36.9 0.7 collective-permute-start.12
  37.6 5.1 %collective-permute-done.11.got_ref.rest_3_ = bf16[9,64,256]{2,1,0:T(8,128)(2,1)S(1)} collective-permute-done((bf16[9,64,256]{2,1,0:T(8,128)(2,1)S(1)}, bf16[9,64,256]{2,1,0:T(8,128)(2,1)S(1)}, u32[]{:S(2)}, u32[]{:S(2)}) %collective-permute-start.11) | collective-permute-done | bytes 294944 | tf_op jit(solution)/shard_map/ppermute | solution.py:608
  44.8 3.7 %collective-permute-done.6.left_ref.right_ref = bf16[4,64,128]{2,1,0:T(8,128)(2,1)S(1)} collective-permute-done((bf16[4,64,128]{2,1,0:T(8,128)(2,1)S(1)}, bf16[4,64,128]{2,1,0:T(8,128)(2,1)S(1)}, u32[]{:S(2)}, u32[]{:S(2)}) %collective-permute-start.6) | collective-permute-done | bytes 65568 | tf_op jit(solution)/shard_map/ppermute | solution.py:467
  48.6 1.3 %collective-permute-start.7 = (bf16[4,64,128]{2,1,0:T(8,128)(2,1)S(1)}, bf16[4,64,128]{2,1,0:T(8,128)(2,1)S(1)}, u32[]{:S(2)}, u32[]{:S(2)}) collective-permute-start(bf16[4,64,128]{2,1,0:T(8,128)(2,1)S(1)} %get-tuple-element.49), channel_id=1, source_target_pairs={{0,2},{2,4},{4,6},{1,3},{3,5},{5,7},{8,10},{10,12},{12,14},{9,11},... | collective-permute-start | bytes 196616 | tf_op jit(solution)/shard_map/ppermute | solution.py:467
  49.9 1.3 %collective-permute-start.8 = (bf16[4,64,128]{2,1,0:T(8,128)(2,1)S(1)}, bf16[4,64,128]{2,1,0:T(8,128)(2,1)S(1)}, u32[]{:S(2)}, u32[]{:S(2)}) collective-permute-start(bf16[4,64,128]{2,1,0:T(8,128)(2,1)S(1)} %get-tuple-element.50), channel_id=1, source_target_pairs={{2,0},{4,2},{6,4},{3,1},{5,3},{7,5},{10,8},{12,10},{14,12},{11,9},... | collective-permute-start | bytes 196616 | tf_op jit(solution)/shard_map/ppermute | solution.py:467
  51.2 3.5 %collective-permute-done.8.bottom_ref = bf16[4,64,128]{2,1,0:T(8,128)(2,1)S(1)} collective-permute-done((bf16[4,64,128]{2,1,0:T(8,128)(2,1)S(1)}, bf16[4,64,128]{2,1,0:T(8,128)(2,1)S(1)}, u32[]{:S(2)}, u32[]{:S(2)}) %collective-permute-start.8) | collective-permute-done | bytes 65568 | tf_op jit(solution)/shard_map/ppermute | solution.py:467
  54.8 6.2 %collective-permute-done.9.got_ref = bf16[2,3,64,128]{3,2,1,0:T(8,128)(2,1)S(1)} collective-permute-done((bf16[2,3,64,128]{3,2,1,0:T(8,128)(2,1)S(1)}, bf16[2,3,64,128]{3,2,1,0:T(8,128)(2,1)S(1)}, u32[]{:S(2)}, u32[]{:S(2)}) %collective-permute-start.9) | collective-permute-done | bytes 98336 | tf_op jit(solution)/shard_map/ppermute | solution.py:471
  61.0 0.8 %collective-permute-start.10 = (bf16[3,64,128]{2,1,0:T(8,128)(2,1)S(1)}, bf16[3,64,128]{2,1,0:T(8,128)(2,1)S(1)}, u32[]{:S(2)}, u32[]{:S(2)}) collective-permute-start(bf16[3,64,128]{2,1,0:T(8,128)(2,1)S(1)} %get-tuple-element.54), channel_id=1, source_target_pairs={{0,16},{8,24},{16,0},{24,8},{1,17},{9,25},{17,1},{25,9},{2,18},{10... | collective-permute-start | bytes 147464 | tf_op jit(solution)/shard_map/ppermute | solution.py:471
  61.8 5.1 %collective-permute-done.10.rest_1_ = bf16[3,64,128]{2,1,0:T(8,128)(2,1)S(1)} collective-permute-done((bf16[3,64,128]{2,1,0:T(8,128)(2,1)S(1)}, bf16[3,64,128]{2,1,0:T(8,128)(2,1)S(1)}, u32[]{:S(2)}, u32[]{:S(2)}) %collective-permute-start.10) | collective-permute-done | bytes 49184 | tf_op jit(solution)/shard_map/ppermute | solution.py:471
  67.0 2.6 %shard_map.110 = f32[64,32,128]{2,1,0:T(8,128)} custom-call(s32[1]{0:T(128)} %bitcast.lev_ref._, s32[1,256]{1,0:T(1,128)S(1)} %bitcast.20, bf16[64,32,128]{2,1,0:T(8,128)(2,1)S(1)} %get-tuple-element.30.own_ref, bf16[3,64,128]{2,1,0:T(8,128)(2,1)S(1)} %get-tuple-element.53.rest_0_, bf16[3,64,128]{2,1,0:T(8,128)(2,1)S(1)} %collective-permute-done.10.rest_1_, ...), custom_call_target="tpu_custom_call" | custom-call | flops 150994944 | bytes 4194304 | tf_op jit(solution)/shard_map/pallas_call | solution.py:659
  (38 shorter events, 2.5 us)
Async XLA Ops:
  2.3 5.6 %collective-permute-start = (bf16[128,256]{1,0:T(8,128)(2,1)S(1)}, bf16[128,256]{1,0:T(8,128)(2,1)S(1)}, u32[]{:S(2)}, u32[]{:S(2)}) collective-permute-start(bf16[128,256]{1,0:T(8,128)(2,1)S(1)} %get-tuple-element.36), channel_id=1, source_target_pairs={{0,2},{2,4},{4,6},{1,3},{3,5},{5,7},{8,10},{10,12},{12,14},{9,11},... | collective-permute-start | bytes 196616 | tf_op jit(solution)/shard_map/ppermute | solution.py:467
  4.7 5.3 %collective-permute-start.1 = (bf16[128,256]{1,0:T(8,128)(2,1)S(1)}, bf16[128,256]{1,0:T(8,128)(2,1)S(1)}, u32[]{:S(2)}, u32[]{:S(2)}) collective-permute-start(bf16[128,256]{1,0:T(8,128)(2,1)S(1)} %get-tuple-element.37), channel_id=1, source_target_pairs={{2,0},{4,2},{6,4},{3,1},{5,3},{7,5},{10,8},{12,10},{14,12},{11,9},... | collective-permute-start | bytes 196616 | tf_op jit(solution)/shard_map/ppermute | solution.py:467
  6.1 5.6 %copy-start.5 = (s32[1,1,256]{2,1,0:T(1,128)S(1)}, s32[1,1,256]{2,1,0:T(1,128)}, u32[]{:S(2)}) copy-start(s32[1,1,256]{2,1,0:T(1,128)} %param.18) | copy-start | bytes 3076
  7.9 7.1 %copy-start.3 = (bf16[4,128,128]{2,1,0:T(8,128)(2,1)S(1)}, bf16[4,128,128]{2,1,0:T(8,128)(2,1)}, u32[]{:S(2)}) copy-start(bf16[4,128,128]{2,1,0:T(8,128)(2,1)} %mid_ref.3) | copy-start | bytes 393220
  7.9 7.1 %copy-start.4 = (bf16[4,48,128]{2,1,0:T(8,128)(2,1)S(1)}, bf16[4,48,128]{2,1,0:T(8,128)(2,1)}, u32[]{:S(2)}) copy-start(bf16[4,48,128]{2,1,0:T(8,128)(2,1)} %outw_ref.3) | copy-start | bytes 147460
  10.1 4.9 %collective-permute-start.2 = (bf16[2,34,256]{2,1,0:T(8,128)(2,1)S(1)}, bf16[2,34,256]{2,1,0:T(8,128)(2,1)S(1)}, u32[]{:S(2)}, u32[]{:S(2)}) collective-permute-start(bf16[2,34,256]{2,1,0:T(8,128)(2,1)S(1)} %pad_maximum_fusion), channel_id=1, source_target_pairs={{0,1},{1,0},{2,3},{3,2},{4,5},{5,4},{6,7},{7,6},{8,9},{9,8},{10,11... | collective-permute-start | bytes 104456 | tf_op jit(solution)/shard_map/ppermute | solution.py:467
  15.0 7.7 %copy-start.6 = (f32[768]{0:T(1024)S(1)}, f32[768]{0:T(1024)}, u32[]{:S(2)}) copy-start(f32[768]{0:T(1024)} %param.17) | copy-start | bytes 9220
  15.0 7.7 %copy-start = (bf16[1024,768]{1,0:T(8,128)(2,1)S(1)}, bf16[1024,768]{1,0:T(8,128)(2,1)}, u32[]{:S(2)}) copy-start(bf16[1024,768]{1,0:T(8,128)(2,1)} %inner_ref.3) | copy-start | bytes 4718596
  15.0 7.7 %copy-start.1 = (bf16[768,1024]{1,0:T(8,128)(2,1)S(1)}, bf16[768,1024]{1,0:T(8,128)(2,1)}, u32[]{:S(2)}) copy-start(bf16[768,1024]{1,0:T(8,128)(2,1)} %outer_ref.3) | copy-start | bytes 4718596
  15.1 7.7 %copy-start.2 = (f32[1,1,256,768]{3,2,1,0:T(8,128)S(1)}, f32[1,1,256,768]{3,2,1,0:T(8,128)}, u32[]{:S(2)}) copy-start(f32[1,1,256,768]{3,2,1,0:T(8,128)} %param.16) | copy-start | bytes 2359300
  17.6 7.0 %collective-permute-start.5 = (bf16[192,256]{1,0:T(8,128)(2,1)S(1)}, bf16[192,256]{1,0:T(8,128)(2,1)S(1)}, u32[]{:S(2)}, u32[]{:S(2)}) collective-permute-start(bf16[192,256]{1,0:T(8,128)(2,1)S(1)} %get-tuple-element.42.rest_0_), channel_id=1, source_target_pairs={{0,24},{8,16},{16,8},{24,0},{1,25},{9,17},{17,9},{25,1},{2,26},{10... | collective-permute-start | bytes 294920 | tf_op jit(solution)/shard_map/ppermute | solution.py:471
  21.3 8.8 %collective-permute-start.4 = (bf16[192,256]{1,0:T(8,128)(2,1)S(1)}, bf16[192,256]{1,0:T(8,128)(2,1)S(1)}, u32[]{:S(2)}, u32[]{:S(2)}) collective-permute-start(bf16[192,256]{1,0:T(8,128)(2,1)S(1)} %get-tuple-element.42.rest_0_), channel_id=1, source_target_pairs={{0,16},{8,24},{16,0},{24,8},{1,17},{9,25},{17,1},{25,9},{2,18},{10... | collective-permute-start | bytes 294920 | tf_op jit(solution)/shard_map/ppermute | solution.py:471
  21.3 8.8 %collective-permute-start.3 = (bf16[192,256]{1,0:T(8,128)(2,1)S(1)}, bf16[192,256]{1,0:T(8,128)(2,1)S(1)}, u32[]{:S(2)}, u32[]{:S(2)}) collective-permute-start(bf16[192,256]{1,0:T(8,128)(2,1)S(1)} %get-tuple-element.42.rest_0_), channel_id=1, source_target_pairs={{0,8},{8,0},{16,24},{24,16},{1,9},{9,1},{17,25},{25,17},{2,10},{10... | collective-permute-start | bytes 294920 | tf_op jit(solution)/shard_map/ppermute | solution.py:471
  33.4 9.4 %collective-permute-start.11 = (bf16[9,64,256]{2,1,0:T(8,128)(2,1)S(1)}, bf16[9,64,256]{2,1,0:T(8,128)(2,1)S(1)}, u32[]{:S(2)}, u32[]{:S(2)}) collective-permute-start(bf16[9,64,256]{2,1,0:T(8,128)(2,1)S(1)} %get-tuple-element.44.rest_1_), channel_id=1, source_target_pairs={{0,8},{8,0},{16,24},{24,16},{1,9},{9,1},{17,25},{25,17},{2,10},{10... | collective-permute-start | bytes 884744 | tf_op jit(solution)/shard_map/ppermute | solution.py:608
  33.4 33.5 %collective-permute-start.13 = (bf16[9,64,256]{2,1,0:T(8,128)(2,1)S(1)}, bf16[9,64,256]{2,1,0:T(8,128)(2,1)S(1)}, u32[]{:S(2)}, u32[]{:S(2)}) collective-permute-start(bf16[9,64,256]{2,1,0:T(8,128)(2,1)S(1)} %get-tuple-element.45.rest_2_), channel_id=1, source_target_pairs={{0,16},{24,8},{1,17},{25,9},{2,18},{26,10},{3,19},{27,11},{4,20},{... | collective-permute-start | bytes 884744 | tf_op jit(solution)/shard_map/ppermute | solution.py:610
  36.9 30.0 %collective-permute-start.12 = (bf16[9,64,256]{2,1,0:T(8,128)(2,1)S(1)}, bf16[9,64,256]{2,1,0:T(8,128)(2,1)S(1)}, u32[]{:S(2)}, u32[]{:S(2)}) collective-permute-start(bf16[9,64,256]{2,1,0:T(8,128)(2,1)S(1)} %get-tuple-element.45.rest_2_), channel_id=1, source_target_pairs={{8,16},{16,8},{9,17},{17,9},{10,18},{18,10},{11,19},{19,11},{12,20... | collective-permute-start | bytes 884744 | tf_op jit(solution)/shard_map/ppermute | solution.py:609
  42.8 24.1 %collective-permute-start.14 = (bf16[9,64,256]{2,1,0:T(8,128)(2,1)S(1)}, bf16[9,64,256]{2,1,0:T(8,128)(2,1)S(1)}, u32[]{:S(2)}, u32[]{:S(2)}) collective-permute-start(bf16[9,64,256]{2,1,0:T(8,128)(2,1)S(1)} %shard_map.109), channel_id=1, source_target_pairs={{0,8},{8,24},{24,16},{16,0},{1,9},{9,25},{25,17},{17,1},{2,10},{10... | collective-permute-start | bytes 884744 | tf_op jit(solution)/shard_map/ppermute | solution.py:614
  44.1 4.3 %collective-permute-start.6 = (bf16[4,64,128]{2,1,0:T(8,128)(2,1)S(1)}, bf16[4,64,128]{2,1,0:T(8,128)(2,1)S(1)}, u32[]{:S(2)}, u32[]{:S(2)}) collective-permute-start(bf16[4,64,128]{2,1,0:T(8,128)(2,1)S(1)} %get-tuple-element.48), channel_id=1, source_target_pairs={{0,1},{1,0},{2,3},{3,2},{4,5},{5,4},{6,7},{7,6},{8,9},{9,8},{10,11... | collective-permute-start | bytes 196616 | tf_op jit(solution)/shard_map/ppermute | solution.py:467
  48.6 2.6 %collective-permute-start.7 = (bf16[4,64,128]{2,1,0:T(8,128)(2,1)S(1)}, bf16[4,64,128]{2,1,0:T(8,128)(2,1)S(1)}, u32[]{:S(2)}, u32[]{:S(2)}) collective-permute-start(bf16[4,64,128]{2,1,0:T(8,128)(2,1)S(1)} %get-tuple-element.49), channel_id=1, source_target_pairs={{0,2},{2,4},{4,6},{1,3},{3,5},{5,7},{8,10},{10,12},{12,14},{9,11},... | collective-permute-start | bytes 196616 | tf_op jit(solution)/shard_map/ppermute | solution.py:467
  49.9 4.8 %collective-permute-start.8 = (bf16[4,64,128]{2,1,0:T(8,128)(2,1)S(1)}, bf16[4,64,128]{2,1,0:T(8,128)(2,1)S(1)}, u32[]{:S(2)}, u32[]{:S(2)}) collective-permute-start(bf16[4,64,128]{2,1,0:T(8,128)(2,1)S(1)} %get-tuple-element.50), channel_id=1, source_target_pairs={{2,0},{4,2},{6,4},{3,1},{5,3},{7,5},{10,8},{12,10},{14,12},{11,9},... | collective-permute-start | bytes 196616 | tf_op jit(solution)/shard_map/ppermute | solution.py:467
  54.8 6.2 %collective-permute-start.9 = (bf16[2,3,64,128]{3,2,1,0:T(8,128)(2,1)S(1)}, bf16[2,3,64,128]{3,2,1,0:T(8,128)(2,1)S(1)}, u32[]{:S(2)}, u32[]{:S(2)}) collective-permute-start(bf16[2,3,64,128]{3,2,1,0:T(8,128)(2,1)S(1)} %get-tuple-element.52), channel_id=1, source_target_pairs={{0,8},{8,0},{16,24},{24,16},{1,9},{9,1},{17,25},{25,17},{2,10},{10... | collective-permute-start | bytes 294920 | tf_op jit(solution)/shard_map/ppermute | solution.py:471
  61.0 5.9 %collective-permute-start.10 = (bf16[3,64,128]{2,1,0:T(8,128)(2,1)S(1)}, bf16[3,64,128]{2,1,0:T(8,128)(2,1)S(1)}, u32[]{:S(2)}, u32[]{:S(2)}) collective-permute-start(bf16[3,64,128]{2,1,0:T(8,128)(2,1)S(1)} %get-tuple-element.54), channel_id=1, source_target_pairs={{0,16},{8,24},{16,0},{24,8},{1,17},{9,25},{17,1},{25,9},{2,18},{10... | collective-permute-start | bytes 147464 | tf_op jit(solution)/shard_map/ppermute | solution.py:471

commit v8 on v7

--- a/solution.py
+++ b/solution.py
@@ -96,7 +96,7 @@
     )
 
 
-STEP = 8
+STEP = 16
 
 VM = pl.BlockSpec(memory_space=pltpu.VMEM)
 SM = pl.BlockSpec(memory_space=pltpu.SMEM)
@@ -234,6 +234,7 @@
 def prepare_kernel(
     lev_ref,
     count_ref,
+    index_ref,
     latent_ref,
     obs_ref,
     weight_ref,
@@ -246,10 +247,20 @@
     outert_ref,
     wt_ref,
     own_ref,
+    across_ref,
+    down_ref,
     turn_ref,
     sem,
 ):
-    portion = own_ref.shape[0]
+    portion, _, cols = own_ref.shape
+    rowc, colc = split(upright(index_ref), cols)
+    count = index_ref.shape[1]
+    cells = lax.broadcasted_iota(jnp.int32, (count, cols), 1)
+    lines = lax.broadcasted_iota(jnp.int32, (count, 128), 1)
+    for b in range(3):
+        across_ref[b * count : (b + 1) * count, :] = hot(colc + (b - 1) == cells)
+    for i, (e, a) in enumerate((e, a) for e in (0, 1) for a in range(3)):
+        down_ref[i * count : (i + 1) * count, :] = hot(rowc + (a + 64 * e) == lines)
     fetch = pltpu.make_async_copy(
         latent_ref.at[pl.ds(pl.multiple_of(lev_ref[0] * portion, 8), portion)], own_ref, sem
     )
@@ -338,16 +349,10 @@
         outs[k][...] = nn(left, grad_one).astype(BF16).reshape(taps, portion, -1)
 
 
-def edge_kernel(rows, cols, index_ref, *rest):
+def edge_kernel(rows, cols, index_ref, across_ref, down_ref, *rest):
     blocks, (rowout_ref, colout_ref) = rest[:-2], rest[-2:]
     row, col = split(index_ref[...], cols)
-    rowc, colc = split(upright(index_ref), cols)
-    slots = row.shape[1]
-    cells = lax.broadcasted_iota(jnp.int32, (slots, cols), 1)
-    lines = lax.broadcasted_iota(jnp.int32, (slots, 128), 1)
     portion = rowout_ref.shape[2]
-    across = jnp.concatenate([hot(colc + (b - 1) == cells) for b in range(3)], 0)
-    down = jnp.concatenate([hot(rowc + (a + 64 * e) == lines) for e in (0, 1) for a in range(3)], 0)
 
     def take(taps, where):
         return jnp.concatenate(
@@ -362,10 +367,10 @@
         )
 
     for e, (edge, a) in enumerate(((0, 0), (rows - 1, 2))):
-        out = nn(take([3 * a + b for b in range(3)], [row == edge] * 3), across)
+        out = nn(take([3 * a + b for b in range(3)], [row == edge] * 3), across_ref[...])
         rowout_ref[e] = out.astype(BF16).reshape(len(blocks), portion, cols)
     taps = [3 * a + b for b in (0, 2) for a in range(3)]
-    out = nn(take(taps, [col == 0] * 3 + [col == cols - 1] * 3), down)
+    out = nn(take(taps, [col == 0] * 3 + [col == cols - 1] * 3), down_ref[...])
     colout_ref[...] = out.astype(BF16).reshape(len(blocks), portion, 128)
 
 
@@ -403,23 +408,21 @@
     out_ref[...] = (block_ref[...].astype(F32) + got_ref[...].astype(F32) * keep).astype(BF16)
 
 
-def final_kernel(rows, cols, count, edges, lev_ref, index_ref, own_ref, *rest):
+def final_kernel(rows, cols, count, edges, lev_ref, index_ref, own_ref, across_ref, *rest):
     rims, own, relayed = rest[:edges], rest[edges], rest[edges + 1]
     parts = rest[edges + 2 : -5]
     out_ref, sum_ref, edge_ref, wait_ref, sems = rest[-5:]
     portion = out_ref.shape[0]
     row, _ = split(index_ref[...], cols)
-    _, colc = split(upright(index_ref), cols)
     slots = row.shape[1]
     total = rims[0][...].astype(F32)
     for block in rims[1:]:
         total = total + block[...].astype(F32)
     edge_ref[...] = total
-    cells = lax.broadcasted_iota(jnp.int32, (slots, cols), 1)
     lane = lax.broadcasted_iota(jnp.int32, (128, cols), 0)
     spot = lax.broadcasted_iota(jnp.int32, (128, cols), 1)
     ends = hot(((lane < 64) & (spot == cols - 1)) | ((lane >= 64) & (spot == 0)))
-    hots = jnp.concatenate([hot(colc + (b - 1) == cells) for b in range(3)] + [ends], 0)
+    hots = jnp.concatenate([across_ref[...], ends], 0)
     lines = lax.broadcasted_iota(jnp.int32, (rows, slots), 0)
     masks = [row + (a - 1) == lines for a in range(3)]
     place_of = lax.broadcasted_iota(jnp.int32, (rows, 128), 1)
@@ -567,16 +570,18 @@
             jax.ShapeDtypeStruct((outer.shape[1], outer.shape[0]), BF16),
             jax.ShapeDtypeStruct((taps, chans, wide), BF16),
             jax.ShapeDtypeStruct((portion, rows, cols), BF16),
+            jax.ShapeDtypeStruct((3 * slots, cols), BF16),
+            jax.ShapeDtypeStruct((6 * slots, 128), BF16),
         ),
-        [SM, SM, HBM] + [VM] * 5,
+        [SM, SM, VM, HBM] + [VM] * 5,
         flops,
         24,
         scratch_shapes=[
             pltpu.VMEM((inner.shape[1], inner.shape[0]), BF16),
             pltpu.SemaphoreType.DMA,
         ],
-    )(lev, obs_count, far, obs_values[0, 0], obs_weight[None, :], inner, outer, w)
-    obs_turned, scale, inner_turned, outer_turned, w_turned, mine = turned
+    )(lev, obs_count, index, far, obs_values[0, 0], obs_weight[None, :], inner, outer, w)
+    obs_turned, scale, inner_turned, outer_turned, w_turned, mine, across, down = turned
 
     patch_shape = jax.ShapeDtypeStruct((taps, portion, slots), BF16)
     patches = call(
@@ -623,10 +628,10 @@
     row_edge, col_edge = call(
         functools.partial(edge_kernel, rows, cols),
         (jax.ShapeDtypeStruct((2, lev_count, portion, cols), BF16), side_shape),
-        [VM] * (1 + lev_count),
+        [VM] * (3 + lev_count),
         flops // 8,
         12,
-    )(index, *patches)
+    )(index, across, down, *patches)
     from_left, from_right = from_sides(col_edge, "lon")
     up, down = call(
         functools.partial(corner_kernel, rows, cols),
@@ -659,7 +664,7 @@
     return call(
         functools.partial(final_kernel, rows, cols, lev_count, len(rims)),
         jax.ShapeDtypeStruct((portion, rows, cols), F32),
-        [SM, VM, VM] + [VM] * (2 + len(parts) + len(rims)),
+        [SM, VM, VM, VM] + [VM] * (2 + len(parts) + len(rims)),
         flops // 4,
         16,
         scratch_shapes=[
@@ -669,7 +674,7 @@
             pltpu.SemaphoreType.DMA((portion // STEP,)),
         ],
         out_specs=HBM,
-    )(lev, index, mine, *rims, patches[0], relayed, *parts)
+    )(lev, index, mine, across, *rims, patches[0], relayed, *parts)
 
 
 def solution(mesh):

time: 69.9 us -> 69.4 us (level)
  no operation moved by 1% of the time
where the time goes in v8:
time: 69.4 us; the launch traced here: 69.1 us
  waiting for transfers between devices  31.2 us (45%)
  starting transfers between devices  18.6 us (27%)
  Pallas kernels  16.5 us (24%)
  local copies, waits for them, and re-layouts  1.89 us (3%)
  between operations  0.95 us (1%)
    ppermute x5, waiting for transfers between devices, paired(): return lax.ppermute(x, 'lev', [(i, i ^ k) for i in range(4)])  16.8 us
    ppermute x6, waiting for transfers between devices, shift(): return lax.ppermute(x, axis, pairs)  9.28 us
    ppermute x6, starting transfers between devices, shift(): return lax.ppermute(x, axis, pairs)  8.48 us
    ppermute x5, starting transfers between devices, paired(): return lax.ppermute(x, 'lev', [(i, i ^ k) for i in range(4)])  5.21 us
    ppermute x1, waiting for transfers between devices, steps(): relayed = lax.ppermute(patches[1], 'lev', [(0, 1), (1, 0), (2, 3), (3, 2)])  5.12 us
    ppermute x1, starting transfers between devices, steps(): parts.append(lax.ppermute(patches[2], 'lev', [(0, 2), (3, 1)]))  3.5 us
    pallas_call x1, Pallas kernels, steps(): call(functools.partial(gather_kernel, rows, cols), jax.ShapeDtypeStruct((...  3.36 us
    pallas_call x1, Pallas kernels, steps(): call(functools.partial(column_kernel, lev_count), (patch_shape,) * lev_co...  3.26 us
  transfers between devices with their start and end apart: 15, of which 7 were waited for; matrix products, arithmetic and copies ran while one was open for 3% of the time, Pallas kernels for 9%

profile of v8, /device:TPU:0, one launch (start us, length us, event | category | flops | bytes accessed | tf_op | source)
XLA Modules:
  0.0 69.1 jit_solution(7409707964321881476)
XLA Ops:
  0.0 2.3 %shard_map.101 = (bf16[4096,256]{1,0:T(8,128)(2,1)S(1)}, bf16[128,256]{1,0:T(8,128)(2,1)S(1)}, bf16[128,256]{1,0:T(8,128)(2,1)S(1)}, bf16[2,32,256]{2,1,0:T(8,128)(2,1)S(1)}) custom-call(s32[1]{0:T(128)} %bitcast.lev_ref._, bf16[256,32,128]{2,1,0:T(8,128)(2,1)} %lat_ref.1), custom_call_target="tpu_custom_call" | custom-call | flops 150994944 | bytes 9043968 | tf_op jit(solution)/shard_map/pallas_call | solution.py:510
  2.3 2.4 %collective-permute-start = (bf16[128,256]{1,0:T(8,128)(2,1)S(1)}, bf16[128,256]{1,0:T(8,128)(2,1)S(1)}, u32[]{:S(2)}, u32[]{:S(2)}) collective-permute-start(bf16[128,256]{1,0:T(8,128)(2,1)S(1)} %get-tuple-element.40), channel_id=1, source_target_pairs={{0,2},{2,4},{4,6},{1,3},{3,5},{5,7},{8,10},{10,12},{12,14},{9,11},... | collective-permute-start | bytes 196616 | tf_op jit(solution)/shard_map/ppermute | solution.py:470
  4.7 1.3 %collective-permute-start.1 = (bf16[128,256]{1,0:T(8,128)(2,1)S(1)}, bf16[128,256]{1,0:T(8,128)(2,1)S(1)}, u32[]{:S(2)}, u32[]{:S(2)}) collective-permute-start(bf16[128,256]{1,0:T(8,128)(2,1)S(1)} %get-tuple-element.41), channel_id=1, source_target_pairs={{2,0},{4,2},{6,4},{3,1},{5,3},{7,5},{10,8},{12,10},{14,12},{11,9},... | collective-permute-start | bytes 196616 | tf_op jit(solution)/shard_map/ppermute | solution.py:470
  6.1 1.8 %copy.11 = bf16[9,4,128,256]{3,2,1,0:T(8,128)(2,1)S(1)} copy(bf16[9,4,128,256]{3,2,0,1:T(8,128)(2,1)} %bitcast.22) | data formatting | bytes 4718592 | tf_op jit(solution)/shard_map/transpose | solution.py:549
  7.9 2.1 %collective-permute-done.1.below_ref = bf16[128,256]{1,0:T(8,128)(2,1)S(1)} collective-permute-done((bf16[128,256]{1,0:T(8,128)(2,1)S(1)}, bf16[128,256]{1,0:T(8,128)(2,1)S(1)}, u32[]{:S(2)}, u32[]{:S(2)}) %collective-permute-start.1) | collective-permute-done | bytes 65568 | tf_op jit(solution)/shard_map/ppermute | solution.py:470
  10.1 1.6 %collective-permute-start.2 = (bf16[2,34,256]{2,1,0:T(8,128)(2,1)S(1)}, bf16[2,34,256]{2,1,0:T(8,128)(2,1)S(1)}, u32[]{:S(2)}, u32[]{:S(2)}) collective-permute-start(bf16[2,34,256]{2,1,0:T(8,128)(2,1)S(1)} %pad_maximum_fusion), channel_id=1, source_target_pairs={{0,1},{1,0},{2,3},{3,2},{4,5},{5,4},{6,7},{7,6},{8,9},{9,8},{10,11... | collective-permute-start | bytes 104456 | tf_op jit(solution)/shard_map/ppermute | solution.py:470
  11.6 3.4 %shard_map.102.x_ref = bf16[9,256,256]{2,1,0:T(8,128)(2,1)S(1)} custom-call(s32[1,256]{1,0:T(1,128)S(1)} %bitcast.16, s32[1,256]{1,0:T(1,128)S(1)} %bitcast.17, bf16[4096,256]{1,0:T(8,128)(2,1)S(1)} %get-tuple-element.39.tile_ref), custom_call_target="tpu_custom_call" | custom-call | flops 603979776 | bytes 4718592 | tf_op jit(solution)/shard_map/pallas_call | solution.py:538
  15.1 2.5 %shard_map.103 = (bf16[512,256]{1,0:T(8,128)(2,1)S(1)}, bf16[512,256]{1,0:T(8,128)(2,1)S(1)}, bf16[192,256]{1,0:T(8,128)(2,1)S(1)}) custom-call(s32[1,256]{1,0:T(1,128)S(1)} %bitcast.18, bf16[9,256,256]{2,1,0:T(8,128)(2,1)S(1)} %shard_map.102.x_ref, bf16[128,256]{1,0:T(8,128)(2,1)S(1)} %collective-permute-done.above_ref, ...), custom_call_target="tpu_custom_call" | custom-call | flops 1207959552 | bytes 2490368 | tf_op jit(solution)/shard_map/pallas_call | solution.py:551
  17.6 3.7 %collective-permute-start.5 = (bf16[192,256]{1,0:T(8,128)(2,1)S(1)}, bf16[192,256]{1,0:T(8,128)(2,1)S(1)}, u32[]{:S(2)}, u32[]{:S(2)}) collective-permute-start(bf16[192,256]{1,0:T(8,128)(2,1)S(1)} %get-tuple-element.46.rest_0_), channel_id=1, source_target_pairs={{0,24},{8,16},{16,8},{24,0},{1,25},{9,17},{17,9},{25,1},{2,26},{10... | collective-permute-start | bytes 294920 | tf_op jit(solution)/shard_map/ppermute | solution.py:474
  21.3 0.8 %collective-permute-start.3 = (bf16[192,256]{1,0:T(8,128)(2,1)S(1)}, bf16[192,256]{1,0:T(8,128)(2,1)S(1)}, u32[]{:S(2)}, u32[]{:S(2)}) collective-permute-start(bf16[192,256]{1,0:T(8,128)(2,1)S(1)} %get-tuple-element.46.rest_0_), channel_id=1, source_target_pairs={{0,8},{8,0},{16,24},{24,16},{1,9},{9,1},{17,25},{25,17},{2,10},{10... | collective-permute-start | bytes 294920 | tf_op jit(solution)/shard_map/ppermute | solution.py:474
  22.8 1.9 %shard_map.100 = (f32[768,256]{1,0:T(8,128)S(1)}, f32[768,256]{1,0:T(8,128)S(1)}, bf16[192,1024]{1,0:T(8,128)(2,1)S(1)}, bf16[1024,768]{1,0:T(8,128)(2,1)S(1)}, ...) custom-call(s32[1]{0:T(128)} %bitcast.lev_ref._, ...), custom_call_target="tpu_custom_call" | custom-call | flops 603979776 | bytes 28049408 | tf_op jit(solution)/shard_map/pallas_call | solution.py:564
  24.7 5.4 %collective-permute-done.4.rest_2_ = bf16[192,256]{1,0:T(8,128)(2,1)S(1)} collective-permute-done((bf16[192,256]{1,0:T(8,128)(2,1)S(1)}, bf16[192,256]{1,0:T(8,128)(2,1)S(1)}, u32[]{:S(2)}, u32[]{:S(2)}) %collective-permute-start.4) | collective-permute-done | bytes 98336 | tf_op jit(solution)/shard_map/ppermute | solution.py:474
  30.1 3.3 %shard_map.104 = (bf16[9,64,256]{2,1,0:T(8,128)(2,1)S(1)}, bf16[9,64,256]{2,1,0:T(8,128)(2,1)S(1)}, bf16[9,64,256]{2,1,0:T(8,128)(2,1)S(1)}, bf16[9,64,256]{2,1,0:T(8,128)(2,1)S(1)}) custom-call(s32[1]{0:T(128)} %bitcast.lev_ref._, bf16[1024,768]{1,0:T(8,128)(2,1)S(1)} %copy-done, bf16[192,1024]{1,0:T(8,128)(2,1)S(1)} %get-tuple-element.35.innert_ref, ...), custom_call_target="tpu_custom_call" | custom-call | flops 2415919104 | bytes 4718592 | tf_op jit(solution)/shard_map/pallas_call | solution.py:587
  33.4 3.5 %collective-permute-start.13 = (bf16[9,64,256]{2,1,0:T(8,128)(2,1)S(1)}, bf16[9,64,256]{2,1,0:T(8,128)(2,1)S(1)}, u32[]{:S(2)}, u32[]{:S(2)}) collective-permute-start(bf16[9,64,256]{2,1,0:T(8,128)(2,1)S(1)} %get-tuple-element.49.rest_2_), channel_id=1, source_target_pairs={{0,16},{24,8},{1,17},{25,9},{2,18},{26,10},{3,19},{27,11},{4,20},{... | collective-permute-start | bytes 884744 | tf_op jit(solution)/shard_map/ppermute | solution.py:615
  36.9 0.7 collective-permute-start.12
  37.6 5.1 %collective-permute-done.11.got_ref.rest_3_ = bf16[9,64,256]{2,1,0:T(8,128)(2,1)S(1)} collective-permute-done((bf16[9,64,256]{2,1,0:T(8,128)(2,1)S(1)}, bf16[9,64,256]{2,1,0:T(8,128)(2,1)S(1)}, u32[]{:S(2)}, u32[]{:S(2)}) %collective-permute-start.11) | collective-permute-done | bytes 294944 | tf_op jit(solution)/shard_map/ppermute | solution.py:613
  44.7 3.7 %collective-permute-done.6.left_ref.right_ref = bf16[4,64,128]{2,1,0:T(8,128)(2,1)S(1)} collective-permute-done((bf16[4,64,128]{2,1,0:T(8,128)(2,1)S(1)}, bf16[4,64,128]{2,1,0:T(8,128)(2,1)S(1)}, u32[]{:S(2)}, u32[]{:S(2)}) %collective-permute-start.6) | collective-permute-done | bytes 65568 | tf_op jit(solution)/shard_map/ppermute | solution.py:470
  48.5 1.3 %collective-permute-start.7 = (bf16[4,64,128]{2,1,0:T(8,128)(2,1)S(1)}, bf16[4,64,128]{2,1,0:T(8,128)(2,1)S(1)}, u32[]{:S(2)}, u32[]{:S(2)}) collective-permute-start(bf16[4,64,128]{2,1,0:T(8,128)(2,1)S(1)} %get-tuple-element.53), channel_id=1, source_target_pairs={{0,2},{2,4},{4,6},{1,3},{3,5},{5,7},{8,10},{10,12},{12,14},{9,11},... | collective-permute-start | bytes 196616 | tf_op jit(solution)/shard_map/ppermute | solution.py:470
  49.8 1.3 %collective-permute-start.8 = (bf16[4,64,128]{2,1,0:T(8,128)(2,1)S(1)}, bf16[4,64,128]{2,1,0:T(8,128)(2,1)S(1)}, u32[]{:S(2)}, u32[]{:S(2)}) collective-permute-start(bf16[4,64,128]{2,1,0:T(8,128)(2,1)S(1)} %get-tuple-element.54), channel_id=1, source_target_pairs={{2,0},{4,2},{6,4},{3,1},{5,3},{7,5},{10,8},{12,10},{14,12},{11,9},... | collective-permute-start | bytes 196616 | tf_op jit(solution)/shard_map/ppermute | solution.py:470
  51.1 3.5 %collective-permute-done.8.bottom_ref = bf16[4,64,128]{2,1,0:T(8,128)(2,1)S(1)} collective-permute-done((bf16[4,64,128]{2,1,0:T(8,128)(2,1)S(1)}, bf16[4,64,128]{2,1,0:T(8,128)(2,1)S(1)}, u32[]{:S(2)}, u32[]{:S(2)}) %collective-permute-start.8) | collective-permute-done | bytes 65568 | tf_op jit(solution)/shard_map/ppermute | solution.py:470
  54.7 6.4 %collective-permute-done.9.got_ref = bf16[2,3,64,128]{3,2,1,0:T(8,128)(2,1)S(1)} collective-permute-done((bf16[2,3,64,128]{3,2,1,0:T(8,128)(2,1)S(1)}, bf16[2,3,64,128]{3,2,1,0:T(8,128)(2,1)S(1)}, u32[]{:S(2)}, u32[]{:S(2)}) %collective-permute-start.9) | collective-permute-done | bytes 98336 | tf_op jit(solution)/shard_map/ppermute | solution.py:474
  61.1 0.7 collective-permute-start.10
  61.8 5.0 %collective-permute-done.10.rest_1_ = bf16[3,64,128]{2,1,0:T(8,128)(2,1)S(1)} collective-permute-done((bf16[3,64,128]{2,1,0:T(8,128)(2,1)S(1)}, bf16[3,64,128]{2,1,0:T(8,128)(2,1)S(1)}, u32[]{:S(2)}, u32[]{:S(2)}) %collective-permute-start.10) | collective-permute-done | bytes 49184 | tf_op jit(solution)/shard_map/ppermute | solution.py:474
  66.8 2.3 %shard_map.110 = f32[64,32,128]{2,1,0:T(8,128)} custom-call(s32[1]{0:T(128)} %bitcast.lev_ref._, s32[1,256]{1,0:T(1,128)S(1)} %bitcast.21, bf16[64,32,128]{2,1,0:T(8,128)(2,1)S(1)} %get-tuple-element.32.own_ref, bf16[768,128]{1,0:T(8,128)(2,1)S(1)} %get-tuple-element.33.across_ref, bf16[3,64,128]{2,1,0:T(8,128)(2,1)S(1)} %get-tuple-element.57.rest_0_, ...), custom_call_target="tpu_custom_call" | custom-call | flops 150994944 | bytes 4194304 | tf_op jit(solution)/shard_map/pallas_call | solution.py:664
  (38 shorter events, 2.4 us)
Async XLA Ops:
  2.3 5.6 %collective-permute-start = (bf16[128,256]{1,0:T(8,128)(2,1)S(1)}, bf16[128,256]{1,0:T(8,128)(2,1)S(1)}, u32[]{:S(2)}, u32[]{:S(2)}) collective-permute-start(bf16[128,256]{1,0:T(8,128)(2,1)S(1)} %get-tuple-element.40), channel_id=1, source_target_pairs={{0,2},{2,4},{4,6},{1,3},{3,5},{5,7},{8,10},{10,12},{12,14},{9,11},... | collective-permute-start | bytes 196616 | tf_op jit(solution)/shard_map/ppermute | solution.py:470
  4.7 5.3 %collective-permute-start.1 = (bf16[128,256]{1,0:T(8,128)(2,1)S(1)}, bf16[128,256]{1,0:T(8,128)(2,1)S(1)}, u32[]{:S(2)}, u32[]{:S(2)}) collective-permute-start(bf16[128,256]{1,0:T(8,128)(2,1)S(1)} %get-tuple-element.41), channel_id=1, source_target_pairs={{2,0},{4,2},{6,4},{3,1},{5,3},{7,5},{10,8},{12,10},{14,12},{11,9},... | collective-permute-start | bytes 196616 | tf_op jit(solution)/shard_map/ppermute | solution.py:470
  6.1 5.6 %copy-start.5 = (s32[1,1,256]{2,1,0:T(1,128)S(1)}, s32[1,1,256]{2,1,0:T(1,128)}, u32[]{:S(2)}) copy-start(s32[1,1,256]{2,1,0:T(1,128)} %param.18) | copy-start | bytes 3076
  7.9 7.1 %copy-start.3 = (bf16[4,128,128]{2,1,0:T(8,128)(2,1)S(1)}, bf16[4,128,128]{2,1,0:T(8,128)(2,1)}, u32[]{:S(2)}) copy-start(bf16[4,128,128]{2,1,0:T(8,128)(2,1)} %mid_ref.3) | copy-start | bytes 393220
  7.9 7.1 %copy-start.4 = (bf16[4,48,128]{2,1,0:T(8,128)(2,1)S(1)}, bf16[4,48,128]{2,1,0:T(8,128)(2,1)}, u32[]{:S(2)}) copy-start(bf16[4,48,128]{2,1,0:T(8,128)(2,1)} %outw_ref.3) | copy-start | bytes 147460
  10.1 4.9 %collective-permute-start.2 = (bf16[2,34,256]{2,1,0:T(8,128)(2,1)S(1)}, bf16[2,34,256]{2,1,0:T(8,128)(2,1)S(1)}, u32[]{:S(2)}, u32[]{:S(2)}) collective-permute-start(bf16[2,34,256]{2,1,0:T(8,128)(2,1)S(1)} %pad_maximum_fusion), channel_id=1, source_target_pairs={{0,1},{1,0},{2,3},{3,2},{4,5},{5,4},{6,7},{7,6},{8,9},{9,8},{10,11... | collective-permute-start | bytes 104456 | tf_op jit(solution)/shard_map/ppermute | solution.py:470
  15.0 7.7 %copy-start.6 = (f32[768]{0:T(1024)S(1)}, f32[768]{0:T(1024)}, u32[]{:S(2)}) copy-start(f32[768]{0:T(1024)} %param.17) | copy-start | bytes 9220
  15.0 7.7 %copy-start = (bf16[1024,768]{1,0:T(8,128)(2,1)S(1)}, bf16[1024,768]{1,0:T(8,128)(2,1)}, u32[]{:S(2)}) copy-start(bf16[1024,768]{1,0:T(8,128)(2,1)} %inner_ref.3) | copy-start | bytes 4718596
  15.0 7.7 %copy-start.1 = (bf16[768,1024]{1,0:T(8,128)(2,1)S(1)}, bf16[768,1024]{1,0:T(8,128)(2,1)}, u32[]{:S(2)}) copy-start(bf16[768,1024]{1,0:T(8,128)(2,1)} %outer_ref.3) | copy-start | bytes 4718596
  15.1 7.7 %copy-start.2 = (f32[1,1,256,768]{3,2,1,0:T(8,128)S(1)}, f32[1,1,256,768]{3,2,1,0:T(8,128)}, u32[]{:S(2)}) copy-start(f32[1,1,256,768]{3,2,1,0:T(8,128)} %param.16) | copy-start | bytes 2359300
  17.6 7.1 %collective-permute-start.5 = (bf16[192,256]{1,0:T(8,128)(2,1)S(1)}, bf16[192,256]{1,0:T(8,128)(2,1)S(1)}, u32[]{:S(2)}, u32[]{:S(2)}) collective-permute-start(bf16[192,256]{1,0:T(8,128)(2,1)S(1)} %get-tuple-element.46.rest_0_), channel_id=1, source_target_pairs={{0,24},{8,16},{16,8},{24,0},{1,25},{9,17},{17,9},{25,1},{2,26},{10... | collective-permute-start | bytes 294920 | tf_op jit(solution)/shard_map/ppermute | solution.py:474
  21.3 8.8 %collective-permute-start.4 = (bf16[192,256]{1,0:T(8,128)(2,1)S(1)}, bf16[192,256]{1,0:T(8,128)(2,1)S(1)}, u32[]{:S(2)}, u32[]{:S(2)}) collective-permute-start(bf16[192,256]{1,0:T(8,128)(2,1)S(1)} %get-tuple-element.46.rest_0_), channel_id=1, source_target_pairs={{0,16},{8,24},{16,0},{24,8},{1,17},{9,25},{17,1},{25,9},{2,18},{10... | collective-permute-start | bytes 294920 | tf_op jit(solution)/shard_map/ppermute | solution.py:474
  21.3 8.8 %collective-permute-start.3 = (bf16[192,256]{1,0:T(8,128)(2,1)S(1)}, bf16[192,256]{1,0:T(8,128)(2,1)S(1)}, u32[]{:S(2)}, u32[]{:S(2)}) collective-permute-start(bf16[192,256]{1,0:T(8,128)(2,1)S(1)} %get-tuple-element.46.rest_0_), channel_id=1, source_target_pairs={{0,8},{8,0},{16,24},{24,16},{1,9},{9,1},{17,25},{25,17},{2,10},{10... | collective-permute-start | bytes 294920 | tf_op jit(solution)/shard_map/ppermute | solution.py:474
  33.3 9.4 %collective-permute-start.11 = (bf16[9,64,256]{2,1,0:T(8,128)(2,1)S(1)}, bf16[9,64,256]{2,1,0:T(8,128)(2,1)S(1)}, u32[]{:S(2)}, u32[]{:S(2)}) collective-permute-start(bf16[9,64,256]{2,1,0:T(8,128)(2,1)S(1)} %get-tuple-element.48.rest_1_), channel_id=1, source_target_pairs={{0,8},{8,0},{16,24},{24,16},{1,9},{9,1},{17,25},{25,17},{2,10},{10... | collective-permute-start | bytes 884744 | tf_op jit(solution)/shard_map/ppermute | solution.py:613
  33.4 33.4 %collective-permute-start.13 = (bf16[9,64,256]{2,1,0:T(8,128)(2,1)S(1)}, bf16[9,64,256]{2,1,0:T(8,128)(2,1)S(1)}, u32[]{:S(2)}, u32[]{:S(2)}) collective-permute-start(bf16[9,64,256]{2,1,0:T(8,128)(2,1)S(1)} %get-tuple-element.49.rest_2_), channel_id=1, source_target_pairs={{0,16},{24,8},{1,17},{25,9},{2,18},{26,10},{3,19},{27,11},{4,20},{... | collective-permute-start | bytes 884744 | tf_op jit(solution)/shard_map/ppermute | solution.py:615
  36.9 29.9 %collective-permute-start.12 = (bf16[9,64,256]{2,1,0:T(8,128)(2,1)S(1)}, bf16[9,64,256]{2,1,0:T(8,128)(2,1)S(1)}, u32[]{:S(2)}, u32[]{:S(2)}) collective-permute-start(bf16[9,64,256]{2,1,0:T(8,128)(2,1)S(1)} %get-tuple-element.49.rest_2_), channel_id=1, source_target_pairs={{8,16},{16,8},{9,17},{17,9},{10,18},{18,10},{11,19},{19,11},{12,20... | collective-permute-start | bytes 884744 | tf_op jit(solution)/shard_map/ppermute | solution.py:614
  42.8 24.0 %collective-permute-start.14 = (bf16[9,64,256]{2,1,0:T(8,128)(2,1)S(1)}, bf16[9,64,256]{2,1,0:T(8,128)(2,1)S(1)}, u32[]{:S(2)}, u32[]{:S(2)}) collective-permute-start(bf16[9,64,256]{2,1,0:T(8,128)(2,1)S(1)} %shard_map.109), channel_id=1, source_target_pairs={{0,8},{8,24},{24,16},{16,0},{1,9},{9,25},{25,17},{17,1},{2,10},{10... | collective-permute-start | bytes 884744 | tf_op jit(solution)/shard_map/ppermute | solution.py:619
  44.0 4.3 %collective-permute-start.6 = (bf16[4,64,128]{2,1,0:T(8,128)(2,1)S(1)}, bf16[4,64,128]{2,1,0:T(8,128)(2,1)S(1)}, u32[]{:S(2)}, u32[]{:S(2)}) collective-permute-start(bf16[4,64,128]{2,1,0:T(8,128)(2,1)S(1)} %get-tuple-element.52), channel_id=1, source_target_pairs={{0,1},{1,0},{2,3},{3,2},{4,5},{5,4},{6,7},{7,6},{8,9},{9,8},{10,11... | collective-permute-start | bytes 196616 | tf_op jit(solution)/shard_map/ppermute | solution.py:470
  48.5 2.6 %collective-permute-start.7 = (bf16[4,64,128]{2,1,0:T(8,128)(2,1)S(1)}, bf16[4,64,128]{2,1,0:T(8,128)(2,1)S(1)}, u32[]{:S(2)}, u32[]{:S(2)}) collective-permute-start(bf16[4,64,128]{2,1,0:T(8,128)(2,1)S(1)} %get-tuple-element.53), channel_id=1, source_target_pairs={{0,2},{2,4},{4,6},{1,3},{3,5},{5,7},{8,10},{10,12},{12,14},{9,11},... | collective-permute-start | bytes 196616 | tf_op jit(solution)/shard_map/ppermute | solution.py:470
  49.8 4.8 %collective-permute-start.8 = (bf16[4,64,128]{2,1,0:T(8,128)(2,1)S(1)}, bf16[4,64,128]{2,1,0:T(8,128)(2,1)S(1)}, u32[]{:S(2)}, u32[]{:S(2)}) collective-permute-start(bf16[4,64,128]{2,1,0:T(8,128)(2,1)S(1)} %get-tuple-element.54), channel_id=1, source_target_pairs={{2,0},{4,2},{6,4},{3,1},{5,3},{7,5},{10,8},{12,10},{14,12},{11,9},... | collective-permute-start | bytes 196616 | tf_op jit(solution)/shard_map/ppermute | solution.py:470
  54.6 6.4 %collective-permute-start.9 = (bf16[2,3,64,128]{3,2,1,0:T(8,128)(2,1)S(1)}, bf16[2,3,64,128]{3,2,1,0:T(8,128)(2,1)S(1)}, u32[]{:S(2)}, u32[]{:S(2)}) collective-permute-start(bf16[2,3,64,128]{3,2,1,0:T(8,128)(2,1)S(1)} %get-tuple-element.56), channel_id=1, source_target_pairs={{0,8},{8,0},{16,24},{24,16},{1,9},{9,1},{17,25},{25,17},{2,10},{10... | collective-permute-start | bytes 294920 | tf_op jit(solution)/shard_map/ppermute | solution.py:474
  61.1 5.7 %collective-permute-start.10 = (bf16[3,64,128]{2,1,0:T(8,128)(2,1)S(1)}, bf16[3,64,128]{2,1,0:T(8,128)(2,1)S(1)}, u32[]{:S(2)}, u32[]{:S(2)}) collective-permute-start(bf16[3,64,128]{2,1,0:T(8,128)(2,1)S(1)} %get-tuple-element.58), channel_id=1, source_target_pairs={{0,16},{8,24},{16,0},{24,8},{1,17},{9,25},{17,1},{25,9},{2,18},{10... | collective-permute-start | bytes 147464 | tf_op jit(solution)/shard_map/ppermute | solution.py:474

commit v9 on v8

--- a/solution.py
+++ b/solution.py
@@ -408,9 +408,17 @@
     out_ref[...] = (block_ref[...].astype(F32) + got_ref[...].astype(F32) * keep).astype(BF16)
 
 
-def final_kernel(rows, cols, count, edges, lev_ref, index_ref, own_ref, across_ref, *rest):
-    rims, own, relayed = rest[:edges], rest[edges], rest[edges + 1]
-    parts = rest[edges + 2 : -5]
+def partial_kernel(count, lev_ref, own_ref, relayed_ref, *rest):
+    parts, out_ref = rest[:-1], rest[-1]
+    keep = jnp.where(relays(lev_ref[0], count), 0.0, 1.0)
+    total = own_ref[...].astype(F32) + relayed_ref[...].astype(F32) * keep
+    for block in parts:
+        total = total + block[...].astype(F32)
+    out_ref[...] = total
+
+
+def final_kernel(rows, cols, edges, lev_ref, index_ref, own_ref, across_ref, *rest):
+    rims, early, last = rest[:edges], rest[edges], rest[edges + 1]
     out_ref, sum_ref, edge_ref, wait_ref, sems = rest[-5:]
     portion = out_ref.shape[0]
     row, _ = split(index_ref[...], cols)
@@ -429,15 +437,11 @@
     line_of = lax.broadcasted_iota(jnp.int32, (rows, 128), 0)
     picks = (place_of == line_of + 1) | (place_of == line_of + 65)
     high = lax.broadcasted_iota(jnp.int32, (rows, cols), 0)
-    keep = jnp.where(relays(lev_ref[0], count), 0.0, 1.0)
     step = sum_ref.shape[2]
     outs = []
     for i, c0 in enumerate(range(0, portion, step)):
         span = slice(c0, c0 + step)
-        total = own[:, span, :].astype(F32) + relayed[:, span, :].astype(F32) * keep
-        for block in parts:
-            total = total + block[:, span, :].astype(F32)
-        sum_ref[i] = total
+        sum_ref[i] = early[:, span, :] + last[:, span, :].astype(F32)
         lefts = []
         for c in range(step):
             pieces = []
@@ -661,10 +665,18 @@
         rims = [joined[0][0]]
         rims += [shift(joined[k], "lev", k)[0] for k in range(1, lev_count)]
 
+    early = call(
+        functools.partial(partial_kernel, lev_count),
+        jax.ShapeDtypeStruct((taps, portion, slots), F32),
+        [SM] + [VM] * (1 + len(parts)),
+        flops // 64,
+        8,
+    )(lev, patches[0], relayed, *parts[:-1])
+
     return call(
-        functools.partial(final_kernel, rows, cols, lev_count, len(rims)),
+        functools.partial(final_kernel, rows, cols, len(rims)),
         jax.ShapeDtypeStruct((portion, rows, cols), F32),
-        [SM, VM, VM, VM] + [VM] * (2 + len(parts) + len(rims)),
+        [SM, VM, VM, VM] + [VM] * (2 + len(rims)),
         flops // 4,
         16,
         scratch_shapes=[
@@ -674,7 +686,7 @@
             pltpu.SemaphoreType.DMA((portion // STEP,)),
         ],
         out_specs=HBM,
-    )(lev, index, mine, across, *rims, patches[0], relayed, *parts)
+    )(lev, index, mine, across, *rims, early, parts[-1])
 
 
 def solution(mesh):

time: 69.4 us -> 69.2 us (level)
    pallas_call x1 -> x2, Pallas kernels: 2.29 us -> 2.24 us  [the longest x1 2.09 us: steps(): call(functools.partial(final_kernel, rows, cols, len(rims)), jax.ShapeDty...]
where the time goes in v9:
time: 69.2 us; the launch traced here: 68.9 us
  waiting for transfers between devices  31 us (45%)
  starting transfers between devices  18.6 us (27%)
  Pallas kernels  16.5 us (24%)
  local copies, waits for them, and re-layouts  1.89 us (3%)
  between operations  0.95 us (1%)
    ppermute x5, waiting for transfers between devices, paired(): return lax.ppermute(x, 'lev', [(i, i ^ k) for i in range(4)])  16.6 us
    ppermute x6, waiting for transfers between devices, shift(): return lax.ppermute(x, axis, pairs)  9.28 us
    ppermute x6, starting transfers between devices, shift(): return lax.ppermute(x, axis, pairs)  8.48 us
    ppermute x5, starting transfers between devices, paired(): return lax.ppermute(x, 'lev', [(i, i ^ k) for i in range(4)])  5.21 us
    ppermute x1, waiting for transfers between devices, steps(): relayed = lax.ppermute(patches[1], 'lev', [(0, 1), (1, 0), (2, 3), (3, 2)])  5.12 us
    ppermute x1, starting transfers between devices, steps(): parts.append(lax.ppermute(patches[2], 'lev', [(0, 2), (3, 1)]))  3.5 us
    pallas_call x1, Pallas kernels, steps(): call(functools.partial(gather_kernel, rows, cols), jax.ShapeDtypeStruct((...  3.36 us
    pallas_call x1, Pallas kernels, steps(): call(functools.partial(column_kernel, lev_count), (patch_shape,) * lev_co...  3.26 us
  transfers between devices with their start and end apart: 15, of which 7 were waited for; matrix products, arithmetic and copies ran while one was open for 3% of the time, Pallas kernels for 9%

profile of v9, /device:TPU:0, one launch (start us, length us, event | category | flops | bytes accessed | tf_op | source)
XLA Modules:
  0.0 68.9 jit_solution(8930378739984391450)
XLA Ops:
  0.0 2.3 %shard_map.101 = (bf16[4096,256]{1,0:T(8,128)(2,1)S(1)}, bf16[128,256]{1,0:T(8,128)(2,1)S(1)}, bf16[128,256]{1,0:T(8,128)(2,1)S(1)}, bf16[2,32,256]{2,1,0:T(8,128)(2,1)S(1)}) custom-call(s32[1]{0:T(128)} %bitcast.lev_ref._, bf16[256,32,128]{2,1,0:T(8,128)(2,1)} %lat_ref.1), custom_call_target="tpu_custom_call" | custom-call | flops 150994944 | bytes 9043968 | tf_op jit(solution)/shard_map/pallas_call | solution.py:514
  2.3 2.4 %collective-permute-start = (bf16[128,256]{1,0:T(8,128)(2,1)S(1)}, bf16[128,256]{1,0:T(8,128)(2,1)S(1)}, u32[]{:S(2)}, u32[]{:S(2)}) collective-permute-start(bf16[128,256]{1,0:T(8,128)(2,1)S(1)} %get-tuple-element.40), channel_id=1, source_target_pairs={{0,2},{2,4},{4,6},{1,3},{3,5},{5,7},{8,10},{10,12},{12,14},{9,11},... | collective-permute-start | bytes 196616 | tf_op jit(solution)/shard_map/ppermute | solution.py:474
  4.7 1.3 %collective-permute-start.1 = (bf16[128,256]{1,0:T(8,128)(2,1)S(1)}, bf16[128,256]{1,0:T(8,128)(2,1)S(1)}, u32[]{:S(2)}, u32[]{:S(2)}) collective-permute-start(bf16[128,256]{1,0:T(8,128)(2,1)S(1)} %get-tuple-element.41), channel_id=1, source_target_pairs={{2,0},{4,2},{6,4},{3,1},{5,3},{7,5},{10,8},{12,10},{14,12},{11,9},... | collective-permute-start | bytes 196616 | tf_op jit(solution)/shard_map/ppermute | solution.py:474
  6.1 1.8 %copy.11 = bf16[9,4,128,256]{3,2,1,0:T(8,128)(2,1)S(1)} copy(bf16[9,4,128,256]{3,2,0,1:T(8,128)(2,1)} %bitcast.22) | data formatting | bytes 4718592 | tf_op jit(solution)/shard_map/transpose | solution.py:553
  7.9 2.1 %collective-permute-done.1.below_ref = bf16[128,256]{1,0:T(8,128)(2,1)S(1)} collective-permute-done((bf16[128,256]{1,0:T(8,128)(2,1)S(1)}, bf16[128,256]{1,0:T(8,128)(2,1)S(1)}, u32[]{:S(2)}, u32[]{:S(2)}) %collective-permute-start.1) | collective-permute-done | bytes 65568 | tf_op jit(solution)/shard_map/ppermute | solution.py:474
  10.1 1.6 %collective-permute-start.2 = (bf16[2,34,256]{2,1,0:T(8,128)(2,1)S(1)}, bf16[2,34,256]{2,1,0:T(8,128)(2,1)S(1)}, u32[]{:S(2)}, u32[]{:S(2)}) collective-permute-start(bf16[2,34,256]{2,1,0:T(8,128)(2,1)S(1)} %pad_maximum_fusion), channel_id=1, source_target_pairs={{0,1},{1,0},{2,3},{3,2},{4,5},{5,4},{6,7},{7,6},{8,9},{9,8},{10,11... | collective-permute-start | bytes 104456 | tf_op jit(solution)/shard_map/ppermute | solution.py:474
  11.6 3.4 %shard_map.102.x_ref = bf16[9,256,256]{2,1,0:T(8,128)(2,1)S(1)} custom-call(s32[1,256]{1,0:T(1,128)S(1)} %bitcast.16, s32[1,256]{1,0:T(1,128)S(1)} %bitcast.17, bf16[4096,256]{1,0:T(8,128)(2,1)S(1)} %get-tuple-element.39.tile_ref), custom_call_target="tpu_custom_call" | custom-call | flops 603979776 | bytes 4718592 | tf_op jit(solution)/shard_map/pallas_call | solution.py:542
  15.1 2.5 %shard_map.103 = (bf16[512,256]{1,0:T(8,128)(2,1)S(1)}, bf16[512,256]{1,0:T(8,128)(2,1)S(1)}, bf16[192,256]{1,0:T(8,128)(2,1)S(1)}) custom-call(s32[1,256]{1,0:T(1,128)S(1)} %bitcast.18, bf16[9,256,256]{2,1,0:T(8,128)(2,1)S(1)} %shard_map.102.x_ref, bf16[128,256]{1,0:T(8,128)(2,1)S(1)} %collective-permute-done.above_ref, ...), custom_call_target="tpu_custom_call" | custom-call | flops 1207959552 | bytes 2490368 | tf_op jit(solution)/shard_map/pallas_call | solution.py:555
  17.6 3.7 %collective-permute-start.5 = (bf16[192,256]{1,0:T(8,128)(2,1)S(1)}, bf16[192,256]{1,0:T(8,128)(2,1)S(1)}, u32[]{:S(2)}, u32[]{:S(2)}) collective-permute-start(bf16[192,256]{1,0:T(8,128)(2,1)S(1)} %get-tuple-element.46.rest_0_), channel_id=1, source_target_pairs={{0,24},{8,16},{16,8},{24,0},{1,25},{9,17},{17,9},{25,1},{2,26},{10... | collective-permute-start | bytes 294920 | tf_op jit(solution)/shard_map/ppermute | solution.py:478
  21.3 0.8 %collective-permute-start.3 = (bf16[192,256]{1,0:T(8,128)(2,1)S(1)}, bf16[192,256]{1,0:T(8,128)(2,1)S(1)}, u32[]{:S(2)}, u32[]{:S(2)}) collective-permute-start(bf16[192,256]{1,0:T(8,128)(2,1)S(1)} %get-tuple-element.46.rest_0_), channel_id=1, source_target_pairs={{0,8},{8,0},{16,24},{24,16},{1,9},{9,1},{17,25},{25,17},{2,10},{10... | collective-permute-start | bytes 294920 | tf_op jit(solution)/shard_map/ppermute | solution.py:478
  22.8 1.9 %shard_map.100 = (f32[768,256]{1,0:T(8,128)S(1)}, f32[768,256]{1,0:T(8,128)S(1)}, bf16[192,1024]{1,0:T(8,128)(2,1)S(1)}, bf16[1024,768]{1,0:T(8,128)(2,1)S(1)}, ...) custom-call(s32[1]{0:T(128)} %bitcast.lev_ref._, ...), custom_call_target="tpu_custom_call" | custom-call | flops 603979776 | bytes 28049408 | tf_op jit(solution)/shard_map/pallas_call | solution.py:568
  24.7 5.4 %collective-permute-done.4.rest_2_ = bf16[192,256]{1,0:T(8,128)(2,1)S(1)} collective-permute-done((bf16[192,256]{1,0:T(8,128)(2,1)S(1)}, bf16[192,256]{1,0:T(8,128)(2,1)S(1)}, u32[]{:S(2)}, u32[]{:S(2)}) %collective-permute-start.4) | collective-permute-done | bytes 98336 | tf_op jit(solution)/shard_map/ppermute | solution.py:478
  30.1 3.3 %shard_map.104 = (bf16[9,64,256]{2,1,0:T(8,128)(2,1)S(1)}, bf16[9,64,256]{2,1,0:T(8,128)(2,1)S(1)}, bf16[9,64,256]{2,1,0:T(8,128)(2,1)S(1)}, bf16[9,64,256]{2,1,0:T(8,128)(2,1)S(1)}) custom-call(s32[1]{0:T(128)} %bitcast.lev_ref._, bf16[1024,768]{1,0:T(8,128)(2,1)S(1)} %copy-done, bf16[192,1024]{1,0:T(8,128)(2,1)S(1)} %get-tuple-element.35.innert_ref, ...), custom_call_target="tpu_custom_call" | custom-call | flops 2415919104 | bytes 4718592 | tf_op jit(solution)/shard_map/pallas_call | solution.py:591
  33.4 3.5 %collective-permute-start.13 = (bf16[9,64,256]{2,1,0:T(8,128)(2,1)S(1)}, bf16[9,64,256]{2,1,0:T(8,128)(2,1)S(1)}, u32[]{:S(2)}, u32[]{:S(2)}) collective-permute-start(bf16[9,64,256]{2,1,0:T(8,128)(2,1)S(1)} %get-tuple-element.49.rest_2_), channel_id=1, source_target_pairs={{0,16},{24,8},{1,17},{25,9},{2,18},{26,10},{3,19},{27,11},{4,20},{... | collective-permute-start | bytes 884744 | tf_op jit(solution)/shard_map/ppermute | solution.py:619
  36.9 0.7 collective-permute-start.12
  37.6 5.1 %collective-permute-done.11.relayed_ref.got_ref = bf16[9,64,256]{2,1,0:T(8,128)(2,1)S(1)} collective-permute-done((bf16[9,64,256]{2,1,0:T(8,128)(2,1)S(1)}, bf16[9,64,256]{2,1,0:T(8,128)(2,1)S(1)}, u32[]{:S(2)}, u32[]{:S(2)}) %collective-permute-start.11) | collective-permute-done | bytes 294944 | tf_op jit(solution)/shard_map/ppermute | solution.py:617
  44.7 3.7 %collective-permute-done.6.left_ref.right_ref = bf16[4,64,128]{2,1,0:T(8,128)(2,1)S(1)} collective-permute-done((bf16[4,64,128]{2,1,0:T(8,128)(2,1)S(1)}, bf16[4,64,128]{2,1,0:T(8,128)(2,1)S(1)}, u32[]{:S(2)}, u32[]{:S(2)}) %collective-permute-start.6) | collective-permute-done | bytes 65568 | tf_op jit(solution)/shard_map/ppermute | solution.py:474
  48.5 1.3 %collective-permute-start.7 = (bf16[4,64,128]{2,1,0:T(8,128)(2,1)S(1)}, bf16[4,64,128]{2,1,0:T(8,128)(2,1)S(1)}, u32[]{:S(2)}, u32[]{:S(2)}) collective-permute-start(bf16[4,64,128]{2,1,0:T(8,128)(2,1)S(1)} %get-tuple-element.53), channel_id=1, source_target_pairs={{0,2},{2,4},{4,6},{1,3},{3,5},{5,7},{8,10},{10,12},{12,14},{9,11},... | collective-permute-start | bytes 196616 | tf_op jit(solution)/shard_map/ppermute | solution.py:474
  49.8 1.3 %collective-permute-start.8 = (bf16[4,64,128]{2,1,0:T(8,128)(2,1)S(1)}, bf16[4,64,128]{2,1,0:T(8,128)(2,1)S(1)}, u32[]{:S(2)}, u32[]{:S(2)}) collective-permute-start(bf16[4,64,128]{2,1,0:T(8,128)(2,1)S(1)} %get-tuple-element.54), channel_id=1, source_target_pairs={{2,0},{4,2},{6,4},{3,1},{5,3},{7,5},{10,8},{12,10},{14,12},{11,9},... | collective-permute-start | bytes 196616 | tf_op jit(solution)/shard_map/ppermute | solution.py:474
  51.1 3.5 %collective-permute-done.8.bottom_ref = bf16[4,64,128]{2,1,0:T(8,128)(2,1)S(1)} collective-permute-done((bf16[4,64,128]{2,1,0:T(8,128)(2,1)S(1)}, bf16[4,64,128]{2,1,0:T(8,128)(2,1)S(1)}, u32[]{:S(2)}, u32[]{:S(2)}) %collective-permute-start.8) | collective-permute-done | bytes 65568 | tf_op jit(solution)/shard_map/ppermute | solution.py:474
  54.7 6.4 %collective-permute-done.9.got_ref = bf16[2,3,64,128]{3,2,1,0:T(8,128)(2,1)S(1)} collective-permute-done((bf16[2,3,64,128]{3,2,1,0:T(8,128)(2,1)S(1)}, bf16[2,3,64,128]{3,2,1,0:T(8,128)(2,1)S(1)}, u32[]{:S(2)}, u32[]{:S(2)}) %collective-permute-start.9) | collective-permute-done | bytes 98336 | tf_op jit(solution)/shard_map/ppermute | solution.py:478
  61.1 0.7 collective-permute-start.10
  62.0 4.9 %collective-permute-done.10.rest_1_ = bf16[3,64,128]{2,1,0:T(8,128)(2,1)S(1)} collective-permute-done((bf16[3,64,128]{2,1,0:T(8,128)(2,1)S(1)}, bf16[3,64,128]{2,1,0:T(8,128)(2,1)S(1)}, u32[]{:S(2)}, u32[]{:S(2)}) %collective-permute-start.10) | collective-permute-done | bytes 49184 | tf_op jit(solution)/shard_map/ppermute | solution.py:478
  66.8 2.1 %shard_map.111 = f32[64,32,128]{2,1,0:T(8,128)} custom-call(s32[1]{0:T(128)} %bitcast.lev_ref._, s32[1,256]{1,0:T(1,128)S(1)} %bitcast.21, bf16[64,32,128]{2,1,0:T(8,128)(2,1)S(1)} %get-tuple-element.32.own_ref, bf16[768,128]{1,0:T(8,128)(2,1)S(1)} %get-tuple-element.33.across_ref, bf16[3,64,128]{2,1,0:T(8,128)(2,1)S(1)} %get-tuple-element.57.rest_0_, ...), custom_call_target="tpu_custom_call" | custom-call | flops 150994944 | bytes 4194304 | tf_op jit(solution)/shard_map/pallas_call | solution.py:676
  (39 shorter events, 2.5 us)
Async XLA Ops:
  2.3 5.6 %collective-permute-start = (bf16[128,256]{1,0:T(8,128)(2,1)S(1)}, bf16[128,256]{1,0:T(8,128)(2,1)S(1)}, u32[]{:S(2)}, u32[]{:S(2)}) collective-permute-start(bf16[128,256]{1,0:T(8,128)(2,1)S(1)} %get-tuple-element.40), channel_id=1, source_target_pairs={{0,2},{2,4},{4,6},{1,3},{3,5},{5,7},{8,10},{10,12},{12,14},{9,11},... | collective-permute-start | bytes 196616 | tf_op jit(solution)/shard_map/ppermute | solution.py:474
  4.7 5.3 %collective-permute-start.1 = (bf16[128,256]{1,0:T(8,128)(2,1)S(1)}, bf16[128,256]{1,0:T(8,128)(2,1)S(1)}, u32[]{:S(2)}, u32[]{:S(2)}) collective-permute-start(bf16[128,256]{1,0:T(8,128)(2,1)S(1)} %get-tuple-element.41), channel_id=1, source_target_pairs={{2,0},{4,2},{6,4},{3,1},{5,3},{7,5},{10,8},{12,10},{14,12},{11,9},... | collective-permute-start | bytes 196616 | tf_op jit(solution)/shard_map/ppermute | solution.py:474
  6.1 5.6 %copy-start.5 = (s32[1,1,256]{2,1,0:T(1,128)S(1)}, s32[1,1,256]{2,1,0:T(1,128)}, u32[]{:S(2)}) copy-start(s32[1,1,256]{2,1,0:T(1,128)} %param.18) | copy-start | bytes 3076
  7.9 7.1 %copy-start.3 = (bf16[4,128,128]{2,1,0:T(8,128)(2,1)S(1)}, bf16[4,128,128]{2,1,0:T(8,128)(2,1)}, u32[]{:S(2)}) copy-start(bf16[4,128,128]{2,1,0:T(8,128)(2,1)} %mid_ref.3) | copy-start | bytes 393220
  7.9 7.1 %copy-start.4 = (bf16[4,48,128]{2,1,0:T(8,128)(2,1)S(1)}, bf16[4,48,128]{2,1,0:T(8,128)(2,1)}, u32[]{:S(2)}) copy-start(bf16[4,48,128]{2,1,0:T(8,128)(2,1)} %outw_ref.3) | copy-start | bytes 147460
  10.1 4.9 %collective-permute-start.2 = (bf16[2,34,256]{2,1,0:T(8,128)(2,1)S(1)}, bf16[2,34,256]{2,1,0:T(8,128)(2,1)S(1)}, u32[]{:S(2)}, u32[]{:S(2)}) collective-permute-start(bf16[2,34,256]{2,1,0:T(8,128)(2,1)S(1)} %pad_maximum_fusion), channel_id=1, source_target_pairs={{0,1},{1,0},{2,3},{3,2},{4,5},{5,4},{6,7},{7,6},{8,9},{9,8},{10,11... | collective-permute-start | bytes 104456 | tf_op jit(solution)/shard_map/ppermute | solution.py:474
  15.0 7.7 %copy-start.6 = (f32[768]{0:T(1024)S(1)}, f32[768]{0:T(1024)}, u32[]{:S(2)}) copy-start(f32[768]{0:T(1024)} %param.17) | copy-start | bytes 9220
  15.0 7.7 %copy-start = (bf16[1024,768]{1,0:T(8,128)(2,1)S(1)}, bf16[1024,768]{1,0:T(8,128)(2,1)}, u32[]{:S(2)}) copy-start(bf16[1024,768]{1,0:T(8,128)(2,1)} %inner_ref.3) | copy-start | bytes 4718596
  15.0 7.7 %copy-start.1 = (bf16[768,1024]{1,0:T(8,128)(2,1)S(1)}, bf16[768,1024]{1,0:T(8,128)(2,1)}, u32[]{:S(2)}) copy-start(bf16[768,1024]{1,0:T(8,128)(2,1)} %outer_ref.3) | copy-start | bytes 4718596
  15.1 7.7 %copy-start.2 = (f32[1,1,256,768]{3,2,1,0:T(8,128)S(1)}, f32[1,1,256,768]{3,2,1,0:T(8,128)}, u32[]{:S(2)}) copy-start(f32[1,1,256,768]{3,2,1,0:T(8,128)} %param.16) | copy-start | bytes 2359300
  17.6 7.1 %collective-permute-start.5 = (bf16[192,256]{1,0:T(8,128)(2,1)S(1)}, bf16[192,256]{1,0:T(8,128)(2,1)S(1)}, u32[]{:S(2)}, u32[]{:S(2)}) collective-permute-start(bf16[192,256]{1,0:T(8,128)(2,1)S(1)} %get-tuple-element.46.rest_0_), channel_id=1, source_target_pairs={{0,24},{8,16},{16,8},{24,0},{1,25},{9,17},{17,9},{25,1},{2,26},{10... | collective-permute-start | bytes 294920 | tf_op jit(solution)/shard_map/ppermute | solution.py:478
  21.3 8.8 %collective-permute-start.4 = (bf16[192,256]{1,0:T(8,128)(2,1)S(1)}, bf16[192,256]{1,0:T(8,128)(2,1)S(1)}, u32[]{:S(2)}, u32[]{:S(2)}) collective-permute-start(bf16[192,256]{1,0:T(8,128)(2,1)S(1)} %get-tuple-element.46.rest_0_), channel_id=1, source_target_pairs={{0,16},{8,24},{16,0},{24,8},{1,17},{9,25},{17,1},{25,9},{2,18},{10... | collective-permute-start | bytes 294920 | tf_op jit(solution)/shard_map/ppermute | solution.py:478
  21.3 8.8 %collective-permute-start.3 = (bf16[192,256]{1,0:T(8,128)(2,1)S(1)}, bf16[192,256]{1,0:T(8,128)(2,1)S(1)}, u32[]{:S(2)}, u32[]{:S(2)}) collective-permute-start(bf16[192,256]{1,0:T(8,128)(2,1)S(1)} %get-tuple-element.46.rest_0_), channel_id=1, source_target_pairs={{0,8},{8,0},{16,24},{24,16},{1,9},{9,1},{17,25},{25,17},{2,10},{10... | collective-permute-start | bytes 294920 | tf_op jit(solution)/shard_map/ppermute | solution.py:478
  33.3 9.4 %collective-permute-start.11 = (bf16[9,64,256]{2,1,0:T(8,128)(2,1)S(1)}, bf16[9,64,256]{2,1,0:T(8,128)(2,1)S(1)}, u32[]{:S(2)}, u32[]{:S(2)}) collective-permute-start(bf16[9,64,256]{2,1,0:T(8,128)(2,1)S(1)} %get-tuple-element.48.rest_1_), channel_id=1, source_target_pairs={{0,8},{8,0},{16,24},{24,16},{1,9},{9,1},{17,25},{25,17},{2,10},{10... | collective-permute-start | bytes 884744 | tf_op jit(solution)/shard_map/ppermute | solution.py:617
  33.4 28.4 %collective-permute-start.13 = (bf16[9,64,256]{2,1,0:T(8,128)(2,1)S(1)}, bf16[9,64,256]{2,1,0:T(8,128)(2,1)S(1)}, u32[]{:S(2)}, u32[]{:S(2)}) collective-permute-start(bf16[9,64,256]{2,1,0:T(8,128)(2,1)S(1)} %get-tuple-element.49.rest_2_), channel_id=1, source_target_pairs={{0,16},{24,8},{1,17},{25,9},{2,18},{26,10},{3,19},{27,11},{4,20},{... | collective-permute-start | bytes 884744 | tf_op jit(solution)/shard_map/ppermute | solution.py:619
  36.9 24.9 %collective-permute-start.12 = (bf16[9,64,256]{2,1,0:T(8,128)(2,1)S(1)}, bf16[9,64,256]{2,1,0:T(8,128)(2,1)S(1)}, u32[]{:S(2)}, u32[]{:S(2)}) collective-permute-start(bf16[9,64,256]{2,1,0:T(8,128)(2,1)S(1)} %get-tuple-element.49.rest_2_), channel_id=1, source_target_pairs={{8,16},{16,8},{9,17},{17,9},{10,18},{18,10},{11,19},{19,11},{12,20... | collective-permute-start | bytes 884744 | tf_op jit(solution)/shard_map/ppermute | solution.py:618
  42.8 24.0 %collective-permute-start.14 = (bf16[9,64,256]{2,1,0:T(8,128)(2,1)S(1)}, bf16[9,64,256]{2,1,0:T(8,128)(2,1)S(1)}, u32[]{:S(2)}, u32[]{:S(2)}) collective-permute-start(bf16[9,64,256]{2,1,0:T(8,128)(2,1)S(1)} %shard_map.110), channel_id=1, source_target_pairs={{0,8},{8,24},{24,16},{16,0},{1,9},{9,25},{25,17},{17,1},{2,10},{10... | collective-permute-start | bytes 884744 | tf_op jit(solution)/shard_map/ppermute | solution.py:623
  44.0 4.3 %collective-permute-start.6 = (bf16[4,64,128]{2,1,0:T(8,128)(2,1)S(1)}, bf16[4,64,128]{2,1,0:T(8,128)(2,1)S(1)}, u32[]{:S(2)}, u32[]{:S(2)}) collective-permute-start(bf16[4,64,128]{2,1,0:T(8,128)(2,1)S(1)} %get-tuple-element.52), channel_id=1, source_target_pairs={{0,1},{1,0},{2,3},{3,2},{4,5},{5,4},{6,7},{7,6},{8,9},{9,8},{10,11... | collective-permute-start | bytes 196616 | tf_op jit(solution)/shard_map/ppermute | solution.py:474
  48.5 2.6 %collective-permute-start.7 = (bf16[4,64,128]{2,1,0:T(8,128)(2,1)S(1)}, bf16[4,64,128]{2,1,0:T(8,128)(2,1)S(1)}, u32[]{:S(2)}, u32[]{:S(2)}) collective-permute-start(bf16[4,64,128]{2,1,0:T(8,128)(2,1)S(1)} %get-tuple-element.53), channel_id=1, source_target_pairs={{0,2},{2,4},{4,6},{1,3},{3,5},{5,7},{8,10},{10,12},{12,14},{9,11},... | collective-permute-start | bytes 196616 | tf_op jit(solution)/shard_map/ppermute | solution.py:474
  49.8 4.8 %collective-permute-start.8 = (bf16[4,64,128]{2,1,0:T(8,128)(2,1)S(1)}, bf16[4,64,128]{2,1,0:T(8,128)(2,1)S(1)}, u32[]{:S(2)}, u32[]{:S(2)}) collective-permute-start(bf16[4,64,128]{2,1,0:T(8,128)(2,1)S(1)} %get-tuple-element.54), channel_id=1, source_target_pairs={{2,0},{4,2},{6,4},{3,1},{5,3},{7,5},{10,8},{12,10},{14,12},{11,9},... | collective-permute-start | bytes 196616 | tf_op jit(solution)/shard_map/ppermute | solution.py:474
  54.6 6.4 %collective-permute-start.9 = (bf16[2,3,64,128]{3,2,1,0:T(8,128)(2,1)S(1)}, bf16[2,3,64,128]{3,2,1,0:T(8,128)(2,1)S(1)}, u32[]{:S(2)}, u32[]{:S(2)}) collective-permute-start(bf16[2,3,64,128]{3,2,1,0:T(8,128)(2,1)S(1)} %get-tuple-element.56), channel_id=1, source_target_pairs={{0,8},{8,0},{16,24},{24,16},{1,9},{9,1},{17,25},{25,17},{2,10},{10... | collective-permute-start | bytes 294920 | tf_op jit(solution)/shard_map/ppermute | solution.py:478
  61.1 5.7 %collective-permute-start.10 = (bf16[3,64,128]{2,1,0:T(8,128)(2,1)S(1)}, bf16[3,64,128]{2,1,0:T(8,128)(2,1)S(1)}, u32[]{:S(2)}, u32[]{:S(2)}) collective-permute-start(bf16[3,64,128]{2,1,0:T(8,128)(2,1)S(1)} %get-tuple-element.58), channel_id=1, source_target_pairs={{0,16},{8,24},{16,0},{24,8},{1,17},{9,25},{17,1},{25,9},{2,18},{10... | collective-permute-start | bytes 147464 | tf_op jit(solution)/shard_map/ppermute | solution.py:478
